TPU v7x, 32 devices: a whole 2x2x4 slice. The times are simulated.
32 devices in a mesh: row: 8 (over z, y), col: 4 (over x, core).
Axes of the slice: x: 2, y: 2, z: 4, core: 2. Of those that a mesh axis runs over, the one named last changes fastest.
Arguments:
- perturbations: bfloat16 [32, 32, 256, 128], P('row', 'col'), may hold values from -6 to 6
- weights: bfloat16 [32, 32, 64, 128], P('row', 'col'), may hold values from -6 to 6
- pattern: int32 [32, 32, 9], P('row', 'col'), may hold values from 0 to 1, as said below
- taper_index: int32 [32, 32, 9], P('row', 'col'), may hold values from 0 to 15, as said below
- tapers: bfloat16 [16, 128, 128], replicated, may hold values from 0 to 1
Outputs:
- increment: float32 [32, 32, 64, 128], P('row', 'col')
Inputs may be any that keep to these rules, and one draw needn't show every extreme that they name: pattern[i, k] = pattern[i + o_k, 8 - k] and taper_index[i, k] = taper_index[i + o_k, 8 - k] wherever both blocks lie in the grid; pattern[i, 4] = 1; pattern is 0 for neighbours outside the grid. `taper_index`: the same symmetry as the pattern.
All inputs are finite; a program needn't handle non-finite values.
Results may differ from a plain program's by a relative error of at most 0.0029.
Values may be sent and summed in bfloat16 or wider, within the bound.
No kernel may reach another device: no remote copies, remote signals or barrier semaphores. Data moves between devices by JAX's collectives and lax.ppermute only.
A program may use at most 128 MiB of HBM per device.

v0:
```python
import jax
import jax.numpy as jnp
from jax import lax
from jax.sharding import PartitionSpec as P

MEMBERS = 256


def padded(block, sides, width):
    for axis, dim in sides:
        count = lax.axis_size(axis)
        forward = [(i, i + 1) for i in range(count - 1)]
        backward = [(target, source) for source, target in forward]
        low = lax.ppermute(
            lax.slice_in_dim(block, block.shape[dim] - width, None, axis=dim), axis, forward
        )
        high = lax.ppermute(lax.slice_in_dim(block, 0, width, axis=dim), axis, backward)
        block = jnp.concatenate([low, block, high], axis=dim)
    return block


def lookup(index_column, tapers):
    count = tapers.shape[0]
    cells = tapers.shape[1]
    lead = index_column.shape
    onehot = (index_column.reshape(-1, 1) == jnp.arange(count, dtype=jnp.int32)[None, :]).astype(
        jnp.bfloat16
    )
    table = jnp.dot(
        onehot, tapers.reshape(count, cells * cells), preferred_element_type=jnp.float32
    )
    return table.reshape(lead + (cells, cells))


def taper_for(index_column, tapers, k):
    rho = lookup(index_column, tapers)
    if k < 4:
        rho = jnp.swapaxes(rho, 2, 3)
    if k == 4:
        rho = 0.5 * (rho + jnp.swapaxes(rho, 2, 3))
    return rho


def block_after_taper(own_u, near_u, rho, live):
    scale = 1.0 / (MEMBERS - 1)
    gram = jnp.einsum("abmc,abmd->abcd", own_u, near_u, preferred_element_type=jnp.float32)
    factor = live.astype(jnp.float32) * scale
    return (rho * gram * factor[:, :, None, None]).astype(jnp.bfloat16)


def body(perturbations, weights, pattern, taper_index, tapers):
    rows, cols, members, cells = perturbations.shape
    columns = weights.shape[2]
    packed = jnp.concatenate([perturbations, weights], axis=2)
    blank = jnp.zeros((rows, cols, columns, cells), jnp.float32)
    running_sum = blank
    extended = padded(packed, (("row", 0), ("col", 1)), 1)
    for k in range(9):
        drow = k // 3 - 1
        dcol = k % 3 - 1
        near = extended[1 + drow : 1 + drow + rows, 1 + dcol : 1 + dcol + cols]
        live = pattern[:, :, k]

        def term(near=near, live=live, k=k):
            rho = taper_for(taper_index[:, :, k], tapers, k)
            tapered_matrix = block_after_taper(perturbations, near[:, :, :members], rho, live)
            return jnp.einsum(
                "abcd,abkd->abkc",
                tapered_matrix,
                near[:, :, members:],
                preferred_element_type=jnp.float32,
            )

        running_sum = running_sum + term()
    return running_sum


def solution(mesh):
    return jax.shard_map(
        body,
        mesh=mesh,
        in_specs=(
            P("row", "col", None, None),
            P("row", "col", None, None),
            P("row", "col", None),
            P("row", "col", None),
            P(),
        ),
        out_specs=P("row", "col", None, None),
        check_vma=False,
    )
```

profile of v0, /device:TPU:22, one launch (start us, length us, event | category | flops | bytes accessed | tf_op | source)
XLA Modules:
  0.0 95.6 jit_solution(409516040203479270)
XLA Ops:
  0.0 0.0 copy-start.3
  0.0 1.8 %constant_dynamic-update-slice_fusion.1 = bf16[4,8,320,128]{3,2,1,0:T(8,128)(2,1)S(1)} fusion(bf16[4,8,256,128]{3,2,1,0:T(8,128)(2,1)} %param.5), kind=kLoop, calls=%fused_computation.193 | loop fusion | bytes 4194304
  1.8 0.0 copy-done.3
  1.8 0.0 copy-start
  1.9 0.1 constant_dynamic-update-slice_fusion
  1.9 1.1 %fusion.204 = (bf16[1,8,320,128]{3,2,1,0:T(8,128)(2,1)}, bf16[1,8,320,128]{3,2,1,0:T(8,128)(2,1)}) fusion(bf16[4,8,320,128]{3,2,1,0:T(8,128)(2,1)S(1)} %constant_dynamic-update-slice_fusion), kind=kLoop, calls=%fused_computation.202 | loop fusion | bytes 2621440 | tf_op jit(solution)/shard_map/slice | solution.py:15
  3.1 3.4 %collective-permute-start = (bf16[1,8,320,128]{3,2,1,0:T(8,128)(2,1)}, bf16[1,8,320,128]{3,2,1,0:T(8,128)(2,1)S(1)}, u32[]{:S(2)}, u32[]{:S(2)}) collective-permute-start(bf16[1,8,320,128]{3,2,1,0:T(8,128)(2,1)} %get-tuple-element.27), channel_id=1, source_target_pairs={{0,4},{4,8},{8,12},{12,16},{16,20},{20,24},{24,28},{1,5},{5,9},{9,... | collective-permute-start | bytes 1966088 | tf_op jit(solution)/shard_map/ppermute | solution.py:14
  6.5 0.0 copy-start.7
  6.5 2.5 %collective-permute-start.1 = (bf16[1,8,320,128]{3,2,1,0:T(8,128)(2,1)}, bf16[1,8,320,128]{3,2,1,0:T(8,128)(2,1)}, u32[]{:S(2)}, u32[]{:S(2)}) collective-permute-start(bf16[1,8,320,128]{3,2,1,0:T(8,128)(2,1)} %get-tuple-element.28), channel_id=1, source_target_pairs={{4,0},{8,4},{12,8},{16,12},{20,16},{24,20},{28,24},{5,1},{9,5},{13... | collective-permute-start | bytes 1966088 | tf_op jit(solution)/shard_map/ppermute | solution.py:17
  9.1 0.0 copy-done
  9.1 2.0 %fusion.205 = f32[4,8,128,128]{3,2,1,0:T(8,128)} fusion(bf16[4,8,256,128]{3,2,1,0:T(8,128)(2,1)S(1)} %copy-done), kind=kOutput, calls=%fused_computation.203 | convolution fusion | flops 268435456 | bytes 4194304 | tf_op jit(solution)/shard_map/abmc,abmd->abcd/dot_general | solution.py:46
  11.1 0.0 copy-start.5
  11.1 0.0 copy-start.6
  11.1 0.0 copy-done.7
  11.1 0.3 copy.114
  11.5 0.1 copy.32
  11.6 0.3 copy-done.5
  11.9 0.0 copy-start.1
  11.9 0.8 slice_reduce_fusion.8
  12.6 0.0 copy-done.6
  12.6 0.2 multiply_reduce_fusion.8
  12.8 1.8 %fusion.161 = f32[4,8,128,128]{3,1,2,0:T(8,128)} fusion(bf16[128,128,16,1]{1,0,2,3:T(8,128)(2,1)S(1)} %bitcast.130, s32[4,8]{1,0:T(4,128)S(1)} %get-tuple-element.19), kind=kOutput, calls=%fused_computation.141 | convolution fusion | flops 16777728 | bytes 2621568 | tf_op jit(solution)/shard_map/dot_general | solution.py:29
  14.7 1.8 %fusion.159 = f32[4,8,128,128]{3,1,2,0:T(8,128)} fusion(bf16[128,128,16,1]{1,0,2,3:T(8,128)(2,1)S(1)} %bitcast.131, s32[4,8]{1,0:T(4,128)S(1)} %get-tuple-element.18), kind=kOutput, calls=%fused_computation.139 | convolution fusion | flops 16777728 | bytes 2621568 | tf_op jit(solution)/shard_map/dot_general | solution.py:29
  16.5 1.8 %fusion.157 = f32[4,8,128,128]{3,1,2,0:T(8,128)} fusion(bf16[128,128,16,1]{1,0,2,3:T(8,128)(2,1)S(1)} %bitcast.132, s32[4,8]{1,0:T(4,128)S(1)} %get-tuple-element.16), kind=kOutput, calls=%fused_computation.137 | convolution fusion | flops 16777728 | bytes 2621568 | tf_op jit(solution)/shard_map/dot_general | solution.py:29
  18.3 1.8 %fusion.155 = f32[4,8,128,128]{3,1,2,0:T(8,128)} fusion(bf16[128,128,16,1]{1,0,2,3:T(8,128)(2,1)S(1)} %bitcast.133, s32[4,8]{1,0:T(4,128)S(1)} %get-tuple-element.15), kind=kOutput, calls=%fused_computation.135 | convolution fusion | flops 16777728 | bytes 2621568 | tf_op jit(solution)/shard_map/dot_general | solution.py:29
  20.1 1.9 %fusion.151 = f32[4,8,128,128]{3,1,2,0:T(8,128)} fusion(bf16[128,128,16,1]{1,0,2,3:T(8,128)(2,1)S(1)} %bitcast.134, s32[4,8]{1,0:T(4,128)S(1)} %get-tuple-element.21), kind=kOutput, calls=%fused_computation.131 | convolution fusion | flops 16777728 | bytes 2621568 | tf_op jit(solution)/shard_map/dot_general | solution.py:29
  22.0 0.0 copy-done.1
  22.0 1.9 %fusion.163 = f32[4,8,128,128]{3,1,2,0:T(8,128)} fusion(bf16[128,128,16,1]{1,0,2,3:T(8,128)(2,1)S(1)} %bitcast.135, s32[4,8]{1,0:T(4,128)S(1)} %get-tuple-element.20), kind=kOutput, calls=%fused_computation.143 | convolution fusion | flops 16777728 | bytes 2621568 | tf_op jit(solution)/shard_map/dot_general | solution.py:29
  23.9 1.8 %fusion.101 = f32[4,8,128,128]{3,1,2,0:T(8,128)} fusion(bf16[2,128,8,128]{3,2,1,0:T(8,128)(2,1)S(1)} %bitcast.138, s32[4,8]{1,0:T(4,128)S(1)} %get-tuple-element.17), kind=kOutput, calls=%fused_computation.78 | convolution fusion | flops 16777728 | bytes 2621568 | tf_op jit(solution)/shard_map/dot_general | solution.py:29
  25.7 2.9 %copy.9 = f32[4,8,128,128]{2,1,3,0:T(8,128)} copy(f32[4,8,128,128]{3,1,2,0:T(8,128)} %fusion.101) | data formatting | bytes 4194304 | tf_op jit(solution)/shard_map/dot_general | solution.py:29
  28.6 0.0 copy-start.4
  28.6 4.4 %fusion.27 = bf16[4,8,128,128]{3,1,2,0:T(8,128)(2,1)S(1)} fusion(f32[4,8,128,128]{3,1,2,0:T(8,128)} %fusion.101, f32[4,8,128,128]{2,1,3,0:T(8,128)} %copy.9, f32[4,8,128,128]{3,2,1,0:T(8,128)} %fusion.205, f32[4,8]{1,0:T(4,128)S(1)} %get-tuple-element.8), kind=kLoop, calls=%fused_computation.36 | loop fusion | flops 2621440 | bytes 7340160 | tf_op jit(solution)/shard_map/convert_element_type | solution.py:48
  33.0 0.0 copy-done.4
  33.0 0.0 copy-start.2
  33.0 1.8 %convolution_bitcast_fusion = f32[4,8,64,128]{3,2,1,0:T(8,128)} fusion(bf16[4,8,64,128]{3,2,1,0:T(8,128)(2,1)S(1)} %copy-done.4, bf16[4,8,128,128]{3,1,2,0:T(8,128)(2,1)S(1)} %fusion.27), kind=kOutput, calls=%fused_computation.58 | convolution fusion | flops 67108864 | bytes 2621440 | tf_op jit(solution)/shard_map/abcd,abkd->abkc/dot_general | solution.py:67
  34.8 0.0 copy-done.2
  34.8 1.8 %fusion.153 = f32[4,8,128,128]{3,1,2,0:T(8,128)} fusion(bf16[128,128,16,1]{1,0,2,3:T(8,128)(2,1)S(1)} %bitcast.136, s32[4,8]{1,0:T(4,128)S(1)} %get-tuple-element.22), kind=kOutput, calls=%fused_computation.133 | convolution fusion | flops 16777728 | bytes 2621568 | tf_op jit(solution)/shard_map/dot_general | solution.py:29
  36.6 1.8 %fusion.165 = f32[4,8,128,128]{3,1,2,0:T(8,128)} fusion(bf16[128,128,16,1]{1,0,2,3:T(8,128)(2,1)S(1)} %bitcast.137, s32[4,8]{1,0:T(4,128)S(1)} %get-tuple-element.14), kind=kOutput, calls=%fused_computation.145 | convolution fusion | flops 16777728 | bytes 2621568 | tf_op jit(solution)/shard_map/dot_general | solution.py:29
  38.4 0.0 collective-permute-done
  38.4 0.0 collective-permute-done.1
  38.4 2.0 %pad_maximum_fusion.15 = (bf16[6,1,320,128]{3,2,1,0:T(8,128)(2,1)}, bf16[6,1,320,128]{3,2,1,0:T(8,128)(2,1)}) fusion(bf16[1,8,320,128]{3,2,1,0:T(8,128)(2,1)} %collective-permute-done.1, bf16[4,8,320,128]{3,2,1,0:T(8,128)(2,1)S(1)} %constant_dynamic-update-slice_fusion, bf16[1,8,320,128]{3,2,1,0:T(8,128)(2,1)S(1)} %collective-permute-done), kind=kLoop, calls=%fused_computation.130 | loop fusion | flops 983040 | bytes 4915200 | tf_op jit(solution)/shard_map/slice | solution.py:15
  40.4 1.9 %collective-permute-start.2 = (bf16[6,1,320,128]{3,2,1,0:T(8,128)(2,1)}, bf16[6,1,320,128]{3,2,1,0:T(8,128)(2,1)}, u32[]{:S(2)}, u32[]{:S(2)}) collective-permute-start(bf16[6,1,320,128]{3,2,1,0:T(8,128)(2,1)} %get-tuple-element.25), channel_id=1, source_target_pairs={{0,1},{1,2},{2,3},{4,5},{5,6},{6,7},{8,9},{9,10},{10,11},{12,13},{... | collective-permute-start | bytes 1474568 | tf_op jit(solution)/shard_map/ppermute | solution.py:14
  42.3 3.8 %collective-permute-start.3 = (bf16[6,1,320,128]{3,2,1,0:T(8,128)(2,1)}, bf16[6,1,320,128]{3,2,1,0:T(8,128)(2,1)}, u32[]{:S(2)}, u32[]{:S(2)}) collective-permute-start(bf16[6,1,320,128]{3,2,1,0:T(8,128)(2,1)} %get-tuple-element.26), channel_id=1, source_target_pairs={{1,0},{2,1},{3,2},{5,4},{6,5},{7,6},{9,8},{10,9},{11,10},{13,12},{... | collective-permute-start | bytes 1474568 | tf_op jit(solution)/shard_map/ppermute | solution.py:17
  46.1 4.5 %fusion.48 = f32[4,8,64,128]{3,2,1,0:T(8,128)} fusion(f32[4,8,128,128]{3,1,2,0:T(8,128)} %fusion.163, bf16[4,8,256,128]{3,2,1,0:T(8,128)(2,1)} %param.5, bf16[4,8,320,128]{3,2,1,0:T(8,128)(2,1)S(1)} %constant_dynamic-update-slice_fusion, bf16[1,8,320,128]{3,2,1,0:T(8,128)(2,1)S(1)} %collective-permute-done, f32[4,8]{1,0:T(4,128)S(1)} %get-tuple-element.11), kind=kOutput, calls=%fused_computation.49 | convolution fusion | flops 342360064 | bytes 8519808 | tf_op jit(solution)/shard_map/abcd,abkd->abkc/dot_general | solution.py:67
  50.6 5.0 %fusion.49 = f32[4,8,64,128]{3,2,1,0:T(8,128)} fusion(f32[4,8,128,128]{3,1,2,0:T(8,128)} %fusion.153, bf16[4,8,256,128]{3,2,1,0:T(8,128)(2,1)} %param.5, bf16[1,8,320,128]{3,2,1,0:T(8,128)(2,1)} %collective-permute-done.1, bf16[4,8,320,128]{3,2,1,0:T(8,128)(2,1)S(1)} %constant_dynamic-update-slice_fusion, f32[4,8]{1,0:T(4,128)S(1)} %get-tuple-element.13), kind=kOutput, calls=%fused_computation.50 | convolution fusion | flops 342360064 | bytes 8519808 | tf_op jit(solution)/shard_map/abcd,abkd->abkc/dot_general | solution.py:67
  55.6 0.0 collective-permute-done.2
  55.6 0.0 collective-permute-done.3
  55.7 5.3 %maximum_maximum_fusion = (bf16[6,9,320,128]{3,2,1,0:T(8,128)(2,1)}, bf16[6,9,320,128]{3,2,1,0:T(8,128)(2,1)}) fusion(bf16[1,8,320,128]{3,2,1,0:T(8,128)(2,1)} %collective-permute-done.1, bf16[4,8,320,128]{3,2,1,0:T(8,128)(2,1)S(1)} %constant_dynamic-update-slice_fusion, bf16[1,8,320,128]{3,2,1,0:T(8,128)(2,1)S(1)} %collective-permute-done, ...), kind=kLoop, calls=%fused_computation | loop fusion | flops 13271040 | bytes 13762560 | tf_op jit(solution)/shard_map/concatenate | solution.py:18
  61.0 5.3 %fusion.57 = f32[4,8,64,128]{3,2,1,0:T(8,128)} fusion(f32[4,8,128,128]{3,1,2,0:T(8,128)} %fusion.161, bf16[4,8,256,128]{3,2,1,0:T(8,128)(2,1)} %param.5, bf16[6,9,320,128]{3,2,1,0:T(8,128)(2,1)} %get-tuple-element.24, f32[4,8]{1,0:T(4,128)S(1)} %get-tuple-element.10, bf16[6,1,320,128]{3,2,1,0:T(8,128)(2,1)} %collective-permute-done.3, ...), kind=kOutput, calls=%fused_computation.53 | convolution fusion | flops 339214336 | bytes 11763840 | tf_op jit(solution)/shard_map/abcd,abkd->abkc/dot_general | solution.py:67
  66.3 5.5 %fusion.63 = f32[4,8,64,128]{3,2,1,0:T(8,128)} fusion(f32[4,8,128,128]{3,1,2,0:T(8,128)} %fusion.157, bf16[4,8,256,128]{3,2,1,0:T(8,128)(2,1)} %param.5, bf16[6,9,320,128]{3,2,1,0:T(8,128)(2,1)} %get-tuple-element.24, f32[4,8]{1,0:T(4,128)S(1)} %get-tuple-element.7, bf16[6,1,320,128]{3,2,1,0:T(8,128)(2,1)} %collective-permute-done.3, ...), kind=kOutput, calls=%fused_computation.55 | convolution fusion | flops 339214336 | bytes 11763840 | tf_op jit(solution)/shard_map/abcd,abkd->abkc/dot_general | solution.py:67
  71.8 5.2 %fusion.60 = f32[4,8,64,128]{3,2,1,0:T(8,128)} fusion(f32[4,8,128,128]{3,1,2,0:T(8,128)} %fusion.159, bf16[4,8,256,128]{3,2,1,0:T(8,128)(2,1)} %param.5, bf16[6,9,320,128]{3,2,1,0:T(8,128)(2,1)} %get-tuple-element.23, f32[4,8]{1,0:T(4,128)S(1)} %get-tuple-element.9, bf16[6,1,320,128]{3,2,1,0:T(8,128)(2,1)} %collective-permute-done.2, ...), kind=kOutput, calls=%fused_computation.54 | convolution fusion | flops 339214336 | bytes 11763840 | tf_op jit(solution)/shard_map/abcd,abkd->abkc/dot_general | solution.py:67
  76.9 5.6 %fusion.66 = f32[4,8,64,128]{3,2,1,0:T(8,128)} fusion(f32[4,8,128,128]{3,1,2,0:T(8,128)} %fusion.155, bf16[4,8,256,128]{3,2,1,0:T(8,128)(2,1)} %param.5, bf16[6,9,320,128]{3,2,1,0:T(8,128)(2,1)} %get-tuple-element.23, f32[4,8]{1,0:T(4,128)S(1)} %get-tuple-element.6, bf16[6,1,320,128]{3,2,1,0:T(8,128)(2,1)} %collective-permute-done.2, ...), kind=kOutput, calls=%fused_computation.56 | convolution fusion | flops 339214336 | bytes 11763840 | tf_op jit(solution)/shard_map/abcd,abkd->abkc/dot_general | solution.py:67
  82.5 5.5 %fusion.69 = f32[4,8,64,128]{3,2,1,0:T(8,128)} fusion(f32[4,8,128,128]{3,1,2,0:T(8,128)} %fusion.151, bf16[4,8,256,128]{3,2,1,0:T(8,128)(2,1)} %param.5, bf16[6,9,320,128]{3,2,1,0:T(8,128)(2,1)} %get-tuple-element.24, f32[4,8]{1,0:T(4,128)S(1)} %get-tuple-element.12, bf16[6,1,320,128]{3,2,1,0:T(8,128)(2,1)} %collective-permute-done.3, ...), kind=kOutput, calls=%fused_computation.57 | convolution fusion | flops 339214336 | bytes 11763840 | tf_op jit(solution)/shard_map/abcd,abkd->abkc/dot_general | solution.py:67
  88.0 7.6 %fusion.89 = f32[4,8,64,128]{3,2,1,0:T(8,128)} fusion(f32[4,8,64,128]{3,2,1,0:T(8,128)} %fusion.69, f32[4,8,64,128]{3,2,1,0:T(8,128)} %fusion.49, f32[4,8,64,128]{3,2,1,0:T(8,128)} %fusion.66, f32[4,8,64,128]{3,2,1,0:T(8,128)} %fusion.63, f32[4,8,64,128]{3,2,1,0:T(8,128)} %convolution_bitcast_fusion, f32[4,8,64,128]{3,2,1,0:T(8,128)} %fusion.60, ...), kind=kOutput, calls=%fused_computation.65 | convolution fusion | flops 341311488 | bytes 20152448 | tf_op jit(solution)/shard_map/abcd,abkd->abkc/dot_general | solution.py:67
Async XLA Ops:
  0.0 1.8 %copy-start.3 = (bf16[4,8,64,128]{3,2,1,0:T(8,128)(2,1)S(1)}, bf16[4,8,64,128]{3,2,1,0:T(8,128)(2,1)}, u32[]{:S(2)}) copy-start(bf16[4,8,64,128]{3,2,1,0:T(8,128)(2,1)} %param.6) | copy-start | bytes 1572868
  1.8 7.2 %copy-start = (bf16[4,8,256,128]{3,2,1,0:T(8,128)(2,1)S(1)}, bf16[4,8,256,128]{3,2,1,0:T(8,128)(2,1)}, u32[]{:S(2)}) copy-start(bf16[4,8,256,128]{3,2,1,0:T(8,128)(2,1)} %param.5) | copy-start | bytes 6291460
  3.1 35.3 %collective-permute-start = (bf16[1,8,320,128]{3,2,1,0:T(8,128)(2,1)}, bf16[1,8,320,128]{3,2,1,0:T(8,128)(2,1)S(1)}, u32[]{:S(2)}, u32[]{:S(2)}) collective-permute-start(bf16[1,8,320,128]{3,2,1,0:T(8,128)(2,1)} %get-tuple-element.27), channel_id=1, source_target_pairs={{0,4},{4,8},{8,12},{12,16},{16,20},{20,24},{24,28},{1,5},{5,9},{9,... | collective-permute-start | bytes 1966088 | tf_op jit(solution)/shard_map/ppermute | solution.py:14
  6.5 4.6 %copy-start.7 = (bf16[16,128,128]{2,1,0:T(8,128)(2,1)S(1)}, bf16[16,128,128]{2,1,0:T(8,128)(2,1)}, u32[]{:S(2)}) copy-start(bf16[16,128,128]{2,1,0:T(8,128)(2,1)} %param.9) | copy-start | bytes 1572868
  6.5 31.9 %collective-permute-start.1 = (bf16[1,8,320,128]{3,2,1,0:T(8,128)(2,1)}, bf16[1,8,320,128]{3,2,1,0:T(8,128)(2,1)}, u32[]{:S(2)}, u32[]{:S(2)}) collective-permute-start(bf16[1,8,320,128]{3,2,1,0:T(8,128)(2,1)} %get-tuple-element.28), channel_id=1, source_target_pairs={{4,0},{8,4},{12,8},{16,12},{20,16},{24,20},{28,24},{5,1},{9,5},{13... | collective-permute-start | bytes 1966088 | tf_op jit(solution)/shard_map/ppermute | solution.py:17
  11.1 0.7 copy-start.5
  11.1 1.5 %copy-start.6 = (s32[4,8,9]{2,1,0:T(8,128)S(1)}, s32[4,8,9]{2,1,0:T(8,128)}, u32[]{:S(2)}) copy-start(s32[4,8,9]{2,1,0:T(8,128)} %param.7) | copy-start | bytes 3460
  11.9 10.2 %copy-start.1 = (bf16[2,8,128,128]{3,2,1,0:T(8,128)(2,1)}, bf16[2,8,128,128]{3,2,1,0:T(8,128)(2,1)S(1)}, u32[]{:S(2)}) copy-start(bf16[2,8,128,128]{3,2,1,0:T(8,128)(2,1)S(1)} %copy.32) | copy-start | bytes 1572868
  28.6 4.4 %copy-start.4 = (bf16[4,8,64,128]{3,2,1,0:T(8,128)(2,1)S(1)}, bf16[4,8,64,128]{3,2,1,0:T(8,128)(2,1)}, u32[]{:S(2)}) copy-start(bf16[4,8,64,128]{3,2,1,0:T(8,128)(2,1)} %param.6) | copy-start | bytes 1572868
  33.0 1.8 %copy-start.2 = (bf16[2,8,128,128]{3,2,1,0:T(8,128)(2,1)S(1)}, bf16[2,8,128,128]{3,2,1,0:T(8,128)(2,1)}, u32[]{:S(2)}) copy-start(bf16[2,8,128,128]{3,2,1,0:T(8,128)(2,1)} %copy-done.1) | copy-start | bytes 1572868
  40.4 15.3 %collective-permute-start.2 = (bf16[6,1,320,128]{3,2,1,0:T(8,128)(2,1)}, bf16[6,1,320,128]{3,2,1,0:T(8,128)(2,1)}, u32[]{:S(2)}, u32[]{:S(2)}) collective-permute-start(bf16[6,1,320,128]{3,2,1,0:T(8,128)(2,1)} %get-tuple-element.25), channel_id=1, source_target_pairs={{0,1},{1,2},{2,3},{4,5},{5,6},{6,7},{8,9},{9,10},{10,11},{12,13},{... | collective-permute-start | bytes 1474568 | tf_op jit(solution)/shard_map/ppermute | solution.py:14
  42.3 13.3 %collective-permute-start.3 = (bf16[6,1,320,128]{3,2,1,0:T(8,128)(2,1)}, bf16[6,1,320,128]{3,2,1,0:T(8,128)(2,1)}, u32[]{:S(2)}, u32[]{:S(2)}) collective-permute-start(bf16[6,1,320,128]{3,2,1,0:T(8,128)(2,1)} %get-tuple-element.26), channel_id=1, source_target_pairs={{1,0},{2,1},{3,2},{5,4},{6,5},{7,6},{9,8},{10,9},{11,10},{13,12},{... | collective-permute-start | bytes 1474568 | tf_op jit(solution)/shard_map/ppermute | solution.py:17
where the time goes:
time: 97 us; the launch traced here: 95.6 us
  matrix products  64.5 us (66%)
  other arithmetic  11.9 us (12%)
  starting transfers between devices  11.7 us (12%)
  local copies, waits for them, and re-layouts  7.44 us (8%)
    dot_general x9, matrix products, term(): jnp.einsum('abcd,abkd->abkc', tapered_matrix, near[:, :, members:], prefe...  46 us
    dot_general x9, matrix products, lookup(): jnp.dot(onehot, tapers.reshape(count, cells * cells), preferred_element_t...  16.4 us
    ppermute x2, starting transfers between devices, padded(): lax.ppermute(lax.slice_in_dim(block, 0, width, axis=dim), axis, backward)  6.37 us
    ppermute x2, starting transfers between devices, padded(): lax.ppermute(lax.slice_in_dim(block, block.shape[dim] - width, None, axis...  5.33 us
    concatenate x1, other arithmetic, padded(): block = jnp.concatenate([low, block, high], axis=dim)  5.32 us
    convert_element_type x1, other arithmetic, block_after_taper(): return (rho * gram * factor[:, :, None, None]).astype(jnp.bfloat16)  4.36 us
    dot_general x1, local copies, waits for them, and re-layouts, lookup(): jnp.dot(onehot, tapers.reshape(count, cells * cells), preferred_element_t...  2.91 us
    unnamed x19, local copies, waits for them, and re-layouts  2.56 us
  transfers between devices with their start and end apart: 4, of which 0 were waited for; matrix products, arithmetic and copies ran while one was open for 40% of the time, Pallas kernels for 0%

commit v1 on v0

v1 whole, which is shorter than its diff:
```python
import jax
import jax.numpy as jnp
from jax import lax
from jax.experimental import pallas as pl
from jax.experimental.pallas import tpu as pltpu
from jax.sharding import PartitionSpec as P

MEMBERS = 256
SCALE = 1.0 / (MEMBERS - 1)
TN = (((0,), (0,)), ((), ()))
NT = (((1,), (1,)), ((), ()))
NN = (((1,), (0,)), ((), ()))
VMEM = pl.BlockSpec(memory_space=pltpu.VMEM)
SMEM = pl.BlockSpec(memory_space=pltpu.SMEM)
ANY = pl.BlockSpec(memory_space=pl.ANY)


def dot(a, b, dims):
    return lax.dot_general(a, b, dims, preferred_element_type=jnp.float32)


def cat(parts, axis):
    return parts[0] if len(parts) == 1 else jnp.concatenate(parts, axis=axis)


def tapered(gram, rho, live):
    factor = live.astype(jnp.float32) * SCALE
    return (rho.astype(jnp.float32) * gram * factor).astype(jnp.bfloat16)


def inner_kernel(u, w, live, index, tapers, out, sym, held):
    rows, cols, _, cells = u.shape
    for n in range(tapers.shape[0]):
        t = tapers[n].astype(jnp.float32)
        sym[n] = 0.5 * (t + t.T)

    def ahead(a, b, last):
        near = [(4, a, b)]
        if b + 1 < cols:
            near.append((5, a, b + 1))
        if not last:
            for k in (6, 7, 8):
                if 0 <= b + k - 7 < cols:
                    near.append((k, a + 1, b + k - 7))
        return near

    def row(a, last):
        for b in range(cols):
            near = ahead(a, b, last)
            gram = dot(u[a, b], cat([u[p, q] for _, p, q in near], 1), TN)
            for n, (k, _, _) in enumerate(near):
                at = index[a, b, k]
                rho = sym[at] if k == 4 else tapers[at]
                held[b, :, (k - 4) * cells : (k - 3) * cells] = tapered(
                    gram[:, n * cells : (n + 1) * cells], rho, live[a, b, k]
                )
        for b in range(cols):
            near = ahead(a, b, last)
            total = dot(
                cat([w[p, q] for _, p, q in near], 1),
                cat([held[b, :, (k - 4) * cells : (k - 3) * cells] for k, _, _ in near], 1),
                NT,
            )
            if b > 0:
                total += dot(w[a, b - 1], held[b - 1, :, cells : 2 * cells], NN)
            out[a, b] += total
            if not last:
                back = [(k, b - (k - 7)) for k in (6, 7, 8) if 0 <= b - (k - 7) < cols]
                out[a + 1, b] = dot(
                    cat([w[a, q] for _, q in back], 1),
                    cat([held[q, :, (k - 4) * cells : (k - 3) * cells] for k, q in back], 0),
                    NN,
                )

    out[0] = jnp.zeros_like(out[0])

    @pl.loop(0, rows - 1)
    def _(a):
        row(a, False)

    row(rows - 1, True)


def inner(u, w, live, index, tapers):
    rows, cols, members, cells = u.shape
    columns = w.shape[2]
    pairs = 5 * rows * cols
    return pl.pallas_call(
        inner_kernel,
        out_shape=jax.ShapeDtypeStruct((rows, cols, columns, cells), jnp.float32),
        in_specs=[VMEM, VMEM, SMEM, SMEM, VMEM],
        out_specs=VMEM,
        scratch_shapes=[
            pltpu.VMEM(tapers.shape, jnp.float32),
            pltpu.VMEM((cols, cells, 5 * cells), jnp.bfloat16),
        ],
        compiler_params=pltpu.CompilerParams(vmem_limit_bytes=24 << 20),
        cost_estimate=pl.CostEstimate(
            flops=2 * pairs * cells * cells * (members + 2 * columns),
            bytes_accessed=4 << 20,
            transcendentals=0,
        ),
        name="inner",
    )(u, w, live, index, tapers)


def above_kernel(s, u, w, left, right, live, index, side, tapers, back, held):
    cols, _, cells = s.shape
    members = u.shape[2]
    deep = members + w.shape[2]

    for c in range(cols):
        grams, weights, lives, rhos = [], [], [], []
        for k in (6, 7, 8):
            q = c + k - 7
            if q < 0:
                near, lively, at = left, side[0], side[1]
            elif q >= cols:
                near, lively, at = right, side[2], side[3]
            else:
                near, lively, at = None, live[0, q, 8 - k], index[0, q, 8 - k]
            grams.append(u[0, q] if near is None else near[0, :members])
            weights.append(w[0, q] if near is None else near[0, members:deep])
            lives.append(lively)
            rhos.append(tapers[at])
        gram = dot(s[c, :members], cat(grams, 1), TN)
        block = cat(
            [tapered(gram[:, n * cells : (n + 1) * cells], rhos[n], lives[n]) for n in range(3)], 1
        )
        held[c] = block
        back[c] = dot(cat(weights, 1), block, NT).astype(jnp.bfloat16)


def above(s, u, w, left, right, live, index, side, tapers):
    cols, _, cells = s.shape
    columns = w.shape[2]
    members = u.shape[2]
    return pl.pallas_call(
        above_kernel,
        out_shape=(
            jax.ShapeDtypeStruct((cols, columns, cells), jnp.bfloat16),
            jax.ShapeDtypeStruct((cols, cells, 3 * cells), jnp.bfloat16),
        ),
        in_specs=[VMEM, VMEM, VMEM, VMEM, VMEM, SMEM, SMEM, SMEM, VMEM],
        out_specs=(VMEM, VMEM),
        compiler_params=pltpu.CompilerParams(vmem_limit_bytes=24 << 20),
        cost_estimate=pl.CostEstimate(
            flops=2 * 3 * cols * cells * cells * (members + columns),
            bytes_accessed=2 << 20,
            transcendentals=0,
        ),
        name="above",
    )(s, u, w, left, right, live, index, side, tapers)


def outer_kernel(inc, held, s, corner, u, w, left, right, live, index, tapers, out):
    rows, cols, members, cells = u.shape
    deep = members + w.shape[2]
    last = cols - 1
    total = {}

    def add(a, q, value):
        total[a, q] = total[a, q] + value if (a, q) in total else value

    for q in range(cols):
        back = [(k, q - (k - 7)) for k in (6, 7, 8) if 0 <= q - (k - 7) < cols]
        sources = [s[c, members:deep] for _, c in back]
        blocks = [held[c, :, (k - 6) * cells : (k - 5) * cells] for k, c in back]
        for edge, k, far in ((0, 8, 0), (last, 6, 1)):
            if q == edge:
                gram = dot(corner[far, :members], u[0, q], TN)
                sources.append(corner[far, members:deep])
                blocks.append(tapered(gram, tapers[index[0, q, 8 - k]], live[0, q, 8 - k]))
        add(0, q, dot(cat(sources, 1), cat(blocks, 0), NN))

    for a in range(rows):
        near = [(5, a)] + ([(8, a + 1)] if a + 1 < rows else [])
        gram = dot(left[a, :members], cat([u[p, 0] for _, p in near], 1), TN)
        blocks = cat(
            [
                tapered(gram[:, n * cells : (n + 1) * cells], tapers[index[p, 0, 8 - k]], live[p, 0, 8 - k])
                for n, (k, p) in enumerate(near)
            ],
            1,
        )
        both = dot(left[a, members:deep], blocks, NN)
        for n, (_, p) in enumerate(near):
            add(p, 0, both[:, n * cells : (n + 1) * cells])
        gram = dot(u[a, last], cat([right[p, :members] for _, p in near], 1), TN)
        blocks = cat(
            [
                tapered(gram[:, n * cells : (n + 1) * cells], tapers[index[a, last, k]], live[a, last, k])
                for n, (k, _) in enumerate(near)
            ],
            1,
        )
        add(a, last, dot(cat([right[p, members:deep] for _, p in near], 1), blocks, NT))
        if a + 1 < rows:
            gram = dot(u[a, 0], left[a + 1, :members], TN)
            block = tapered(gram, tapers[index[a, 0, 6]], live[a, 0, 6])
            add(a, 0, dot(left[a + 1, members:deep], block, NT))
            gram = dot(right[a, :members], u[a + 1, last], TN)
            block = tapered(gram, tapers[index[a + 1, last, 2]], live[a + 1, last, 2])
            add(a + 1, last, dot(right[a, members:deep], block, NN))

    for a in range(rows):
        for q in range(cols):
            out[a, q] = inc[a, q] + total[a, q] if (a, q) in total else inc[a, q]


def outer(inc, held, s, corner, u, w, left, right, live, index, tapers):
    rows, cols, members, cells = u.shape
    columns = w.shape[2]
    return pl.pallas_call(
        outer_kernel,
        out_shape=jax.ShapeDtypeStruct(inc.shape, inc.dtype),
        in_specs=[VMEM] * 8 + [SMEM, SMEM, VMEM],
        out_specs=VMEM,
        input_output_aliases={0: 0},
        compiler_params=pltpu.CompilerParams(vmem_limit_bytes=24 << 20),
        cost_estimate=pl.CostEstimate(
            flops=2 * (6 * rows + 3 * cols) * cells * cells * (members + columns),
            bytes_accessed=4 << 20,
            transcendentals=0,
        ),
        name="outer",
    )(inc, held, s, corner, u, w, left, right, live, index, tapers)


def forward(axis):
    return [(i, i + 1) for i in range(lax.axis_size(axis) - 1)]


def backward(axis):
    return [(i + 1, i) for i in range(lax.axis_size(axis) - 1)]


def pack_row_kernel(u, w, out, sem):
    rows, _, members, _ = u.shape
    deep = members + w.shape[2]
    copies = [
        pltpu.make_async_copy(u.at[rows - 1], out.at[:, :members], sem.at[0]),
        pltpu.make_async_copy(w.at[rows - 1], out.at[:, members:deep], sem.at[1]),
    ]
    for copy in copies:
        copy.start()
    for copy in copies:
        copy.wait()


def pack_row(u, w):
    _, cols, members, cells = u.shape
    shape = (cols, members + w.shape[2], cells)
    return pl.pallas_call(
        pack_row_kernel,
        out_shape=jax.ShapeDtypeStruct(shape, u.dtype),
        in_specs=[ANY, ANY],
        out_specs=ANY,
        scratch_shapes=[pltpu.SemaphoreType.DMA((2,))],
        cost_estimate=pl.CostEstimate(flops=0, bytes_accessed=4 * cols * shape[1] * cells, transcendentals=0),
        name="pack_row",
    )(u, w)


def pack_columns_kernel(u, w, live, index, row, first, final, notes, sem):
    del row
    rows, cols, members, cells = u.shape
    deep = members + w.shape[2]
    copies = []
    for n, (out, b) in enumerate(((first, 0), (final, cols - 1))):
        copies.append(pltpu.make_async_copy(u.at[:, b], out.at[:, :members], sem.at[n, 0]))
        copies.append(pltpu.make_async_copy(w.at[:, b], out.at[:, members:deep], sem.at[n, 1]))
    for copy in copies:
        copy.start()
    for n, (out, b) in enumerate(((first, 0), (final, cols - 1))):
        for a in range(rows):
            lines = jnp.concatenate([live[a], index[a]], 0).astype(jnp.float32)
            blank = jnp.zeros((2 * cols, cells - live.shape[2]), jnp.float32)
            notes[n, a] = jnp.concatenate([lines, blank], 1).astype(jnp.bfloat16)
        copies.append(pltpu.make_async_copy(notes.at[n], out.at[:, deep:], sem.at[n, 2]))
        copies[-1].start()
    for copy in copies:
        copy.wait()


def pack_columns(u, w, live, index, row):
    rows, cols, members, cells = u.shape
    shape = (rows, members + w.shape[2] + 2 * cols, cells)
    return pl.pallas_call(
        pack_columns_kernel,
        out_shape=(jax.ShapeDtypeStruct(shape, u.dtype),) * 2,
        in_specs=[ANY, ANY, VMEM, VMEM, ANY],
        out_specs=(ANY, ANY),
        scratch_shapes=[pltpu.VMEM((2, rows, 2 * cols, cells), jnp.bfloat16), pltpu.SemaphoreType.DMA((2, 3))],
        cost_estimate=pl.CostEstimate(flops=0, bytes_accessed=8 * rows * shape[1] * cells, transcendentals=0),
        name="pack_columns",
    )(u, w, live, index, row)


def body(perturbations, weights, live, index, tapers):
    u, w = perturbations, weights
    rows, cols, members, cells = u.shape
    deep = members + w.shape[2]
    row = pack_row(u, w)
    s = lax.ppermute(row, "row", forward("row"))
    first, final = pack_columns(u, w, live, index, row)
    left = lax.ppermute(final, "col", forward("col"))
    right = lax.ppermute(first, "col", backward("col"))
    corner = lax.ppermute(
        jnp.stack([left[rows - 1, :deep], right[rows - 1, :deep]]), "row", forward("row")
    )
    inc = inner(u, w, live, index, tapers)
    side = jnp.stack(
        [
            left[0, deep + cols - 1, 2],
            left[0, deep + 2 * cols - 1, 2],
            right[0, deep, 0],
            right[0, deep + cols, 0],
        ]
    ).astype(jnp.int32)
    inc, s = lax.optimization_barrier((inc, s))
    back, held = above(s, u, w, left, right, live, index, side, tapers)
    back = lax.ppermute(back, "row", backward("row"))
    inc = outer(inc, held, s, corner, u, w, left, right, live, index, tapers)
    return lax.dynamic_update_index_in_dim(inc, inc[rows - 1] + back.astype(jnp.float32), rows - 1, 0)


def solution(mesh):
    return jax.shard_map(
        body,
        mesh=mesh,
        in_specs=(
            P("row", "col", None, None),
            P("row", "col", None, None),
            P("row", "col", None),
            P("row", "col", None),
            P(),
        ),
        out_specs=P("row", "col", None, None),
        check_vma=False,
    )
```

time: 97 us -> 80.4 us (0.83)
  matrix products: 64.5 us -> 0 us
  Pallas kernels: 0 us -> 55.8 us
  other arithmetic: 11.9 us -> 4.27 us
  local copies, waits for them, and re-layouts: 7.44 us -> 1.28 us
  starting transfers between devices: 11.7 us -> 15.7 us
  waiting for transfers between devices: 0.01 us -> 2.73 us
    dot_general x19 -> x0, matrix products: 64.5 us -> none  [the longest x9 46 us: term(): jnp.einsum('abcd,abkd->abkc', tapered_matrix, near[:, :, members:], prefe...]
    pallas_call x0 -> x5, Pallas kernels: none -> 55.8 us  [the longest x1 21.9 us: pack_columns(): pl.pallas_call(pack_columns_kernel, out_shape=(jax.ShapeDtypeStruct(shape...]
    concatenate x1 -> x0, other arithmetic: 5.32 us -> none  [padded(): block = jnp.concatenate([low, block, high], axis=dim)]
    ppermute x4 -> x5, starting transfers between devices: 11.7 us -> 15.7 us  [the longest x1 3.64 us: body(): right = lax.ppermute(first, 'col', backward('col'))]
    dot_general x1 -> x0, local copies, waits for them, and re-layouts: 2.91 us -> none  [lookup(): jnp.dot(onehot, tapers.reshape(count, cells * cells), preferred_element_t...]
    ppermute x4 -> x5, waiting for transfers between devices: 0.01 us -> 2.73 us  [the longest x1 2.15 us: body(): s = lax.ppermute(row, 'row', forward('row'))]
    unnamed x19 -> x10, local copies, waits for them, and re-layouts: 2.56 us -> 0.03 us
    slice x1 -> x0, other arithmetic: 1.99 us -> none  [padded(): lax.slice_in_dim(block, block.shape[dim] - width, None, axis=dim)]
  transfers between devices with their start and end apart: 4 -> 5, of which waited for: 0 -> 2; matrix products, arithmetic and copies ran while one was open for 40% -> 5% of each run, Pallas kernels for 0% -> 16%
where the time goes in v1:
time: 80.4 us; the launch traced here: 80 us
  Pallas kernels  55.8 us (69%)
  starting transfers between devices  15.7 us (20%)
  other arithmetic  4.27 us (5%)
  waiting for transfers between devices  2.73 us (3%)
  local copies, waits for them, and re-layouts  1.28 us (2%)
    pallas_call x1, Pallas kernels, pack_columns(): pl.pallas_call(pack_columns_kernel, out_shape=(jax.ShapeDtypeStruct(shape...  21.9 us
    pallas_call x1, Pallas kernels, pack_row(): pl.pallas_call(pack_row_kernel, out_shape=jax.ShapeDtypeStruct(shape, u.d...  21 us
    pallas_call x1, Pallas kernels, inner(): pl.pallas_call(inner_kernel, out_shape=jax.ShapeDtypeStruct((rows, cols,...  6.36 us
    pallas_call x1, Pallas kernels, outer(): pl.pallas_call(outer_kernel, out_shape=jax.ShapeDtypeStruct(inc.shape, in...  3.85 us
    ppermute x1, starting transfers between devices, body(): right = lax.ppermute(first, 'col', backward('col'))  3.64 us
    ppermute x1, starting transfers between devices, body(): s = lax.ppermute(row, 'row', forward('row'))  3.43 us
    ppermute x1, starting transfers between devices, body(): lax.ppermute(jnp.stack([left[rows - 1, :deep], right[rows - 1, :deep]]),...  3.41 us
    ppermute x1, starting transfers between devices, body(): back = lax.ppermute(back, 'row', backward('row'))  3.32 us
  transfers between devices with their start and end apart: 5, of which 2 were waited for; matrix products, arithmetic and copies ran while one was open for 5% of the time, Pallas kernels for 16%

profile of v1, /device:TPU:22, one launch (start us, length us, event | category | flops | bytes accessed | tf_op | source)
XLA Modules:
  0.0 80.0 jit_solution(15727098483696101949)
XLA Ops:
  0.0 21.0 %pack_row.1.row = bf16[8,320,128]{2,1,0:T(8,128)(2,1)} custom-call(bf16[4,8,256,128]{3,2,1,0:T(8,128)(2,1)} %u.9, bf16[4,8,64,128]{3,2,1,0:T(8,128)(2,1)} %w.9), custom_call_target="tpu_custom_call" | custom-call | bytes 1310720 | tf_op jit(solution)/shard_map/pack_row/pallas_call | solution.py:254
  21.0 0.0 copy-start
  21.0 0.0 copy-start.1
  21.0 0.0 copy-start.2
  21.0 0.0 copy-start.3
  21.0 0.0 copy-start.4
  21.0 21.9 %pack_columns.1 = (bf16[4,336,128]{2,1,0:T(8,128)(2,1)}, bf16[4,336,128]{2,1,0:T(8,128)(2,1)}) custom-call(bf16[4,8,256,128]{3,2,1,0:T(8,128)(2,1)} %u.9, bf16[4,8,64,128]{3,2,1,0:T(8,128)(2,1)} %w.9, s32[4,8,9]{2,1,0:T(8,128)} %live.7, s32[4,8,9]{2,1,0:T(8,128)} %index.7, bf16[8,320,128]{2,1,0:T(8,128)(2,1)} %pack_row.1.row), custom_call_target="tpu_custom_call" | custom-call | bytes 1376256 | tf_op jit(solution)/shard_map/pack_columns/pallas_call | solution.py:289
  42.9 1.9 %collective-permute-start.1 = (bf16[4,336,128]{2,1,0:T(8,128)(2,1)}, bf16[4,336,128]{2,1,0:T(8,128)(2,1)S(1)}, u32[]{:S(2)}, u32[]{:S(2)}) collective-permute-start(bf16[4,336,128]{2,1,0:T(8,128)(2,1)} %get-tuple-element.13), channel_id=1, source_target_pairs={{0,1},{1,2},{2,3},{4,5},{5,6},{6,7},{8,9},{9,10},{10,11},{12,13},{... | collective-permute-start | bytes 1032200 | tf_op jit(solution)/shard_map/ppermute | solution.py:307
  44.9 3.6 %collective-permute-start.2 = (bf16[4,336,128]{2,1,0:T(8,128)(2,1)}, bf16[4,336,128]{2,1,0:T(8,128)(2,1)S(1)}, u32[]{:S(2)}, u32[]{:S(2)}) collective-permute-start(bf16[4,336,128]{2,1,0:T(8,128)(2,1)} %get-tuple-element.14), channel_id=1, source_target_pairs={{1,0},{2,1},{3,2},{5,4},{6,5},{7,6},{9,8},{10,9},{11,10},{13,12},{... | collective-permute-start | bytes 1032200 | tf_op jit(solution)/shard_map/ppermute | solution.py:308
  48.5 3.4 %collective-permute-start = (bf16[8,320,128]{2,1,0:T(8,128)(2,1)}, bf16[8,320,128]{2,1,0:T(8,128)(2,1)S(1)}, u32[]{:S(2)}, u32[]{:S(2)}) collective-permute-start(bf16[8,320,128]{2,1,0:T(8,128)(2,1)} %pack_row.1.row), channel_id=1, source_target_pairs={{0,4},{4,8},{8,12},{12,16},{16,20},{20,24},{24,28},{1,5},{5,9},{9,... | collective-permute-start | bytes 1966088 | tf_op jit(solution)/shard_map/ppermute | solution.py:305
  52.0 0.0 copy-done
  52.0 0.0 copy-done.1
  52.0 0.0 copy-done.2
  52.0 0.0 copy-done.3
  52.0 0.0 copy-done.4
  52.0 6.4 %inner.1.inc = f32[4,8,64,128]{3,2,1,0:T(8,128)} custom-call(bf16[4,8,256,128]{3,2,1,0:T(8,128)(2,1)S(1)} %copy-done, bf16[4,8,64,128]{3,2,1,0:T(8,128)(2,1)S(1)} %copy-done.1, s32[4,8,9]{2,1,0:T(8,128)S(1)} %copy-done.3, s32[4,8,9]{2,1,0:T(8,128)S(1)} %copy-done.4, bf16[16,128,128]{2,1,0:T(8,128)(2,1)S(1)} %copy-done.2), custom_call_target="tpu_custom_call" | custom-call | flops 2013265920 | bytes 4194304 | tf_op jit(solution)/shard_map/inner/pallas_call | solution.py:88
  58.4 0.0 collective-permute-done.1.left
  58.4 0.0 collective-permute-done.2.right
  58.4 3.4 %collective-permute-start.3 = (bf16[2,320,128]{2,1,0:T(8,128)(2,1)S(1)}, bf16[2,320,128]{2,1,0:T(8,128)(2,1)S(1)}, u32[]{:S(2)}, u32[]{:S(2)}) collective-permute-start(bf16[2,320,128]{2,1,0:T(8,128)(2,1)S(1)} %pad_maximum_fusion), channel_id=1, source_target_pairs={{0,4},{4,8},{8,12},{12,16},{16,20},{20,24},{24,28},{1,5},{5,9},{9,... | collective-permute-start | bytes 491528 | tf_op jit(solution)/shard_map/ppermute | solution.py:309
  61.8 0.6 fusion.4
  62.4 0.7 fusion.3
  63.1 2.6 %maximum_convert_fusion.side = s32[4]{0:T(128)S(1)} fusion(bf16[1]{0:T(256)(128)(2,1)} %bitcast.3, bf16[1]{0:T(256)(128)(2,1)} %bitcast.2, bf16[1]{0:T(256)(128)(2,1)} %bitcast.1, bf16[1]{0:T(256)(128)(2,1)} %bitcast), kind=kLoop, calls=%fused_computation.5 | loop fusion | flops 32 | bytes 24 | tf_op jit(solution)/shard_map/convert_element_type | solution.py:320
  65.7 2.1 %collective-permute-done.s = bf16[8,320,128]{2,1,0:T(8,128)(2,1)S(1)} collective-permute-done((bf16[8,320,128]{2,1,0:T(8,128)(2,1)}, bf16[8,320,128]{2,1,0:T(8,128)(2,1)S(1)}, u32[]{:S(2)}, u32[]{:S(2)}) %collective-permute-start) | collective-permute-done | bytes 655392 | tf_op jit(solution)/shard_map/ppermute | solution.py:305
  67.8 2.7 %above.1 = (bf16[8,64,128]{2,1,0:T(8,128)(2,1)S(1)}, bf16[8,128,384]{2,1,0:T(8,128)(2,1)S(1)}) custom-call(bf16[8,320,128]{2,1,0:T(8,128)(2,1)S(1)} %collective-permute-done.s, bf16[4,8,256,128]{3,2,1,0:T(8,128)(2,1)S(1)} %copy-done, bf16[4,8,64,128]{3,2,1,0:T(8,128)(2,1)S(1)} %copy-done.1, bf16[4,336,128]{2,1,0:T(8,128)(2,1)S(1)} %collective-permute-done.1.left, ...), custom_call_target="tpu_custom_call" | custom-call | flops 251658240 | bytes 2097152 | tf_op jit(solution)/shard_map/above/pallas_call | solution.py:138
  70.6 3.3 %collective-permute-start.4 = (bf16[8,64,128]{2,1,0:T(8,128)(2,1)S(1)}, bf16[8,64,128]{2,1,0:T(8,128)(2,1)S(1)}, u32[]{:S(2)}, u32[]{:S(2)}) collective-permute-start(bf16[8,64,128]{2,1,0:T(8,128)(2,1)S(1)} %get-tuple-element.16), channel_id=1, source_target_pairs={{4,0},{8,4},{12,8},{16,12},{20,16},{24,20},{28,24},{5,1},{9,5},{13... | collective-permute-start | bytes 393224 | tf_op jit(solution)/shard_map/ppermute | solution.py:323
  73.9 0.0 collective-permute-done.3.corner
  73.9 3.8 %outer.1 = f32[4,8,64,128]{3,2,1,0:T(8,128)} custom-call(f32[4,8,64,128]{3,2,1,0:T(8,128)} %inner.1.inc, bf16[8,128,384]{2,1,0:T(8,128)(2,1)S(1)} %get-tuple-element.15.held, bf16[8,320,128]{2,1,0:T(8,128)(2,1)S(1)} %collective-permute-done.s, bf16[2,320,128]{2,1,0:T(8,128)(2,1)S(1)} %collective-permute-done.3.corner, ...), custom_call_target="tpu_custom_call", output_to_operand_aliasing={{}: (0, {})} | custom-call | flops 503316480 | bytes 4194304 | tf_op jit(solution)/shard_map/outer/pallas_call | solution.py:214
  77.7 0.6 collective-permute-done.4
  78.3 1.7 %fusion.2 = f32[4,8,64,128]{3,2,1,0:T(8,128)} fusion(f32[4,8,64,128]{3,2,1,0:T(8,128)} %outer.1, bf16[8,64,128]{2,1,0:T(8,128)(2,1)S(1)} %collective-permute-done.4), kind=kLoop, calls=%fused_computation.3 | loop fusion | flops 131072 | bytes 655360 | tf_op jit(solution)/shard_map/jit(dynamic_update_index_in_dim)/dynamic_update_slice | solution.py:325
  (3 shorter events, 0.0 us)
Async XLA Ops:
  21.0 31.0 %copy-start = (bf16[4,8,256,128]{3,2,1,0:T(8,128)(2,1)S(1)}, bf16[4,8,256,128]{3,2,1,0:T(8,128)(2,1)}, u32[]{:S(2)}) copy-start(bf16[4,8,256,128]{3,2,1,0:T(8,128)(2,1)} %u.9) | copy-start | bytes 6291460
  21.0 31.0 %copy-start.1 = (bf16[4,8,64,128]{3,2,1,0:T(8,128)(2,1)S(1)}, bf16[4,8,64,128]{3,2,1,0:T(8,128)(2,1)}, u32[]{:S(2)}) copy-start(bf16[4,8,64,128]{3,2,1,0:T(8,128)(2,1)} %w.9) | copy-start | bytes 1572868
  21.0 31.0 %copy-start.2 = (bf16[16,128,128]{2,1,0:T(8,128)(2,1)S(1)}, bf16[16,128,128]{2,1,0:T(8,128)(2,1)}, u32[]{:S(2)}) copy-start(bf16[16,128,128]{2,1,0:T(8,128)(2,1)} %tapers.5) | copy-start | bytes 1572868
  21.0 31.0 %copy-start.3 = (s32[4,8,9]{2,1,0:T(8,128)S(1)}, s32[4,8,9]{2,1,0:T(8,128)}, u32[]{:S(2)}) copy-start(s32[4,8,9]{2,1,0:T(8,128)} %live.7) | copy-start | bytes 3460
  21.0 31.0 %copy-start.4 = (s32[4,8,9]{2,1,0:T(8,128)S(1)}, s32[4,8,9]{2,1,0:T(8,128)}, u32[]{:S(2)}) copy-start(s32[4,8,9]{2,1,0:T(8,128)} %index.7) | copy-start | bytes 3460
  42.9 15.4 %collective-permute-start.1 = (bf16[4,336,128]{2,1,0:T(8,128)(2,1)}, bf16[4,336,128]{2,1,0:T(8,128)(2,1)S(1)}, u32[]{:S(2)}, u32[]{:S(2)}) collective-permute-start(bf16[4,336,128]{2,1,0:T(8,128)(2,1)} %get-tuple-element.13), channel_id=1, source_target_pairs={{0,1},{1,2},{2,3},{4,5},{5,6},{6,7},{8,9},{9,10},{10,11},{12,13},{... | collective-permute-start | bytes 1032200 | tf_op jit(solution)/shard_map/ppermute | solution.py:307
  44.9 13.5 %collective-permute-start.2 = (bf16[4,336,128]{2,1,0:T(8,128)(2,1)}, bf16[4,336,128]{2,1,0:T(8,128)(2,1)S(1)}, u32[]{:S(2)}, u32[]{:S(2)}) collective-permute-start(bf16[4,336,128]{2,1,0:T(8,128)(2,1)} %get-tuple-element.14), channel_id=1, source_target_pairs={{1,0},{2,1},{3,2},{5,4},{6,5},{7,6},{9,8},{10,9},{11,10},{13,12},{... | collective-permute-start | bytes 1032200 | tf_op jit(solution)/shard_map/ppermute | solution.py:308
  48.5 19.3 %collective-permute-start = (bf16[8,320,128]{2,1,0:T(8,128)(2,1)}, bf16[8,320,128]{2,1,0:T(8,128)(2,1)S(1)}, u32[]{:S(2)}, u32[]{:S(2)}) collective-permute-start(bf16[8,320,128]{2,1,0:T(8,128)(2,1)} %pack_row.1.row), channel_id=1, source_target_pairs={{0,4},{4,8},{8,12},{12,16},{16,20},{20,24},{24,28},{1,5},{5,9},{9,... | collective-permute-start | bytes 1966088 | tf_op jit(solution)/shard_map/ppermute | solution.py:305
  58.4 15.5 %collective-permute-start.3 = (bf16[2,320,128]{2,1,0:T(8,128)(2,1)S(1)}, bf16[2,320,128]{2,1,0:T(8,128)(2,1)S(1)}, u32[]{:S(2)}, u32[]{:S(2)}) collective-permute-start(bf16[2,320,128]{2,1,0:T(8,128)(2,1)S(1)} %pad_maximum_fusion), channel_id=1, source_target_pairs={{0,4},{4,8},{8,12},{12,16},{16,20},{20,24},{24,28},{1,5},{5,9},{9,... | collective-permute-start | bytes 491528 | tf_op jit(solution)/shard_map/ppermute | solution.py:309
  70.6 7.8 %collective-permute-start.4 = (bf16[8,64,128]{2,1,0:T(8,128)(2,1)S(1)}, bf16[8,64,128]{2,1,0:T(8,128)(2,1)S(1)}, u32[]{:S(2)}, u32[]{:S(2)}) collective-permute-start(bf16[8,64,128]{2,1,0:T(8,128)(2,1)S(1)} %get-tuple-element.16), channel_id=1, source_target_pairs={{4,0},{8,4},{12,8},{16,12},{20,16},{24,20},{28,24},{5,1},{9,5},{13... | collective-permute-start | bytes 393224 | tf_op jit(solution)/shard_map/ppermute | solution.py:323

commit v2 on v1

--- a/solution.py
+++ b/solution.py
@@ -6,6 +6,7 @@
 from jax.sharding import PartitionSpec as P
 
 MEMBERS = 256
+GRANT = 16 << 20
 SCALE = 1.0 / (MEMBERS - 1)
 TN = (((0,), (0,)), ((), ()))
 NT = (((1,), (1,)), ((), ()))
@@ -13,6 +14,7 @@
 VMEM = pl.BlockSpec(memory_space=pltpu.VMEM)
 SMEM = pl.BlockSpec(memory_space=pltpu.SMEM)
 ANY = pl.BlockSpec(memory_space=pl.ANY)
+HBM = pl.BlockSpec(memory_space=pltpu.HBM)
 
 
 def dot(a, b, dims):
@@ -28,7 +30,7 @@
     return (rho.astype(jnp.float32) * gram * factor).astype(jnp.bfloat16)
 
 
-def inner_kernel(u, w, live, index, tapers, out, sym, held):
+def inner_kernel(u, w, live, index, tapers, out, done, sym, held):
     rows, cols, _, cells = u.shape
     for n in range(tapers.shape[0]):
         t = tapers[n].astype(jnp.float32)
@@ -79,6 +81,7 @@
         row(a, False)
 
     row(rows - 1, True)
+    done[...] = jnp.zeros_like(done)
 
 
 def inner(u, w, live, index, tapers):
@@ -87,14 +90,17 @@
     pairs = 5 * rows * cols
     return pl.pallas_call(
         inner_kernel,
-        out_shape=jax.ShapeDtypeStruct((rows, cols, columns, cells), jnp.float32),
+        out_shape=(
+            jax.ShapeDtypeStruct((rows, cols, columns, cells), jnp.float32),
+            jax.ShapeDtypeStruct((8, cells), jnp.float32),
+        ),
         in_specs=[VMEM, VMEM, SMEM, SMEM, VMEM],
-        out_specs=VMEM,
+        out_specs=(VMEM, VMEM),
         scratch_shapes=[
             pltpu.VMEM(tapers.shape, jnp.float32),
             pltpu.VMEM((cols, cells, 5 * cells), jnp.bfloat16),
         ],
-        compiler_params=pltpu.CompilerParams(vmem_limit_bytes=24 << 20),
+        compiler_params=pltpu.CompilerParams(vmem_limit_bytes=GRANT),
         cost_estimate=pl.CostEstimate(
             flops=2 * pairs * cells * cells * (members + 2 * columns),
             bytes_accessed=4 << 20,
@@ -104,10 +110,12 @@
     )(u, w, live, index, tapers)
 
 
-def above_kernel(s, u, w, left, right, live, index, side, tapers, back, held):
+def above_kernel(s, u, w, left, right, live, index, tapers, back, held):
     cols, _, cells = s.shape
     members = u.shape[2]
     deep = members + w.shape[2]
+    notes = [near[0, deep:].astype(jnp.int32) for near in (left, right)]
+    side = [notes[0][cols - 1, 2], notes[0][2 * cols - 1, 2], notes[1][0, 0], notes[1][cols, 0]]
 
     for c in range(cols):
         grams, weights, lives, rhos = [], [], [], []
@@ -131,7 +139,7 @@
         back[c] = dot(cat(weights, 1), block, NT).astype(jnp.bfloat16)
 
 
-def above(s, u, w, left, right, live, index, side, tapers):
+def above(s, u, w, left, right, live, index, tapers):
     cols, _, cells = s.shape
     columns = w.shape[2]
     members = u.shape[2]
@@ -141,19 +149,19 @@
             jax.ShapeDtypeStruct((cols, columns, cells), jnp.bfloat16),
             jax.ShapeDtypeStruct((cols, cells, 3 * cells), jnp.bfloat16),
         ),
-        in_specs=[VMEM, VMEM, VMEM, VMEM, VMEM, SMEM, SMEM, SMEM, VMEM],
+        in_specs=[VMEM, VMEM, VMEM, VMEM, VMEM, SMEM, SMEM, VMEM],
         out_specs=(VMEM, VMEM),
-        compiler_params=pltpu.CompilerParams(vmem_limit_bytes=24 << 20),
+        compiler_params=pltpu.CompilerParams(vmem_limit_bytes=GRANT),
         cost_estimate=pl.CostEstimate(
             flops=2 * 3 * cols * cells * cells * (members + columns),
             bytes_accessed=2 << 20,
             transcendentals=0,
         ),
         name="above",
-    )(s, u, w, left, right, live, index, side, tapers)
-
-
-def outer_kernel(inc, held, s, corner, u, w, left, right, live, index, tapers, out):
+    )(s, u, w, left, right, live, index, tapers)
+
+
+def outer_kernel(inc, held, s, corner, u, w, left, right, live, index, tapers, out, low):
     rows, cols, members, cells = u.shape
     deep = members + w.shape[2]
     last = cols - 1
@@ -205,7 +213,10 @@
 
     for a in range(rows):
         for q in range(cols):
-            out[a, q] = inc[a, q] + total[a, q] if (a, q) in total else inc[a, q]
+            value = inc[a, q] + total[a, q] if (a, q) in total else inc[a, q]
+            out[a, q] = value
+            if a == rows - 1:
+                low[q] = value
 
 
 def outer(inc, held, s, corner, u, w, left, right, live, index, tapers):
@@ -213,11 +224,10 @@
     columns = w.shape[2]
     return pl.pallas_call(
         outer_kernel,
-        out_shape=jax.ShapeDtypeStruct(inc.shape, inc.dtype),
+        out_shape=(jax.ShapeDtypeStruct(inc.shape, inc.dtype), jax.ShapeDtypeStruct(inc.shape[1:], inc.dtype)),
         in_specs=[VMEM] * 8 + [SMEM, SMEM, VMEM],
-        out_specs=VMEM,
-        input_output_aliases={0: 0},
-        compiler_params=pltpu.CompilerParams(vmem_limit_bytes=24 << 20),
+        out_specs=(VMEM, VMEM),
+        compiler_params=pltpu.CompilerParams(vmem_limit_bytes=GRANT),
         cost_estimate=pl.CostEstimate(
             flops=2 * (6 * rows + 3 * cols) * cells * cells * (members + columns),
             bytes_accessed=4 << 20,
@@ -225,6 +235,28 @@
         ),
         name="outer",
     )(inc, held, s, corner, u, w, left, right, live, index, tapers)
+
+
+def finish_kernel(inc, low, back, out, total, sem):
+    del inc
+    total[...] = low[...] + back[...].astype(jnp.float32)
+    copy = pltpu.make_async_copy(total, out.at[out.shape[0] - 1], sem)
+    copy.start()
+    copy.wait()
+
+
+def finish(inc, low, back):
+    return pl.pallas_call(
+        finish_kernel,
+        out_shape=jax.ShapeDtypeStruct(inc.shape, inc.dtype),
+        in_specs=[ANY, VMEM, VMEM],
+        out_specs=ANY,
+        scratch_shapes=[pltpu.VMEM(low.shape, low.dtype), pltpu.SemaphoreType.DMA(())],
+        input_output_aliases={0: 0},
+        compiler_params=pltpu.CompilerParams(vmem_limit_bytes=GRANT),
+        cost_estimate=pl.CostEstimate(flops=low.size, bytes_accessed=10 * low.size, transcendentals=0),
+        name="finish",
+    )(inc, low, back)
 
 
 def forward(axis):
@@ -254,16 +286,17 @@
     return pl.pallas_call(
         pack_row_kernel,
         out_shape=jax.ShapeDtypeStruct(shape, u.dtype),
-        in_specs=[ANY, ANY],
-        out_specs=ANY,
+        in_specs=[HBM, HBM],
+        out_specs=VMEM,
         scratch_shapes=[pltpu.SemaphoreType.DMA((2,))],
+        compiler_params=pltpu.CompilerParams(vmem_limit_bytes=GRANT),
         cost_estimate=pl.CostEstimate(flops=0, bytes_accessed=4 * cols * shape[1] * cells, transcendentals=0),
         name="pack_row",
     )(u, w)
 
 
-def pack_columns_kernel(u, w, live, index, row, first, final, notes, sem):
-    del row
+def pack_columns_kernel(u, w, live, index, done, first, final, sem):
+    del done
     rows, cols, members, cells = u.shape
     deep = members + w.shape[2]
     copies = []
@@ -272,57 +305,47 @@
         copies.append(pltpu.make_async_copy(w.at[:, b], out.at[:, members:deep], sem.at[n, 1]))
     for copy in copies:
         copy.start()
-    for n, (out, b) in enumerate(((first, 0), (final, cols - 1))):
-        for a in range(rows):
-            lines = jnp.concatenate([live[a], index[a]], 0).astype(jnp.float32)
-            blank = jnp.zeros((2 * cols, cells - live.shape[2]), jnp.float32)
-            notes[n, a] = jnp.concatenate([lines, blank], 1).astype(jnp.bfloat16)
-        copies.append(pltpu.make_async_copy(notes.at[n], out.at[:, deep:], sem.at[n, 2]))
-        copies[-1].start()
+    for a in range(rows):
+        lines = jnp.concatenate([live[a], index[a]], 0).astype(jnp.float32)
+        blank = jnp.zeros((2 * cols, cells - live.shape[2]), jnp.float32)
+        note = jnp.concatenate([lines, blank], 1).astype(jnp.bfloat16)
+        first[a, deep:] = note
+        final[a, deep:] = note
     for copy in copies:
         copy.wait()
 
 
-def pack_columns(u, w, live, index, row):
+def pack_columns(u, w, live, index, done):
     rows, cols, members, cells = u.shape
     shape = (rows, members + w.shape[2] + 2 * cols, cells)
     return pl.pallas_call(
         pack_columns_kernel,
         out_shape=(jax.ShapeDtypeStruct(shape, u.dtype),) * 2,
-        in_specs=[ANY, ANY, VMEM, VMEM, ANY],
-        out_specs=(ANY, ANY),
-        scratch_shapes=[pltpu.VMEM((2, rows, 2 * cols, cells), jnp.bfloat16), pltpu.SemaphoreType.DMA((2, 3))],
+        in_specs=[ANY, ANY, VMEM, VMEM, VMEM],
+        out_specs=(VMEM, VMEM),
+        scratch_shapes=[pltpu.SemaphoreType.DMA((2, 2))],
+        compiler_params=pltpu.CompilerParams(vmem_limit_bytes=GRANT),
         cost_estimate=pl.CostEstimate(flops=0, bytes_accessed=8 * rows * shape[1] * cells, transcendentals=0),
         name="pack_columns",
-    )(u, w, live, index, row)
+    )(u, w, live, index, done)
 
 
 def body(perturbations, weights, live, index, tapers):
     u, w = perturbations, weights
     rows, cols, members, cells = u.shape
     deep = members + w.shape[2]
-    row = pack_row(u, w)
-    s = lax.ppermute(row, "row", forward("row"))
-    first, final = pack_columns(u, w, live, index, row)
+    s = lax.ppermute(pack_row(u, w), "row", forward("row"))
+    inc, done = inner(u, w, live, index, tapers)
+    first, final = pack_columns(u, w, live, index, done)
     left = lax.ppermute(final, "col", forward("col"))
     right = lax.ppermute(first, "col", backward("col"))
     corner = lax.ppermute(
         jnp.stack([left[rows - 1, :deep], right[rows - 1, :deep]]), "row", forward("row")
     )
-    inc = inner(u, w, live, index, tapers)
-    side = jnp.stack(
-        [
-            left[0, deep + cols - 1, 2],
-            left[0, deep + 2 * cols - 1, 2],
-            right[0, deep, 0],
-            right[0, deep + cols, 0],
-        ]
-    ).astype(jnp.int32)
-    inc, s = lax.optimization_barrier((inc, s))
-    back, held = above(s, u, w, left, right, live, index, side, tapers)
+    back, held = above(s, u, w, left, right, live, index, tapers)
     back = lax.ppermute(back, "row", backward("row"))
-    inc = outer(inc, held, s, corner, u, w, left, right, live, index, tapers)
-    return lax.dynamic_update_index_in_dim(inc, inc[rows - 1] + back.astype(jnp.float32), rows - 1, 0)
+    inc, low = outer(inc, held, s, corner, u, w, left, right, live, index, tapers)
+    return finish(inc, low, back)
 
 
 def solution(mesh):

time: 80.4 us -> 37.9 us (0.47)
  the two profiles are of different devices: /device:TPU:22 before, /device:TPU:1 now
where the time goes in v2:
time: 37.9 us; the launch traced here: 37.6 us
  starting transfers between devices  14.7 us (39%)
  Pallas kernels  12.7 us (34%)
  waiting for transfers between devices  7.36 us (19%)
  local copies, waits for them, and re-layouts  2.66 us (7%)
    pallas_call x1, Pallas kernels, inner(): pl.pallas_call(inner_kernel, out_shape=(jax.ShapeDtypeStruct((rows, cols,...  5.36 us
    ppermute x1, waiting for transfers between devices, body(): right = lax.ppermute(first, 'col', backward('col'))  4.39 us
    ppermute x1, starting transfers between devices, body(): s = lax.ppermute(pack_row(u, w), 'row', forward('row'))  4.15 us
    ppermute x1, starting transfers between devices, body(): left = lax.ppermute(final, 'col', forward('col'))  3.98 us
    pallas_call x1, Pallas kernels, outer(): pl.pallas_call(outer_kernel, out_shape=(jax.ShapeDtypeStruct(inc.shape, i...  3.68 us
    ppermute x1, starting transfers between devices, body(): lax.ppermute(jnp.stack([left[rows - 1, :deep], right[rows - 1, :deep]]),...  3.41 us
    pallas_call x1, Pallas kernels, above(): pl.pallas_call(above_kernel, out_shape=(jax.ShapeDtypeStruct((cols, colum...  2.75 us
    unnamed x10, local copies, waits for them, and re-layouts  2.64 us
  transfers between devices with their start and end apart: 5, of which 3 were waited for; matrix products, arithmetic and copies ran while one was open for 0% of the time, Pallas kernels for 32%

profile of v2, /device:TPU:1, one launch (start us, length us, event | category | flops | bytes accessed | tf_op | source)
XLA Modules:
  0.0 37.6 jit_solution(1851905431508047702)
XLA Ops:
  0.0 0.0 copy-start
  0.0 1.6 %copy-done = bf16[4,8,256,128]{3,2,1,0:T(8,128)(2,1)S(1)} copy-done((bf16[4,8,256,128]{3,2,1,0:T(8,128)(2,1)S(1)}, bf16[4,8,256,128]{3,2,1,0:T(8,128)(2,1)}, u32[]{:S(2)}) %copy-start) | copy-done | bytes 2097176
  1.6 0.0 copy-start.1
  1.6 1.0 %copy-done.1 = bf16[4,8,64,128]{3,2,1,0:T(8,128)(2,1)S(1)} copy-done((bf16[4,8,64,128]{3,2,1,0:T(8,128)(2,1)S(1)}, bf16[4,8,64,128]{3,2,1,0:T(8,128)(2,1)}, u32[]{:S(2)}) %copy-start.1) | copy-done | bytes 524312
  2.6 0.0 copy-start.2
  2.6 0.0 copy-start.3
  2.6 0.0 copy-start.4
  2.6 0.1 pack_row.1
  2.7 4.1 %collective-permute-start = (bf16[8,320,128]{2,1,0:T(8,128)(2,1)S(1)}, bf16[8,320,128]{2,1,0:T(8,128)(2,1)S(1)}, u32[]{:S(2)}, u32[]{:S(2)}) collective-permute-start(bf16[8,320,128]{2,1,0:T(8,128)(2,1)S(1)} %pack_row.1), channel_id=1, source_target_pairs={{0,4},{4,8},{8,12},{12,16},{16,20},{20,24},{24,28},{1,5},{5,9},{9,... | collective-permute-start | bytes 1966088 | tf_op jit(solution)/shard_map/ppermute | solution.py:337
  6.9 0.0 copy-done.2
  6.9 0.0 copy-done.3
  6.9 0.0 copy-done.4
  6.9 5.4 %inner.1 = (f32[4,8,64,128]{3,2,1,0:T(8,128)S(1)}, f32[8,128]{1,0:T(8,128)S(1)}) custom-call(bf16[4,8,256,128]{3,2,1,0:T(8,128)(2,1)S(1)} %copy-done, bf16[4,8,64,128]{3,2,1,0:T(8,128)(2,1)S(1)} %copy-done.1, s32[4,8,9]{2,1,0:T(8,128)S(1)} %copy-done.3, s32[4,8,9]{2,1,0:T(8,128)S(1)} %copy-done.4, bf16[16,128,128]{2,1,0:T(8,128)(2,1)S(1)} %copy-done.2), custom_call_target="tpu_custom_call" | custom-call | flops 2013265920 | bytes 4194304 | tf_op jit(solution)/shard_map/inner/pallas_call | solution.py:91
  12.3 0.1 pack_columns.1
  12.4 4.0 %collective-permute-start.1 = (bf16[4,336,128]{2,1,0:T(8,128)(2,1)S(1)}, bf16[4,336,128]{2,1,0:T(8,128)(2,1)S(1)}, u32[]{:S(2)}, u32[]{:S(2)}) collective-permute-start(bf16[4,336,128]{2,1,0:T(8,128)(2,1)S(1)} %get-tuple-element.15), channel_id=1, source_target_pairs={{0,1},{1,2},{2,3},{4,5},{5,6},{6,7},{8,9},{9,10},{10,11},{12,13},{... | collective-permute-start | bytes 1032200 | tf_op jit(solution)/shard_map/ppermute | solution.py:340
  16.4 1.9 %collective-permute-start.2 = (bf16[4,336,128]{2,1,0:T(8,128)(2,1)S(1)}, bf16[4,336,128]{2,1,0:T(8,128)(2,1)S(1)}, u32[]{:S(2)}, u32[]{:S(2)}) collective-permute-start(bf16[4,336,128]{2,1,0:T(8,128)(2,1)S(1)} %get-tuple-element.16), channel_id=1, source_target_pairs={{1,0},{2,1},{3,2},{5,4},{6,5},{7,6},{9,8},{10,9},{11,10},{13,12},{... | collective-permute-start | bytes 1032200 | tf_op jit(solution)/shard_map/ppermute | solution.py:341
  18.3 2.2 %collective-permute-done.1.left = bf16[4,336,128]{2,1,0:T(8,128)(2,1)S(1)} collective-permute-done((bf16[4,336,128]{2,1,0:T(8,128)(2,1)S(1)}, bf16[4,336,128]{2,1,0:T(8,128)(2,1)S(1)}, u32[]{:S(2)}, u32[]{:S(2)}) %collective-permute-start.1) | collective-permute-done | bytes 344096 | tf_op jit(solution)/shard_map/ppermute | solution.py:340
  20.6 4.4 %collective-permute-done.2.right = bf16[4,336,128]{2,1,0:T(8,128)(2,1)S(1)} collective-permute-done((bf16[4,336,128]{2,1,0:T(8,128)(2,1)S(1)}, bf16[4,336,128]{2,1,0:T(8,128)(2,1)S(1)}, u32[]{:S(2)}, u32[]{:S(2)}) %collective-permute-start.2) | collective-permute-done | bytes 344096 | tf_op jit(solution)/shard_map/ppermute | solution.py:341
  25.0 3.4 %collective-permute-start.3 = (bf16[2,320,128]{2,1,0:T(8,128)(2,1)S(1)}, bf16[2,320,128]{2,1,0:T(8,128)(2,1)S(1)}, u32[]{:S(2)}, u32[]{:S(2)}) collective-permute-start(bf16[2,320,128]{2,1,0:T(8,128)(2,1)S(1)} %pad_maximum_fusion), channel_id=1, source_target_pairs={{0,4},{4,8},{8,12},{12,16},{16,20},{20,24},{24,28},{1,5},{5,9},{9,... | collective-permute-start | bytes 491528 | tf_op jit(solution)/shard_map/ppermute | solution.py:342
  28.4 0.0 collective-permute-done.s
  28.4 2.7 %above.1 = (bf16[8,64,128]{2,1,0:T(8,128)(2,1)S(1)}, bf16[8,128,384]{2,1,0:T(8,128)(2,1)S(1)}) custom-call(bf16[8,320,128]{2,1,0:T(8,128)(2,1)S(1)} %collective-permute-done.s, bf16[4,8,256,128]{3,2,1,0:T(8,128)(2,1)S(1)} %copy-done, bf16[4,8,64,128]{3,2,1,0:T(8,128)(2,1)S(1)} %copy-done.1, bf16[4,336,128]{2,1,0:T(8,128)(2,1)S(1)} %collective-permute-done.1.left, ...), custom_call_target="tpu_custom_call" | custom-call | flops 251658240 | bytes 2097152 | tf_op jit(solution)/shard_map/above/pallas_call | solution.py:146
  31.2 1.3 %collective-permute-start.4 = (bf16[8,64,128]{2,1,0:T(8,128)(2,1)S(1)}, bf16[8,64,128]{2,1,0:T(8,128)(2,1)S(1)}, u32[]{:S(2)}, u32[]{:S(2)}) collective-permute-start(bf16[8,64,128]{2,1,0:T(8,128)(2,1)S(1)} %get-tuple-element.20), channel_id=1, source_target_pairs={{4,0},{8,4},{12,8},{16,12},{20,16},{24,20},{28,24},{5,1},{9,5},{13... | collective-permute-start | bytes 393224 | tf_op jit(solution)/shard_map/ppermute | solution.py:346
  32.5 0.0 collective-permute-done.3.corner
  32.5 3.7 %outer.1 = (f32[4,8,64,128]{3,2,1,0:T(8,128)}, f32[8,64,128]{2,1,0:T(8,128)S(1)}) custom-call(f32[4,8,64,128]{3,2,1,0:T(8,128)S(1)} %get-tuple-element.13.inc, bf16[8,128,384]{2,1,0:T(8,128)(2,1)S(1)} %get-tuple-element.17.held, bf16[8,320,128]{2,1,0:T(8,128)(2,1)S(1)} %collective-permute-done.s, bf16[2,320,128]{2,1,0:T(8,128)(2,1)S(1)} %collective-permute-done.3.corner, ...), custom_call_target="tpu_custom_call" | custom-call | flops 503316480 | bytes 4194304 | tf_op jit(solution)/shard_map/outer/pallas_call | solution.py:225
  36.2 0.7 %collective-permute-done.4.back = bf16[8,64,128]{2,1,0:T(8,128)(2,1)S(1)} collective-permute-done((bf16[8,64,128]{2,1,0:T(8,128)(2,1)S(1)}, bf16[8,64,128]{2,1,0:T(8,128)(2,1)S(1)}, u32[]{:S(2)}, u32[]{:S(2)}) %collective-permute-start.4) | collective-permute-done | bytes 131104 | tf_op jit(solution)/shard_map/ppermute | solution.py:346
  36.9 0.7 %finish.1 = f32[4,8,64,128]{3,2,1,0:T(8,128)} custom-call(f32[4,8,64,128]{3,2,1,0:T(8,128)} %get-tuple-element.18.inc, f32[8,64,128]{2,1,0:T(8,128)S(1)} %get-tuple-element.19.low, bf16[8,64,128]{2,1,0:T(8,128)(2,1)S(1)} %collective-permute-done.4.back), custom_call_target="tpu_custom_call", output_to_operand_aliasing={{}: (0, {})} | custom-call | flops 65536 | bytes 655360 | tf_op jit(solution)/shard_map/finish/pallas_call | solution.py:249
  (3 shorter events, 0.0 us)
Async XLA Ops:
  0.0 1.6 %copy-start = (bf16[4,8,256,128]{3,2,1,0:T(8,128)(2,1)S(1)}, bf16[4,8,256,128]{3,2,1,0:T(8,128)(2,1)}, u32[]{:S(2)}) copy-start(bf16[4,8,256,128]{3,2,1,0:T(8,128)(2,1)} %u.9) | copy-start | bytes 6291460
  1.6 1.0 %copy-start.1 = (bf16[4,8,64,128]{3,2,1,0:T(8,128)(2,1)S(1)}, bf16[4,8,64,128]{3,2,1,0:T(8,128)(2,1)}, u32[]{:S(2)}) copy-start(bf16[4,8,64,128]{3,2,1,0:T(8,128)(2,1)} %w.9) | copy-start | bytes 1572868
  2.6 4.2 %copy-start.2 = (bf16[16,128,128]{2,1,0:T(8,128)(2,1)S(1)}, bf16[16,128,128]{2,1,0:T(8,128)(2,1)}, u32[]{:S(2)}) copy-start(bf16[16,128,128]{2,1,0:T(8,128)(2,1)} %tapers.5) | copy-start | bytes 1572868
  2.6 4.3 %copy-start.3 = (s32[4,8,9]{2,1,0:T(8,128)S(1)}, s32[4,8,9]{2,1,0:T(8,128)}, u32[]{:S(2)}) copy-start(s32[4,8,9]{2,1,0:T(8,128)} %live.7) | copy-start | bytes 3460
  2.6 4.3 %copy-start.4 = (s32[4,8,9]{2,1,0:T(8,128)S(1)}, s32[4,8,9]{2,1,0:T(8,128)}, u32[]{:S(2)}) copy-start(s32[4,8,9]{2,1,0:T(8,128)} %index.7) | copy-start | bytes 3460
  2.7 25.7 %collective-permute-start = (bf16[8,320,128]{2,1,0:T(8,128)(2,1)S(1)}, bf16[8,320,128]{2,1,0:T(8,128)(2,1)S(1)}, u32[]{:S(2)}, u32[]{:S(2)}) collective-permute-start(bf16[8,320,128]{2,1,0:T(8,128)(2,1)S(1)} %pack_row.1), channel_id=1, source_target_pairs={{0,4},{4,8},{8,12},{12,16},{16,20},{20,24},{24,28},{1,5},{5,9},{9,... | collective-permute-start | bytes 1966088 | tf_op jit(solution)/shard_map/ppermute | solution.py:337
  12.4 8.2 %collective-permute-start.1 = (bf16[4,336,128]{2,1,0:T(8,128)(2,1)S(1)}, bf16[4,336,128]{2,1,0:T(8,128)(2,1)S(1)}, u32[]{:S(2)}, u32[]{:S(2)}) collective-permute-start(bf16[4,336,128]{2,1,0:T(8,128)(2,1)S(1)} %get-tuple-element.15), channel_id=1, source_target_pairs={{0,1},{1,2},{2,3},{4,5},{5,6},{6,7},{8,9},{9,10},{10,11},{12,13},{... | collective-permute-start | bytes 1032200 | tf_op jit(solution)/shard_map/ppermute | solution.py:340
  16.4 8.6 %collective-permute-start.2 = (bf16[4,336,128]{2,1,0:T(8,128)(2,1)S(1)}, bf16[4,336,128]{2,1,0:T(8,128)(2,1)S(1)}, u32[]{:S(2)}, u32[]{:S(2)}) collective-permute-start(bf16[4,336,128]{2,1,0:T(8,128)(2,1)S(1)} %get-tuple-element.16), channel_id=1, source_target_pairs={{1,0},{2,1},{3,2},{5,4},{6,5},{7,6},{9,8},{10,9},{11,10},{13,12},{... | collective-permute-start | bytes 1032200 | tf_op jit(solution)/shard_map/ppermute | solution.py:341
  25.0 7.5 %collective-permute-start.3 = (bf16[2,320,128]{2,1,0:T(8,128)(2,1)S(1)}, bf16[2,320,128]{2,1,0:T(8,128)(2,1)S(1)}, u32[]{:S(2)}, u32[]{:S(2)}) collective-permute-start(bf16[2,320,128]{2,1,0:T(8,128)(2,1)S(1)} %pad_maximum_fusion), channel_id=1, source_target_pairs={{0,4},{4,8},{8,12},{12,16},{16,20},{20,24},{24,28},{1,5},{5,9},{9,... | collective-permute-start | bytes 491528 | tf_op jit(solution)/shard_map/ppermute | solution.py:342
  31.2 5.7 %collective-permute-start.4 = (bf16[8,64,128]{2,1,0:T(8,128)(2,1)S(1)}, bf16[8,64,128]{2,1,0:T(8,128)(2,1)S(1)}, u32[]{:S(2)}, u32[]{:S(2)}) collective-permute-start(bf16[8,64,128]{2,1,0:T(8,128)(2,1)S(1)} %get-tuple-element.20), channel_id=1, source_target_pairs={{4,0},{8,4},{12,8},{16,12},{20,16},{24,20},{28,24},{5,1},{9,5},{13... | collective-permute-start | bytes 393224 | tf_op jit(solution)/shard_map/ppermute | solution.py:346

commit v3 on v2

--- a/solution.py
+++ b/solution.py
@@ -12,7 +12,6 @@
 NT = (((1,), (1,)), ((), ()))
 NN = (((1,), (0,)), ((), ()))
 VMEM = pl.BlockSpec(memory_space=pltpu.VMEM)
-SMEM = pl.BlockSpec(memory_space=pltpu.SMEM)
 ANY = pl.BlockSpec(memory_space=pl.ANY)
 HBM = pl.BlockSpec(memory_space=pltpu.HBM)
 
@@ -30,12 +29,26 @@
     return (rho.astype(jnp.float32) * gram * factor).astype(jnp.bfloat16)
 
 
-def inner_kernel(u, w, live, index, tapers, out, done, sym, held):
-    rows, cols, _, cells = u.shape
+def prepare_kernel(tapers, sym):
     for n in range(tapers.shape[0]):
         t = tapers[n].astype(jnp.float32)
         sym[n] = 0.5 * (t + t.T)
 
+
+def prepare(tapers):
+    return pl.pallas_call(
+        prepare_kernel,
+        out_shape=jax.ShapeDtypeStruct(tapers.shape, jnp.float32),
+        in_specs=[VMEM],
+        out_specs=VMEM,
+        compiler_params=pltpu.CompilerParams(vmem_limit_bytes=GRANT),
+        cost_estimate=pl.CostEstimate(flops=0, bytes_accessed=16 << 20, transcendentals=0),
+        name="prepare",
+    )(tapers)
+
+
+def inner_kernel(u, w, live, index, tapers, sym, out, held):
+    rows, cols, _, cells = u.shape
     def ahead(a, b, last):
         near = [(4, a, b)]
         if b + 1 < cols:
@@ -47,14 +60,15 @@
         return near
 
     def row(a, last):
+        on, which = live[a], index[a]
         for b in range(cols):
             near = ahead(a, b, last)
             gram = dot(u[a, b], cat([u[p, q] for _, p, q in near], 1), TN)
             for n, (k, _, _) in enumerate(near):
-                at = index[a, b, k]
+                at = which[b, k]
                 rho = sym[at] if k == 4 else tapers[at]
                 held[b, :, (k - 4) * cells : (k - 3) * cells] = tapered(
-                    gram[:, n * cells : (n + 1) * cells], rho, live[a, b, k]
+                    gram[:, n * cells : (n + 1) * cells], rho, on[b, k]
                 )
         for b in range(cols):
             near = ahead(a, b, last)
@@ -81,25 +95,18 @@
         row(a, False)
 
     row(rows - 1, True)
-    done[...] = jnp.zeros_like(done)
-
-
-def inner(u, w, live, index, tapers):
+
+
+def inner(u, w, live, index, tapers, sym):
     rows, cols, members, cells = u.shape
     columns = w.shape[2]
     pairs = 5 * rows * cols
     return pl.pallas_call(
         inner_kernel,
-        out_shape=(
-            jax.ShapeDtypeStruct((rows, cols, columns, cells), jnp.float32),
-            jax.ShapeDtypeStruct((8, cells), jnp.float32),
-        ),
-        in_specs=[VMEM, VMEM, SMEM, SMEM, VMEM],
-        out_specs=(VMEM, VMEM),
-        scratch_shapes=[
-            pltpu.VMEM(tapers.shape, jnp.float32),
-            pltpu.VMEM((cols, cells, 5 * cells), jnp.bfloat16),
-        ],
+        out_shape=jax.ShapeDtypeStruct((rows, cols, columns, cells), jnp.float32),
+        in_specs=[VMEM] * 6,
+        out_specs=VMEM,
+        scratch_shapes=[pltpu.VMEM((cols, cells, 5 * cells), jnp.bfloat16)],
         compiler_params=pltpu.CompilerParams(vmem_limit_bytes=GRANT),
         cost_estimate=pl.CostEstimate(
             flops=2 * pairs * cells * cells * (members + 2 * columns),
@@ -107,16 +114,18 @@
             transcendentals=0,
         ),
         name="inner",
-    )(u, w, live, index, tapers)
+    )(u, w, live, index, tapers, sym)
 
 
 def above_kernel(s, u, w, left, right, live, index, tapers, back, held):
     cols, _, cells = s.shape
     members = u.shape[2]
     deep = members + w.shape[2]
+    on, which = live[0], index[0]
     notes = [near[0, deep:].astype(jnp.int32) for near in (left, right)]
     side = [notes[0][cols - 1, 2], notes[0][2 * cols - 1, 2], notes[1][0, 0], notes[1][cols, 0]]
 
+    sources = []
     for c in range(cols):
         grams, weights, lives, rhos = [], [], [], []
         for k in (6, 7, 8):
@@ -126,7 +135,7 @@
             elif q >= cols:
                 near, lively, at = right, side[2], side[3]
             else:
-                near, lively, at = None, live[0, q, 8 - k], index[0, q, 8 - k]
+                near, lively, at = None, on[q, 8 - k], which[q, 8 - k]
             grams.append(u[0, q] if near is None else near[0, :members])
             weights.append(w[0, q] if near is None else near[0, members:deep])
             lives.append(lively)
@@ -136,7 +145,9 @@
             [tapered(gram[:, n * cells : (n + 1) * cells], rhos[n], lives[n]) for n in range(3)], 1
         )
         held[c] = block
-        back[c] = dot(cat(weights, 1), block, NT).astype(jnp.bfloat16)
+        sources.append(cat(weights, 1))
+    for c in range(cols):
+        back[c] = dot(sources[c], held[c], NT).astype(jnp.bfloat16)
 
 
 def above(s, u, w, left, right, live, index, tapers):
@@ -149,7 +160,7 @@
             jax.ShapeDtypeStruct((cols, columns, cells), jnp.bfloat16),
             jax.ShapeDtypeStruct((cols, cells, 3 * cells), jnp.bfloat16),
         ),
-        in_specs=[VMEM, VMEM, VMEM, VMEM, VMEM, SMEM, SMEM, VMEM],
+        in_specs=[VMEM] * 8,
         out_specs=(VMEM, VMEM),
         compiler_params=pltpu.CompilerParams(vmem_limit_bytes=GRANT),
         cost_estimate=pl.CostEstimate(
@@ -165,6 +176,8 @@
     rows, cols, members, cells = u.shape
     deep = members + w.shape[2]
     last = cols - 1
+    on = [live[a] for a in range(rows)]
+    which = [index[a] for a in range(rows)]
     total = {}
 
     def add(a, q, value):
@@ -178,7 +191,7 @@
             if q == edge:
                 gram = dot(corner[far, :members], u[0, q], TN)
                 sources.append(corner[far, members:deep])
-                blocks.append(tapered(gram, tapers[index[0, q, 8 - k]], live[0, q, 8 - k]))
+                blocks.append(tapered(gram, tapers[which[0][q, 8 - k]], on[0][q, 8 - k]))
         add(0, q, dot(cat(sources, 1), cat(blocks, 0), NN))
 
     for a in range(rows):
@@ -186,7 +199,7 @@
         gram = dot(left[a, :members], cat([u[p, 0] for _, p in near], 1), TN)
         blocks = cat(
             [
-                tapered(gram[:, n * cells : (n + 1) * cells], tapers[index[p, 0, 8 - k]], live[p, 0, 8 - k])
+                tapered(gram[:, n * cells : (n + 1) * cells], tapers[which[p][0, 8 - k]], on[p][0, 8 - k])
                 for n, (k, p) in enumerate(near)
             ],
             1,
@@ -197,7 +210,7 @@
         gram = dot(u[a, last], cat([right[p, :members] for _, p in near], 1), TN)
         blocks = cat(
             [
-                tapered(gram[:, n * cells : (n + 1) * cells], tapers[index[a, last, k]], live[a, last, k])
+                tapered(gram[:, n * cells : (n + 1) * cells], tapers[which[a][last, k]], on[a][last, k])
                 for n, (k, _) in enumerate(near)
             ],
             1,
@@ -205,10 +218,10 @@
         add(a, last, dot(cat([right[p, members:deep] for _, p in near], 1), blocks, NT))
         if a + 1 < rows:
             gram = dot(u[a, 0], left[a + 1, :members], TN)
-            block = tapered(gram, tapers[index[a, 0, 6]], live[a, 0, 6])
+            block = tapered(gram, tapers[which[a][0, 6]], on[a][0, 6])
             add(a, 0, dot(left[a + 1, members:deep], block, NT))
             gram = dot(right[a, :members], u[a + 1, last], TN)
-            block = tapered(gram, tapers[index[a + 1, last, 2]], live[a + 1, last, 2])
+            block = tapered(gram, tapers[which[a + 1][last, 2]], on[a + 1][last, 2])
             add(a + 1, last, dot(right[a, members:deep], block, NN))
 
     for a in range(rows):
@@ -225,7 +238,7 @@
     return pl.pallas_call(
         outer_kernel,
         out_shape=(jax.ShapeDtypeStruct(inc.shape, inc.dtype), jax.ShapeDtypeStruct(inc.shape[1:], inc.dtype)),
-        in_specs=[VMEM] * 8 + [SMEM, SMEM, VMEM],
+        in_specs=[VMEM] * 11,
         out_specs=(VMEM, VMEM),
         compiler_params=pltpu.CompilerParams(vmem_limit_bytes=GRANT),
         cost_estimate=pl.CostEstimate(
@@ -289,14 +302,13 @@
         in_specs=[HBM, HBM],
         out_specs=VMEM,
         scratch_shapes=[pltpu.SemaphoreType.DMA((2,))],
-        compiler_params=pltpu.CompilerParams(vmem_limit_bytes=GRANT),
         cost_estimate=pl.CostEstimate(flops=0, bytes_accessed=4 * cols * shape[1] * cells, transcendentals=0),
         name="pack_row",
     )(u, w)
 
 
-def pack_columns_kernel(u, w, live, index, done, first, final, sem):
-    del done
+def pack_columns_kernel(u, w, live, index, sym, first, final, sem):
+    del sym
     rows, cols, members, cells = u.shape
     deep = members + w.shape[2]
     copies = []
@@ -315,7 +327,7 @@
         copy.wait()
 
 
-def pack_columns(u, w, live, index, done):
+def pack_columns(u, w, live, index, sym):
     rows, cols, members, cells = u.shape
     shape = (rows, members + w.shape[2] + 2 * cols, cells)
     return pl.pallas_call(
@@ -327,7 +339,7 @@
         compiler_params=pltpu.CompilerParams(vmem_limit_bytes=GRANT),
         cost_estimate=pl.CostEstimate(flops=0, bytes_accessed=8 * rows * shape[1] * cells, transcendentals=0),
         name="pack_columns",
-    )(u, w, live, index, done)
+    )(u, w, live, index, sym)
 
 
 def body(perturbations, weights, live, index, tapers):
@@ -335,10 +347,11 @@
     rows, cols, members, cells = u.shape
     deep = members + w.shape[2]
     s = lax.ppermute(pack_row(u, w), "row", forward("row"))
-    inc, done = inner(u, w, live, index, tapers)
-    first, final = pack_columns(u, w, live, index, done)
+    sym = prepare(tapers)
+    first, final = pack_columns(u, w, live, index, sym)
     left = lax.ppermute(final, "col", forward("col"))
     right = lax.ppermute(first, "col", backward("col"))
+    inc, left, right = lax.optimization_barrier((inner(u, w, live, index, tapers, sym), left, right))
     corner = lax.ppermute(
         jnp.stack([left[rows - 1, :deep], right[rows - 1, :deep]]), "row", forward("row")
     )

time: 37.9 us -> 31.7 us (0.84)
  the two profiles are of different devices: /device:TPU:1 before, /device:TPU:22 now
where the time goes in v3:
time: 31.7 us; the launch traced here: 31.2 us
  starting transfers between devices  15.7 us (50%)
  Pallas kernels  11 us (35%)
  waiting for transfers between devices  4.18 us (13%)
    pallas_call x1, Pallas kernels, inner(): pl.pallas_call(inner_kernel, out_shape=jax.ShapeDtypeStruct((rows, cols,...  4.44 us
    ppermute x1, starting transfers between devices, body(): right = lax.ppermute(first, 'col', backward('col'))  3.64 us
    ppermute x1, starting transfers between devices, body(): lax.ppermute(jnp.stack([left[rows - 1, :deep], right[rows - 1, :deep]]),...  3.43 us
    ppermute x1, starting transfers between devices, body(): s = lax.ppermute(pack_row(u, w), 'row', forward('row'))  3.43 us
    ppermute x1, starting transfers between devices, body(): back = lax.ppermute(back, 'row', backward('row'))  3.32 us
    pallas_call x1, Pallas kernels, outer(): pl.pallas_call(outer_kernel, out_shape=(jax.ShapeDtypeStruct(inc.shape, i...  2.63 us
    pallas_call x1, Pallas kernels, pack_row(): pl.pallas_call(pack_row_kernel, out_shape=jax.ShapeDtypeStruct(shape, u.d...  2.08 us
    ppermute x1, waiting for transfers between devices, body(): s = lax.ppermute(pack_row(u, w), 'row', forward('row'))  2.08 us
  transfers between devices with their start and end apart: 5, of which 3 were waited for; matrix products, arithmetic and copies ran while one was open for 0% of the time, Pallas kernels for 26%

profile of v3, /device:TPU:22, one launch (start us, length us, event | category | flops | bytes accessed | tf_op | source)
XLA Modules:
  0.0 31.2 jit_solution(5291718277713865501)
XLA Ops:
  0.0 0.0 copy-start.1
  0.0 0.0 copy-start
  0.0 0.0 copy-start.2
  0.0 0.0 copy-start.4
  0.0 0.0 copy-start.3
  0.0 2.1 %pack_row.1 = bf16[8,320,128]{2,1,0:T(8,128)(2,1)} custom-call(bf16[4,8,256,128]{3,2,1,0:T(8,128)(2,1)} %u.9, bf16[4,8,64,128]{3,2,1,0:T(8,128)(2,1)} %w.9), custom_call_target="tpu_custom_call" | custom-call | bytes 1310720 | tf_op jit(solution)/shard_map/pack_row/pallas_call | solution.py:299
  2.1 3.4 %collective-permute-start.2 = (bf16[8,320,128]{2,1,0:T(8,128)(2,1)}, bf16[8,320,128]{2,1,0:T(8,128)(2,1)S(1)}, u32[]{:S(2)}, u32[]{:S(2)}) collective-permute-start(bf16[8,320,128]{2,1,0:T(8,128)(2,1)} %pack_row.1), channel_id=1, source_target_pairs={{0,4},{4,8},{8,12},{12,16},{16,20},{20,24},{24,28},{1,5},{5,9},{9,... | collective-permute-start | bytes 1966088 | tf_op jit(solution)/shard_map/ppermute | solution.py:349
  5.6 0.0 copy-done.2
  5.6 0.2 prepare.1.sym
  5.8 0.0 copy-done.1
  5.8 0.0 copy-done
  5.8 0.0 copy-done.4
  5.8 0.0 copy-done.3
  5.8 0.1 pack_columns.1
  6.0 1.9 %collective-permute-start = (bf16[4,336,128]{2,1,0:T(8,128)(2,1)S(1)}, bf16[4,336,128]{2,1,0:T(8,128)(2,1)S(1)}, u32[]{:S(2)}, u32[]{:S(2)}) collective-permute-start(bf16[4,336,128]{2,1,0:T(8,128)(2,1)S(1)} %get-tuple-element.14), channel_id=1, source_target_pairs={{0,1},{1,2},{2,3},{4,5},{5,6},{6,7},{8,9},{9,10},{10,11},{12,13},{... | collective-permute-start | bytes 1032200 | tf_op jit(solution)/shard_map/ppermute | solution.py:352
  7.9 3.6 %collective-permute-start.1 = (bf16[4,336,128]{2,1,0:T(8,128)(2,1)S(1)}, bf16[4,336,128]{2,1,0:T(8,128)(2,1)S(1)}, u32[]{:S(2)}, u32[]{:S(2)}) collective-permute-start(bf16[4,336,128]{2,1,0:T(8,128)(2,1)S(1)} %get-tuple-element.15), channel_id=1, source_target_pairs={{1,0},{2,1},{3,2},{5,4},{6,5},{7,6},{9,8},{10,9},{11,10},{13,12},{... | collective-permute-start | bytes 1032200 | tf_op jit(solution)/shard_map/ppermute | solution.py:353
  11.5 4.4 %inner.1.inc = f32[4,8,64,128]{3,2,1,0:T(8,128)S(1)} custom-call(bf16[4,8,256,128]{3,2,1,0:T(8,128)(2,1)S(1)} %copy-done, bf16[4,8,64,128]{3,2,1,0:T(8,128)(2,1)S(1)} %copy-done.1, s32[4,8,9]{2,1,0:T(8,128)S(1)} %copy-done.3, s32[4,8,9]{2,1,0:T(8,128)S(1)} %copy-done.4, bf16[16,128,128]{2,1,0:T(8,128)(2,1)S(1)} %copy-done.2, f32[16,128,128]{2,1,0:T(8,128)S(1)} %prepare.1.sym), custom_call_target="tpu_custom_call" | custom-call | flops 2013265920 | bytes 4194304 | tf_op jit(solution)/shard_map/inner/pallas_call | solution.py:104
  16.0 0.0 collective-permute-done.left
  16.0 0.3 collective-permute-done.1.right
  16.3 3.4 %collective-permute-start.3 = (bf16[2,320,128]{2,1,0:T(8,128)(2,1)S(1)}, bf16[2,320,128]{2,1,0:T(8,128)(2,1)S(1)}, u32[]{:S(2)}, u32[]{:S(2)}) collective-permute-start(bf16[2,320,128]{2,1,0:T(8,128)(2,1)S(1)} %pad_maximum_fusion), channel_id=1, source_target_pairs={{0,4},{4,8},{8,12},{12,16},{16,20},{20,24},{24,28},{1,5},{5,9},{9,... | collective-permute-start | bytes 491528 | tf_op jit(solution)/shard_map/ppermute | solution.py:355
  19.8 2.1 %collective-permute-done.2.s = bf16[8,320,128]{2,1,0:T(8,128)(2,1)S(1)} collective-permute-done((bf16[8,320,128]{2,1,0:T(8,128)(2,1)}, bf16[8,320,128]{2,1,0:T(8,128)(2,1)S(1)}, u32[]{:S(2)}, u32[]{:S(2)}) %collective-permute-start.2) | collective-permute-done | bytes 655392 | tf_op jit(solution)/shard_map/ppermute | solution.py:349
  21.8 0.8 %above.1 = (bf16[8,64,128]{2,1,0:T(8,128)(2,1)S(1)}, bf16[8,128,384]{2,1,0:T(8,128)(2,1)S(1)}) custom-call(bf16[8,320,128]{2,1,0:T(8,128)(2,1)S(1)} %collective-permute-done.2.s, bf16[4,8,256,128]{3,2,1,0:T(8,128)(2,1)S(1)} %copy-done, bf16[4,8,64,128]{3,2,1,0:T(8,128)(2,1)S(1)} %copy-done.1, bf16[4,336,128]{2,1,0:T(8,128)(2,1)S(1)} %collective-permute-done.left, ...), custom_call_target="tpu_custom_call" | custom-call | flops 251658240 | bytes 2097152 | tf_op jit(solution)/shard_map/above/pallas_call | solution.py:157
  22.7 3.3 %collective-permute-start.4 = (bf16[8,64,128]{2,1,0:T(8,128)(2,1)S(1)}, bf16[8,64,128]{2,1,0:T(8,128)(2,1)S(1)}, u32[]{:S(2)}, u32[]{:S(2)}) collective-permute-start(bf16[8,64,128]{2,1,0:T(8,128)(2,1)S(1)} %get-tuple-element.22), channel_id=1, source_target_pairs={{4,0},{8,4},{12,8},{16,12},{20,16},{24,20},{28,24},{5,1},{9,5},{13... | collective-permute-start | bytes 393224 | tf_op jit(solution)/shard_map/ppermute | solution.py:359
  26.0 0.0 collective-permute-done.3.corner
  26.0 2.6 %outer.1 = (f32[4,8,64,128]{3,2,1,0:T(8,128)}, f32[8,64,128]{2,1,0:T(8,128)S(1)}) custom-call(f32[4,8,64,128]{3,2,1,0:T(8,128)S(1)} %inner.1.inc, bf16[8,128,384]{2,1,0:T(8,128)(2,1)S(1)} %get-tuple-element.19.held, bf16[8,320,128]{2,1,0:T(8,128)(2,1)S(1)} %collective-permute-done.2.s, bf16[2,320,128]{2,1,0:T(8,128)(2,1)S(1)} %collective-permute-done.3.corner, ...), custom_call_target="tpu_custom_call" | custom-call | flops 503316480 | bytes 4194304 | tf_op jit(solution)/shard_map/outer/pallas_call | solution.py:238
  28.6 1.8 %collective-permute-done.4.back = bf16[8,64,128]{2,1,0:T(8,128)(2,1)S(1)} collective-permute-done((bf16[8,64,128]{2,1,0:T(8,128)(2,1)S(1)}, bf16[8,64,128]{2,1,0:T(8,128)(2,1)S(1)}, u32[]{:S(2)}, u32[]{:S(2)}) %collective-permute-start.4) | collective-permute-done | bytes 131104 | tf_op jit(solution)/shard_map/ppermute | solution.py:359
  30.4 0.7 %finish.1 = f32[4,8,64,128]{3,2,1,0:T(8,128)} custom-call(f32[4,8,64,128]{3,2,1,0:T(8,128)} %get-tuple-element.20.inc, f32[8,64,128]{2,1,0:T(8,128)S(1)} %get-tuple-element.21.low, bf16[8,64,128]{2,1,0:T(8,128)(2,1)S(1)} %collective-permute-done.4.back), custom_call_target="tpu_custom_call", output_to_operand_aliasing={{}: (0, {})} | custom-call | flops 65536 | bytes 655360 | tf_op jit(solution)/shard_map/finish/pallas_call | solution.py:262
  (3 shorter events, 0.0 us)
Async XLA Ops:
  0.0 5.8 %copy-start.1 = (bf16[4,8,64,128]{3,2,1,0:T(8,128)(2,1)S(1)}, bf16[4,8,64,128]{3,2,1,0:T(8,128)(2,1)}, u32[]{:S(2)}) copy-start(bf16[4,8,64,128]{3,2,1,0:T(8,128)(2,1)} %w.9) | copy-start | bytes 1572868
  0.0 5.8 %copy-start = (bf16[4,8,256,128]{3,2,1,0:T(8,128)(2,1)S(1)}, bf16[4,8,256,128]{3,2,1,0:T(8,128)(2,1)}, u32[]{:S(2)}) copy-start(bf16[4,8,256,128]{3,2,1,0:T(8,128)(2,1)} %u.9) | copy-start | bytes 6291460
  0.0 5.6 %copy-start.2 = (bf16[16,128,128]{2,1,0:T(8,128)(2,1)S(1)}, bf16[16,128,128]{2,1,0:T(8,128)(2,1)}, u32[]{:S(2)}) copy-start(bf16[16,128,128]{2,1,0:T(8,128)(2,1)} %tapers.7) | copy-start | bytes 1572868
  0.0 5.8 %copy-start.4 = (s32[4,8,9]{2,1,0:T(8,128)S(1)}, s32[4,8,9]{2,1,0:T(8,128)}, u32[]{:S(2)}) copy-start(s32[4,8,9]{2,1,0:T(8,128)} %index.7) | copy-start | bytes 3460
  0.0 5.8 %copy-start.3 = (s32[4,8,9]{2,1,0:T(8,128)S(1)}, s32[4,8,9]{2,1,0:T(8,128)}, u32[]{:S(2)}) copy-start(s32[4,8,9]{2,1,0:T(8,128)} %live.7) | copy-start | bytes 3460
  2.1 19.7 %collective-permute-start.2 = (bf16[8,320,128]{2,1,0:T(8,128)(2,1)}, bf16[8,320,128]{2,1,0:T(8,128)(2,1)S(1)}, u32[]{:S(2)}, u32[]{:S(2)}) collective-permute-start(bf16[8,320,128]{2,1,0:T(8,128)(2,1)} %pack_row.1), channel_id=1, source_target_pairs={{0,4},{4,8},{8,12},{12,16},{16,20},{20,24},{24,28},{1,5},{5,9},{9,... | collective-permute-start | bytes 1966088 | tf_op jit(solution)/shard_map/ppermute | solution.py:349
  6.0 10.0 %collective-permute-start = (bf16[4,336,128]{2,1,0:T(8,128)(2,1)S(1)}, bf16[4,336,128]{2,1,0:T(8,128)(2,1)S(1)}, u32[]{:S(2)}, u32[]{:S(2)}) collective-permute-start(bf16[4,336,128]{2,1,0:T(8,128)(2,1)S(1)} %get-tuple-element.14), channel_id=1, source_target_pairs={{0,1},{1,2},{2,3},{4,5},{5,6},{6,7},{8,9},{9,10},{10,11},{12,13},{... | collective-permute-start | bytes 1032200 | tf_op jit(solution)/shard_map/ppermute | solution.py:352
  7.9 8.4 %collective-permute-start.1 = (bf16[4,336,128]{2,1,0:T(8,128)(2,1)S(1)}, bf16[4,336,128]{2,1,0:T(8,128)(2,1)S(1)}, u32[]{:S(2)}, u32[]{:S(2)}) collective-permute-start(bf16[4,336,128]{2,1,0:T(8,128)(2,1)S(1)} %get-tuple-element.15), channel_id=1, source_target_pairs={{1,0},{2,1},{3,2},{5,4},{6,5},{7,6},{9,8},{10,9},{11,10},{13,12},{... | collective-permute-start | bytes 1032200 | tf_op jit(solution)/shard_map/ppermute | solution.py:353
  16.3 9.7 %collective-permute-start.3 = (bf16[2,320,128]{2,1,0:T(8,128)(2,1)S(1)}, bf16[2,320,128]{2,1,0:T(8,128)(2,1)S(1)}, u32[]{:S(2)}, u32[]{:S(2)}) collective-permute-start(bf16[2,320,128]{2,1,0:T(8,128)(2,1)S(1)} %pad_maximum_fusion), channel_id=1, source_target_pairs={{0,4},{4,8},{8,12},{12,16},{16,20},{20,24},{24,28},{1,5},{5,9},{9,... | collective-permute-start | bytes 491528 | tf_op jit(solution)/shard_map/ppermute | solution.py:355
  22.7 7.8 %collective-permute-start.4 = (bf16[8,64,128]{2,1,0:T(8,128)(2,1)S(1)}, bf16[8,64,128]{2,1,0:T(8,128)(2,1)S(1)}, u32[]{:S(2)}, u32[]{:S(2)}) collective-permute-start(bf16[8,64,128]{2,1,0:T(8,128)(2,1)S(1)} %get-tuple-element.22), channel_id=1, source_target_pairs={{4,0},{8,4},{12,8},{16,12},{20,16},{24,20},{28,24},{5,1},{9,5},{13... | collective-permute-start | bytes 393224 | tf_op jit(solution)/shard_map/ppermute | solution.py:359

commit v4 on v3

--- a/solution.py
+++ b/solution.py
@@ -27,6 +27,18 @@
 def tapered(gram, rho, live):
     factor = live.astype(jnp.float32) * SCALE
     return (rho.astype(jnp.float32) * gram * factor).astype(jnp.bfloat16)
+
+
+def even_column():
+    return lax.rem(lax.axis_index("col"), 2) == 0
+
+
+def sides(inside, outside):
+    even = even_column()
+    return (
+        lambda *at: jnp.where(even, outside[at], inside[at]),
+        lambda *at: jnp.where(even, inside[at], outside[at]),
+    )
 
 
 def prepare_kernel(tapers, sym):
@@ -117,12 +129,13 @@
     )(u, w, live, index, tapers, sym)
 
 
-def above_kernel(s, u, w, left, right, live, index, tapers, back, held):
+def above_kernel(s, u, w, inside, outside, live, index, tapers, back, held):
     cols, _, cells = s.shape
     members = u.shape[2]
     deep = members + w.shape[2]
+    left, right = sides(inside, outside)
     on, which = live[0], index[0]
-    notes = [near[0, deep:].astype(jnp.int32) for near in (left, right)]
+    notes = [near(0, slice(deep, None)).astype(jnp.int32) for near in (left, right)]
     side = [notes[0][cols - 1, 2], notes[0][2 * cols - 1, 2], notes[1][0, 0], notes[1][cols, 0]]
 
     sources = []
@@ -136,8 +149,8 @@
                 near, lively, at = right, side[2], side[3]
             else:
                 near, lively, at = None, on[q, 8 - k], which[q, 8 - k]
-            grams.append(u[0, q] if near is None else near[0, :members])
-            weights.append(w[0, q] if near is None else near[0, members:deep])
+            grams.append(u[0, q] if near is None else near(0, slice(0, members)))
+            weights.append(w[0, q] if near is None else near(0, slice(members, deep)))
             lives.append(lively)
             rhos.append(tapers[at])
         gram = dot(s[c, :members], cat(grams, 1), TN)
@@ -150,7 +163,7 @@
         back[c] = dot(sources[c], held[c], NT).astype(jnp.bfloat16)
 
 
-def above(s, u, w, left, right, live, index, tapers):
+def above(s, u, w, inside, outside, live, index, tapers):
     cols, _, cells = s.shape
     columns = w.shape[2]
     members = u.shape[2]
@@ -169,13 +182,15 @@
             transcendentals=0,
         ),
         name="above",
-    )(s, u, w, left, right, live, index, tapers)
-
-
-def outer_kernel(inc, held, s, corner, u, w, left, right, live, index, tapers, out, low):
+    )(s, u, w, inside, outside, live, index, tapers)
+
+
+def outer_kernel(inc, held, s, corner, u, w, inside, outside, live, index, tapers, out, low):
     rows, cols, members, cells = u.shape
     deep = members + w.shape[2]
     last = cols - 1
+    left, right = sides(inside, outside)
+    first = even_column().astype(jnp.int32)
     on = [live[a] for a in range(rows)]
     which = [index[a] for a in range(rows)]
     total = {}
@@ -187,7 +202,7 @@
         back = [(k, q - (k - 7)) for k in (6, 7, 8) if 0 <= q - (k - 7) < cols]
         sources = [s[c, members:deep] for _, c in back]
         blocks = [held[c, :, (k - 6) * cells : (k - 5) * cells] for k, c in back]
-        for edge, k, far in ((0, 8, 0), (last, 6, 1)):
+        for edge, k, far in ((0, 8, first), (last, 6, 1 - first)):
             if q == edge:
                 gram = dot(corner[far, :members], u[0, q], TN)
                 sources.append(corner[far, members:deep])
@@ -196,7 +211,7 @@
 
     for a in range(rows):
         near = [(5, a)] + ([(8, a + 1)] if a + 1 < rows else [])
-        gram = dot(left[a, :members], cat([u[p, 0] for _, p in near], 1), TN)
+        gram = dot(left(a, slice(0, members)), cat([u[p, 0] for _, p in near], 1), TN)
         blocks = cat(
             [
                 tapered(gram[:, n * cells : (n + 1) * cells], tapers[which[p][0, 8 - k]], on[p][0, 8 - k])
@@ -204,10 +219,10 @@
             ],
             1,
         )
-        both = dot(left[a, members:deep], blocks, NN)
+        both = dot(left(a, slice(members, deep)), blocks, NN)
         for n, (_, p) in enumerate(near):
             add(p, 0, both[:, n * cells : (n + 1) * cells])
-        gram = dot(u[a, last], cat([right[p, :members] for _, p in near], 1), TN)
+        gram = dot(u[a, last], cat([right(p, slice(0, members)) for _, p in near], 1), TN)
         blocks = cat(
             [
                 tapered(gram[:, n * cells : (n + 1) * cells], tapers[which[a][last, k]], on[a][last, k])
@@ -215,14 +230,14 @@
             ],
             1,
         )
-        add(a, last, dot(cat([right[p, members:deep] for _, p in near], 1), blocks, NT))
+        add(a, last, dot(cat([right(p, slice(members, deep)) for _, p in near], 1), blocks, NT))
         if a + 1 < rows:
-            gram = dot(u[a, 0], left[a + 1, :members], TN)
+            gram = dot(u[a, 0], left(a + 1, slice(0, members)), TN)
             block = tapered(gram, tapers[which[a][0, 6]], on[a][0, 6])
-            add(a, 0, dot(left[a + 1, members:deep], block, NT))
-            gram = dot(right[a, :members], u[a + 1, last], TN)
+            add(a, 0, dot(left(a + 1, slice(members, deep)), block, NT))
+            gram = dot(right(a, slice(0, members)), u[a + 1, last], TN)
             block = tapered(gram, tapers[which[a + 1][last, 2]], on[a + 1][last, 2])
-            add(a + 1, last, dot(right[a, members:deep], block, NN))
+            add(a + 1, last, dot(right(a, slice(members, deep)), block, NN))
 
     for a in range(rows):
         for q in range(cols):
@@ -232,7 +247,7 @@
                 low[q] = value
 
 
-def outer(inc, held, s, corner, u, w, left, right, live, index, tapers):
+def outer(inc, held, s, corner, u, w, inside, outside, live, index, tapers):
     rows, cols, members, cells = u.shape
     columns = w.shape[2]
     return pl.pallas_call(
@@ -247,7 +262,7 @@
             transcendentals=0,
         ),
         name="outer",
-    )(inc, held, s, corner, u, w, left, right, live, index, tapers)
+    )(inc, held, s, corner, u, w, inside, outside, live, index, tapers)
 
 
 def finish_kernel(inc, low, back, out, total, sem):
@@ -274,6 +289,11 @@
 
 def forward(axis):
     return [(i, i + 1) for i in range(lax.axis_size(axis) - 1)]
+
+
+def swaps(axis, start):
+    pairs = [(i, i + 1) for i in range(start, lax.axis_size(axis) - 1, 2)]
+    return pairs + [(b, a) for a, b in pairs]
 
 
 def backward(axis):
@@ -298,7 +318,7 @@
     shape = (cols, members + w.shape[2], cells)
     return pl.pallas_call(
         pack_row_kernel,
-        out_shape=jax.ShapeDtypeStruct(shape, u.dtype),
+        out_shape=pltpu.VMEM(shape, u.dtype),
         in_specs=[HBM, HBM],
         out_specs=VMEM,
         scratch_shapes=[pltpu.SemaphoreType.DMA((2,))],
@@ -307,12 +327,13 @@
     )(u, w)
 
 
-def pack_columns_kernel(u, w, live, index, sym, first, final, sem):
+def pack_columns_kernel(u, w, live, index, sym, inner_side, outer_side, sem):
     del sym
     rows, cols, members, cells = u.shape
     deep = members + w.shape[2]
+    turn = (cols - 1) * even_column().astype(jnp.int32)
     copies = []
-    for n, (out, b) in enumerate(((first, 0), (final, cols - 1))):
+    for n, (out, b) in enumerate(((inner_side, turn), (outer_side, cols - 1 - turn))):
         copies.append(pltpu.make_async_copy(u.at[:, b], out.at[:, :members], sem.at[n, 0]))
         copies.append(pltpu.make_async_copy(w.at[:, b], out.at[:, members:deep], sem.at[n, 1]))
     for copy in copies:
@@ -321,8 +342,8 @@
         lines = jnp.concatenate([live[a], index[a]], 0).astype(jnp.float32)
         blank = jnp.zeros((2 * cols, cells - live.shape[2]), jnp.float32)
         note = jnp.concatenate([lines, blank], 1).astype(jnp.bfloat16)
-        first[a, deep:] = note
-        final[a, deep:] = note
+        inner_side[a, deep:] = note
+        outer_side[a, deep:] = note
     for copy in copies:
         copy.wait()
 
@@ -343,21 +364,22 @@
 
 
 def body(perturbations, weights, live, index, tapers):
-    u, w = perturbations, weights
-    rows, cols, members, cells = u.shape
-    deep = members + w.shape[2]
-    s = lax.ppermute(pack_row(u, w), "row", forward("row"))
+    rows, cols, members, cells = perturbations.shape
+    deep = members + weights.shape[2]
+    row = pack_row(perturbations, weights)
+    row, u, w, tapers = lax.optimization_barrier((row, perturbations, weights, tapers))
+    s = lax.ppermute(row, "row", forward("row"))
     sym = prepare(tapers)
-    first, final = pack_columns(u, w, live, index, sym)
-    left = lax.ppermute(final, "col", forward("col"))
-    right = lax.ppermute(first, "col", backward("col"))
-    inc, left, right = lax.optimization_barrier((inner(u, w, live, index, tapers, sym), left, right))
+    inner_side, outer_side = pack_columns(u, w, live, index, sym)
+    inside = lax.ppermute(inner_side, "col", swaps("col", 0))
+    outside = lax.ppermute(outer_side, "col", swaps("col", 1))
+    inc, inside, outside = lax.optimization_barrier((inner(u, w, live, index, tapers, sym), inside, outside))
     corner = lax.ppermute(
-        jnp.stack([left[rows - 1, :deep], right[rows - 1, :deep]]), "row", forward("row")
+        jnp.stack([inside[rows - 1, :deep], outside[rows - 1, :deep]]), "row", forward("row")
     )
-    back, held = above(s, u, w, left, right, live, index, tapers)
+    back, held = above(s, u, w, inside, outside, live, index, tapers)
     back = lax.ppermute(back, "row", backward("row"))
-    inc, low = outer(inc, held, s, corner, u, w, left, right, live, index, tapers)
+    inc, low = outer(inc, held, s, corner, u, w, inside, outside, live, index, tapers)
     return finish(inc, low, back)
 
 

time: 31.7 us -> 30.3 us (0.956)
  starting transfers between devices: 15.7 us -> 12.8 us
  waiting for transfers between devices: 4.18 us -> 5.86 us
  local copies, waits for them, and re-layouts: 0.03 us -> 1.07 us
  Pallas kernels: 11 us -> 10.2 us
    ppermute x4, starting transfers between devices: 12.4 us -> 9.46 us  [the longest x1 3.43 us: body(): s = lax.ppermute(row, 'row', forward('row'))]
    ppermute x4, waiting for transfers between devices: 2.38 us -> 4.06 us  [the longest x1 2.49 us: body(): s = lax.ppermute(row, 'row', forward('row'))]
    unnamed x10 -> x12, local copies, waits for them, and re-layouts: 0.02 us -> 1.06 us
    pallas_call x1, Pallas kernels: 2.08 us -> 1.23 us  [pack_row(): pl.pallas_call(pack_row_kernel, out_shape=pltpu.VMEM(shape, u.dtype), in_...]
  transfers between devices with their start and end apart: 5 -> 5, of which waited for: 3 -> 3; matrix products, arithmetic and copies ran while one was open for 0% -> 0% of each run, Pallas kernels for 26% -> 27%
where the time goes in v4:
time: 30.3 us; the launch traced here: 30.1 us
  starting transfers between devices  12.8 us (42%)
  Pallas kernels  10.2 us (34%)
  waiting for transfers between devices  5.86 us (19%)
  local copies, waits for them, and re-layouts  1.07 us (4%)
    pallas_call x1, Pallas kernels, inner(): pl.pallas_call(inner_kernel, out_shape=jax.ShapeDtypeStruct((rows, cols,...  4.44 us
    ppermute x1, starting transfers between devices, body(): s = lax.ppermute(row, 'row', forward('row'))  3.43 us
    ppermute x1, starting transfers between devices, body(): lax.ppermute(jnp.stack([inside[rows - 1, :deep], outside[rows - 1, :deep]...  3.43 us
    ppermute x1, starting transfers between devices, body(): back = lax.ppermute(back, 'row', backward('row'))  3.31 us
    pallas_call x1, Pallas kernels, outer(): pl.pallas_call(outer_kernel, out_shape=(jax.ShapeDtypeStruct(inc.shape, i...  2.63 us
    ppermute x1, starting transfers between devices, body(): outside = lax.ppermute(outer_side, 'col', swaps('col', 1))  2.53 us
    ppermute x1, waiting for transfers between devices, body(): s = lax.ppermute(row, 'row', forward('row'))  2.49 us
    ppermute x1, waiting for transfers between devices, body(): back = lax.ppermute(back, 'row', backward('row'))  1.81 us
  transfers between devices with their start and end apart: 5, of which 3 were waited for; matrix products, arithmetic and copies ran while one was open for 0% of the time, Pallas kernels for 27%

profile of v4, /device:TPU:22, one launch (start us, length us, event | category | flops | bytes accessed | tf_op | source)
XLA Modules:
  0.0 30.1 jit_solution(7691637212190635572)
XLA Ops:
  0.0 0.0 copy-start.1
  0.0 0.0 copy-start
  0.0 0.0 copy-start.5
  0.0 0.0 copy-start.4
  0.0 1.2 %pack_row.1 = bf16[8,320,128]{2,1,0:T(8,128)(2,1)S(1)} custom-call(bf16[4,8,256,128]{3,2,1,0:T(8,128)(2,1)} %u.5, bf16[4,8,64,128]{3,2,1,0:T(8,128)(2,1)} %w.5), custom_call_target="tpu_custom_call" | custom-call | bytes 1310720 | tf_op jit(solution)/shard_map/pack_row/pallas_call | solution.py:319
  1.3 3.4 %collective-permute-start.2 = (bf16[8,320,128]{2,1,0:T(8,128)(2,1)S(1)}, bf16[8,320,128]{2,1,0:T(8,128)(2,1)S(1)}, u32[]{:S(2)}, u32[]{:S(2)}) collective-permute-start(bf16[8,320,128]{2,1,0:T(8,128)(2,1)S(1)} %pack_row.1), channel_id=1, source_target_pairs={{0,4},{4,8},{8,12},{12,16},{16,20},{20,24},{24,28},{1,5},{5,9},{9,... | collective-permute-start | bytes 1966088 | tf_op jit(solution)/shard_map/ppermute | solution.py:371
  4.7 0.0 copy-start.2
  4.7 1.0 %copy-done.2 = bf16[16,128,128]{2,1,0:T(8,128)(2,1)S(1)} copy-done((bf16[16,128,128]{2,1,0:T(8,128)(2,1)S(1)}, bf16[16,128,128]{2,1,0:T(8,128)(2,1)}, u32[]{:S(2)}) %copy-start.2) | copy-done | bytes 524312
  5.7 0.2 prepare.1.sym
  6.0 0.0 copy-done.1
  6.0 0.0 copy-done
  6.0 0.0 copy-done.5
  6.0 0.0 copy-done.4
  6.0 0.0 copy-start.3
  6.0 0.1 pack_columns.1
  6.2 0.1 collective-permute-start
  6.2 2.5 %collective-permute-start.1 = (bf16[4,336,128]{2,1,0:T(8,128)(2,1)S(1)}, bf16[4,336,128]{2,1,0:T(8,128)(2,1)S(1)}, u32[]{:S(2)}, u32[]{:S(2)}) collective-permute-start(bf16[4,336,128]{2,1,0:T(8,128)(2,1)S(1)} %get-tuple-element.22), channel_id=1, source_target_pairs={{1,2},{2,1},{5,6},{6,5},{9,10},{10,9},{13,14},{14,13},{17,18},{18,... | collective-permute-start | bytes 1032200 | tf_op jit(solution)/shard_map/ppermute | solution.py:375
  8.8 0.0 copy-done.3
  8.8 4.4 %inner.1.inc = f32[4,8,64,128]{3,2,1,0:T(8,128)S(1)} custom-call(bf16[4,8,256,128]{3,2,1,0:T(8,128)(2,1)S(1)} %copy-done, bf16[4,8,64,128]{3,2,1,0:T(8,128)(2,1)S(1)} %copy-done.1, s32[4,8,9]{2,1,0:T(8,128)S(1)} %copy-done.4, s32[4,8,9]{2,1,0:T(8,128)S(1)} %copy-done.5, bf16[16,128,128]{2,1,0:T(8,128)(2,1)S(1)} %copy-done.3, f32[16,128,128]{2,1,0:T(8,128)S(1)} %prepare.1.sym), custom_call_target="tpu_custom_call" | custom-call | flops 2013265920 | bytes 4194304 | tf_op jit(solution)/shard_map/inner/pallas_call | solution.py:116
  13.2 0.0 collective-permute-done.inside
  13.2 1.6 %collective-permute-done.1.outside = bf16[4,336,128]{2,1,0:T(8,128)(2,1)S(1)} collective-permute-done((bf16[4,336,128]{2,1,0:T(8,128)(2,1)S(1)}, bf16[4,336,128]{2,1,0:T(8,128)(2,1)S(1)}, u32[]{:S(2)}, u32[]{:S(2)}) %collective-permute-start.1) | collective-permute-done | bytes 344096 | tf_op jit(solution)/shard_map/ppermute | solution.py:375
  14.8 3.4 %collective-permute-start.3 = (bf16[2,320,128]{2,1,0:T(8,128)(2,1)S(1)}, bf16[2,320,128]{2,1,0:T(8,128)(2,1)S(1)}, u32[]{:S(2)}, u32[]{:S(2)}) collective-permute-start(bf16[2,320,128]{2,1,0:T(8,128)(2,1)S(1)} %pad_maximum_fusion), channel_id=1, source_target_pairs={{0,4},{4,8},{8,12},{12,16},{16,20},{20,24},{24,28},{1,5},{5,9},{9,... | collective-permute-start | bytes 491528 | tf_op jit(solution)/shard_map/ppermute | solution.py:377
  18.3 2.5 %collective-permute-done.2.s = bf16[8,320,128]{2,1,0:T(8,128)(2,1)S(1)} collective-permute-done((bf16[8,320,128]{2,1,0:T(8,128)(2,1)S(1)}, bf16[8,320,128]{2,1,0:T(8,128)(2,1)S(1)}, u32[]{:S(2)}, u32[]{:S(2)}) %collective-permute-start.2) | collective-permute-done | bytes 655392 | tf_op jit(solution)/shard_map/ppermute | solution.py:371
  20.8 0.8 %above.1 = (bf16[8,64,128]{2,1,0:T(8,128)(2,1)S(1)}, bf16[8,128,384]{2,1,0:T(8,128)(2,1)S(1)}) custom-call(bf16[8,320,128]{2,1,0:T(8,128)(2,1)S(1)} %collective-permute-done.2.s, bf16[4,8,256,128]{3,2,1,0:T(8,128)(2,1)S(1)} %copy-done, bf16[4,8,64,128]{3,2,1,0:T(8,128)(2,1)S(1)} %copy-done.1, bf16[4,336,128]{2,1,0:T(8,128)(2,1)S(1)} %collective-permute-done.inside, ...), custom_call_target="tpu_custom_call" | custom-call | flops 251658240 | bytes 2097152 | tf_op jit(solution)/shard_map/above/pallas_call | solution.py:170
  21.6 3.3 %collective-permute-start.4 = (bf16[8,64,128]{2,1,0:T(8,128)(2,1)S(1)}, bf16[8,64,128]{2,1,0:T(8,128)(2,1)S(1)}, u32[]{:S(2)}, u32[]{:S(2)}) collective-permute-start(bf16[8,64,128]{2,1,0:T(8,128)(2,1)S(1)} %get-tuple-element.30), channel_id=1, source_target_pairs={{4,0},{8,4},{12,8},{16,12},{20,16},{24,20},{28,24},{5,1},{9,5},{13... | collective-permute-start | bytes 393224 | tf_op jit(solution)/shard_map/ppermute | solution.py:381
  24.9 0.0 collective-permute-done.3.corner
  24.9 2.6 %outer.1 = (f32[4,8,64,128]{3,2,1,0:T(8,128)}, f32[8,64,128]{2,1,0:T(8,128)S(1)}) custom-call(f32[4,8,64,128]{3,2,1,0:T(8,128)S(1)} %inner.1.inc, bf16[8,128,384]{2,1,0:T(8,128)(2,1)S(1)} %get-tuple-element.27.held, bf16[8,320,128]{2,1,0:T(8,128)(2,1)S(1)} %collective-permute-done.2.s, bf16[2,320,128]{2,1,0:T(8,128)(2,1)S(1)} %collective-permute-done.3.corner, ...), custom_call_target="tpu_custom_call" | custom-call | flops 503316480 | bytes 4194304 | tf_op jit(solution)/shard_map/outer/pallas_call | solution.py:253
  27.5 1.8 %collective-permute-done.4.back = bf16[8,64,128]{2,1,0:T(8,128)(2,1)S(1)} collective-permute-done((bf16[8,64,128]{2,1,0:T(8,128)(2,1)S(1)}, bf16[8,64,128]{2,1,0:T(8,128)(2,1)S(1)}, u32[]{:S(2)}, u32[]{:S(2)}) %collective-permute-start.4) | collective-permute-done | bytes 131104 | tf_op jit(solution)/shard_map/ppermute | solution.py:381
  29.3 0.7 %finish.1 = f32[4,8,64,128]{3,2,1,0:T(8,128)} custom-call(f32[4,8,64,128]{3,2,1,0:T(8,128)} %get-tuple-element.28.inc, f32[8,64,128]{2,1,0:T(8,128)S(1)} %get-tuple-element.29.low, bf16[8,64,128]{2,1,0:T(8,128)(2,1)S(1)} %collective-permute-done.4.back), custom_call_target="tpu_custom_call", output_to_operand_aliasing={{}: (0, {})} | custom-call | flops 65536 | bytes 655360 | tf_op jit(solution)/shard_map/finish/pallas_call | solution.py:277
  (3 shorter events, 0.0 us)
Async XLA Ops:
  0.0 6.0 %copy-start.1 = (bf16[4,8,64,128]{3,2,1,0:T(8,128)(2,1)S(1)}, bf16[4,8,64,128]{3,2,1,0:T(8,128)(2,1)}, u32[]{:S(2)}) copy-start(bf16[4,8,64,128]{3,2,1,0:T(8,128)(2,1)} %w.5) | copy-start | bytes 1572868
  0.0 6.0 %copy-start = (bf16[4,8,256,128]{3,2,1,0:T(8,128)(2,1)S(1)}, bf16[4,8,256,128]{3,2,1,0:T(8,128)(2,1)}, u32[]{:S(2)}) copy-start(bf16[4,8,256,128]{3,2,1,0:T(8,128)(2,1)} %u.5) | copy-start | bytes 6291460
  0.0 6.0 %copy-start.5 = (s32[4,8,9]{2,1,0:T(8,128)S(1)}, s32[4,8,9]{2,1,0:T(8,128)}, u32[]{:S(2)}) copy-start(s32[4,8,9]{2,1,0:T(8,128)} %index.7) | copy-start | bytes 3460
  0.0 6.0 %copy-start.4 = (s32[4,8,9]{2,1,0:T(8,128)S(1)}, s32[4,8,9]{2,1,0:T(8,128)}, u32[]{:S(2)}) copy-start(s32[4,8,9]{2,1,0:T(8,128)} %live.7) | copy-start | bytes 3460
  1.3 19.5 %collective-permute-start.2 = (bf16[8,320,128]{2,1,0:T(8,128)(2,1)S(1)}, bf16[8,320,128]{2,1,0:T(8,128)(2,1)S(1)}, u32[]{:S(2)}, u32[]{:S(2)}) collective-permute-start(bf16[8,320,128]{2,1,0:T(8,128)(2,1)S(1)} %pack_row.1), channel_id=1, source_target_pairs={{0,4},{4,8},{8,12},{12,16},{16,20},{20,24},{24,28},{1,5},{5,9},{9,... | collective-permute-start | bytes 1966088 | tf_op jit(solution)/shard_map/ppermute | solution.py:371
  4.7 1.0 %copy-start.2 = (bf16[16,128,128]{2,1,0:T(8,128)(2,1)S(1)}, bf16[16,128,128]{2,1,0:T(8,128)(2,1)}, u32[]{:S(2)}) copy-start(bf16[16,128,128]{2,1,0:T(8,128)(2,1)} %tapers.3) | copy-start | bytes 1572868
  6.0 2.8 %copy-start.3 = (bf16[16,128,128]{2,1,0:T(8,128)(2,1)S(1)}, bf16[16,128,128]{2,1,0:T(8,128)(2,1)}, u32[]{:S(2)}) copy-start(bf16[16,128,128]{2,1,0:T(8,128)(2,1)} %tapers.3) | copy-start | bytes 1572868
  6.2 7.1 %collective-permute-start = (bf16[4,336,128]{2,1,0:T(8,128)(2,1)S(1)}, bf16[4,336,128]{2,1,0:T(8,128)(2,1)S(1)}, u32[]{:S(2)}, u32[]{:S(2)}) collective-permute-start(bf16[4,336,128]{2,1,0:T(8,128)(2,1)S(1)} %get-tuple-element.21), channel_id=1, source_target_pairs={{0,1},{2,3},{1,0},{3,2},{4,5},{6,7},{5,4},{7,6},{8,9},{10,11},{9,8... | collective-permute-start | bytes 1032200 | tf_op jit(solution)/shard_map/ppermute | solution.py:374
  6.2 8.6 %collective-permute-start.1 = (bf16[4,336,128]{2,1,0:T(8,128)(2,1)S(1)}, bf16[4,336,128]{2,1,0:T(8,128)(2,1)S(1)}, u32[]{:S(2)}, u32[]{:S(2)}) collective-permute-start(bf16[4,336,128]{2,1,0:T(8,128)(2,1)S(1)} %get-tuple-element.22), channel_id=1, source_target_pairs={{1,2},{2,1},{5,6},{6,5},{9,10},{10,9},{13,14},{14,13},{17,18},{18,... | collective-permute-start | bytes 1032200 | tf_op jit(solution)/shard_map/ppermute | solution.py:375
  14.8 10.0 %collective-permute-start.3 = (bf16[2,320,128]{2,1,0:T(8,128)(2,1)S(1)}, bf16[2,320,128]{2,1,0:T(8,128)(2,1)S(1)}, u32[]{:S(2)}, u32[]{:S(2)}) collective-permute-start(bf16[2,320,128]{2,1,0:T(8,128)(2,1)S(1)} %pad_maximum_fusion), channel_id=1, source_target_pairs={{0,4},{4,8},{8,12},{12,16},{16,20},{20,24},{24,28},{1,5},{5,9},{9,... | collective-permute-start | bytes 491528 | tf_op jit(solution)/shard_map/ppermute | solution.py:377
  21.6 7.8 %collective-permute-start.4 = (bf16[8,64,128]{2,1,0:T(8,128)(2,1)S(1)}, bf16[8,64,128]{2,1,0:T(8,128)(2,1)S(1)}, u32[]{:S(2)}, u32[]{:S(2)}) collective-permute-start(bf16[8,64,128]{2,1,0:T(8,128)(2,1)S(1)} %get-tuple-element.30), channel_id=1, source_target_pairs={{4,0},{8,4},{12,8},{16,12},{20,16},{24,20},{28,24},{5,1},{9,5},{13... | collective-permute-start | bytes 393224 | tf_op jit(solution)/shard_map/ppermute | solution.py:381

commit v5 on v4

--- a/solution.py
+++ b/solution.py
@@ -1,3 +1,5 @@
+import functools
+
 import jax
 import jax.numpy as jnp
 from jax import lax
@@ -7,6 +9,7 @@
 
 MEMBERS = 256
 GRANT = 16 << 20
+ENDS = 3
 SCALE = 1.0 / (MEMBERS - 1)
 TN = (((0,), (0,)), ((), ()))
 NT = (((1,), (1,)), ((), ()))
@@ -41,26 +44,33 @@
     )
 
 
-def prepare_kernel(tapers, sym):
-    for n in range(tapers.shape[0]):
-        t = tapers[n].astype(jnp.float32)
+def prepare_kernel(start, tapers, after, sym):
+    del after
+    for n in range(sym.shape[0]):
+        t = tapers[start + n].astype(jnp.float32)
         sym[n] = 0.5 * (t + t.T)
 
 
-def prepare(tapers):
-    return pl.pallas_call(
-        prepare_kernel,
-        out_shape=jax.ShapeDtypeStruct(tapers.shape, jnp.float32),
-        in_specs=[VMEM],
+def prepare(tapers, start, count, after):
+    cells = tapers.shape[1]
+    return pl.pallas_call(
+        functools.partial(prepare_kernel, start),
+        out_shape=jax.ShapeDtypeStruct((count, cells, cells), jnp.float32),
+        in_specs=[VMEM, VMEM],
         out_specs=VMEM,
         compiler_params=pltpu.CompilerParams(vmem_limit_bytes=GRANT),
-        cost_estimate=pl.CostEstimate(flops=0, bytes_accessed=16 << 20, transcendentals=0),
+        cost_estimate=pl.CostEstimate(flops=0, bytes_accessed=6 * count * cells * cells, transcendentals=0),
         name="prepare",
-    )(tapers)
-
-
-def inner_kernel(u, w, live, index, tapers, sym, out, held):
+    )(tapers, after)
+
+
+def inner_kernel(u, w, live, index, tapers, low, high, out, held):
     rows, cols, _, cells = u.shape
+    half = low.shape[0]
+
+    def own_taper(at):
+        return jnp.where(at < half, low[jnp.minimum(at, half - 1)], high[jnp.maximum(at - half, 0)])
+
     def ahead(a, b, last):
         near = [(4, a, b)]
         if b + 1 < cols:
@@ -78,7 +88,7 @@
             gram = dot(u[a, b], cat([u[p, q] for _, p, q in near], 1), TN)
             for n, (k, _, _) in enumerate(near):
                 at = which[b, k]
-                rho = sym[at] if k == 4 else tapers[at]
+                rho = own_taper(at) if k == 4 else tapers[at]
                 held[b, :, (k - 4) * cells : (k - 3) * cells] = tapered(
                     gram[:, n * cells : (n + 1) * cells], rho, on[b, k]
                 )
@@ -109,14 +119,14 @@
     row(rows - 1, True)
 
 
-def inner(u, w, live, index, tapers, sym):
+def inner(u, w, live, index, tapers, low, high):
     rows, cols, members, cells = u.shape
     columns = w.shape[2]
     pairs = 5 * rows * cols
     return pl.pallas_call(
         inner_kernel,
         out_shape=jax.ShapeDtypeStruct((rows, cols, columns, cells), jnp.float32),
-        in_specs=[VMEM] * 6,
+        in_specs=[VMEM] * 7,
         out_specs=VMEM,
         scratch_shapes=[pltpu.VMEM((cols, cells, 5 * cells), jnp.bfloat16)],
         compiler_params=pltpu.CompilerParams(vmem_limit_bytes=GRANT),
@@ -126,54 +136,103 @@
             transcendentals=0,
         ),
         name="inner",
-    )(u, w, live, index, tapers, sym)
-
-
-def above_kernel(s, u, w, inside, outside, live, index, tapers, back, held):
-    cols, _, cells = s.shape
-    members = u.shape[2]
+    )(u, w, live, index, tapers, low, high)
+
+
+def edges_kernel(s, u, w, inside, outside, live, index, tapers, back, held, to_inside, to_outside):
+    cols, members, cells = u.shape[1:]
     deep = members + w.shape[2]
     left, right = sides(inside, outside)
     on, which = live[0], index[0]
-    notes = [near(0, slice(deep, None)).astype(jnp.int32) for near in (left, right)]
-    side = [notes[0][cols - 1, 2], notes[0][2 * cols - 1, 2], notes[1][0, 0], notes[1][cols, 0]]
-
+    places = end_places(cols)
+    beyond = {}
+    for q, near, k, line in ((-1, left, 2, cols - 1), (cols, right, 0, 0)):
+        note = near(0, slice(deep, None)).astype(jnp.int32)
+        beyond[q] = near, note[line, k], note[cols + line, k]
     sources = []
-    for c in range(cols):
+    for n, c in enumerate(places):
         grams, weights, lives, rhos = [], [], [], []
         for k in (6, 7, 8):
             q = c + k - 7
-            if q < 0:
-                near, lively, at = left, side[0], side[1]
-            elif q >= cols:
-                near, lively, at = right, side[2], side[3]
+            if q in beyond:
+                near, lively, at = beyond[q]
+                grams.append(near(0, slice(0, members)))
+                weights.append(near(0, slice(members, deep)))
             else:
-                near, lively, at = None, on[q, 8 - k], which[q, 8 - k]
-            grams.append(u[0, q] if near is None else near(0, slice(0, members)))
-            weights.append(w[0, q] if near is None else near(0, slice(members, deep)))
+                lively, at = on[q, 8 - k], which[q, 8 - k]
+                grams.append(u[0, q])
+                weights.append(w[0, q])
             lives.append(lively)
             rhos.append(tapers[at])
-        gram = dot(s[c, :members], cat(grams, 1), TN)
-        block = cat(
-            [tapered(gram[:, n * cells : (n + 1) * cells], rhos[n], lives[n]) for n in range(3)], 1
+        gram = dot(s[n, :members], cat(grams, 1), TN)
+        held[n] = cat([tapered(gram[:, m * cells : (m + 1) * cells], rhos[m], lives[m]) for m in range(3)], 1)
+        sources.append(cat(weights, 1))
+    for n in range(len(places)):
+        back[n] = dot(sources[n], held[n], NT).astype(jnp.bfloat16)
+    final = len(places) - 1
+    to_left = dot(s[0, members:deep], held[0, :, :cells], NN)
+    to_right = dot(s[final, members:deep], held[final, :, 2 * cells :], NN)
+    even = even_column()
+    to_inside[...] = jnp.where(even, to_right, to_left)
+    to_outside[...] = jnp.where(even, to_left, to_right)
+
+
+def end_places(cols):
+    return list(range(ENDS)) + list(range(cols - ENDS, cols))
+
+
+def edges(s, u, w, inside, outside, live, index, tapers):
+    cells = u.shape[3]
+    members = u.shape[2]
+    columns = w.shape[2]
+    part = jax.ShapeDtypeStruct((columns, cells), jnp.float32)
+    return pl.pallas_call(
+        edges_kernel,
+        out_shape=(
+            jax.ShapeDtypeStruct((2 * ENDS, columns, cells), jnp.bfloat16),
+            jax.ShapeDtypeStruct((2 * ENDS, cells, 3 * cells), jnp.bfloat16),
+            part,
+            part,
+        ),
+        in_specs=[VMEM] * 8,
+        out_specs=(VMEM,) * 4,
+        compiler_params=pltpu.CompilerParams(vmem_limit_bytes=GRANT),
+        cost_estimate=pl.CostEstimate(
+            flops=2 * 6 * ENDS * cells * cells * (members + columns), bytes_accessed=1 << 20, transcendentals=0
+        ),
+        name="edges",
+    )(s, u, w, inside, outside, live, index, tapers)
+
+
+def above_kernel(s, edge_back, u, w, live, index, tapers, back, held):
+    cols, members, cells = u.shape[1:]
+    on, which = live[0], index[0]
+    for c in range(ENDS, cols - ENDS):
+        near = [(k, c + k - 7) for k in (6, 7, 8)]
+        gram = dot(s[c - ENDS, :members], cat([u[0, q] for _, q in near], 1), TN)
+        held[c - ENDS] = cat(
+            [
+                tapered(gram[:, n * cells : (n + 1) * cells], tapers[which[q, 8 - k]], on[q, 8 - k])
+                for n, (k, q) in enumerate(near)
+            ],
+            1,
         )
-        held[c] = block
-        sources.append(cat(weights, 1))
-    for c in range(cols):
-        back[c] = dot(sources[c], held[c], NT).astype(jnp.bfloat16)
-
-
-def above(s, u, w, inside, outside, live, index, tapers):
-    cols, _, cells = s.shape
+    for c in range(ENDS, cols - ENDS):
+        back[c] = dot(cat([w[0, c + n] for n in (-1, 0, 1)], 1), held[c - ENDS], NT).astype(jnp.bfloat16)
+    for n, c in enumerate(end_places(cols)):
+        back[c] = edge_back[n]
+
+
+def above(s, edge_back, u, w, live, index, tapers):
+    cols, members, cells = u.shape[1:]
     columns = w.shape[2]
-    members = u.shape[2]
     return pl.pallas_call(
         above_kernel,
         out_shape=(
             jax.ShapeDtypeStruct((cols, columns, cells), jnp.bfloat16),
-            jax.ShapeDtypeStruct((cols, cells, 3 * cells), jnp.bfloat16),
-        ),
-        in_specs=[VMEM] * 8,
+            jax.ShapeDtypeStruct((cols - 2 * ENDS, cells, 3 * cells), jnp.bfloat16),
+        ),
+        in_specs=[VMEM] * 7,
         out_specs=(VMEM, VMEM),
         compiler_params=pltpu.CompilerParams(vmem_limit_bytes=GRANT),
         cost_estimate=pl.CostEstimate(
@@ -182,15 +241,16 @@
             transcendentals=0,
         ),
         name="above",
-    )(s, u, w, inside, outside, live, index, tapers)
-
-
-def outer_kernel(inc, held, s, corner, u, w, inside, outside, live, index, tapers, out, low):
+    )(s, edge_back, u, w, live, index, tapers)
+
+
+def outer_kernel(
+    inc, ends, end_held, s, held, from_inside, from_outside, u, w, inside, outside, live, index, tapers, out, low
+):
     rows, cols, members, cells = u.shape
     deep = members + w.shape[2]
     last = cols - 1
     left, right = sides(inside, outside)
-    first = even_column().astype(jnp.int32)
     on = [live[a] for a in range(rows)]
     which = [index[a] for a in range(rows)]
     total = {}
@@ -198,16 +258,21 @@
     def add(a, q, value):
         total[a, q] = total[a, q] + value if (a, q) in total else value
 
+    places = end_places(cols)
+
+    def source(c):
+        if c in places:
+            n = places.index(c)
+            return ends[n, members:deep], end_held[n]
+        return s[c - ENDS, members:deep], held[c - ENDS]
+
     for q in range(cols):
-        back = [(k, q - (k - 7)) for k in (6, 7, 8) if 0 <= q - (k - 7) < cols]
-        sources = [s[c, members:deep] for _, c in back]
-        blocks = [held[c, :, (k - 6) * cells : (k - 5) * cells] for k, c in back]
-        for edge, k, far in ((0, 8, first), (last, 6, 1 - first)):
-            if q == edge:
-                gram = dot(corner[far, :members], u[0, q], TN)
-                sources.append(corner[far, members:deep])
-                blocks.append(tapered(gram, tapers[which[0][q, 8 - k]], on[0][q, 8 - k]))
-        add(0, q, dot(cat(sources, 1), cat(blocks, 0), NN))
+        back = [(k, source(q - (k - 7))) for k in (6, 7, 8) if 0 <= q - (k - 7) < cols]
+        blocks = [block[:, (k - 6) * cells : (k - 5) * cells] for k, (_, block) in back]
+        add(0, q, dot(cat([weight for _, (weight, _) in back], 1), cat(blocks, 0), NN))
+    even = even_column()
+    add(0, 0, jnp.where(even, from_outside[...], from_inside[...]))
+    add(0, last, jnp.where(even, from_inside[...], from_outside[...]))
 
     for a in range(rows):
         near = [(5, a)] + ([(8, a + 1)] if a + 1 < rows else [])
@@ -247,13 +312,14 @@
                 low[q] = value
 
 
-def outer(inc, held, s, corner, u, w, inside, outside, live, index, tapers):
+def outer(inc, *around):
+    ends, end_held, s, held, from_inside, from_outside, u, w, inside, outside, live, index, tapers = around
     rows, cols, members, cells = u.shape
     columns = w.shape[2]
     return pl.pallas_call(
         outer_kernel,
         out_shape=(jax.ShapeDtypeStruct(inc.shape, inc.dtype), jax.ShapeDtypeStruct(inc.shape[1:], inc.dtype)),
-        in_specs=[VMEM] * 11,
+        in_specs=[VMEM] * 14,
         out_specs=(VMEM, VMEM),
         compiler_params=pltpu.CompilerParams(vmem_limit_bytes=GRANT),
         cost_estimate=pl.CostEstimate(
@@ -262,7 +328,7 @@
             transcendentals=0,
         ),
         name="outer",
-    )(inc, held, s, corner, u, w, inside, outside, live, index, tapers)
+    )(inc, *around)
 
 
 def finish_kernel(inc, low, back, out, total, sem):
@@ -300,12 +366,42 @@
     return [(i + 1, i) for i in range(lax.axis_size(axis) - 1)]
 
 
-def pack_row_kernel(u, w, out, sem):
-    rows, _, members, _ = u.shape
+def pack_ends_kernel(u, w, out, sem):
+    rows, cols, members, _ = u.shape
     deep = members + w.shape[2]
+    copies = []
+    for n, q in enumerate((0, cols - ENDS)):
+        to = out.at[ENDS * n : ENDS * n + ENDS]
+        copies.append(pltpu.make_async_copy(u.at[rows - 1, q : q + ENDS], to.at[:, :members], sem.at[n, 0]))
+        copies.append(pltpu.make_async_copy(w.at[rows - 1, q : q + ENDS], to.at[:, members:deep], sem.at[n, 1]))
+    for copy in copies:
+        copy.start()
+    for copy in copies:
+        copy.wait()
+
+
+def pack_ends(u, w):
+    members, cells = u.shape[2:]
+    shape = (2 * ENDS, members + w.shape[2], cells)
+    return pl.pallas_call(
+        pack_ends_kernel,
+        out_shape=pltpu.VMEM(shape, u.dtype),
+        in_specs=[HBM, HBM],
+        out_specs=VMEM,
+        scratch_shapes=[pltpu.SemaphoreType.DMA((2, 2))],
+        cost_estimate=pl.CostEstimate(flops=0, bytes_accessed=8 * ENDS * shape[1] * cells, transcendentals=0),
+        name="pack_ends",
+    )(u, w)
+
+
+def pack_row_kernel(u, w, sym, out, sem):
+    del sym
+    rows, cols, members, _ = u.shape
+    deep = members + w.shape[2]
+    between = slice(ENDS, cols - ENDS)
     copies = [
-        pltpu.make_async_copy(u.at[rows - 1], out.at[:, :members], sem.at[0]),
-        pltpu.make_async_copy(w.at[rows - 1], out.at[:, members:deep], sem.at[1]),
+        pltpu.make_async_copy(u.at[rows - 1, between], out.at[:, :members], sem.at[0]),
+        pltpu.make_async_copy(w.at[rows - 1, between], out.at[:, members:deep], sem.at[1]),
     ]
     for copy in copies:
         copy.start()
@@ -313,18 +409,19 @@
         copy.wait()
 
 
-def pack_row(u, w):
-    _, cols, members, cells = u.shape
-    shape = (cols, members + w.shape[2], cells)
+def pack_row(u, w, sym):
+    cols, members, cells = u.shape[1:]
+    shape = (cols - 2 * ENDS, members + w.shape[2], cells)
     return pl.pallas_call(
         pack_row_kernel,
-        out_shape=pltpu.VMEM(shape, u.dtype),
-        in_specs=[HBM, HBM],
+        out_shape=jax.ShapeDtypeStruct(shape, u.dtype),
+        in_specs=[ANY, ANY, VMEM],
         out_specs=VMEM,
         scratch_shapes=[pltpu.SemaphoreType.DMA((2,))],
-        cost_estimate=pl.CostEstimate(flops=0, bytes_accessed=4 * cols * shape[1] * cells, transcendentals=0),
+        compiler_params=pltpu.CompilerParams(vmem_limit_bytes=GRANT),
+        cost_estimate=pl.CostEstimate(flops=0, bytes_accessed=4 * shape[0] * shape[1] * cells, transcendentals=0),
         name="pack_row",
-    )(u, w)
+    )(u, w, sym)
 
 
 def pack_columns_kernel(u, w, live, index, sym, inner_side, outer_side, sem):
@@ -363,24 +460,29 @@
     )(u, w, live, index, sym)
 
 
-def body(perturbations, weights, live, index, tapers):
-    rows, cols, members, cells = perturbations.shape
-    deep = members + weights.shape[2]
-    row = pack_row(perturbations, weights)
-    row, u, w, tapers = lax.optimization_barrier((row, perturbations, weights, tapers))
-    s = lax.ppermute(row, "row", forward("row"))
-    sym = prepare(tapers)
-    inner_side, outer_side = pack_columns(u, w, live, index, sym)
+def body(u, w, live, index, tapers):
+    half = tapers.shape[0] // 2
+    packed = pack_ends(u, w)
+    ends = lax.ppermute(packed, "row", forward("row"))
+    low = prepare(tapers, 0, half, packed)
+    inner_side, outer_side = pack_columns(u, w, live, index, low)
     inside = lax.ppermute(inner_side, "col", swaps("col", 0))
     outside = lax.ppermute(outer_side, "col", swaps("col", 1))
-    inc, inside, outside = lax.optimization_barrier((inner(u, w, live, index, tapers, sym), inside, outside))
-    corner = lax.ppermute(
-        jnp.stack([inside[rows - 1, :deep], outside[rows - 1, :deep]]), "row", forward("row")
+    high = prepare(tapers, half, tapers.shape[0] - half, outer_side)
+    row = lax.ppermute(pack_row(u, w, high), "row", forward("row"))
+    inc, inside, outside, ends = lax.optimization_barrier(
+        (inner(u, w, live, index, tapers, low, high), inside, outside, ends)
     )
-    back, held = above(s, u, w, inside, outside, live, index, tapers)
+    end_back, end_held, to_inside, to_outside = edges(ends, u, w, inside, outside, live, index, tapers)
+    from_inside = lax.ppermute(to_inside, "col", swaps("col", 0))
+    from_outside = lax.ppermute(to_outside, "col", swaps("col", 1))
+    row, from_inside, from_outside = lax.optimization_barrier((row, from_inside, from_outside))
+    back, held = above(row, end_back, u, w, live, index, tapers)
     back = lax.ppermute(back, "row", backward("row"))
-    inc, low = outer(inc, held, s, corner, u, w, inside, outside, live, index, tapers)
-    return finish(inc, low, back)
+    inc, low_row = outer(
+        inc, ends, end_held, row, held, from_inside, from_outside, u, w, inside, outside, live, index, tapers
+    )
+    return finish(inc, low_row, back)
 
 
 def solution(mesh):

time: 30.3 us -> 32.4 us (1.069)
  starting transfers between devices: 12.8 us -> 15.4 us
  waiting for transfers between devices: 5.86 us -> 4.71 us
  Pallas kernels: 10.2 us -> 10.8 us
    ppermute x2 -> x4, starting transfers between devices: 6.86 us -> 9.49 us  [the longest x1 3.43 us: body(): ends = lax.ppermute(packed, 'row', forward('row'))]
    ppermute x1, waiting for transfers between devices: 1.56 us -> 0.01 us  [body(): outside = lax.ppermute(outer_side, 'col', swaps('col', 1))]
    pallas_call x2 -> x5, Pallas kernels: 1.44 us -> 2.31 us  [the longest x1 1.23 us: pack_ends(): pl.pallas_call(pack_ends_kernel, out_shape=pltpu.VMEM(shape, u.dtype), in...]
    pallas_call x1, Pallas kernels: 0.78 us -> 0.4 us  [above(): pl.pallas_call(above_kernel, out_shape=(jax.ShapeDtypeStruct((cols, colum...]
    ppermute x2 -> x4, waiting for transfers between devices: 2.49 us -> 2.84 us  [the longest x1 2.64 us: body(): from_outside = lax.ppermute(to_outside, 'col', swaps('col', 1))]
  transfers between devices with their start and end apart: 5 -> 7, of which waited for: 3 -> 3; matrix products, arithmetic and copies ran while one was open for 0% -> 0% of each run, Pallas kernels for 27% -> 26%
where the time goes in v5:
time: 32.4 us; the launch traced here: 32.2 us
  starting transfers between devices  15.4 us (48%)
  Pallas kernels  10.8 us (33%)
  waiting for transfers between devices  4.71 us (15%)
  local copies, waits for them, and re-layouts  1.06 us (3%)
    pallas_call x1, Pallas kernels, inner(): pl.pallas_call(inner_kernel, out_shape=jax.ShapeDtypeStruct((rows, cols,...  4.61 us
    ppermute x1, starting transfers between devices, body(): ends = lax.ppermute(packed, 'row', forward('row'))  3.43 us
    ppermute x1, starting transfers between devices, body(): row = lax.ppermute(pack_row(u, w, high), 'row', forward('row'))  3.43 us
    ppermute x1, starting transfers between devices, body(): back = lax.ppermute(back, 'row', backward('row'))  3.31 us
    ppermute x1, waiting for transfers between devices, body(): from_outside = lax.ppermute(to_outside, 'col', swaps('col', 1))  2.64 us
    pallas_call x1, Pallas kernels, outer(): pl.pallas_call(outer_kernel, out_shape=(jax.ShapeDtypeStruct(inc.shape, i...  2.57 us
    ppermute x1, starting transfers between devices, body(): from_outside = lax.ppermute(to_outside, 'col', swaps('col', 1))  2.56 us
    ppermute x1, starting transfers between devices, body(): outside = lax.ppermute(outer_side, 'col', swaps('col', 1))  2.53 us
  transfers between devices with their start and end apart: 7, of which 3 were waited for; matrix products, arithmetic and copies ran while one was open for 0% of the time, Pallas kernels for 26%

profile of v5, /device:TPU:22, one launch (start us, length us, event | category | flops | bytes accessed | tf_op | source)
XLA Modules:
  0.0 32.2 jit_solution(3214442988229943950)
XLA Ops:
  0.0 0.0 copy-start.1
  0.0 0.0 copy-start
  0.0 0.0 copy-start.5
  0.0 0.0 copy-start.4
  0.0 1.2 %pack_ends.1.after = bf16[6,320,128]{2,1,0:T(8,128)(2,1)S(1)} custom-call(bf16[4,8,256,128]{3,2,1,0:T(8,128)(2,1)} %u.13, bf16[4,8,64,128]{3,2,1,0:T(8,128)(2,1)} %w.13), custom_call_target="tpu_custom_call" | custom-call | bytes 983040 | tf_op jit(solution)/shard_map/pack_ends/pallas_call | solution.py:386
  1.3 3.4 %collective-permute-start.2 = (bf16[6,320,128]{2,1,0:T(8,128)(2,1)S(1)}, bf16[6,320,128]{2,1,0:T(8,128)(2,1)S(1)}, u32[]{:S(2)}, u32[]{:S(2)}) collective-permute-start(bf16[6,320,128]{2,1,0:T(8,128)(2,1)S(1)} %pack_ends.1.after), channel_id=1, source_target_pairs={{0,4},{4,8},{8,12},{12,16},{16,20},{20,24},{24,28},{1,5},{5,9},{9,... | collective-permute-start | bytes 1474568 | tf_op jit(solution)/shard_map/ppermute | solution.py:466
  4.7 0.0 copy-start.2
  4.7 1.0 %copy-done.2 = bf16[16,128,128]{2,1,0:T(8,128)(2,1)S(1)} copy-done((bf16[16,128,128]{2,1,0:T(8,128)(2,1)S(1)}, bf16[16,128,128]{2,1,0:T(8,128)(2,1)}, u32[]{:S(2)}) %copy-start.2) | copy-done | bytes 524312
  5.7 0.0 copy-start.3
  5.7 0.1 prepare.2.sym.low
  5.9 0.0 copy-done.1
  5.9 0.0 copy-done
  5.9 0.0 copy-done.5
  5.9 0.0 copy-done.4
  5.9 0.1 pack_columns.1
  6.1 0.1 collective-permute-start
  6.2 2.5 %collective-permute-start.1 = (bf16[4,336,128]{2,1,0:T(8,128)(2,1)S(1)}, bf16[4,336,128]{2,1,0:T(8,128)(2,1)S(1)}, u32[]{:S(2)}, u32[]{:S(2)}) collective-permute-start(bf16[4,336,128]{2,1,0:T(8,128)(2,1)S(1)} %get-tuple-element.22.after), channel_id=1, source_target_pairs={{1,2},{2,1},{5,6},{6,5},{9,10},{10,9},{13,14},{14,13},{17,18},{18,... | collective-permute-start | bytes 1032200 | tf_op jit(solution)/shard_map/ppermute | solution.py:470
  8.7 0.0 copy-done.3
  8.7 0.1 prepare.3.high.sym
  8.9 0.1 pack_row.1
  9.0 3.4 %collective-permute-start.3 = (bf16[2,320,128]{2,1,0:T(8,128)(2,1)S(1)}, bf16[2,320,128]{2,1,0:T(8,128)(2,1)S(1)}, u32[]{:S(2)}, u32[]{:S(2)}) collective-permute-start(bf16[2,320,128]{2,1,0:T(8,128)(2,1)S(1)} %pack_row.1), channel_id=1, source_target_pairs={{0,4},{4,8},{8,12},{12,16},{16,20},{20,24},{24,28},{1,5},{5,9},{9,... | collective-permute-start | bytes 491528 | tf_op jit(solution)/shard_map/ppermute | solution.py:472
  12.4 4.6 %inner.1.inc = f32[4,8,64,128]{3,2,1,0:T(8,128)S(1)} custom-call(bf16[4,8,256,128]{3,2,1,0:T(8,128)(2,1)S(1)} %copy-done, bf16[4,8,64,128]{3,2,1,0:T(8,128)(2,1)S(1)} %copy-done.1, s32[4,8,9]{2,1,0:T(8,128)S(1)} %copy-done.4, s32[4,8,9]{2,1,0:T(8,128)S(1)} %copy-done.5, bf16[16,128,128]{2,1,0:T(8,128)(2,1)S(1)} %copy-done.3, ...), custom_call_target="tpu_custom_call" | custom-call | flops 2013265920 | bytes 4194304 | tf_op jit(solution)/shard_map/inner/pallas_call | solution.py:126
  17.0 0.0 collective-permute-done.inside
  17.1 0.0 collective-permute-done.1.outside
  17.1 0.2 collective-permute-done.2.s.ends
  17.3 0.7 %edges.1 = (bf16[6,64,128]{2,1,0:T(8,128)(2,1)S(1)}, bf16[6,128,384]{2,1,0:T(8,128)(2,1)S(1)}, f32[64,128]{1,0:T(8,128)S(1)}, f32[64,128]{1,0:T(8,128)S(1)}) custom-call(bf16[6,320,128]{2,1,0:T(8,128)(2,1)S(1)} %collective-permute-done.2.s.ends, bf16[4,8,256,128]{3,2,1,0:T(8,128)(2,1)S(1)} %copy-done, bf16[4,8,64,128]{3,2,1,0:T(8,128)(2,1)S(1)} %copy-done.1, ...), custom_call_target="tpu_custom_call" | custom-call | flops 188743680 | bytes 1048576 | tf_op jit(solution)/shard_map/edges/pallas_call | solution.py:189
  17.9 0.1 collective-permute-start.4
  18.0 2.6 %collective-permute-start.5 = (f32[64,128]{1,0:T(8,128)S(1)}, f32[64,128]{1,0:T(8,128)S(1)}, u32[]{:S(2)}, u32[]{:S(2)}) collective-permute-start(f32[64,128]{1,0:T(8,128)S(1)} %get-tuple-element.30), channel_id=1, source_target_pairs={{1,2},{2,1},{5,6},{6,5},{9,10},{10,9},{13,14},{14,13},{17,18},{18,... | collective-permute-start | bytes 98312 | tf_op jit(solution)/shard_map/ppermute | solution.py:478
  20.6 0.0 collective-permute-done.3.s
  20.6 0.0 collective-permute-done.4.from_inside
  20.6 2.6 %collective-permute-done.5.from_outside = f32[64,128]{1,0:T(8,128)S(1)} collective-permute-done((f32[64,128]{1,0:T(8,128)S(1)}, f32[64,128]{1,0:T(8,128)S(1)}, u32[]{:S(2)}, u32[]{:S(2)}) %collective-permute-start.5) | collective-permute-done | bytes 32800 | tf_op jit(solution)/shard_map/ppermute | solution.py:478
  23.2 0.4 %above.1 = (bf16[8,64,128]{2,1,0:T(8,128)(2,1)S(1)}, bf16[2,128,384]{2,1,0:T(8,128)(2,1)S(1)}) custom-call(bf16[2,320,128]{2,1,0:T(8,128)(2,1)S(1)} %collective-permute-done.3.s, bf16[6,64,128]{2,1,0:T(8,128)(2,1)S(1)} %get-tuple-element.32.edge_back, bf16[4,8,256,128]{3,2,1,0:T(8,128)(2,1)S(1)} %copy-done, bf16[4,8,64,128]{3,2,1,0:T(8,128)(2,1)S(1)} %copy-done.1, ...), custom_call_target="tpu_custom_call" | custom-call | flops 251658240 | bytes 2097152 | tf_op jit(solution)/shard_map/above/pallas_call | solution.py:229
  23.7 3.3 %collective-permute-start.6 = (bf16[8,64,128]{2,1,0:T(8,128)(2,1)S(1)}, bf16[8,64,128]{2,1,0:T(8,128)(2,1)S(1)}, u32[]{:S(2)}, u32[]{:S(2)}) collective-permute-start(bf16[8,64,128]{2,1,0:T(8,128)(2,1)S(1)} %get-tuple-element.38), channel_id=1, source_target_pairs={{4,0},{8,4},{12,8},{16,12},{20,16},{24,20},{28,24},{5,1},{9,5},{13... | collective-permute-start | bytes 393224 | tf_op jit(solution)/shard_map/ppermute | solution.py:481
  27.0 2.6 %outer.1 = (f32[4,8,64,128]{3,2,1,0:T(8,128)}, f32[8,64,128]{2,1,0:T(8,128)S(1)}) custom-call(f32[4,8,64,128]{3,2,1,0:T(8,128)S(1)} %inner.1.inc, bf16[6,320,128]{2,1,0:T(8,128)(2,1)S(1)} %collective-permute-done.2.s.ends, bf16[6,128,384]{2,1,0:T(8,128)(2,1)S(1)} %get-tuple-element.28.end_held, bf16[2,320,128]{2,1,0:T(8,128)(2,1)S(1)} %collective-permute-done.3.s, ...), custom_call_target="tpu_custom_call" | custom-call | flops 503316480 | bytes 4194304 | tf_op jit(solution)/shard_map/outer/pallas_call | solution.py:319
  29.6 1.9 %collective-permute-done.6.back = bf16[8,64,128]{2,1,0:T(8,128)(2,1)S(1)} collective-permute-done((bf16[8,64,128]{2,1,0:T(8,128)(2,1)S(1)}, bf16[8,64,128]{2,1,0:T(8,128)(2,1)S(1)}, u32[]{:S(2)}, u32[]{:S(2)}) %collective-permute-start.6) | collective-permute-done | bytes 131104 | tf_op jit(solution)/shard_map/ppermute | solution.py:481
  31.4 0.7 %finish.1 = f32[4,8,64,128]{3,2,1,0:T(8,128)} custom-call(f32[4,8,64,128]{3,2,1,0:T(8,128)} %get-tuple-element.36.inc, f32[8,64,128]{2,1,0:T(8,128)S(1)} %get-tuple-element.37.low, bf16[8,64,128]{2,1,0:T(8,128)(2,1)S(1)} %collective-permute-done.6.back), custom_call_target="tpu_custom_call", output_to_operand_aliasing={{}: (0, {})} | custom-call | flops 65536 | bytes 655360 | tf_op jit(solution)/shard_map/finish/pallas_call | solution.py:343
Async XLA Ops:
  0.0 5.9 %copy-start.1 = (bf16[4,8,64,128]{3,2,1,0:T(8,128)(2,1)S(1)}, bf16[4,8,64,128]{3,2,1,0:T(8,128)(2,1)}, u32[]{:S(2)}) copy-start(bf16[4,8,64,128]{3,2,1,0:T(8,128)(2,1)} %w.13) | copy-start | bytes 1572868
  0.0 5.9 %copy-start = (bf16[4,8,256,128]{3,2,1,0:T(8,128)(2,1)S(1)}, bf16[4,8,256,128]{3,2,1,0:T(8,128)(2,1)}, u32[]{:S(2)}) copy-start(bf16[4,8,256,128]{3,2,1,0:T(8,128)(2,1)} %u.13) | copy-start | bytes 6291460
  0.0 5.9 %copy-start.5 = (s32[4,8,9]{2,1,0:T(8,128)S(1)}, s32[4,8,9]{2,1,0:T(8,128)}, u32[]{:S(2)}) copy-start(s32[4,8,9]{2,1,0:T(8,128)} %index.9) | copy-start | bytes 3460
  0.0 5.9 %copy-start.4 = (s32[4,8,9]{2,1,0:T(8,128)S(1)}, s32[4,8,9]{2,1,0:T(8,128)}, u32[]{:S(2)}) copy-start(s32[4,8,9]{2,1,0:T(8,128)} %live.9) | copy-start | bytes 3460
  1.3 16.0 %collective-permute-start.2 = (bf16[6,320,128]{2,1,0:T(8,128)(2,1)S(1)}, bf16[6,320,128]{2,1,0:T(8,128)(2,1)S(1)}, u32[]{:S(2)}, u32[]{:S(2)}) collective-permute-start(bf16[6,320,128]{2,1,0:T(8,128)(2,1)S(1)} %pack_ends.1.after), channel_id=1, source_target_pairs={{0,4},{4,8},{8,12},{12,16},{16,20},{20,24},{24,28},{1,5},{5,9},{9,... | collective-permute-start | bytes 1474568 | tf_op jit(solution)/shard_map/ppermute | solution.py:466
  4.7 1.0 %copy-start.2 = (bf16[16,128,128]{2,1,0:T(8,128)(2,1)S(1)}, bf16[16,128,128]{2,1,0:T(8,128)(2,1)}, u32[]{:S(2)}) copy-start(bf16[16,128,128]{2,1,0:T(8,128)(2,1)} %tapers.11) | copy-start | bytes 1572868
  5.7 3.0 %copy-start.3 = (bf16[16,128,128]{2,1,0:T(8,128)(2,1)S(1)}, bf16[16,128,128]{2,1,0:T(8,128)(2,1)}, u32[]{:S(2)}) copy-start(bf16[16,128,128]{2,1,0:T(8,128)(2,1)} %tapers.11) | copy-start | bytes 1572868
  6.1 11.0 %collective-permute-start = (bf16[4,336,128]{2,1,0:T(8,128)(2,1)S(1)}, bf16[4,336,128]{2,1,0:T(8,128)(2,1)S(1)}, u32[]{:S(2)}, u32[]{:S(2)}) collective-permute-start(bf16[4,336,128]{2,1,0:T(8,128)(2,1)S(1)} %get-tuple-element.23), channel_id=1, source_target_pairs={{0,1},{2,3},{1,0},{3,2},{4,5},{6,7},{5,4},{7,6},{8,9},{10,11},{9,8... | collective-permute-start | bytes 1032200 | tf_op jit(solution)/shard_map/ppermute | solution.py:469
  6.2 10.9 %collective-permute-start.1 = (bf16[4,336,128]{2,1,0:T(8,128)(2,1)S(1)}, bf16[4,336,128]{2,1,0:T(8,128)(2,1)S(1)}, u32[]{:S(2)}, u32[]{:S(2)}) collective-permute-start(bf16[4,336,128]{2,1,0:T(8,128)(2,1)S(1)} %get-tuple-element.22.after), channel_id=1, source_target_pairs={{1,2},{2,1},{5,6},{6,5},{9,10},{10,9},{13,14},{14,13},{17,18},{18,... | collective-permute-start | bytes 1032200 | tf_op jit(solution)/shard_map/ppermute | solution.py:470
  9.0 11.6 %collective-permute-start.3 = (bf16[2,320,128]{2,1,0:T(8,128)(2,1)S(1)}, bf16[2,320,128]{2,1,0:T(8,128)(2,1)S(1)}, u32[]{:S(2)}, u32[]{:S(2)}) collective-permute-start(bf16[2,320,128]{2,1,0:T(8,128)(2,1)S(1)} %pack_row.1), channel_id=1, source_target_pairs={{0,4},{4,8},{8,12},{12,16},{16,20},{20,24},{24,28},{1,5},{5,9},{9,... | collective-permute-start | bytes 491528 | tf_op jit(solution)/shard_map/ppermute | solution.py:472
  17.9 2.7 %collective-permute-start.4 = (f32[64,128]{1,0:T(8,128)S(1)}, f32[64,128]{1,0:T(8,128)S(1)}, u32[]{:S(2)}, u32[]{:S(2)}) collective-permute-start(f32[64,128]{1,0:T(8,128)S(1)} %get-tuple-element.29), channel_id=1, source_target_pairs={{0,1},{2,3},{1,0},{3,2},{4,5},{6,7},{5,4},{7,6},{8,9},{10,11},{9,8... | collective-permute-start | bytes 98312 | tf_op jit(solution)/shard_map/ppermute | solution.py:477
  18.0 5.2 %collective-permute-start.5 = (f32[64,128]{1,0:T(8,128)S(1)}, f32[64,128]{1,0:T(8,128)S(1)}, u32[]{:S(2)}, u32[]{:S(2)}) collective-permute-start(f32[64,128]{1,0:T(8,128)S(1)} %get-tuple-element.30), channel_id=1, source_target_pairs={{1,2},{2,1},{5,6},{6,5},{9,10},{10,9},{13,14},{14,13},{17,18},{18,... | collective-permute-start | bytes 98312 | tf_op jit(solution)/shard_map/ppermute | solution.py:478
  23.7 7.8 %collective-permute-start.6 = (bf16[8,64,128]{2,1,0:T(8,128)(2,1)S(1)}, bf16[8,64,128]{2,1,0:T(8,128)(2,1)S(1)}, u32[]{:S(2)}, u32[]{:S(2)}) collective-permute-start(bf16[8,64,128]{2,1,0:T(8,128)(2,1)S(1)} %get-tuple-element.38), channel_id=1, source_target_pairs={{4,0},{8,4},{12,8},{16,12},{20,16},{24,20},{28,24},{5,1},{9,5},{13... | collective-permute-start | bytes 393224 | tf_op jit(solution)/shard_map/ppermute | solution.py:481

commit v6 on v5

v6 whole, which is shorter than its diff:
```python
import jax
import jax.numpy as jnp
from jax import lax
from jax.experimental import pallas as pl
from jax.experimental.pallas import tpu as pltpu
from jax.sharding import PartitionSpec as P

MEMBERS = 256
GRANT = 16 << 20
ENDS = 2
SCALE = 1.0 / (MEMBERS - 1)
TN = (((0,), (0,)), ((), ()))
NT = (((1,), (1,)), ((), ()))
NN = (((1,), (0,)), ((), ()))
VMEM = pl.BlockSpec(memory_space=pltpu.VMEM)
ANY = pl.BlockSpec(memory_space=pl.ANY)
HBM = pl.BlockSpec(memory_space=pltpu.HBM)


def dot(a, b, dims):
    return lax.dot_general(a, b, dims, preferred_element_type=jnp.float32)


def cat(parts, axis):
    return parts[0] if len(parts) == 1 else jnp.concatenate(parts, axis=axis)


def tapered(gram, rho, live):
    factor = live.astype(jnp.float32) * SCALE
    return (rho.astype(jnp.float32) * gram * factor).astype(jnp.bfloat16)


def even_column():
    return lax.rem(lax.axis_index("col"), 2) == 0


def sides(inside, outside):
    even = even_column()
    return (
        lambda *at: jnp.where(even, outside[at], inside[at]),
        lambda *at: jnp.where(even, inside[at], outside[at]),
    )


def inner_kernel(u, w, live, index, tapers, ends, out, sym, held):
    rows, cols, _, cells = u.shape
    del ends
    for n in range(tapers.shape[0]):
        t = tapers[n].astype(jnp.float32)
        sym[n] = 0.5 * (t + t.T)

    def ahead(a, b, last):
        near = [(4, a, b)]
        if b + 1 < cols:
            near.append((5, a, b + 1))
        if not last:
            for k in (6, 7, 8):
                if 0 <= b + k - 7 < cols:
                    near.append((k, a + 1, b + k - 7))
        return near

    def row(a, last):
        on, which = live[a], index[a]
        for b in range(cols):
            near = ahead(a, b, last)
            gram = dot(u[a, b], cat([u[p, q] for _, p, q in near], 1), TN)
            for n, (k, _, _) in enumerate(near):
                at = which[b, k]
                rho = sym[at] if k == 4 else tapers[at]
                held[b, :, (k - 4) * cells : (k - 3) * cells] = tapered(
                    gram[:, n * cells : (n + 1) * cells], rho, on[b, k]
                )
        for b in range(cols):
            near = ahead(a, b, last)
            total = dot(
                cat([w[p, q] for _, p, q in near], 1),
                cat([held[b, :, (k - 4) * cells : (k - 3) * cells] for k, _, _ in near], 1),
                NT,
            )
            if b > 0:
                total += dot(w[a, b - 1], held[b - 1, :, cells : 2 * cells], NN)
            out[a, b] += total
            if not last:
                back = [(k, b - (k - 7)) for k in (6, 7, 8) if 0 <= b - (k - 7) < cols]
                out[a + 1, b] = dot(
                    cat([w[a, q] for _, q in back], 1),
                    cat([held[q, :, (k - 4) * cells : (k - 3) * cells] for k, q in back], 0),
                    NN,
                )

    out[0] = jnp.zeros_like(out[0])

    @pl.loop(0, rows - 1)
    def _(a):
        row(a, False)

    row(rows - 1, True)


def inner(u, w, live, index, tapers, ends):
    rows, cols, members, cells = u.shape
    columns = w.shape[2]
    pairs = 5 * rows * cols
    return pl.pallas_call(
        inner_kernel,
        out_shape=jax.ShapeDtypeStruct((rows, cols, columns, cells), jnp.float32),
        in_specs=[VMEM] * 6,
        out_specs=VMEM,
        scratch_shapes=[
            pltpu.VMEM(tapers.shape, jnp.float32),
            pltpu.VMEM((cols, cells, 5 * cells), jnp.bfloat16),
        ],
        compiler_params=pltpu.CompilerParams(vmem_limit_bytes=GRANT),
        cost_estimate=pl.CostEstimate(
            flops=2 * pairs * cells * cells * (members + 2 * columns),
            bytes_accessed=4 << 20,
            transcendentals=0,
        ),
        name="inner",
    )(u, w, live, index, tapers, ends)


def edges_kernel(s, u, w, inside, outside, live, index, tapers, back, held, to_inside, to_outside, side):
    rows, cols, members, cells = u.shape
    last = cols - 1
    deep = members + w.shape[2]
    left, right = sides(inside, outside)
    on = [live[a] for a in range(rows)]
    which = [index[a] for a in range(rows)]
    places = end_places(cols)
    beyond = {}
    for q, near, k, line in ((-1, left, 2, cols - 1), (cols, right, 0, 0)):
        note = near(0, slice(deep, None)).astype(jnp.int32)
        beyond[q] = near, note[line, k], note[cols + line, k]
    sources = []
    for n, c in enumerate(places):
        grams, weights, lives, rhos = [], [], [], []
        for k in (6, 7, 8):
            q = c + k - 7
            if q in beyond:
                near, lively, at = beyond[q]
                grams.append(near(0, slice(0, members)))
                weights.append(near(0, slice(members, deep)))
            else:
                lively, at = on[0][q, 8 - k], which[0][q, 8 - k]
                grams.append(u[0, q])
                weights.append(w[0, q])
            lives.append(lively)
            rhos.append(tapers[at])
        gram = dot(s[n, :members], cat(grams, 1), TN)
        held[n] = cat([tapered(gram[:, m * cells : (m + 1) * cells], rhos[m], lives[m]) for m in range(3)], 1)
        sources.append(cat(weights, 1))
    for n in range(len(places)):
        back[n] = dot(sources[n], held[n], NT).astype(jnp.bfloat16)
    final = len(places) - 1
    to_left = dot(s[0, members:deep], held[0, :, :cells], NN)
    to_right = dot(s[final, members:deep], held[final, :, 2 * cells :], NN)
    even = even_column()
    to_inside[...] = jnp.where(even, to_right, to_left)
    to_outside[...] = jnp.where(even, to_left, to_right)

    total = {}

    def add(a, q, value):
        total[a, q] = total[a, q] + value if (a, q) in total else value

    for a in range(rows):
        near = [(5, a)] + ([(8, a + 1)] if a + 1 < rows else [])
        gram = dot(left(a, slice(0, members)), cat([u[p, 0] for _, p in near], 1), TN)
        blocks = cat(
            [
                tapered(gram[:, n * cells : (n + 1) * cells], tapers[which[p][0, 8 - k]], on[p][0, 8 - k])
                for n, (k, p) in enumerate(near)
            ],
            1,
        )
        both = dot(left(a, slice(members, deep)), blocks, NN)
        for n, (_, p) in enumerate(near):
            add(p, 0, both[:, n * cells : (n + 1) * cells])
        gram = dot(u[a, last], cat([right(p, slice(0, members)) for _, p in near], 1), TN)
        blocks = cat(
            [
                tapered(gram[:, n * cells : (n + 1) * cells], tapers[which[a][last, k]], on[a][last, k])
                for n, (k, _) in enumerate(near)
            ],
            1,
        )
        add(a, last, dot(cat([right(p, slice(members, deep)) for _, p in near], 1), blocks, NT))
        if a + 1 < rows:
            gram = dot(u[a, 0], left(a + 1, slice(0, members)), TN)
            block = tapered(gram, tapers[which[a][0, 6]], on[a][0, 6])
            add(a, 0, dot(left(a + 1, slice(members, deep)), block, NT))
            gram = dot(right(a, slice(0, members)), u[a + 1, last], TN)
            block = tapered(gram, tapers[which[a + 1][last, 2]], on[a + 1][last, 2])
            add(a + 1, last, dot(right(a, slice(members, deep)), block, NN))
    for a in range(rows):
        side[0, a] = total[a, 0]
        side[1, a] = total[a, last]


def end_places(cols):
    return list(range(ENDS)) + list(range(cols - ENDS, cols))


def edges(s, u, w, inside, outside, live, index, tapers):
    cells = u.shape[3]
    members = u.shape[2]
    columns = w.shape[2]
    part = jax.ShapeDtypeStruct((columns, cells), jnp.float32)
    return pl.pallas_call(
        edges_kernel,
        out_shape=(
            jax.ShapeDtypeStruct((2 * ENDS, columns, cells), jnp.bfloat16),
            jax.ShapeDtypeStruct((2 * ENDS, cells, 3 * cells), jnp.bfloat16),
            part,
            part,
            jax.ShapeDtypeStruct((2, u.shape[0], columns, cells), jnp.float32),
        ),
        in_specs=[VMEM] * 8,
        out_specs=(VMEM,) * 5,
        compiler_params=pltpu.CompilerParams(vmem_limit_bytes=GRANT),
        cost_estimate=pl.CostEstimate(
            flops=2 * 6 * ENDS * cells * cells * (members + columns), bytes_accessed=1 << 20, transcendentals=0
        ),
        name="edges",
    )(s, u, w, inside, outside, live, index, tapers)


def above_kernel(s, edge_back, u, w, live, index, tapers, back, held):
    cols, members, cells = u.shape[1:]
    on, which = live[0], index[0]
    for c in range(ENDS, cols - ENDS):
        near = [(k, c + k - 7) for k in (6, 7, 8)]
        gram = dot(s[c - ENDS, :members], cat([u[0, q] for _, q in near], 1), TN)
        held[c - ENDS] = cat(
            [
                tapered(gram[:, n * cells : (n + 1) * cells], tapers[which[q, 8 - k]], on[q, 8 - k])
                for n, (k, q) in enumerate(near)
            ],
            1,
        )
    for c in range(ENDS, cols - ENDS):
        back[c] = dot(cat([w[0, c + n] for n in (-1, 0, 1)], 1), held[c - ENDS], NT).astype(jnp.bfloat16)
    for n, c in enumerate(end_places(cols)):
        back[c] = edge_back[n]


def above(s, edge_back, u, w, live, index, tapers):
    cols, members, cells = u.shape[1:]
    columns = w.shape[2]
    return pl.pallas_call(
        above_kernel,
        out_shape=(
            jax.ShapeDtypeStruct((cols, columns, cells), jnp.bfloat16),
            jax.ShapeDtypeStruct((cols - 2 * ENDS, cells, 3 * cells), jnp.bfloat16),
        ),
        in_specs=[VMEM] * 7,
        out_specs=(VMEM, VMEM),
        compiler_params=pltpu.CompilerParams(vmem_limit_bytes=GRANT),
        cost_estimate=pl.CostEstimate(
            flops=2 * 3 * cols * cells * cells * (members + columns),
            bytes_accessed=2 << 20,
            transcendentals=0,
        ),
        name="above",
    )(s, edge_back, u, w, live, index, tapers)


def outer_kernel(inc, side, ends, end_held, s, held, out, top, low):
    rows, cols, _, cells = inc.shape
    deep = s.shape[1]
    members = deep - inc.shape[2]
    last = cols - 1
    places = end_places(cols)

    def source(c):
        if c in places:
            n = places.index(c)
            return ends[n, members:deep], end_held[n]
        return s[c - ENDS, members:deep], held[c - ENDS]

    for q in range(cols):
        back = [(k, source(q - (k - 7))) for k in (6, 7, 8) if 0 <= q - (k - 7) < cols]
        blocks = [block[:, (k - 6) * cells : (k - 5) * cells] for k, (_, block) in back]
        above = dot(cat([weight for _, (weight, _) in back], 1), cat(blocks, 0), NN)
        if q in (0, last):
            above += side[q // last, 0]
            top[q // last] = inc[0, q] + above
        out[0, q] = inc[0, q] + above
    for a in range(1, rows):
        for q in range(cols):
            value = inc[a, q] + side[q // last, a] if q in (0, last) else inc[a, q]
            out[a, q] = value
            if a == rows - 1:
                low[q] = value


def outer(inc, side, ends, end_held, s, held):
    rows, cols, columns, cells = inc.shape
    return pl.pallas_call(
        outer_kernel,
        out_shape=(
            jax.ShapeDtypeStruct(inc.shape, inc.dtype),
            jax.ShapeDtypeStruct((2, columns, cells), inc.dtype),
            jax.ShapeDtypeStruct(inc.shape[1:], inc.dtype),
        ),
        in_specs=[VMEM] * 6,
        out_specs=(VMEM,) * 3,
        compiler_params=pltpu.CompilerParams(vmem_limit_bytes=GRANT),
        cost_estimate=pl.CostEstimate(
            flops=6 * cols * cells * cells * columns, bytes_accessed=4 << 20, transcendentals=0
        ),
        name="outer",
    )(inc, side, ends, end_held, s, held)


def finish_kernel(inc, top, low, back, from_inside, from_outside, out, ends, total, sem):
    del inc
    rows, cols = out.shape[:2]
    even = even_column()
    total[...] = low[...] + back[...].astype(jnp.float32)
    copies = [pltpu.make_async_copy(total, out.at[rows - 1], sem.at[0])]
    copies[0].start()
    ends[0] = top[0] + jnp.where(even, from_outside[...], from_inside[...])
    ends[1] = top[1] + jnp.where(even, from_inside[...], from_outside[...])
    for n, q in enumerate((0, cols - 1)):
        copies.append(pltpu.make_async_copy(ends.at[n], out.at[0, q], sem.at[1 + n]))
        copies[-1].start()
    for copy in copies:
        copy.wait()


def finish(inc, top, low, back, from_inside, from_outside):
    return pl.pallas_call(
        finish_kernel,
        out_shape=jax.ShapeDtypeStruct(inc.shape, inc.dtype),
        in_specs=[ANY] + [VMEM] * 5,
        out_specs=ANY,
        scratch_shapes=[
            pltpu.VMEM(top.shape, top.dtype),
            pltpu.VMEM(low.shape, low.dtype),
            pltpu.SemaphoreType.DMA((3,)),
        ],
        input_output_aliases={0: 0},
        compiler_params=pltpu.CompilerParams(vmem_limit_bytes=GRANT),
        cost_estimate=pl.CostEstimate(flops=low.size, bytes_accessed=10 * low.size, transcendentals=0),
        name="finish",
    )(inc, top, low, back, from_inside, from_outside)


def forward(axis):
    return [(i, i + 1) for i in range(lax.axis_size(axis) - 1)]


def swaps(axis, start):
    pairs = [(i, i + 1) for i in range(start, lax.axis_size(axis) - 1, 2)]
    return pairs + [(b, a) for a, b in pairs]


def backward(axis):
    return [(i + 1, i) for i in range(lax.axis_size(axis) - 1)]


def pack_ends_kernel(u, w, out, sem):
    rows, cols, members, _ = u.shape
    deep = members + w.shape[2]
    copies = []
    for n, q in enumerate((0, cols - ENDS)):
        to = out.at[ENDS * n : ENDS * n + ENDS]
        copies.append(pltpu.make_async_copy(u.at[rows - 1, q : q + ENDS], to.at[:, :members], sem.at[n, 0]))
        copies.append(pltpu.make_async_copy(w.at[rows - 1, q : q + ENDS], to.at[:, members:deep], sem.at[n, 1]))
    for copy in copies:
        copy.start()
    for copy in copies:
        copy.wait()


def pack_ends(u, w):
    members, cells = u.shape[2:]
    shape = (2 * ENDS, members + w.shape[2], cells)
    return pl.pallas_call(
        pack_ends_kernel,
        out_shape=pltpu.VMEM(shape, u.dtype),
        in_specs=[HBM, HBM],
        out_specs=VMEM,
        scratch_shapes=[pltpu.SemaphoreType.DMA((2, 2))],
        cost_estimate=pl.CostEstimate(flops=0, bytes_accessed=8 * ENDS * shape[1] * cells, transcendentals=0),
        name="pack_ends",
    )(u, w)


def pack_row_kernel(u, w, out, sem):
    rows, cols, members, _ = u.shape
    deep = members + w.shape[2]
    between = slice(ENDS, cols - ENDS)
    copies = [
        pltpu.make_async_copy(u.at[rows - 1, between], out.at[:, :members], sem.at[0]),
        pltpu.make_async_copy(w.at[rows - 1, between], out.at[:, members:deep], sem.at[1]),
    ]
    for copy in copies:
        copy.start()
    for copy in copies:
        copy.wait()


def pack_row(u, w):
    cols, members, cells = u.shape[1:]
    shape = (cols - 2 * ENDS, members + w.shape[2], cells)
    return pl.pallas_call(
        pack_row_kernel,
        out_shape=jax.ShapeDtypeStruct(shape, u.dtype),
        in_specs=[ANY, ANY],
        out_specs=VMEM,
        scratch_shapes=[pltpu.SemaphoreType.DMA((2,))],
        compiler_params=pltpu.CompilerParams(vmem_limit_bytes=GRANT),
        cost_estimate=pl.CostEstimate(flops=0, bytes_accessed=4 * shape[0] * shape[1] * cells, transcendentals=0),
        name="pack_row",
    )(u, w)


def pack_columns_kernel(u, w, live, index, packed, inner_side, outer_side, sem):
    del packed
    rows, cols, members, cells = u.shape
    deep = members + w.shape[2]
    turn = (cols - 1) * even_column().astype(jnp.int32)
    copies = []
    for n, (out, b) in enumerate(((inner_side, turn), (outer_side, cols - 1 - turn))):
        copies.append(pltpu.make_async_copy(u.at[:, b], out.at[:, :members], sem.at[n, 0]))
        copies.append(pltpu.make_async_copy(w.at[:, b], out.at[:, members:deep], sem.at[n, 1]))
    for copy in copies:
        copy.start()
    for a in range(rows):
        lines = jnp.concatenate([live[a], index[a]], 0).astype(jnp.float32)
        blank = jnp.zeros((2 * cols, cells - live.shape[2]), jnp.float32)
        note = jnp.concatenate([lines, blank], 1).astype(jnp.bfloat16)
        inner_side[a, deep:] = note
        outer_side[a, deep:] = note
    for copy in copies:
        copy.wait()


def pack_columns(u, w, live, index, packed):
    rows, cols, members, cells = u.shape
    shape = (rows, members + w.shape[2] + 2 * cols, cells)
    return pl.pallas_call(
        pack_columns_kernel,
        out_shape=(jax.ShapeDtypeStruct(shape, u.dtype),) * 2,
        in_specs=[ANY, ANY, VMEM, VMEM, VMEM],
        out_specs=(VMEM, VMEM),
        scratch_shapes=[pltpu.SemaphoreType.DMA((2, 2))],
        compiler_params=pltpu.CompilerParams(vmem_limit_bytes=GRANT),
        cost_estimate=pl.CostEstimate(flops=0, bytes_accessed=8 * rows * shape[1] * cells, transcendentals=0),
        name="pack_columns",
    )(u, w, live, index, packed)


def body(u, w, live, index, tapers):
    packed = pack_ends(u, w)
    ends = lax.ppermute(packed, "row", forward("row"))
    inner_side, outer_side = pack_columns(u, w, live, index, packed)
    inside = lax.ppermute(inner_side, "col", swaps("col", 0))
    outside = lax.ppermute(outer_side, "col", swaps("col", 1))
    row = lax.ppermute(pack_row(u, w), "row", forward("row"))
    inc = inner(u, w, live, index, tapers, ends)
    inc, inside, outside = lax.optimization_barrier((inc, inside, outside))
    end_back, end_held, to_inside, to_outside, side = edges(ends, u, w, inside, outside, live, index, tapers)
    from_inside = lax.ppermute(to_inside, "col", swaps("col", 0))
    from_outside = lax.ppermute(to_outside, "col", swaps("col", 1))
    back, held = above(row, end_back, u, w, live, index, tapers)
    back = lax.ppermute(back, "row", backward("row"))
    inc, top, low = outer(inc, side, ends, end_held, row, held)
    return finish(inc, top, low, back, from_inside, from_outside)


def solution(mesh):
    return jax.shard_map(
        body,
        mesh=mesh,
        in_specs=(
            P("row", "col", None, None),
            P("row", "col", None, None),
            P("row", "col", None),
            P("row", "col", None),
            P(),
        ),
        out_specs=P("row", "col", None, None),
        check_vma=False,
    )
```

time: 32.4 us -> 30.5 us (0.941)
  local copies, waits for them, and re-layouts: 1.06 us -> 0.02 us
  starting transfers between devices: 15.4 us -> 14.8 us
    ppermute x1, waiting for transfers between devices: 0.19 us -> 2.72 us  [body(): ends = lax.ppermute(packed, 'row', forward('row'))]
    ppermute x1, waiting for transfers between devices: 1.87 us -> 0.01 us  [body(): back = lax.ppermute(back, 'row', backward('row'))]
    pallas_call x1, Pallas kernels: 2.57 us -> 1.24 us  [outer(): pl.pallas_call(outer_kernel, out_shape=(jax.ShapeDtypeStruct(inc.shape, i...]
    pallas_call x1, Pallas kernels: 0.67 us -> 1.9 us  [edges(): pl.pallas_call(edges_kernel, out_shape=(jax.ShapeDtypeStruct((2 * ENDS, c...]
    unnamed x12 -> x10, local copies, waits for them, and re-layouts: 1.06 us -> 0.02 us
    ppermute x1, starting transfers between devices: 2.56 us -> 1.92 us  [body(): from_outside = lax.ppermute(to_outside, 'col', swaps('col', 1))]
    ppermute x1, waiting for transfers between devices: 2.64 us -> 2.06 us  [body(): from_outside = lax.ppermute(to_outside, 'col', swaps('col', 1))]
  transfers between devices with their start and end apart: 7 -> 7, of which waited for: 3 -> 2; matrix products, arithmetic and copies ran while one was open for 0% -> 0% of each run, Pallas kernels for 26% -> 26%
where the time goes in v6:
time: 30.5 us; the launch traced here: 30.2 us
  starting transfers between devices  14.8 us (49%)
  Pallas kernels  10.5 us (34%)
  waiting for transfers between devices  4.8 us (16%)
    pallas_call x1, Pallas kernels, inner(): pl.pallas_call(inner_kernel, out_shape=jax.ShapeDtypeStruct((rows, cols,...  4.64 us
    ppermute x1, starting transfers between devices, body(): ends = lax.ppermute(packed, 'row', forward('row'))  3.43 us
    ppermute x1, starting transfers between devices, body(): row = lax.ppermute(pack_row(u, w), 'row', forward('row'))  3.43 us
    ppermute x1, starting transfers between devices, body(): back = lax.ppermute(back, 'row', backward('row'))  3.32 us
    ppermute x1, waiting for transfers between devices, body(): ends = lax.ppermute(packed, 'row', forward('row'))  2.72 us
    ppermute x1, starting transfers between devices, body(): outside = lax.ppermute(outer_side, 'col', swaps('col', 1))  2.53 us
    ppermute x1, waiting for transfers between devices, body(): from_outside = lax.ppermute(to_outside, 'col', swaps('col', 1))  2.06 us
    ppermute x1, starting transfers between devices, body(): from_outside = lax.ppermute(to_outside, 'col', swaps('col', 1))  1.92 us
  transfers between devices with their start and end apart: 7, of which 2 were waited for; matrix products, arithmetic and copies ran while one was open for 0% of the time, Pallas kernels for 26%

profile of v6, /device:TPU:22, one launch (start us, length us, event | category | flops | bytes accessed | tf_op | source)
XLA Modules:
  0.0 30.2 jit_solution(10166817405940768095)
XLA Ops:
  0.0 0.0 copy-start.1
  0.0 0.0 copy-start
  0.0 0.0 copy-start.4
  0.0 0.0 copy-start.3
  0.0 1.2 %pack_ends.1.packed = bf16[4,320,128]{2,1,0:T(8,128)(2,1)S(1)} custom-call(bf16[4,8,256,128]{3,2,1,0:T(8,128)(2,1)} %u.11, bf16[4,8,64,128]{3,2,1,0:T(8,128)(2,1)} %w.11), custom_call_target="tpu_custom_call" | custom-call | bytes 655360 | tf_op jit(solution)/shard_map/pack_ends/pallas_call | solution.py:381
  1.2 3.4 %collective-permute-start = (bf16[4,320,128]{2,1,0:T(8,128)(2,1)S(1)}, bf16[4,320,128]{2,1,0:T(8,128)(2,1)S(1)}, u32[]{:S(2)}, u32[]{:S(2)}) collective-permute-start(bf16[4,320,128]{2,1,0:T(8,128)(2,1)S(1)} %pack_ends.1.packed), channel_id=1, source_target_pairs={{0,4},{4,8},{8,12},{12,16},{16,20},{20,24},{24,28},{1,5},{5,9},{9,... | collective-permute-start | bytes 983048 | tf_op jit(solution)/shard_map/ppermute | solution.py:459
  4.6 0.0 copy-done.1
  4.6 0.0 copy-done
  4.7 0.0 copy-done.4
  4.7 0.0 copy-done.3
  4.7 0.1 pack_columns.1
  4.8 0.0 copy-start.2
  4.8 0.1 collective-permute-start.1
  4.9 2.5 %collective-permute-start.2 = (bf16[4,336,128]{2,1,0:T(8,128)(2,1)S(1)}, bf16[4,336,128]{2,1,0:T(8,128)(2,1)S(1)}, u32[]{:S(2)}, u32[]{:S(2)}) collective-permute-start(bf16[4,336,128]{2,1,0:T(8,128)(2,1)S(1)} %get-tuple-element.21), channel_id=1, source_target_pairs={{1,2},{2,1},{5,6},{6,5},{9,10},{10,9},{13,14},{14,13},{17,18},{18,... | collective-permute-start | bytes 1032200 | tf_op jit(solution)/shard_map/ppermute | solution.py:462
  7.5 0.1 pack_row.1
  7.5 3.4 %collective-permute-start.3 = (bf16[4,320,128]{2,1,0:T(8,128)(2,1)S(1)}, bf16[4,320,128]{2,1,0:T(8,128)(2,1)S(1)}, u32[]{:S(2)}, u32[]{:S(2)}) collective-permute-start(bf16[4,320,128]{2,1,0:T(8,128)(2,1)S(1)} %pack_row.1), channel_id=1, source_target_pairs={{0,4},{4,8},{8,12},{12,16},{16,20},{20,24},{24,28},{1,5},{5,9},{9,... | collective-permute-start | bytes 983048 | tf_op jit(solution)/shard_map/ppermute | solution.py:463
  11.0 2.7 %collective-permute-done.ends.s = bf16[4,320,128]{2,1,0:T(8,128)(2,1)S(1)} collective-permute-done((bf16[4,320,128]{2,1,0:T(8,128)(2,1)S(1)}, bf16[4,320,128]{2,1,0:T(8,128)(2,1)S(1)}, u32[]{:S(2)}, u32[]{:S(2)}) %collective-permute-start) | collective-permute-done | bytes 327712 | tf_op jit(solution)/shard_map/ppermute | solution.py:459
  13.7 0.0 copy-done.2
  13.7 4.6 %inner.1.inc = f32[4,8,64,128]{3,2,1,0:T(8,128)S(1)} custom-call(bf16[4,8,256,128]{3,2,1,0:T(8,128)(2,1)S(1)} %copy-done, bf16[4,8,64,128]{3,2,1,0:T(8,128)(2,1)S(1)} %copy-done.1, s32[4,8,9]{2,1,0:T(8,128)S(1)} %copy-done.3, s32[4,8,9]{2,1,0:T(8,128)S(1)} %copy-done.4, bf16[16,128,128]{2,1,0:T(8,128)(2,1)S(1)} %copy-done.2, ...), custom_call_target="tpu_custom_call" | custom-call | flops 2013265920 | bytes 4194304 | tf_op jit(solution)/shard_map/inner/pallas_call | solution.py:104
  18.3 0.0 collective-permute-done.1.inside
  18.3 0.0 collective-permute-done.2.outside
  18.4 1.9 %edges.1 = (bf16[4,64,128]{2,1,0:T(8,128)(2,1)S(1)}, bf16[4,128,384]{2,1,0:T(8,128)(2,1)S(1)}, f32[64,128]{1,0:T(8,128)S(1)}, f32[64,128]{1,0:T(8,128)S(1)}, f32[2,4,64,128]{3,2,1,0:T(8,128)S(1)}) custom-call(bf16[4,320,128]{2,1,0:T(8,128)(2,1)S(1)} %collective-permute-done.ends.s, bf16[4,8,256,128]{3,2,1,0:T(8,128)(2,1)S(1)} %copy-done, ...), custom_call_target="tpu_custom_call" | custom-call | flops 125829120 | bytes 1048576 | tf_op jit(solution)/shard_map/edges/pallas_call | solution.py:210
  20.3 0.0 collective-permute-done.3.s
  20.3 0.5 %above.1 = (bf16[8,64,128]{2,1,0:T(8,128)(2,1)S(1)}, bf16[4,128,384]{2,1,0:T(8,128)(2,1)S(1)}) custom-call(bf16[4,320,128]{2,1,0:T(8,128)(2,1)S(1)} %collective-permute-done.3.s, bf16[4,64,128]{2,1,0:T(8,128)(2,1)S(1)} %get-tuple-element.27.edge_back, bf16[4,8,256,128]{3,2,1,0:T(8,128)(2,1)S(1)} %copy-done, bf16[4,8,64,128]{3,2,1,0:T(8,128)(2,1)S(1)} %copy-done.1, ...), custom_call_target="tpu_custom_call" | custom-call | flops 251658240 | bytes 2097152 | tf_op jit(solution)/shard_map/above/pallas_call | solution.py:251
  20.8 3.3 %collective-permute-start.4 = (bf16[8,64,128]{2,1,0:T(8,128)(2,1)S(1)}, bf16[8,64,128]{2,1,0:T(8,128)(2,1)S(1)}, u32[]{:S(2)}, u32[]{:S(2)}) collective-permute-start(bf16[8,64,128]{2,1,0:T(8,128)(2,1)S(1)} %get-tuple-element.32), channel_id=1, source_target_pairs={{4,0},{8,4},{12,8},{16,12},{20,16},{24,20},{28,24},{5,1},{9,5},{13... | collective-permute-start | bytes 393224 | tf_op jit(solution)/shard_map/ppermute | solution.py:470
  24.1 0.1 collective-permute-start.5
  24.2 1.9 %collective-permute-start.6 = (f32[64,128]{1,0:T(8,128)S(1)}, f32[64,128]{1,0:T(8,128)S(1)}, u32[]{:S(2)}, u32[]{:S(2)}) collective-permute-start(f32[64,128]{1,0:T(8,128)S(1)} %get-tuple-element.34), channel_id=1, source_target_pairs={{1,2},{2,1},{5,6},{6,5},{9,10},{10,9},{13,14},{14,13},{17,18},{18,... | collective-permute-start | bytes 98312 | tf_op jit(solution)/shard_map/ppermute | solution.py:468
  26.1 1.2 %outer.1 = (f32[4,8,64,128]{3,2,1,0:T(8,128)}, f32[2,64,128]{2,1,0:T(8,128)S(1)}, f32[8,64,128]{2,1,0:T(8,128)S(1)}) custom-call(f32[4,8,64,128]{3,2,1,0:T(8,128)S(1)} %inner.1.inc, f32[2,4,64,128]{3,2,1,0:T(8,128)S(1)} %get-tuple-element.25.side, bf16[4,320,128]{2,1,0:T(8,128)(2,1)S(1)} %collective-permute-done.ends.s, ...), custom_call_target="tpu_custom_call" | custom-call | flops 50331648 | bytes 4194304 | tf_op jit(solution)/shard_map/outer/pallas_call | solution.py:300
  27.4 0.0 collective-permute-done.5.from_inside
  27.4 2.1 %collective-permute-done.6.from_outside = f32[64,128]{1,0:T(8,128)S(1)} collective-permute-done((f32[64,128]{1,0:T(8,128)S(1)}, f32[64,128]{1,0:T(8,128)S(1)}, u32[]{:S(2)}, u32[]{:S(2)}) %collective-permute-start.6) | collective-permute-done | bytes 32800 | tf_op jit(solution)/shard_map/ppermute | solution.py:468
  29.5 0.0 collective-permute-done.4.back
  29.5 0.8 %finish.1 = f32[4,8,64,128]{3,2,1,0:T(8,128)} custom-call(f32[4,8,64,128]{3,2,1,0:T(8,128)} %get-tuple-element.29.inc, f32[2,64,128]{2,1,0:T(8,128)S(1)} %get-tuple-element.30.top, f32[8,64,128]{2,1,0:T(8,128)S(1)} %get-tuple-element.31.low, bf16[8,64,128]{2,1,0:T(8,128)(2,1)S(1)} %collective-permute-done.4.back, ...), custom_call_target="tpu_custom_call", output_to_operand_aliasing={{}: (0, {})} | custom-call | flops 65536 | bytes 655360 | tf_op jit(solution)/shard_map/finish/pallas_call | solution.py:334
Async XLA Ops:
  0.0 4.6 %copy-start.1 = (bf16[4,8,64,128]{3,2,1,0:T(8,128)(2,1)S(1)}, bf16[4,8,64,128]{3,2,1,0:T(8,128)(2,1)}, u32[]{:S(2)}) copy-start(bf16[4,8,64,128]{3,2,1,0:T(8,128)(2,1)} %w.11) | copy-start | bytes 1572868
  0.0 4.6 %copy-start = (bf16[4,8,256,128]{3,2,1,0:T(8,128)(2,1)S(1)}, bf16[4,8,256,128]{3,2,1,0:T(8,128)(2,1)}, u32[]{:S(2)}) copy-start(bf16[4,8,256,128]{3,2,1,0:T(8,128)(2,1)} %u.11) | copy-start | bytes 6291460
  0.0 4.7 %copy-start.4 = (s32[4,8,9]{2,1,0:T(8,128)S(1)}, s32[4,8,9]{2,1,0:T(8,128)}, u32[]{:S(2)}) copy-start(s32[4,8,9]{2,1,0:T(8,128)} %index.7) | copy-start | bytes 3460
  0.0 4.7 %copy-start.3 = (s32[4,8,9]{2,1,0:T(8,128)S(1)}, s32[4,8,9]{2,1,0:T(8,128)}, u32[]{:S(2)}) copy-start(s32[4,8,9]{2,1,0:T(8,128)} %live.7) | copy-start | bytes 3460
  1.2 12.5 %collective-permute-start = (bf16[4,320,128]{2,1,0:T(8,128)(2,1)S(1)}, bf16[4,320,128]{2,1,0:T(8,128)(2,1)S(1)}, u32[]{:S(2)}, u32[]{:S(2)}) collective-permute-start(bf16[4,320,128]{2,1,0:T(8,128)(2,1)S(1)} %pack_ends.1.packed), channel_id=1, source_target_pairs={{0,4},{4,8},{8,12},{12,16},{16,20},{20,24},{24,28},{1,5},{5,9},{9,... | collective-permute-start | bytes 983048 | tf_op jit(solution)/shard_map/ppermute | solution.py:459
  4.8 8.9 %copy-start.2 = (bf16[16,128,128]{2,1,0:T(8,128)(2,1)S(1)}, bf16[16,128,128]{2,1,0:T(8,128)(2,1)}, u32[]{:S(2)}) copy-start(bf16[16,128,128]{2,1,0:T(8,128)(2,1)} %tapers.5) | copy-start | bytes 1572868
  4.8 13.5 %collective-permute-start.1 = (bf16[4,336,128]{2,1,0:T(8,128)(2,1)S(1)}, bf16[4,336,128]{2,1,0:T(8,128)(2,1)S(1)}, u32[]{:S(2)}, u32[]{:S(2)}) collective-permute-start(bf16[4,336,128]{2,1,0:T(8,128)(2,1)S(1)} %get-tuple-element.20), channel_id=1, source_target_pairs={{0,1},{2,3},{1,0},{3,2},{4,5},{6,7},{5,4},{7,6},{8,9},{10,11},{9,8... | collective-permute-start | bytes 1032200 | tf_op jit(solution)/shard_map/ppermute | solution.py:461
  4.9 13.4 %collective-permute-start.2 = (bf16[4,336,128]{2,1,0:T(8,128)(2,1)S(1)}, bf16[4,336,128]{2,1,0:T(8,128)(2,1)S(1)}, u32[]{:S(2)}, u32[]{:S(2)}) collective-permute-start(bf16[4,336,128]{2,1,0:T(8,128)(2,1)S(1)} %get-tuple-element.21), channel_id=1, source_target_pairs={{1,2},{2,1},{5,6},{6,5},{9,10},{10,9},{13,14},{14,13},{17,18},{18,... | collective-permute-start | bytes 1032200 | tf_op jit(solution)/shard_map/ppermute | solution.py:462
  7.5 12.7 %collective-permute-start.3 = (bf16[4,320,128]{2,1,0:T(8,128)(2,1)S(1)}, bf16[4,320,128]{2,1,0:T(8,128)(2,1)S(1)}, u32[]{:S(2)}, u32[]{:S(2)}) collective-permute-start(bf16[4,320,128]{2,1,0:T(8,128)(2,1)S(1)} %pack_row.1), channel_id=1, source_target_pairs={{0,4},{4,8},{8,12},{12,16},{16,20},{20,24},{24,28},{1,5},{5,9},{9,... | collective-permute-start | bytes 983048 | tf_op jit(solution)/shard_map/ppermute | solution.py:463
  20.8 8.6 %collective-permute-start.4 = (bf16[8,64,128]{2,1,0:T(8,128)(2,1)S(1)}, bf16[8,64,128]{2,1,0:T(8,128)(2,1)S(1)}, u32[]{:S(2)}, u32[]{:S(2)}) collective-permute-start(bf16[8,64,128]{2,1,0:T(8,128)(2,1)S(1)} %get-tuple-element.32), channel_id=1, source_target_pairs={{4,0},{8,4},{12,8},{16,12},{20,16},{24,20},{28,24},{5,1},{9,5},{13... | collective-permute-start | bytes 393224 | tf_op jit(solution)/shard_map/ppermute | solution.py:470
  24.1 3.3 %collective-permute-start.5 = (f32[64,128]{1,0:T(8,128)S(1)}, f32[64,128]{1,0:T(8,128)S(1)}, u32[]{:S(2)}, u32[]{:S(2)}) collective-permute-start(f32[64,128]{1,0:T(8,128)S(1)} %get-tuple-element.33), channel_id=1, source_target_pairs={{0,1},{2,3},{1,0},{3,2},{4,5},{6,7},{5,4},{7,6},{8,9},{10,11},{9,8... | collective-permute-start | bytes 98312 | tf_op jit(solution)/shard_map/ppermute | solution.py:467
  24.2 5.2 %collective-permute-start.6 = (f32[64,128]{1,0:T(8,128)S(1)}, f32[64,128]{1,0:T(8,128)S(1)}, u32[]{:S(2)}, u32[]{:S(2)}) collective-permute-start(f32[64,128]{1,0:T(8,128)S(1)} %get-tuple-element.34), channel_id=1, source_target_pairs={{1,2},{2,1},{5,6},{6,5},{9,10},{10,9},{13,14},{14,13},{17,18},{18,... | collective-permute-start | bytes 98312 | tf_op jit(solution)/shard_map/ppermute | solution.py:468

commit v7 on v4

--- a/solution.py
+++ b/solution.py
@@ -41,26 +41,12 @@
     )
 
 
-def prepare_kernel(tapers, sym):
+def inner_kernel(u, w, live, index, tapers, out, sym, held):
+    rows, cols, _, cells = u.shape
     for n in range(tapers.shape[0]):
         t = tapers[n].astype(jnp.float32)
         sym[n] = 0.5 * (t + t.T)
 
-
-def prepare(tapers):
-    return pl.pallas_call(
-        prepare_kernel,
-        out_shape=jax.ShapeDtypeStruct(tapers.shape, jnp.float32),
-        in_specs=[VMEM],
-        out_specs=VMEM,
-        compiler_params=pltpu.CompilerParams(vmem_limit_bytes=GRANT),
-        cost_estimate=pl.CostEstimate(flops=0, bytes_accessed=16 << 20, transcendentals=0),
-        name="prepare",
-    )(tapers)
-
-
-def inner_kernel(u, w, live, index, tapers, sym, out, held):
-    rows, cols, _, cells = u.shape
     def ahead(a, b, last):
         near = [(4, a, b)]
         if b + 1 < cols:
@@ -109,16 +95,19 @@
     row(rows - 1, True)
 
 
-def inner(u, w, live, index, tapers, sym):
+def inner(u, w, live, index, tapers):
     rows, cols, members, cells = u.shape
     columns = w.shape[2]
     pairs = 5 * rows * cols
     return pl.pallas_call(
         inner_kernel,
         out_shape=jax.ShapeDtypeStruct((rows, cols, columns, cells), jnp.float32),
-        in_specs=[VMEM] * 6,
+        in_specs=[VMEM] * 5,
         out_specs=VMEM,
-        scratch_shapes=[pltpu.VMEM((cols, cells, 5 * cells), jnp.bfloat16)],
+        scratch_shapes=[
+            pltpu.VMEM(tapers.shape, jnp.float32),
+            pltpu.VMEM((cols, cells, 5 * cells), jnp.bfloat16),
+        ],
         compiler_params=pltpu.CompilerParams(vmem_limit_bytes=GRANT),
         cost_estimate=pl.CostEstimate(
             flops=2 * pairs * cells * cells * (members + 2 * columns),
@@ -126,55 +115,56 @@
             transcendentals=0,
         ),
         name="inner",
-    )(u, w, live, index, tapers, sym)
-
-
-def above_kernel(s, u, w, inside, outside, live, index, tapers, back, held):
-    cols, _, cells = s.shape
-    members = u.shape[2]
+    )(u, w, live, index, tapers)
+
+
+def above_kernel(s, u, w, inside, outside, live, index, tapers, back, held, to_inside):
+    cols, members, cells = u.shape[1:]
     deep = members + w.shape[2]
+    last = cols - 1
     left, right = sides(inside, outside)
     on, which = live[0], index[0]
-    notes = [near(0, slice(deep, None)).astype(jnp.int32) for near in (left, right)]
-    side = [notes[0][cols - 1, 2], notes[0][2 * cols - 1, 2], notes[1][0, 0], notes[1][cols, 0]]
-
+    beyond = {}
+    for q, near, k, line in ((-1, left, 2, last), (cols, right, 0, 0)):
+        note = near(0, slice(deep, None)).astype(jnp.int32)
+        beyond[q] = near, note[line, k], note[cols + line, k]
     sources = []
     for c in range(cols):
         grams, weights, lives, rhos = [], [], [], []
         for k in (6, 7, 8):
             q = c + k - 7
-            if q < 0:
-                near, lively, at = left, side[0], side[1]
-            elif q >= cols:
-                near, lively, at = right, side[2], side[3]
+            if q in beyond:
+                near, lively, at = beyond[q]
+                grams.append(near(0, slice(0, members)))
+                weights.append(near(0, slice(members, deep)))
             else:
-                near, lively, at = None, on[q, 8 - k], which[q, 8 - k]
-            grams.append(u[0, q] if near is None else near(0, slice(0, members)))
-            weights.append(w[0, q] if near is None else near(0, slice(members, deep)))
+                lively, at = on[q, 8 - k], which[q, 8 - k]
+                grams.append(u[0, q])
+                weights.append(w[0, q])
             lives.append(lively)
             rhos.append(tapers[at])
         gram = dot(s[c, :members], cat(grams, 1), TN)
-        block = cat(
-            [tapered(gram[:, n * cells : (n + 1) * cells], rhos[n], lives[n]) for n in range(3)], 1
-        )
-        held[c] = block
+        held[c] = cat([tapered(gram[:, m * cells : (m + 1) * cells], rhos[m], lives[m]) for m in range(3)], 1)
         sources.append(cat(weights, 1))
     for c in range(cols):
         back[c] = dot(sources[c], held[c], NT).astype(jnp.bfloat16)
+    even = even_column()
+    weight = jnp.where(even, s[last, members:deep], s[0, members:deep])
+    to_inside[...] = dot(weight, jnp.where(even, held[last, :, 2 * cells :], held[0, :, :cells]), NN)
 
 
 def above(s, u, w, inside, outside, live, index, tapers):
-    cols, _, cells = s.shape
+    cols, members, cells = u.shape[1:]
     columns = w.shape[2]
-    members = u.shape[2]
     return pl.pallas_call(
         above_kernel,
         out_shape=(
             jax.ShapeDtypeStruct((cols, columns, cells), jnp.bfloat16),
             jax.ShapeDtypeStruct((cols, cells, 3 * cells), jnp.bfloat16),
+            jax.ShapeDtypeStruct((columns, cells), jnp.float32),
         ),
         in_specs=[VMEM] * 8,
-        out_specs=(VMEM, VMEM),
+        out_specs=(VMEM,) * 3,
         compiler_params=pltpu.CompilerParams(vmem_limit_bytes=GRANT),
         cost_estimate=pl.CostEstimate(
             flops=2 * 3 * cols * cells * cells * (members + columns),
@@ -185,12 +175,12 @@
     )(s, u, w, inside, outside, live, index, tapers)
 
 
-def outer_kernel(inc, held, s, corner, u, w, inside, outside, live, index, tapers, out, low):
+def outer_kernel(inc, held, s, corner, u, w, inside, outside, live, index, tapers, out, top, low):
     rows, cols, members, cells = u.shape
     deep = members + w.shape[2]
     last = cols - 1
     left, right = sides(inside, outside)
-    first = even_column().astype(jnp.int32)
+    even = even_column()
     on = [live[a] for a in range(rows)]
     which = [index[a] for a in range(rows)]
     total = {}
@@ -200,14 +190,15 @@
 
     for q in range(cols):
         back = [(k, q - (k - 7)) for k in (6, 7, 8) if 0 <= q - (k - 7) < cols]
-        sources = [s[c, members:deep] for _, c in back]
         blocks = [held[c, :, (k - 6) * cells : (k - 5) * cells] for k, c in back]
-        for edge, k, far in ((0, 8, first), (last, 6, 1 - first)):
-            if q == edge:
-                gram = dot(corner[far, :members], u[0, q], TN)
-                sources.append(corner[far, members:deep])
-                blocks.append(tapered(gram, tapers[which[0][q, 8 - k]], on[0][q, 8 - k]))
-        add(0, q, dot(cat(sources, 1), cat(blocks, 0), NN))
+        add(0, q, dot(cat([s[c, members:deep] for _, c in back], 1), cat(blocks, 0), NN))
+    gram = dot(corner[1, :members], jnp.where(even, u[0, 0], u[0, last]), TN)
+    at = jnp.where(even, which[0][0, 0], which[0][last, 2])
+    block = tapered(gram, tapers[at], jnp.where(even, on[0][0, 0], on[0][last, 2]))
+    far = dot(corner[1, members:deep], block, NN)
+    blank = jnp.zeros_like(far)
+    add(0, 0, jnp.where(even, far, blank))
+    add(0, last, jnp.where(even, blank, far))
 
     for a in range(rows):
         near = [(5, a)] + ([(8, a + 1)] if a + 1 < rows else [])
@@ -243,6 +234,8 @@
         for q in range(cols):
             value = inc[a, q] + total[a, q] if (a, q) in total else inc[a, q]
             out[a, q] = value
+            if a == 0 and q in (0, last):
+                top[q // last] = value
             if a == rows - 1:
                 low[q] = value
 
@@ -252,9 +245,13 @@
     columns = w.shape[2]
     return pl.pallas_call(
         outer_kernel,
-        out_shape=(jax.ShapeDtypeStruct(inc.shape, inc.dtype), jax.ShapeDtypeStruct(inc.shape[1:], inc.dtype)),
+        out_shape=(
+            jax.ShapeDtypeStruct(inc.shape, inc.dtype),
+            jax.ShapeDtypeStruct((2, columns, cells), inc.dtype),
+            jax.ShapeDtypeStruct(inc.shape[1:], inc.dtype),
+        ),
         in_specs=[VMEM] * 11,
-        out_specs=(VMEM, VMEM),
+        out_specs=(VMEM,) * 3,
         compiler_params=pltpu.CompilerParams(vmem_limit_bytes=GRANT),
         cost_estimate=pl.CostEstimate(
             flops=2 * (6 * rows + 3 * cols) * cells * cells * (members + columns),
@@ -265,26 +262,39 @@
     )(inc, held, s, corner, u, w, inside, outside, live, index, tapers)
 
 
-def finish_kernel(inc, low, back, out, total, sem):
+def finish_kernel(inc, top, low, back, from_inside, out, end, total, sem):
     del inc
-    total[...] = low[...] + back[...].astype(jnp.float32)
-    copy = pltpu.make_async_copy(total, out.at[out.shape[0] - 1], sem)
-    copy.start()
-    copy.wait()
-
-
-def finish(inc, low, back):
+    rows, cols = out.shape[:2]
+    half = cols // 2
+    side = even_column().astype(jnp.int32)
+    copies = []
+    for n, part in enumerate((slice(0, half), slice(half, cols))):
+        total[part] = low[part] + back[part].astype(jnp.float32)
+        copies.append(pltpu.make_async_copy(total.at[part], out.at[rows - 1, part], sem.at[n]))
+        copies[-1].start()
+    end[...] = top[side] + from_inside[...]
+    copies.append(pltpu.make_async_copy(end, out.at[0, side * (cols - 1)], sem.at[2]))
+    copies[-1].start()
+    for copy in copies:
+        copy.wait()
+
+
+def finish(inc, top, low, back, from_inside):
     return pl.pallas_call(
         finish_kernel,
         out_shape=jax.ShapeDtypeStruct(inc.shape, inc.dtype),
-        in_specs=[ANY, VMEM, VMEM],
+        in_specs=[ANY] + [VMEM] * 4,
         out_specs=ANY,
-        scratch_shapes=[pltpu.VMEM(low.shape, low.dtype), pltpu.SemaphoreType.DMA(())],
+        scratch_shapes=[
+            pltpu.VMEM(top.shape[1:], top.dtype),
+            pltpu.VMEM(low.shape, low.dtype),
+            pltpu.SemaphoreType.DMA((3,)),
+        ],
         input_output_aliases={0: 0},
         compiler_params=pltpu.CompilerParams(vmem_limit_bytes=GRANT),
         cost_estimate=pl.CostEstimate(flops=low.size, bytes_accessed=10 * low.size, transcendentals=0),
         name="finish",
-    )(inc, low, back)
+    )(inc, top, low, back, from_inside)
 
 
 def forward(axis):
@@ -314,7 +324,7 @@
 
 
 def pack_row(u, w):
-    _, cols, members, cells = u.shape
+    cols, members, cells = u.shape[1:]
     shape = (cols, members + w.shape[2], cells)
     return pl.pallas_call(
         pack_row_kernel,
@@ -327,8 +337,8 @@
     )(u, w)
 
 
-def pack_columns_kernel(u, w, live, index, sym, inner_side, outer_side, sem):
-    del sym
+def pack_columns_kernel(u, w, live, index, packed, inner_side, outer_side, sem):
+    del packed
     rows, cols, members, cells = u.shape
     deep = members + w.shape[2]
     turn = (cols - 1) * even_column().astype(jnp.int32)
@@ -348,7 +358,7 @@
         copy.wait()
 
 
-def pack_columns(u, w, live, index, sym):
+def pack_columns(u, w, live, index, packed):
     rows, cols, members, cells = u.shape
     shape = (rows, members + w.shape[2] + 2 * cols, cells)
     return pl.pallas_call(
@@ -360,27 +370,30 @@
         compiler_params=pltpu.CompilerParams(vmem_limit_bytes=GRANT),
         cost_estimate=pl.CostEstimate(flops=0, bytes_accessed=8 * rows * shape[1] * cells, transcendentals=0),
         name="pack_columns",
-    )(u, w, live, index, sym)
-
-
-def body(perturbations, weights, live, index, tapers):
-    rows, cols, members, cells = perturbations.shape
-    deep = members + weights.shape[2]
-    row = pack_row(perturbations, weights)
-    row, u, w, tapers = lax.optimization_barrier((row, perturbations, weights, tapers))
-    s = lax.ppermute(row, "row", forward("row"))
-    sym = prepare(tapers)
-    inner_side, outer_side = pack_columns(u, w, live, index, sym)
+    )(u, w, live, index, packed)
+
+
+def inward(row, col):
+    wide = lax.axis_size(col)
+    return [
+        (r * wide + c, (r + 1) * wide + c) for r in range(lax.axis_size(row) - 1) for c in range(1, wide - 1)
+    ]
+
+
+def body(u, w, live, index, tapers):
+    rows = u.shape[0]
+    packed = pack_row(u, w)
+    s = lax.ppermute(packed, "row", forward("row"))
+    inner_side, outer_side = pack_columns(u, w, live, index, packed)
     inside = lax.ppermute(inner_side, "col", swaps("col", 0))
     outside = lax.ppermute(outer_side, "col", swaps("col", 1))
-    inc, inside, outside = lax.optimization_barrier((inner(u, w, live, index, tapers, sym), inside, outside))
-    corner = lax.ppermute(
-        jnp.stack([inside[rows - 1, :deep], outside[rows - 1, :deep]]), "row", forward("row")
-    )
-    back, held = above(s, u, w, inside, outside, live, index, tapers)
+    inc, inside, outside = lax.optimization_barrier((inner(u, w, live, index, tapers), inside, outside))
+    corner = lax.ppermute(outside[rows - 2 :], ("row", "col"), inward("row", "col"))
+    back, held, to_inside = above(s, u, w, inside, outside, live, index, tapers)
     back = lax.ppermute(back, "row", backward("row"))
-    inc, low = outer(inc, held, s, corner, u, w, inside, outside, live, index, tapers)
-    return finish(inc, low, back)
+    from_inside = lax.ppermute(to_inside, "col", swaps("col", 0))
+    inc, top, low = outer(inc, held, s, corner, u, w, inside, outside, live, index, tapers)
+    return finish(inc, top, low, back, from_inside)
 
 
 def solution(mesh):

time: 30.3 us -> 30.1 us (level)
  the two profiles are of different devices: /device:TPU:22 before, /device:TPU:0 now
where the time goes in v7:
time: 30.1 us; the launch traced here: 29.9 us
  waiting for transfers between devices  11.5 us (38%)
  Pallas kernels  10.3 us (34%)
  starting transfers between devices  7.85 us (26%)
    ppermute x1, waiting for transfers between devices, body(): s = lax.ppermute(packed, 'row', forward('row'))  8.34 us
    ppermute x1, starting transfers between devices, body(): s = lax.ppermute(packed, 'row', forward('row'))  5.06 us
    pallas_call x1, Pallas kernels, inner(): pl.pallas_call(inner_kernel, out_shape=jax.ShapeDtypeStruct((rows, cols,...  4.63 us
    ppermute x1, waiting for transfers between devices, body(): back = lax.ppermute(back, 'row', backward('row'))  3.18 us
    pallas_call x1, Pallas kernels, outer(): pl.pallas_call(outer_kernel, out_shape=(jax.ShapeDtypeStruct(inc.shape, i...  2.76 us
    ppermute x1, starting transfers between devices, body(): back = lax.ppermute(back, 'row', backward('row'))  1.29 us
    pallas_call x1, Pallas kernels, pack_row(): pl.pallas_call(pack_row_kernel, out_shape=pltpu.VMEM(shape, u.dtype), in_...  1.23 us
    pallas_call x1, Pallas kernels, above(): pl.pallas_call(above_kernel, out_shape=(jax.ShapeDtypeStruct((cols, colum...  0.79 us
  transfers between devices with their start and end apart: 6, of which 2 were waited for; matrix products, arithmetic and copies ran while one was open for 0% of the time, Pallas kernels for 28%

profile of v7, /device:TPU:0, one launch (start us, length us, event | category | flops | bytes accessed | tf_op | source)
XLA Modules:
  0.0 29.9 jit_solution(9204962121860993369)
XLA Ops:
  0.0 0.0 copy-start.1
  0.0 0.0 copy-start
  0.0 0.0 copy-start.4
  0.0 0.0 copy-start.3
  0.0 1.2 %pack_row.1.packed = bf16[8,320,128]{2,1,0:T(8,128)(2,1)S(1)} custom-call(bf16[4,8,256,128]{3,2,1,0:T(8,128)(2,1)} %u.9, bf16[4,8,64,128]{3,2,1,0:T(8,128)(2,1)} %w.9), custom_call_target="tpu_custom_call" | custom-call | bytes 1310720 | tf_op jit(solution)/shard_map/pack_row/pallas_call | solution.py:329
  1.2 0.0 copy-start.2
  1.3 5.1 %collective-permute-start.2 = (bf16[8,320,128]{2,1,0:T(8,128)(2,1)S(1)}, bf16[8,320,128]{2,1,0:T(8,128)(2,1)S(1)}, u32[]{:S(2)}, u32[]{:S(2)}) collective-permute-start(bf16[8,320,128]{2,1,0:T(8,128)(2,1)S(1)} %pack_row.1.packed), channel_id=1, source_target_pairs={{0,4},{4,8},{8,12},{12,16},{16,20},{20,24},{24,28},{1,5},{5,9},{9,... | collective-permute-start | bytes 1966088 | tf_op jit(solution)/shard_map/ppermute | solution.py:386
  6.3 0.0 copy-done.1
  6.3 0.0 copy-done
  6.3 0.0 copy-done.4
  6.4 0.0 copy-done.3
  6.4 0.1 pack_columns.1
  6.5 0.1 collective-permute-start
  6.6 0.7 %collective-permute-start.1 = (bf16[4,336,128]{2,1,0:T(8,128)(2,1)S(1)}, bf16[4,336,128]{2,1,0:T(8,128)(2,1)S(1)}, u32[]{:S(2)}, u32[]{:S(2)}) collective-permute-start(bf16[4,336,128]{2,1,0:T(8,128)(2,1)S(1)} %get-tuple-element.17), channel_id=1, source_target_pairs={{1,2},{2,1},{5,6},{6,5},{9,10},{10,9},{13,14},{14,13},{17,18},{18,... | collective-permute-start | bytes 1032200 | tf_op jit(solution)/shard_map/ppermute | solution.py:389
  7.3 0.0 copy-done.2
  7.3 4.6 %inner.1.inc = f32[4,8,64,128]{3,2,1,0:T(8,128)S(1)} custom-call(bf16[4,8,256,128]{3,2,1,0:T(8,128)(2,1)S(1)} %copy-done, bf16[4,8,64,128]{3,2,1,0:T(8,128)(2,1)S(1)} %copy-done.1, s32[4,8,9]{2,1,0:T(8,128)S(1)} %copy-done.3, s32[4,8,9]{2,1,0:T(8,128)S(1)} %copy-done.4, bf16[16,128,128]{2,1,0:T(8,128)(2,1)S(1)} %copy-done.2), custom_call_target="tpu_custom_call" | custom-call | flops 2013265920 | bytes 4194304 | tf_op jit(solution)/shard_map/inner/pallas_call | solution.py:102
  11.9 0.0 collective-permute-done.inside
  11.9 0.0 collective-permute-done.1.outside
  12.0 0.7 %collective-permute-start.3 = (bf16[2,336,128]{2,1,0:T(8,128)(2,1)S(1)}, bf16[2,336,128]{2,1,0:T(8,128)(2,1)S(1)}, u32[]{:S(2)}, u32[]{:S(2)}) collective-permute-start(bf16[2,336,128]{2,1,0:T(8,128)(2,1)S(1)} %slice.3), channel_id=1, source_target_pairs={{1,5},{2,6},{5,9},{6,10},{9,13},{10,14},{13,17},{14,18},{17,21},{1... | collective-permute-start | bytes 516104 | tf_op jit(solution)/shard_map/ppermute | solution.py:391
  12.7 8.3 %collective-permute-done.2.s = bf16[8,320,128]{2,1,0:T(8,128)(2,1)S(1)} collective-permute-done((bf16[8,320,128]{2,1,0:T(8,128)(2,1)S(1)}, bf16[8,320,128]{2,1,0:T(8,128)(2,1)S(1)}, u32[]{:S(2)}, u32[]{:S(2)}) %collective-permute-start.2) | collective-permute-done | bytes 655392 | tf_op jit(solution)/shard_map/ppermute | solution.py:386
  21.0 0.8 %above.1 = (bf16[8,64,128]{2,1,0:T(8,128)(2,1)S(1)}, bf16[8,128,384]{2,1,0:T(8,128)(2,1)S(1)}, f32[64,128]{1,0:T(8,128)S(1)}) custom-call(bf16[8,320,128]{2,1,0:T(8,128)(2,1)S(1)} %collective-permute-done.2.s, bf16[4,8,256,128]{3,2,1,0:T(8,128)(2,1)S(1)} %copy-done, bf16[4,8,64,128]{3,2,1,0:T(8,128)(2,1)S(1)} %copy-done.1, ...), custom_call_target="tpu_custom_call" | custom-call | flops 251658240 | bytes 2097152 | tf_op jit(solution)/shard_map/above/pallas_call | solution.py:159
  21.8 1.3 %collective-permute-start.4 = (bf16[8,64,128]{2,1,0:T(8,128)(2,1)S(1)}, bf16[8,64,128]{2,1,0:T(8,128)(2,1)S(1)}, u32[]{:S(2)}, u32[]{:S(2)}) collective-permute-start(bf16[8,64,128]{2,1,0:T(8,128)(2,1)S(1)} %get-tuple-element.25), channel_id=1, source_target_pairs={{4,0},{8,4},{12,8},{16,12},{20,16},{24,20},{28,24},{5,1},{9,5},{13... | collective-permute-start | bytes 393224 | tf_op jit(solution)/shard_map/ppermute | solution.py:393
  23.1 0.1 collective-permute-start.5
  23.2 0.0 collective-permute-done.3.corner
  23.2 2.8 %outer.1 = (f32[4,8,64,128]{3,2,1,0:T(8,128)}, f32[2,64,128]{2,1,0:T(8,128)S(1)}, f32[8,64,128]{2,1,0:T(8,128)S(1)}) custom-call(f32[4,8,64,128]{3,2,1,0:T(8,128)S(1)} %inner.1.inc, bf16[8,128,384]{2,1,0:T(8,128)(2,1)S(1)} %get-tuple-element.21.held, bf16[8,320,128]{2,1,0:T(8,128)(2,1)S(1)} %collective-permute-done.2.s, ...), custom_call_target="tpu_custom_call" | custom-call | flops 503316480 | bytes 4194304 | tf_op jit(solution)/shard_map/outer/pallas_call | solution.py:246
  25.9 0.0 collective-permute-done.5.from_inside
  25.9 3.2 %collective-permute-done.4.back = bf16[8,64,128]{2,1,0:T(8,128)(2,1)S(1)} collective-permute-done((bf16[8,64,128]{2,1,0:T(8,128)(2,1)S(1)}, bf16[8,64,128]{2,1,0:T(8,128)(2,1)S(1)}, u32[]{:S(2)}, u32[]{:S(2)}) %collective-permute-start.4) | collective-permute-done | bytes 131104 | tf_op jit(solution)/shard_map/ppermute | solution.py:393
  29.1 0.7 %finish.1 = f32[4,8,64,128]{3,2,1,0:T(8,128)} custom-call(f32[4,8,64,128]{3,2,1,0:T(8,128)} %get-tuple-element.22.inc, f32[2,64,128]{2,1,0:T(8,128)S(1)} %get-tuple-element.23.top, f32[8,64,128]{2,1,0:T(8,128)S(1)} %get-tuple-element.24.low, bf16[8,64,128]{2,1,0:T(8,128)(2,1)S(1)} %collective-permute-done.4.back, ...), custom_call_target="tpu_custom_call", output_to_operand_aliasing={{}: (0, {})} | custom-call | flops 65536 | bytes 655360 | tf_op jit(solution)/shard_map/finish/pallas_call | solution.py:283
  (1 shorter events, 0.0 us)
Async XLA Ops:
  0.0 6.3 %copy-start.1 = (bf16[4,8,64,128]{3,2,1,0:T(8,128)(2,1)S(1)}, bf16[4,8,64,128]{3,2,1,0:T(8,128)(2,1)}, u32[]{:S(2)}) copy-start(bf16[4,8,64,128]{3,2,1,0:T(8,128)(2,1)} %w.9) | copy-start | bytes 1572868
  0.0 6.3 %copy-start = (bf16[4,8,256,128]{3,2,1,0:T(8,128)(2,1)S(1)}, bf16[4,8,256,128]{3,2,1,0:T(8,128)(2,1)}, u32[]{:S(2)}) copy-start(bf16[4,8,256,128]{3,2,1,0:T(8,128)(2,1)} %u.9) | copy-start | bytes 6291460
  0.0 6.3 %copy-start.4 = (s32[4,8,9]{2,1,0:T(8,128)S(1)}, s32[4,8,9]{2,1,0:T(8,128)}, u32[]{:S(2)}) copy-start(s32[4,8,9]{2,1,0:T(8,128)} %index.7) | copy-start | bytes 3460
  0.0 6.3 %copy-start.3 = (s32[4,8,9]{2,1,0:T(8,128)S(1)}, s32[4,8,9]{2,1,0:T(8,128)}, u32[]{:S(2)}) copy-start(s32[4,8,9]{2,1,0:T(8,128)} %live.7) | copy-start | bytes 3460
  1.2 6.0 %copy-start.2 = (bf16[16,128,128]{2,1,0:T(8,128)(2,1)S(1)}, bf16[16,128,128]{2,1,0:T(8,128)(2,1)}, u32[]{:S(2)}) copy-start(bf16[16,128,128]{2,1,0:T(8,128)(2,1)} %tapers.5) | copy-start | bytes 1572868
  1.3 19.7 %collective-permute-start.2 = (bf16[8,320,128]{2,1,0:T(8,128)(2,1)S(1)}, bf16[8,320,128]{2,1,0:T(8,128)(2,1)S(1)}, u32[]{:S(2)}, u32[]{:S(2)}) collective-permute-start(bf16[8,320,128]{2,1,0:T(8,128)(2,1)S(1)} %pack_row.1.packed), channel_id=1, source_target_pairs={{0,4},{4,8},{8,12},{12,16},{16,20},{20,24},{24,28},{1,5},{5,9},{9,... | collective-permute-start | bytes 1966088 | tf_op jit(solution)/shard_map/ppermute | solution.py:386
  6.5 5.4 %collective-permute-start = (bf16[4,336,128]{2,1,0:T(8,128)(2,1)S(1)}, bf16[4,336,128]{2,1,0:T(8,128)(2,1)S(1)}, u32[]{:S(2)}, u32[]{:S(2)}) collective-permute-start(bf16[4,336,128]{2,1,0:T(8,128)(2,1)S(1)} %get-tuple-element.16), channel_id=1, source_target_pairs={{0,1},{2,3},{1,0},{3,2},{4,5},{6,7},{5,4},{7,6},{8,9},{10,11},{9,8... | collective-permute-start | bytes 1032200 | tf_op jit(solution)/shard_map/ppermute | solution.py:388
  6.6 5.4 %collective-permute-start.1 = (bf16[4,336,128]{2,1,0:T(8,128)(2,1)S(1)}, bf16[4,336,128]{2,1,0:T(8,128)(2,1)S(1)}, u32[]{:S(2)}, u32[]{:S(2)}) collective-permute-start(bf16[4,336,128]{2,1,0:T(8,128)(2,1)S(1)} %get-tuple-element.17), channel_id=1, source_target_pairs={{1,2},{2,1},{5,6},{6,5},{9,10},{10,9},{13,14},{14,13},{17,18},{18,... | collective-permute-start | bytes 1032200 | tf_op jit(solution)/shard_map/ppermute | solution.py:389
  12.0 11.2 %collective-permute-start.3 = (bf16[2,336,128]{2,1,0:T(8,128)(2,1)S(1)}, bf16[2,336,128]{2,1,0:T(8,128)(2,1)S(1)}, u32[]{:S(2)}, u32[]{:S(2)}) collective-permute-start(bf16[2,336,128]{2,1,0:T(8,128)(2,1)S(1)} %slice.3), channel_id=1, source_target_pairs={{1,5},{2,6},{5,9},{6,10},{9,13},{10,14},{13,17},{14,18},{17,21},{1... | collective-permute-start | bytes 516104 | tf_op jit(solution)/shard_map/ppermute | solution.py:391
  21.8 7.3 %collective-permute-start.4 = (bf16[8,64,128]{2,1,0:T(8,128)(2,1)S(1)}, bf16[8,64,128]{2,1,0:T(8,128)(2,1)S(1)}, u32[]{:S(2)}, u32[]{:S(2)}) collective-permute-start(bf16[8,64,128]{2,1,0:T(8,128)(2,1)S(1)} %get-tuple-element.25), channel_id=1, source_target_pairs={{4,0},{8,4},{12,8},{16,12},{20,16},{24,20},{28,24},{5,1},{9,5},{13... | collective-permute-start | bytes 393224 | tf_op jit(solution)/shard_map/ppermute | solution.py:393
  23.1 2.9 %collective-permute-start.5 = (f32[64,128]{1,0:T(8,128)S(1)}, f32[64,128]{1,0:T(8,128)S(1)}, u32[]{:S(2)}, u32[]{:S(2)}) collective-permute-start(f32[64,128]{1,0:T(8,128)S(1)} %get-tuple-element.26), channel_id=1, source_target_pairs={{0,1},{2,3},{1,0},{3,2},{4,5},{6,7},{5,4},{7,6},{8,9},{10,11},{9,8... | collective-permute-start | bytes 98312 | tf_op jit(solution)/shard_map/ppermute | solution.py:394

commit v8 on v7

--- a/solution.py
+++ b/solution.py
@@ -143,14 +143,13 @@
                 weights.append(w[0, q])
             lives.append(lively)
             rhos.append(tapers[at])
-        gram = dot(s[c, :members], cat(grams, 1), TN)
+        gram = dot(s[c * members : (c + 1) * members], cat(grams, 1), TN)
         held[c] = cat([tapered(gram[:, m * cells : (m + 1) * cells], rhos[m], lives[m]) for m in range(3)], 1)
         sources.append(cat(weights, 1))
     for c in range(cols):
         back[c] = dot(sources[c], held[c], NT).astype(jnp.bfloat16)
     even = even_column()
-    weight = jnp.where(even, s[last, members:deep], s[0, members:deep])
-    to_inside[...] = dot(weight, jnp.where(even, held[last, :, 2 * cells :], held[0, :, :cells]), NN)
+    to_inside[...] = dot(s[cols * members :], jnp.where(even, held[last, :, 2 * cells :], held[0, :, :cells]), NN)
 
 
 def above(s, u, w, inside, outside, live, index, tapers):
@@ -175,30 +174,17 @@
     )(s, u, w, inside, outside, live, index, tapers)
 
 
-def outer_kernel(inc, held, s, corner, u, w, inside, outside, live, index, tapers, out, top, low):
+def columns_kernel(u, w, inside, outside, live, index, tapers, side):
     rows, cols, members, cells = u.shape
     deep = members + w.shape[2]
     last = cols - 1
     left, right = sides(inside, outside)
-    even = even_column()
     on = [live[a] for a in range(rows)]
     which = [index[a] for a in range(rows)]
     total = {}
 
     def add(a, q, value):
         total[a, q] = total[a, q] + value if (a, q) in total else value
-
-    for q in range(cols):
-        back = [(k, q - (k - 7)) for k in (6, 7, 8) if 0 <= q - (k - 7) < cols]
-        blocks = [held[c, :, (k - 6) * cells : (k - 5) * cells] for k, c in back]
-        add(0, q, dot(cat([s[c, members:deep] for _, c in back], 1), cat(blocks, 0), NN))
-    gram = dot(corner[1, :members], jnp.where(even, u[0, 0], u[0, last]), TN)
-    at = jnp.where(even, which[0][0, 0], which[0][last, 2])
-    block = tapered(gram, tapers[at], jnp.where(even, on[0][0, 0], on[0][last, 2]))
-    far = dot(corner[1, members:deep], block, NN)
-    blank = jnp.zeros_like(far)
-    add(0, 0, jnp.where(even, far, blank))
-    add(0, last, jnp.where(even, blank, far))
 
     for a in range(rows):
         near = [(5, a)] + ([(8, a + 1)] if a + 1 < rows else [])
@@ -231,35 +217,70 @@
             add(a + 1, last, dot(right(a, slice(members, deep)), block, NN))
 
     for a in range(rows):
+        side[0, a] = total[a, 0]
+        side[1, a] = total[a, last]
+
+
+def columns(u, w, inside, outside, live, index, tapers):
+    rows, _, members, cells = u.shape
+    width = w.shape[2]
+    return pl.pallas_call(
+        columns_kernel,
+        out_shape=jax.ShapeDtypeStruct((2, rows, width, cells), jnp.float32),
+        in_specs=[VMEM] * 7,
+        out_specs=VMEM,
+        compiler_params=pltpu.CompilerParams(vmem_limit_bytes=GRANT),
+        cost_estimate=pl.CostEstimate(
+            flops=12 * rows * cells * cells * (members + width), bytes_accessed=2 << 20, transcendentals=0
+        ),
+        name="columns",
+    )(u, w, inside, outside, live, index, tapers)
+
+
+def outer_kernel(inc, side, held, rest, u, live, index, tapers, out, top, low):
+    rows, cols, members, cells = u.shape
+    width = inc.shape[2]
+    last = cols - 1
+    even = even_column()
+    on, which = live[0], index[0]
+    start = cols * width
+    gram = dot(rest[start : start + members], jnp.where(even, u[0, 0], u[0, last]), TN)
+    at = jnp.where(even, which[0, 0], which[last, 2])
+    block = tapered(gram, tapers[at], jnp.where(even, on[0, 0], on[last, 2]))
+    far = dot(rest[start + members :], block, NN)
+    blank = jnp.zeros_like(far)
+    for q in range(cols):
+        back = [(k, q - (k - 7)) for k in (6, 7, 8) if 0 <= q - (k - 7) < cols]
+        blocks = [held[c, :, (k - 6) * cells : (k - 5) * cells] for k, c in back]
+        value = inc[0, q] + dot(cat([rest[c * width : (c + 1) * width] for _, c in back], 1), cat(blocks, 0), NN)
+        if q in (0, last):
+            value += side[q // last, 0]
+            value += jnp.where(even, far, blank) if q == 0 else jnp.where(even, blank, far)
+            top[q // last] = value
+        out[0, q] = value
+    for a in range(1, rows):
         for q in range(cols):
-            value = inc[a, q] + total[a, q] if (a, q) in total else inc[a, q]
+            value = inc[a, q] + side[q // last, a] if q in (0, last) else inc[a, q]
             out[a, q] = value
-            if a == 0 and q in (0, last):
-                top[q // last] = value
             if a == rows - 1:
                 low[q] = value
 
 
-def outer(inc, held, s, corner, u, w, inside, outside, live, index, tapers):
-    rows, cols, members, cells = u.shape
-    columns = w.shape[2]
+def outer(inc, side, held, rest, u, live, index, tapers):
+    rows, cols, width, cells = inc.shape
     return pl.pallas_call(
         outer_kernel,
         out_shape=(
             jax.ShapeDtypeStruct(inc.shape, inc.dtype),
-            jax.ShapeDtypeStruct((2, columns, cells), inc.dtype),
+            jax.ShapeDtypeStruct((2, width, cells), inc.dtype),
             jax.ShapeDtypeStruct(inc.shape[1:], inc.dtype),
         ),
-        in_specs=[VMEM] * 11,
+        in_specs=[VMEM] * 8,
         out_specs=(VMEM,) * 3,
         compiler_params=pltpu.CompilerParams(vmem_limit_bytes=GRANT),
-        cost_estimate=pl.CostEstimate(
-            flops=2 * (6 * rows + 3 * cols) * cells * cells * (members + columns),
-            bytes_accessed=4 << 20,
-            transcendentals=0,
-        ),
+        cost_estimate=pl.CostEstimate(flops=6 * cols * cells * cells * width, bytes_accessed=4 << 20, transcendentals=0),
         name="outer",
-    )(inc, held, s, corner, u, w, inside, outside, live, index, tapers)
+    )(inc, side, held, rest, u, live, index, tapers)
 
 
 def finish_kernel(inc, top, low, back, from_inside, out, end, total, sem):
@@ -311,12 +332,13 @@
 
 
 def pack_row_kernel(u, w, out, sem):
-    rows, _, members, _ = u.shape
-    deep = members + w.shape[2]
+    rows, cols, members, _ = u.shape
+    beside = (cols - 1) * even_column().astype(jnp.int32)
     copies = [
-        pltpu.make_async_copy(u.at[rows - 1], out.at[:, :members], sem.at[0]),
-        pltpu.make_async_copy(w.at[rows - 1], out.at[:, members:deep], sem.at[1]),
+        pltpu.make_async_copy(u.at[rows - 1, q], out.at[q * members : (q + 1) * members], sem.at[q])
+        for q in range(cols)
     ]
+    copies.append(pltpu.make_async_copy(w.at[rows - 1, beside], out.at[cols * members :], sem.at[cols]))
     for copy in copies:
         copy.start()
     for copy in copies:
@@ -324,17 +346,38 @@
 
 
 def pack_row(u, w):
-    cols, members, cells = u.shape[1:]
-    shape = (cols, members + w.shape[2], cells)
+    _, cols, members, cells = u.shape
+    shape = (cols * members + w.shape[2], cells)
     return pl.pallas_call(
         pack_row_kernel,
         out_shape=pltpu.VMEM(shape, u.dtype),
         in_specs=[HBM, HBM],
         out_specs=VMEM,
-        scratch_shapes=[pltpu.SemaphoreType.DMA((2,))],
-        cost_estimate=pl.CostEstimate(flops=0, bytes_accessed=4 * cols * shape[1] * cells, transcendentals=0),
+        scratch_shapes=[pltpu.SemaphoreType.DMA((cols + 1,))],
+        cost_estimate=pl.CostEstimate(flops=0, bytes_accessed=4 * shape[0] * cells, transcendentals=0),
         name="pack_row",
     )(u, w)
+
+
+def pack_rest_kernel(w, outside, out):
+    rows, cols, width, _ = w.shape
+    for q in range(cols):
+        out[q * width : (q + 1) * width] = w[rows - 1, q]
+    deep = out.shape[0] - cols * width
+    out[cols * width :] = outside[rows - 1, :deep]
+
+
+def pack_rest(w, outside, members):
+    _, cols, width, cells = w.shape
+    return pl.pallas_call(
+        pack_rest_kernel,
+        out_shape=jax.ShapeDtypeStruct((cols * width + members + width, cells), w.dtype),
+        in_specs=[VMEM, VMEM],
+        out_specs=VMEM,
+        compiler_params=pltpu.CompilerParams(vmem_limit_bytes=GRANT),
+        cost_estimate=pl.CostEstimate(flops=0, bytes_accessed=8 * cols * width * cells, transcendentals=0),
+        name="pack_rest",
+    )(w, outside)
 
 
 def pack_columns_kernel(u, w, live, index, packed, inner_side, outer_side, sem):
@@ -373,26 +416,19 @@
     )(u, w, live, index, packed)
 
 
-def inward(row, col):
-    wide = lax.axis_size(col)
-    return [
-        (r * wide + c, (r + 1) * wide + c) for r in range(lax.axis_size(row) - 1) for c in range(1, wide - 1)
-    ]
-
-
 def body(u, w, live, index, tapers):
-    rows = u.shape[0]
     packed = pack_row(u, w)
     s = lax.ppermute(packed, "row", forward("row"))
     inner_side, outer_side = pack_columns(u, w, live, index, packed)
     inside = lax.ppermute(inner_side, "col", swaps("col", 0))
     outside = lax.ppermute(outer_side, "col", swaps("col", 1))
     inc, inside, outside = lax.optimization_barrier((inner(u, w, live, index, tapers), inside, outside))
-    corner = lax.ppermute(outside[rows - 2 :], ("row", "col"), inward("row", "col"))
+    rest = lax.ppermute(pack_rest(w, outside, u.shape[2]), "row", forward("row"))
     back, held, to_inside = above(s, u, w, inside, outside, live, index, tapers)
     back = lax.ppermute(back, "row", backward("row"))
     from_inside = lax.ppermute(to_inside, "col", swaps("col", 0))
-    inc, top, low = outer(inc, held, s, corner, u, w, inside, outside, live, index, tapers)
+    side = columns(u, w, inside, outside, live, index, tapers)
+    inc, top, low = outer(inc, side, held, rest, u, live, index, tapers)
     return finish(inc, top, low, back, from_inside)
 
 

time: 30.1 us -> 28.2 us (0.937)
  the two profiles are of different devices: /device:TPU:0 before, /device:TPU:22 now
where the time goes in v8:
time: 28.2 us; the launch traced here: 27.8 us
  starting transfers between devices  13 us (46%)
  Pallas kernels  10.5 us (37%)
  waiting for transfers between devices  4.12 us (15%)
    pallas_call x1, Pallas kernels, inner(): pl.pallas_call(inner_kernel, out_shape=jax.ShapeDtypeStruct((rows, cols,...  4.64 us
    ppermute x1, starting transfers between devices, body(): s = lax.ppermute(packed, 'row', forward('row'))  3.56 us
    ppermute x1, starting transfers between devices, body(): lax.ppermute(pack_rest(w, outside, u.shape[2]), 'row', forward('row'))  3.43 us
    ppermute x1, starting transfers between devices, body(): back = lax.ppermute(back, 'row', backward('row'))  3.31 us
    ppermute x1, starting transfers between devices, body(): outside = lax.ppermute(outer_side, 'col', swaps('col', 1))  2.53 us
    pallas_call x1, Pallas kernels, columns(): pl.pallas_call(columns_kernel, out_shape=jax.ShapeDtypeStruct((2, rows, w...  1.48 us
    pallas_call x1, Pallas kernels, outer(): pl.pallas_call(outer_kernel, out_shape=(jax.ShapeDtypeStruct(inc.shape, i...  1.43 us
    ppermute x1, waiting for transfers between devices, body(): back = lax.ppermute(back, 'row', backward('row'))  1.42 us
  transfers between devices with their start and end apart: 6, of which 3 were waited for; matrix products, arithmetic and copies ran while one was open for 0% of the time, Pallas kernels for 31%

profile of v8, /device:TPU:22, one launch (start us, length us, event | category | flops | bytes accessed | tf_op | source)
XLA Modules:
  0.0 27.8 jit_solution(16656031599766067833)
XLA Ops:
  0.0 0.0 copy-start.1
  0.0 0.0 copy-start
  0.0 0.0 copy-start.4
  0.0 0.0 copy-start.3
  0.0 1.3 %pack_row.1.packed = bf16[2112,128]{1,0:T(8,128)(2,1)S(1)} custom-call(bf16[4,8,256,128]{3,2,1,0:T(8,128)(2,1)} %u.11, bf16[4,8,64,128]{3,2,1,0:T(8,128)(2,1)} %w.11), custom_call_target="tpu_custom_call" | custom-call | bytes 1081344 | tf_op jit(solution)/shard_map/pack_row/pallas_call | solution.py:351
  1.3 0.0 copy-start.2
  1.3 3.6 %collective-permute-start.2 = (bf16[2112,128]{1,0:T(8,128)(2,1)S(1)}, bf16[2112,128]{1,0:T(8,128)(2,1)S(1)}, u32[]{:S(2)}, u32[]{:S(2)}) collective-permute-start(bf16[2112,128]{1,0:T(8,128)(2,1)S(1)} %pack_row.1.packed), channel_id=1, source_target_pairs={{0,4},{4,8},{8,12},{12,16},{16,20},{20,24},{24,28},{1,5},{5,9},{9,... | collective-permute-start | bytes 1622024 | tf_op jit(solution)/shard_map/ppermute | solution.py:421
  4.9 0.0 copy-done.1
  4.9 0.0 copy-done
  4.9 0.0 copy-done.4
  4.9 0.0 copy-done.3
  4.9 0.1 pack_columns.1
  5.1 0.1 collective-permute-start
  5.2 2.5 %collective-permute-start.1 = (bf16[4,336,128]{2,1,0:T(8,128)(2,1)S(1)}, bf16[4,336,128]{2,1,0:T(8,128)(2,1)S(1)}, u32[]{:S(2)}, u32[]{:S(2)}) collective-permute-start(bf16[4,336,128]{2,1,0:T(8,128)(2,1)S(1)} %get-tuple-element.17), channel_id=1, source_target_pairs={{1,2},{2,1},{5,6},{6,5},{9,10},{10,9},{13,14},{14,13},{17,18},{18,... | collective-permute-start | bytes 1032200 | tf_op jit(solution)/shard_map/ppermute | solution.py:424
  7.7 0.0 copy-done.2
  7.7 4.6 %inner.1.inc = f32[4,8,64,128]{3,2,1,0:T(8,128)S(1)} custom-call(bf16[4,8,256,128]{3,2,1,0:T(8,128)(2,1)S(1)} %copy-done, bf16[4,8,64,128]{3,2,1,0:T(8,128)(2,1)S(1)} %copy-done.1, s32[4,8,9]{2,1,0:T(8,128)S(1)} %copy-done.3, s32[4,8,9]{2,1,0:T(8,128)S(1)} %copy-done.4, bf16[16,128,128]{2,1,0:T(8,128)(2,1)S(1)} %copy-done.2), custom_call_target="tpu_custom_call" | custom-call | flops 2013265920 | bytes 4194304 | tf_op jit(solution)/shard_map/inner/pallas_call | solution.py:102
  12.4 0.0 collective-permute-done.inside
  12.4 1.4 %collective-permute-done.1.outside = bf16[4,336,128]{2,1,0:T(8,128)(2,1)S(1)} collective-permute-done((bf16[4,336,128]{2,1,0:T(8,128)(2,1)S(1)}, bf16[4,336,128]{2,1,0:T(8,128)(2,1)S(1)}, u32[]{:S(2)}, u32[]{:S(2)}) %collective-permute-start.1) | collective-permute-done | bytes 344096 | tf_op jit(solution)/shard_map/ppermute | solution.py:424
  13.8 3.4 %collective-permute-start.3 = (bf16[832,128]{1,0:T(8,128)(2,1)S(1)}, bf16[832,128]{1,0:T(8,128)(2,1)S(1)}, u32[]{:S(2)}, u32[]{:S(2)}) collective-permute-start(bf16[832,128]{1,0:T(8,128)(2,1)S(1)} %pack_rest.1), channel_id=1, source_target_pairs={{0,4},{4,8},{8,12},{12,16},{16,20},{20,24},{24,28},{1,5},{5,9},{9,... | collective-permute-start | bytes 638984 | tf_op jit(solution)/shard_map/ppermute | solution.py:426
  17.2 1.3 %collective-permute-done.2.s = bf16[2112,128]{1,0:T(8,128)(2,1)S(1)} collective-permute-done((bf16[2112,128]{1,0:T(8,128)(2,1)S(1)}, bf16[2112,128]{1,0:T(8,128)(2,1)S(1)}, u32[]{:S(2)}, u32[]{:S(2)}) %collective-permute-start.2) | collective-permute-done | bytes 540704 | tf_op jit(solution)/shard_map/ppermute | solution.py:421
  18.5 0.8 %above.1 = (bf16[8,64,128]{2,1,0:T(8,128)(2,1)S(1)}, bf16[8,128,384]{2,1,0:T(8,128)(2,1)S(1)}, f32[64,128]{1,0:T(8,128)S(1)}) custom-call(bf16[2112,128]{1,0:T(8,128)(2,1)S(1)} %collective-permute-done.2.s, bf16[4,8,256,128]{3,2,1,0:T(8,128)(2,1)S(1)} %copy-done, bf16[4,8,64,128]{3,2,1,0:T(8,128)(2,1)S(1)} %copy-done.1, ...), custom_call_target="tpu_custom_call" | custom-call | flops 251658240 | bytes 2097152 | tf_op jit(solution)/shard_map/above/pallas_call | solution.py:158
  19.3 3.3 %collective-permute-start.4 = (bf16[8,64,128]{2,1,0:T(8,128)(2,1)S(1)}, bf16[8,64,128]{2,1,0:T(8,128)(2,1)S(1)}, u32[]{:S(2)}, u32[]{:S(2)}) collective-permute-start(bf16[8,64,128]{2,1,0:T(8,128)(2,1)S(1)} %get-tuple-element.25), channel_id=1, source_target_pairs={{4,0},{8,4},{12,8},{16,12},{20,16},{24,20},{28,24},{5,1},{9,5},{13... | collective-permute-start | bytes 393224 | tf_op jit(solution)/shard_map/ppermute | solution.py:428
  22.6 0.1 collective-permute-start.5
  22.7 1.5 %columns.1.side = f32[2,4,64,128]{3,2,1,0:T(8,128)S(1)} custom-call(bf16[4,8,256,128]{3,2,1,0:T(8,128)(2,1)S(1)} %copy-done, bf16[4,8,64,128]{3,2,1,0:T(8,128)(2,1)S(1)} %copy-done.1, bf16[4,336,128]{2,1,0:T(8,128)(2,1)S(1)} %collective-permute-done.inside, bf16[4,336,128]{2,1,0:T(8,128)(2,1)S(1)} %collective-permute-done.1.outside, ...), custom_call_target="tpu_custom_call" | custom-call | flops 251658240 | bytes 2097152 | tf_op jit(solution)/shard_map/columns/pallas_call | solution.py:227
  24.2 0.0 collective-permute-done.3.rest
  24.2 1.4 %outer.1 = (f32[4,8,64,128]{3,2,1,0:T(8,128)}, f32[2,64,128]{2,1,0:T(8,128)S(1)}, f32[8,64,128]{2,1,0:T(8,128)S(1)}) custom-call(f32[4,8,64,128]{3,2,1,0:T(8,128)S(1)} %inner.1.inc, f32[2,4,64,128]{3,2,1,0:T(8,128)S(1)} %columns.1.side, bf16[8,128,384]{2,1,0:T(8,128)(2,1)S(1)} %get-tuple-element.21.held, bf16[832,128]{1,0:T(8,128)(2,1)S(1)} %collective-permute-done.3.rest, ...), custom_call_target="tpu_custom_call" | custom-call | flops 50331648 | bytes 4194304 | tf_op jit(solution)/shard_map/outer/pallas_call | solution.py:271
  25.7 0.0 collective-permute-done.5.from_inside
  25.7 1.4 %collective-permute-done.4.back = bf16[8,64,128]{2,1,0:T(8,128)(2,1)S(1)} collective-permute-done((bf16[8,64,128]{2,1,0:T(8,128)(2,1)S(1)}, bf16[8,64,128]{2,1,0:T(8,128)(2,1)S(1)}, u32[]{:S(2)}, u32[]{:S(2)}) %collective-permute-start.4) | collective-permute-done | bytes 131104 | tf_op jit(solution)/shard_map/ppermute | solution.py:428
  27.1 0.7 %finish.1 = f32[4,8,64,128]{3,2,1,0:T(8,128)} custom-call(f32[4,8,64,128]{3,2,1,0:T(8,128)} %get-tuple-element.22.inc, f32[2,64,128]{2,1,0:T(8,128)S(1)} %get-tuple-element.23.top, f32[8,64,128]{2,1,0:T(8,128)S(1)} %get-tuple-element.24.low, bf16[8,64,128]{2,1,0:T(8,128)(2,1)S(1)} %collective-permute-done.4.back, ...), custom_call_target="tpu_custom_call", output_to_operand_aliasing={{}: (0, {})} | custom-call | flops 65536 | bytes 655360 | tf_op jit(solution)/shard_map/finish/pallas_call | solution.py:304
  (1 shorter events, 0.0 us)
Async XLA Ops:
  0.0 4.9 %copy-start.1 = (bf16[4,8,64,128]{3,2,1,0:T(8,128)(2,1)S(1)}, bf16[4,8,64,128]{3,2,1,0:T(8,128)(2,1)}, u32[]{:S(2)}) copy-start(bf16[4,8,64,128]{3,2,1,0:T(8,128)(2,1)} %w.11) | copy-start | bytes 1572868
  0.0 4.9 %copy-start = (bf16[4,8,256,128]{3,2,1,0:T(8,128)(2,1)S(1)}, bf16[4,8,256,128]{3,2,1,0:T(8,128)(2,1)}, u32[]{:S(2)}) copy-start(bf16[4,8,256,128]{3,2,1,0:T(8,128)(2,1)} %u.11) | copy-start | bytes 6291460
  0.0 4.9 %copy-start.4 = (s32[4,8,9]{2,1,0:T(8,128)S(1)}, s32[4,8,9]{2,1,0:T(8,128)}, u32[]{:S(2)}) copy-start(s32[4,8,9]{2,1,0:T(8,128)} %index.9) | copy-start | bytes 3460
  0.0 4.9 %copy-start.3 = (s32[4,8,9]{2,1,0:T(8,128)S(1)}, s32[4,8,9]{2,1,0:T(8,128)}, u32[]{:S(2)}) copy-start(s32[4,8,9]{2,1,0:T(8,128)} %live.9) | copy-start | bytes 3460
  1.3 6.4 %copy-start.2 = (bf16[16,128,128]{2,1,0:T(8,128)(2,1)S(1)}, bf16[16,128,128]{2,1,0:T(8,128)(2,1)}, u32[]{:S(2)}) copy-start(bf16[16,128,128]{2,1,0:T(8,128)(2,1)} %tapers.7) | copy-start | bytes 1572868
  1.3 17.2 %collective-permute-start.2 = (bf16[2112,128]{1,0:T(8,128)(2,1)S(1)}, bf16[2112,128]{1,0:T(8,128)(2,1)S(1)}, u32[]{:S(2)}, u32[]{:S(2)}) collective-permute-start(bf16[2112,128]{1,0:T(8,128)(2,1)S(1)} %pack_row.1.packed), channel_id=1, source_target_pairs={{0,4},{4,8},{8,12},{12,16},{16,20},{20,24},{24,28},{1,5},{5,9},{9,... | collective-permute-start | bytes 1622024 | tf_op jit(solution)/shard_map/ppermute | solution.py:421
  5.1 7.3 %collective-permute-start = (bf16[4,336,128]{2,1,0:T(8,128)(2,1)S(1)}, bf16[4,336,128]{2,1,0:T(8,128)(2,1)S(1)}, u32[]{:S(2)}, u32[]{:S(2)}) collective-permute-start(bf16[4,336,128]{2,1,0:T(8,128)(2,1)S(1)} %get-tuple-element.16), channel_id=1, source_target_pairs={{0,1},{2,3},{1,0},{3,2},{4,5},{6,7},{5,4},{7,6},{8,9},{10,11},{9,8... | collective-permute-start | bytes 1032200 | tf_op jit(solution)/shard_map/ppermute | solution.py:423
  5.2 8.6 %collective-permute-start.1 = (bf16[4,336,128]{2,1,0:T(8,128)(2,1)S(1)}, bf16[4,336,128]{2,1,0:T(8,128)(2,1)S(1)}, u32[]{:S(2)}, u32[]{:S(2)}) collective-permute-start(bf16[4,336,128]{2,1,0:T(8,128)(2,1)S(1)} %get-tuple-element.17), channel_id=1, source_target_pairs={{1,2},{2,1},{5,6},{6,5},{9,10},{10,9},{13,14},{14,13},{17,18},{18,... | collective-permute-start | bytes 1032200 | tf_op jit(solution)/shard_map/ppermute | solution.py:424
  13.8 10.5 %collective-permute-start.3 = (bf16[832,128]{1,0:T(8,128)(2,1)S(1)}, bf16[832,128]{1,0:T(8,128)(2,1)S(1)}, u32[]{:S(2)}, u32[]{:S(2)}) collective-permute-start(bf16[832,128]{1,0:T(8,128)(2,1)S(1)} %pack_rest.1), channel_id=1, source_target_pairs={{0,4},{4,8},{8,12},{12,16},{16,20},{20,24},{24,28},{1,5},{5,9},{9,... | collective-permute-start | bytes 638984 | tf_op jit(solution)/shard_map/ppermute | solution.py:426
  19.3 7.8 %collective-permute-start.4 = (bf16[8,64,128]{2,1,0:T(8,128)(2,1)S(1)}, bf16[8,64,128]{2,1,0:T(8,128)(2,1)S(1)}, u32[]{:S(2)}, u32[]{:S(2)}) collective-permute-start(bf16[8,64,128]{2,1,0:T(8,128)(2,1)S(1)} %get-tuple-element.25), channel_id=1, source_target_pairs={{4,0},{8,4},{12,8},{16,12},{20,16},{24,20},{28,24},{5,1},{9,5},{13... | collective-permute-start | bytes 393224 | tf_op jit(solution)/shard_map/ppermute | solution.py:428
  22.6 3.0 %collective-permute-start.5 = (f32[64,128]{1,0:T(8,128)S(1)}, f32[64,128]{1,0:T(8,128)S(1)}, u32[]{:S(2)}, u32[]{:S(2)}) collective-permute-start(f32[64,128]{1,0:T(8,128)S(1)} %get-tuple-element.26), channel_id=1, source_target_pairs={{0,1},{2,3},{1,0},{3,2},{4,5},{6,7},{5,4},{7,6},{8,9},{10,11},{9,8... | collective-permute-start | bytes 98312 | tf_op jit(solution)/shard_map/ppermute | solution.py:429

commit v9 on v8

--- a/solution.py
+++ b/solution.py
@@ -7,6 +7,7 @@
 
 MEMBERS = 256
 GRANT = 16 << 20
+WIDE = 52 << 20
 SCALE = 1.0 / (MEMBERS - 1)
 TN = (((0,), (0,)), ((), ()))
 NT = (((1,), (1,)), ((), ()))
@@ -118,7 +119,7 @@
     )(u, w, live, index, tapers)
 
 
-def above_kernel(s, u, w, inside, outside, live, index, tapers, back, held, to_inside):
+def above_kernel(s, u, w, inside, outside, live, index, tapers, back, held, to_inside, tail):
     cols, members, cells = u.shape[1:]
     deep = members + w.shape[2]
     last = cols - 1
@@ -149,6 +150,7 @@
     for c in range(cols):
         back[c] = dot(sources[c], held[c], NT).astype(jnp.bfloat16)
     even = even_column()
+    tail[...] = s[cols * members :]
     to_inside[...] = dot(s[cols * members :], jnp.where(even, held[last, :, 2 * cells :], held[0, :, :cells]), NN)
 
 
@@ -161,9 +163,10 @@
             jax.ShapeDtypeStruct((cols, columns, cells), jnp.bfloat16),
             jax.ShapeDtypeStruct((cols, cells, 3 * cells), jnp.bfloat16),
             jax.ShapeDtypeStruct((columns, cells), jnp.float32),
+            jax.ShapeDtypeStruct((columns, cells), jnp.bfloat16),
         ),
         in_specs=[VMEM] * 8,
-        out_specs=(VMEM,) * 3,
+        out_specs=(VMEM,) * 4,
         compiler_params=pltpu.CompilerParams(vmem_limit_bytes=GRANT),
         cost_estimate=pl.CostEstimate(
             flops=2 * 3 * cols * cells * cells * (members + columns),
@@ -237,22 +240,27 @@
     )(u, w, inside, outside, live, index, tapers)
 
 
-def outer_kernel(inc, side, held, rest, u, live, index, tapers, out, top, low):
+def outer_kernel(inc, side, held, tail, rest, u, live, index, tapers, out, top, low):
     rows, cols, members, cells = u.shape
     width = inc.shape[2]
     last = cols - 1
     even = even_column()
     on, which = live[0], index[0]
-    start = cols * width
+    start = (cols - 1) * width
     gram = dot(rest[start : start + members], jnp.where(even, u[0, 0], u[0, last]), TN)
     at = jnp.where(even, which[0, 0], which[last, 2])
     block = tapered(gram, tapers[at], jnp.where(even, on[0, 0], on[last, 2]))
     far = dot(rest[start + members :], block, NN)
     blank = jnp.zeros_like(far)
+    parts = [rest[c * width : (c + 1) * width] for c in range(cols - 1)]
+    tail = tail[...]
+    weights = [jnp.where(even, parts[0], tail)]
+    weights += [jnp.where(even, parts[c], parts[c - 1]) for c in range(1, last)]
+    weights.append(jnp.where(even, tail, parts[last - 1]))
     for q in range(cols):
         back = [(k, q - (k - 7)) for k in (6, 7, 8) if 0 <= q - (k - 7) < cols]
         blocks = [held[c, :, (k - 6) * cells : (k - 5) * cells] for k, c in back]
-        value = inc[0, q] + dot(cat([rest[c * width : (c + 1) * width] for _, c in back], 1), cat(blocks, 0), NN)
+        value = inc[0, q] + dot(cat([weights[c] for _, c in back], 1), cat(blocks, 0), NN)
         if q in (0, last):
             value += side[q // last, 0]
             value += jnp.where(even, far, blank) if q == 0 else jnp.where(even, blank, far)
@@ -266,7 +274,7 @@
                 low[q] = value
 
 
-def outer(inc, side, held, rest, u, live, index, tapers):
+def outer(inc, side, held, tail, rest, u, live, index, tapers):
     rows, cols, width, cells = inc.shape
     return pl.pallas_call(
         outer_kernel,
@@ -275,12 +283,12 @@
             jax.ShapeDtypeStruct((2, width, cells), inc.dtype),
             jax.ShapeDtypeStruct(inc.shape[1:], inc.dtype),
         ),
-        in_specs=[VMEM] * 8,
+        in_specs=[VMEM] * 9,
         out_specs=(VMEM,) * 3,
         compiler_params=pltpu.CompilerParams(vmem_limit_bytes=GRANT),
         cost_estimate=pl.CostEstimate(flops=6 * cols * cells * cells * width, bytes_accessed=4 << 20, transcendentals=0),
         name="outer",
-    )(inc, side, held, rest, u, live, index, tapers)
+    )(inc, side, held, tail, rest, u, live, index, tapers)
 
 
 def finish_kernel(inc, top, low, back, from_inside, out, end, total, sem):
@@ -331,7 +339,7 @@
     return [(i + 1, i) for i in range(lax.axis_size(axis) - 1)]
 
 
-def pack_row_kernel(u, w, out, sem):
+def pack_row_kernel(u, w, out, done, sem):
     rows, cols, members, _ = u.shape
     beside = (cols - 1) * even_column().astype(jnp.int32)
     copies = [
@@ -343,6 +351,7 @@
         copy.start()
     for copy in copies:
         copy.wait()
+    done[...] = jnp.zeros_like(done)
 
 
 def pack_row(u, w):
@@ -350,9 +359,9 @@
     shape = (cols * members + w.shape[2], cells)
     return pl.pallas_call(
         pack_row_kernel,
-        out_shape=pltpu.VMEM(shape, u.dtype),
+        out_shape=(pltpu.VMEM(shape, u.dtype), jax.ShapeDtypeStruct((8, cells), jnp.float32)),
         in_specs=[HBM, HBM],
-        out_specs=VMEM,
+        out_specs=(VMEM, VMEM),
         scratch_shapes=[pltpu.SemaphoreType.DMA((cols + 1,))],
         cost_estimate=pl.CostEstimate(flops=0, bytes_accessed=4 * shape[0] * cells, transcendentals=0),
         name="pack_row",
@@ -361,17 +370,18 @@
 
 def pack_rest_kernel(w, outside, out):
     rows, cols, width, _ = w.shape
-    for q in range(cols):
-        out[q * width : (q + 1) * width] = w[rows - 1, q]
-    deep = out.shape[0] - cols * width
-    out[cols * width :] = outside[rows - 1, :deep]
+    skip = 1 - even_column().astype(jnp.int32)
+    for q in range(cols - 1):
+        out[q * width : (q + 1) * width] = w[rows - 1, q + skip]
+    start = (cols - 1) * width
+    out[start:] = outside[rows - 1, : out.shape[0] - start]
 
 
 def pack_rest(w, outside, members):
     _, cols, width, cells = w.shape
     return pl.pallas_call(
         pack_rest_kernel,
-        out_shape=jax.ShapeDtypeStruct((cols * width + members + width, cells), w.dtype),
+        out_shape=jax.ShapeDtypeStruct(((cols - 1) * width + members + width, cells), w.dtype),
         in_specs=[VMEM, VMEM],
         out_specs=VMEM,
         compiler_params=pltpu.CompilerParams(vmem_limit_bytes=GRANT),
@@ -380,15 +390,13 @@
     )(w, outside)
 
 
-def pack_columns_kernel(u, w, live, index, packed, inner_side, outer_side, sem):
-    del packed
+def load_kernel(u, w, live, index, done, u_here, w_here, inner_side, outer_side, sem):
+    del done
     rows, cols, members, cells = u.shape
     deep = members + w.shape[2]
     turn = (cols - 1) * even_column().astype(jnp.int32)
-    copies = []
-    for n, (out, b) in enumerate(((inner_side, turn), (outer_side, cols - 1 - turn))):
-        copies.append(pltpu.make_async_copy(u.at[:, b], out.at[:, :members], sem.at[n, 0]))
-        copies.append(pltpu.make_async_copy(w.at[:, b], out.at[:, members:deep], sem.at[n, 1]))
+    copies = [pltpu.make_async_copy(w, w_here, sem.at[rows])]
+    copies += [pltpu.make_async_copy(u.at[a], u_here.at[a], sem.at[a]) for a in range(rows)]
     for copy in copies:
         copy.start()
     for a in range(rows):
@@ -397,38 +405,42 @@
         note = jnp.concatenate([lines, blank], 1).astype(jnp.bfloat16)
         inner_side[a, deep:] = note
         outer_side[a, deep:] = note
-    for copy in copies:
-        copy.wait()
-
-
-def pack_columns(u, w, live, index, packed):
+    copies[0].wait()
+    for a in range(rows):
+        copies[1 + a].wait()
+        for side, b in ((inner_side, turn), (outer_side, cols - 1 - turn)):
+            side[a, :members] = u_here[a, b]
+            side[a, members:deep] = w_here[a, b]
+
+
+def load(u, w, live, index, done):
     rows, cols, members, cells = u.shape
-    shape = (rows, members + w.shape[2] + 2 * cols, cells)
-    return pl.pallas_call(
-        pack_columns_kernel,
-        out_shape=(jax.ShapeDtypeStruct(shape, u.dtype),) * 2,
-        in_specs=[ANY, ANY, VMEM, VMEM, VMEM],
-        out_specs=(VMEM, VMEM),
-        scratch_shapes=[pltpu.SemaphoreType.DMA((2, 2))],
-        compiler_params=pltpu.CompilerParams(vmem_limit_bytes=GRANT),
-        cost_estimate=pl.CostEstimate(flops=0, bytes_accessed=8 * rows * shape[1] * cells, transcendentals=0),
-        name="pack_columns",
-    )(u, w, live, index, packed)
-
-
-def body(u, w, live, index, tapers):
-    packed = pack_row(u, w)
+    side = pltpu.VMEM((rows, members + w.shape[2] + 2 * cols, cells), u.dtype)
+    return pl.pallas_call(
+        load_kernel,
+        out_shape=(pltpu.VMEM(u.shape, u.dtype), pltpu.VMEM(w.shape, w.dtype), side, side),
+        in_specs=[HBM, HBM, VMEM, VMEM, VMEM],
+        out_specs=(VMEM,) * 4,
+        scratch_shapes=[pltpu.SemaphoreType.DMA((rows + 1,))],
+        compiler_params=pltpu.CompilerParams(vmem_limit_bytes=WIDE),
+        cost_estimate=pl.CostEstimate(flops=0, bytes_accessed=4 * u.size + 4 * w.size, transcendentals=0),
+        name="load",
+    )(u, w, live, index, done)
+
+
+def body(perturbations, weights, live, index, tapers):
+    packed, done = pack_row(perturbations, weights)
     s = lax.ppermute(packed, "row", forward("row"))
-    inner_side, outer_side = pack_columns(u, w, live, index, packed)
+    u, w, inner_side, outer_side = load(perturbations, weights, live, index, done)
     inside = lax.ppermute(inner_side, "col", swaps("col", 0))
     outside = lax.ppermute(outer_side, "col", swaps("col", 1))
     inc, inside, outside = lax.optimization_barrier((inner(u, w, live, index, tapers), inside, outside))
     rest = lax.ppermute(pack_rest(w, outside, u.shape[2]), "row", forward("row"))
-    back, held, to_inside = above(s, u, w, inside, outside, live, index, tapers)
+    back, held, to_inside, tail = above(s, u, w, inside, outside, live, index, tapers)
     back = lax.ppermute(back, "row", backward("row"))
     from_inside = lax.ppermute(to_inside, "col", swaps("col", 0))
     side = columns(u, w, inside, outside, live, index, tapers)
-    inc, top, low = outer(inc, side, held, rest, u, live, index, tapers)
+    inc, top, low = outer(inc, side, held, tail, rest, u, live, index, tapers)
     return finish(inc, top, low, back, from_inside)
 
 

time: 28.2 us -> 29.5 us (1.046)
  Pallas kernels: 10.5 us -> 13.4 us
  starting transfers between devices: 13 us -> 11.9 us
  waiting for transfers between devices: 4.12 us -> 3.68 us
    pallas_call x3, Pallas kernels: 1.45 us -> 4.28 us  [the longest x1 2.47 us: load(): pl.pallas_call(load_kernel, out_shape=(pltpu.VMEM(u.shape, u.dtype), pltp...]
    ppermute x1, waiting for transfers between devices: 1.32 us -> 0.01 us  [body(): s = lax.ppermute(packed, 'row', forward('row'))]
    ppermute x1, starting transfers between devices: 3.31 us -> 2.42 us  [body(): back = lax.ppermute(back, 'row', backward('row'))]
    ppermute x1, waiting for transfers between devices: 0.01 us -> 0.71 us  [body(): lax.ppermute(pack_rest(w, outside, u.shape[2]), 'row', forward('row'))]
  transfers between devices with their start and end apart: 6 -> 6, of which waited for: 3 -> 3; matrix products, arithmetic and copies ran while one was open for 0% -> 0% of each run, Pallas kernels for 31% -> 37%
where the time goes in v9:
time: 29.5 us; the launch traced here: 29.2 us
  Pallas kernels  13.4 us (45%)
  starting transfers between devices  11.9 us (40%)
  waiting for transfers between devices  3.68 us (12%)
    pallas_call x1, Pallas kernels, inner(): pl.pallas_call(inner_kernel, out_shape=jax.ShapeDtypeStruct((rows, cols,...  4.64 us
    ppermute x1, starting transfers between devices, body(): s = lax.ppermute(packed, 'row', forward('row'))  3.43 us
    ppermute x1, starting transfers between devices, body(): lax.ppermute(pack_rest(w, outside, u.shape[2]), 'row', forward('row'))  3.43 us
    ppermute x1, starting transfers between devices, body(): outside = lax.ppermute(outer_side, 'col', swaps('col', 1))  2.53 us
    pallas_call x1, Pallas kernels, load(): pl.pallas_call(load_kernel, out_shape=(pltpu.VMEM(u.shape, u.dtype), pltp...  2.47 us
    ppermute x1, starting transfers between devices, body(): back = lax.ppermute(back, 'row', backward('row'))  2.42 us
    pallas_call x1, Pallas kernels, pack_row(): pl.pallas_call(pack_row_kernel, out_shape=(pltpu.VMEM(shape, u.dtype), ja...  1.8 us
    ppermute x1, waiting for transfers between devices, body(): back = lax.ppermute(back, 'row', backward('row'))  1.62 us
  transfers between devices with their start and end apart: 6, of which 3 were waited for; matrix products, arithmetic and copies ran while one was open for 0% of the time, Pallas kernels for 37%

profile of v9, /device:TPU:22, one launch (start us, length us, event | category | flops | bytes accessed | tf_op | source)
XLA Modules:
  0.0 29.2 jit_solution(17253038606725435966)
XLA Ops:
  0.0 0.0 copy-start.1
  0.0 0.0 copy-start.2
  0.0 0.0 copy-start
  0.0 1.8 %pack_row.1 = (bf16[2112,128]{1,0:T(8,128)(2,1)S(1)}, f32[8,128]{1,0:T(8,128)}) custom-call(bf16[4,8,256,128]{3,2,1,0:T(8,128)(2,1)} %u.3, bf16[4,8,64,128]{3,2,1,0:T(8,128)(2,1)} %w.3), custom_call_target="tpu_custom_call" | custom-call | bytes 1081344 | tf_op jit(solution)/shard_map/pack_row/pallas_call | solution.py:360
  1.8 3.4 %collective-permute-start.2 = (bf16[2112,128]{1,0:T(8,128)(2,1)S(1)}, bf16[2112,128]{1,0:T(8,128)(2,1)S(1)}, u32[]{:S(2)}, u32[]{:S(2)}) collective-permute-start(bf16[2112,128]{1,0:T(8,128)(2,1)S(1)} %get-tuple-element.29), channel_id=1, source_target_pairs={{0,4},{4,8},{8,12},{12,16},{16,20},{20,24},{24,28},{1,5},{5,9},{9,... | collective-permute-start | bytes 1622024 | tf_op jit(solution)/shard_map/ppermute | solution.py:433
  5.2 2.5 %load.1 = (bf16[4,8,256,128]{3,2,1,0:T(8,128)(2,1)S(1)}, bf16[4,8,64,128]{3,2,1,0:T(8,128)(2,1)S(1)}, bf16[4,336,128]{2,1,0:T(8,128)(2,1)S(1)}, bf16[4,336,128]{2,1,0:T(8,128)(2,1)S(1)}) custom-call(bf16[4,8,256,128]{3,2,1,0:T(8,128)(2,1)} %u.3, bf16[4,8,64,128]{3,2,1,0:T(8,128)(2,1)} %w.3, s32[4,8,9]{2,1,0:T(8,128)} %live.9, s32[4,8,9]{2,1,0:T(8,128)} %index.9, ...), custom_call_target="tpu_custom_call" | custom-call | bytes 5242880 | tf_op jit(solution)/shard_map/load/pallas_call | solution.py:419
  7.7 0.1 collective-permute-start
  7.8 2.5 %collective-permute-start.1 = (bf16[4,336,128]{2,1,0:T(8,128)(2,1)S(1)}, bf16[4,336,128]{2,1,0:T(8,128)(2,1)S(1)}, u32[]{:S(2)}, u32[]{:S(2)}) collective-permute-start(bf16[4,336,128]{2,1,0:T(8,128)(2,1)S(1)} %get-tuple-element.25), channel_id=1, source_target_pairs={{1,2},{2,1},{5,6},{6,5},{9,10},{10,9},{13,14},{14,13},{17,18},{18,... | collective-permute-start | bytes 1032200 | tf_op jit(solution)/shard_map/ppermute | solution.py:436
  10.3 0.0 copy-done.1
  10.4 0.0 copy-done.2
  10.4 0.0 copy-done
  10.4 4.6 %inner.1.inc = f32[4,8,64,128]{3,2,1,0:T(8,128)S(1)} custom-call(bf16[4,8,256,128]{3,2,1,0:T(8,128)(2,1)S(1)} %get-tuple-element.22.u, bf16[4,8,64,128]{3,2,1,0:T(8,128)(2,1)S(1)} %get-tuple-element.23.w, s32[4,8,9]{2,1,0:T(8,128)S(1)} %copy-done.1, s32[4,8,9]{2,1,0:T(8,128)S(1)} %copy-done.2, bf16[16,128,128]{2,1,0:T(8,128)(2,1)S(1)} %copy-done), custom_call_target="tpu_custom_call" | custom-call | flops 2013265920 | bytes 4194304 | tf_op jit(solution)/shard_map/inner/pallas_call | solution.py:103
  15.0 0.0 collective-permute-done.inside
  15.0 1.3 %collective-permute-done.1.outside = bf16[4,336,128]{2,1,0:T(8,128)(2,1)S(1)} collective-permute-done((bf16[4,336,128]{2,1,0:T(8,128)(2,1)S(1)}, bf16[4,336,128]{2,1,0:T(8,128)(2,1)S(1)}, u32[]{:S(2)}, u32[]{:S(2)}) %collective-permute-start.1) | collective-permute-done | bytes 344096 | tf_op jit(solution)/shard_map/ppermute | solution.py:436
  16.4 3.4 %collective-permute-start.3 = (bf16[768,128]{1,0:T(8,128)(2,1)S(1)}, bf16[768,128]{1,0:T(8,128)(2,1)S(1)}, u32[]{:S(2)}, u32[]{:S(2)}) collective-permute-start(bf16[768,128]{1,0:T(8,128)(2,1)S(1)} %pack_rest.1), channel_id=1, source_target_pairs={{0,4},{4,8},{8,12},{12,16},{16,20},{20,24},{24,28},{1,5},{5,9},{9,... | collective-permute-start | bytes 589832 | tf_op jit(solution)/shard_map/ppermute | solution.py:438
  19.8 0.0 collective-permute-done.2.s
  19.8 0.8 %above.1 = (bf16[8,64,128]{2,1,0:T(8,128)(2,1)S(1)}, bf16[8,128,384]{2,1,0:T(8,128)(2,1)S(1)}, f32[64,128]{1,0:T(8,128)S(1)}, bf16[64,128]{1,0:T(8,128)(2,1)S(1)}) custom-call(bf16[2112,128]{1,0:T(8,128)(2,1)S(1)} %collective-permute-done.2.s, bf16[4,8,256,128]{3,2,1,0:T(8,128)(2,1)S(1)} %get-tuple-element.22.u, ...), custom_call_target="tpu_custom_call" | custom-call | flops 251658240 | bytes 2097152 | tf_op jit(solution)/shard_map/above/pallas_call | solution.py:160
  20.7 2.4 %collective-permute-start.4 = (bf16[8,64,128]{2,1,0:T(8,128)(2,1)S(1)}, bf16[8,64,128]{2,1,0:T(8,128)(2,1)S(1)}, u32[]{:S(2)}, u32[]{:S(2)}) collective-permute-start(bf16[8,64,128]{2,1,0:T(8,128)(2,1)S(1)} %get-tuple-element.35), channel_id=1, source_target_pairs={{4,0},{8,4},{12,8},{16,12},{20,16},{24,20},{28,24},{5,1},{9,5},{13... | collective-permute-start | bytes 393224 | tf_op jit(solution)/shard_map/ppermute | solution.py:440
  23.1 0.1 collective-permute-start.5
  23.2 1.5 %columns.1.side = f32[2,4,64,128]{3,2,1,0:T(8,128)S(1)} custom-call(bf16[4,8,256,128]{3,2,1,0:T(8,128)(2,1)S(1)} %get-tuple-element.22.u, bf16[4,8,64,128]{3,2,1,0:T(8,128)(2,1)S(1)} %get-tuple-element.23.w, bf16[4,336,128]{2,1,0:T(8,128)(2,1)S(1)} %collective-permute-done.inside, bf16[4,336,128]{2,1,0:T(8,128)(2,1)S(1)} %collective-permute-done.1.outside, ...), custom_call_target="tpu_custom_call" | custom-call | flops 251658240 | bytes 2097152 | tf_op jit(solution)/shard_map/columns/pallas_call | solution.py:230
  24.6 0.7 %collective-permute-done.3.rest = bf16[768,128]{1,0:T(8,128)(2,1)S(1)} collective-permute-done((bf16[768,128]{1,0:T(8,128)(2,1)S(1)}, bf16[768,128]{1,0:T(8,128)(2,1)S(1)}, u32[]{:S(2)}, u32[]{:S(2)}) %collective-permute-start.3) | collective-permute-done | bytes 196640 | tf_op jit(solution)/shard_map/ppermute | solution.py:438
  25.4 1.4 %outer.1 = (f32[4,8,64,128]{3,2,1,0:T(8,128)}, f32[2,64,128]{2,1,0:T(8,128)S(1)}, f32[8,64,128]{2,1,0:T(8,128)S(1)}) custom-call(f32[4,8,64,128]{3,2,1,0:T(8,128)S(1)} %inner.1.inc, f32[2,4,64,128]{3,2,1,0:T(8,128)S(1)} %columns.1.side, bf16[8,128,384]{2,1,0:T(8,128)(2,1)S(1)} %get-tuple-element.30.held, bf16[64,128]{1,0:T(8,128)(2,1)S(1)} %get-tuple-element.31.tail, ...), custom_call_target="tpu_custom_call" | custom-call | flops 50331648 | bytes 4194304 | tf_op jit(solution)/shard_map/outer/pallas_call | solution.py:279
  26.8 0.0 collective-permute-done.5.from_inside
  26.8 1.6 %collective-permute-done.4.back = bf16[8,64,128]{2,1,0:T(8,128)(2,1)S(1)} collective-permute-done((bf16[8,64,128]{2,1,0:T(8,128)(2,1)S(1)}, bf16[8,64,128]{2,1,0:T(8,128)(2,1)S(1)}, u32[]{:S(2)}, u32[]{:S(2)}) %collective-permute-start.4) | collective-permute-done | bytes 131104 | tf_op jit(solution)/shard_map/ppermute | solution.py:440
  28.4 0.7 %finish.1 = f32[4,8,64,128]{3,2,1,0:T(8,128)} custom-call(f32[4,8,64,128]{3,2,1,0:T(8,128)} %get-tuple-element.32.inc, f32[2,64,128]{2,1,0:T(8,128)S(1)} %get-tuple-element.33.top, f32[8,64,128]{2,1,0:T(8,128)S(1)} %get-tuple-element.34.low, bf16[8,64,128]{2,1,0:T(8,128)(2,1)S(1)} %collective-permute-done.4.back, ...), custom_call_target="tpu_custom_call", output_to_operand_aliasing={{}: (0, {})} | custom-call | flops 65536 | bytes 655360 | tf_op jit(solution)/shard_map/finish/pallas_call | solution.py:312
  (1 shorter events, 0.0 us)
Async XLA Ops:
  0.0 10.3 %copy-start.1 = (s32[4,8,9]{2,1,0:T(8,128)S(1)}, s32[4,8,9]{2,1,0:T(8,128)}, u32[]{:S(2)}) copy-start(s32[4,8,9]{2,1,0:T(8,128)} %live.9) | copy-start | bytes 3460
  0.0 10.4 %copy-start.2 = (s32[4,8,9]{2,1,0:T(8,128)S(1)}, s32[4,8,9]{2,1,0:T(8,128)}, u32[]{:S(2)}) copy-start(s32[4,8,9]{2,1,0:T(8,128)} %index.9) | copy-start | bytes 3460
  0.0 10.4 %copy-start = (bf16[16,128,128]{2,1,0:T(8,128)(2,1)S(1)}, bf16[16,128,128]{2,1,0:T(8,128)(2,1)}, u32[]{:S(2)}) copy-start(bf16[16,128,128]{2,1,0:T(8,128)(2,1)} %tapers.7) | copy-start | bytes 1572868
  1.8 18.0 %collective-permute-start.2 = (bf16[2112,128]{1,0:T(8,128)(2,1)S(1)}, bf16[2112,128]{1,0:T(8,128)(2,1)S(1)}, u32[]{:S(2)}, u32[]{:S(2)}) collective-permute-start(bf16[2112,128]{1,0:T(8,128)(2,1)S(1)} %get-tuple-element.29), channel_id=1, source_target_pairs={{0,4},{4,8},{8,12},{12,16},{16,20},{20,24},{24,28},{1,5},{5,9},{9,... | collective-permute-start | bytes 1622024 | tf_op jit(solution)/shard_map/ppermute | solution.py:433
  7.7 7.3 %collective-permute-start = (bf16[4,336,128]{2,1,0:T(8,128)(2,1)S(1)}, bf16[4,336,128]{2,1,0:T(8,128)(2,1)S(1)}, u32[]{:S(2)}, u32[]{:S(2)}) collective-permute-start(bf16[4,336,128]{2,1,0:T(8,128)(2,1)S(1)} %get-tuple-element.24), channel_id=1, source_target_pairs={{0,1},{2,3},{1,0},{3,2},{4,5},{6,7},{5,4},{7,6},{8,9},{10,11},{9,8... | collective-permute-start | bytes 1032200 | tf_op jit(solution)/shard_map/ppermute | solution.py:435
  7.8 8.6 %collective-permute-start.1 = (bf16[4,336,128]{2,1,0:T(8,128)(2,1)S(1)}, bf16[4,336,128]{2,1,0:T(8,128)(2,1)S(1)}, u32[]{:S(2)}, u32[]{:S(2)}) collective-permute-start(bf16[4,336,128]{2,1,0:T(8,128)(2,1)S(1)} %get-tuple-element.25), channel_id=1, source_target_pairs={{1,2},{2,1},{5,6},{6,5},{9,10},{10,9},{13,14},{14,13},{17,18},{18,... | collective-permute-start | bytes 1032200 | tf_op jit(solution)/shard_map/ppermute | solution.py:436
  16.4 9.0 %collective-permute-start.3 = (bf16[768,128]{1,0:T(8,128)(2,1)S(1)}, bf16[768,128]{1,0:T(8,128)(2,1)S(1)}, u32[]{:S(2)}, u32[]{:S(2)}) collective-permute-start(bf16[768,128]{1,0:T(8,128)(2,1)S(1)} %pack_rest.1), channel_id=1, source_target_pairs={{0,4},{4,8},{8,12},{12,16},{16,20},{20,24},{24,28},{1,5},{5,9},{9,... | collective-permute-start | bytes 589832 | tf_op jit(solution)/shard_map/ppermute | solution.py:438
  20.7 7.8 %collective-permute-start.4 = (bf16[8,64,128]{2,1,0:T(8,128)(2,1)S(1)}, bf16[8,64,128]{2,1,0:T(8,128)(2,1)S(1)}, u32[]{:S(2)}, u32[]{:S(2)}) collective-permute-start(bf16[8,64,128]{2,1,0:T(8,128)(2,1)S(1)} %get-tuple-element.35), channel_id=1, source_target_pairs={{4,0},{8,4},{12,8},{16,12},{20,16},{24,20},{28,24},{5,1},{9,5},{13... | collective-permute-start | bytes 393224 | tf_op jit(solution)/shard_map/ppermute | solution.py:440
  23.1 3.7 %collective-permute-start.5 = (f32[64,128]{1,0:T(8,128)S(1)}, f32[64,128]{1,0:T(8,128)S(1)}, u32[]{:S(2)}, u32[]{:S(2)}) collective-permute-start(f32[64,128]{1,0:T(8,128)S(1)} %get-tuple-element.36), channel_id=1, source_target_pairs={{0,1},{2,3},{1,0},{3,2},{4,5},{6,7},{5,4},{7,6},{8,9},{10,11},{9,8... | collective-permute-start | bytes 98312 | tf_op jit(solution)/shard_map/ppermute | solution.py:441

commit v10 on v8

--- a/solution.py
+++ b/solution.py
@@ -118,7 +118,7 @@
     )(u, w, live, index, tapers)
 
 
-def above_kernel(s, u, w, inside, outside, live, index, tapers, back, held, to_inside):
+def above_kernel(s, u, w, inside, outside, live, index, tapers, back, held, to_inside, tail):
     cols, members, cells = u.shape[1:]
     deep = members + w.shape[2]
     last = cols - 1
@@ -149,6 +149,7 @@
     for c in range(cols):
         back[c] = dot(sources[c], held[c], NT).astype(jnp.bfloat16)
     even = even_column()
+    tail[...] = s[cols * members :]
     to_inside[...] = dot(s[cols * members :], jnp.where(even, held[last, :, 2 * cells :], held[0, :, :cells]), NN)
 
 
@@ -161,9 +162,10 @@
             jax.ShapeDtypeStruct((cols, columns, cells), jnp.bfloat16),
             jax.ShapeDtypeStruct((cols, cells, 3 * cells), jnp.bfloat16),
             jax.ShapeDtypeStruct((columns, cells), jnp.float32),
+            jax.ShapeDtypeStruct((columns, cells), jnp.bfloat16),
         ),
         in_specs=[VMEM] * 8,
-        out_specs=(VMEM,) * 3,
+        out_specs=(VMEM,) * 4,
         compiler_params=pltpu.CompilerParams(vmem_limit_bytes=GRANT),
         cost_estimate=pl.CostEstimate(
             flops=2 * 3 * cols * cells * cells * (members + columns),
@@ -237,22 +239,27 @@
     )(u, w, inside, outside, live, index, tapers)
 
 
-def outer_kernel(inc, side, held, rest, u, live, index, tapers, out, top, low):
+def outer_kernel(inc, side, held, tail, rest, u, live, index, tapers, out, top, low):
     rows, cols, members, cells = u.shape
     width = inc.shape[2]
     last = cols - 1
     even = even_column()
     on, which = live[0], index[0]
-    start = cols * width
+    start = (cols - 1) * width
     gram = dot(rest[start : start + members], jnp.where(even, u[0, 0], u[0, last]), TN)
     at = jnp.where(even, which[0, 0], which[last, 2])
     block = tapered(gram, tapers[at], jnp.where(even, on[0, 0], on[last, 2]))
     far = dot(rest[start + members :], block, NN)
     blank = jnp.zeros_like(far)
+    parts = [rest[c * width : (c + 1) * width] for c in range(cols - 1)]
+    tail = tail[...]
+    weights = [jnp.where(even, parts[0], tail)]
+    weights += [jnp.where(even, parts[c], parts[c - 1]) for c in range(1, last)]
+    weights.append(jnp.where(even, tail, parts[last - 1]))
     for q in range(cols):
         back = [(k, q - (k - 7)) for k in (6, 7, 8) if 0 <= q - (k - 7) < cols]
         blocks = [held[c, :, (k - 6) * cells : (k - 5) * cells] for k, c in back]
-        value = inc[0, q] + dot(cat([rest[c * width : (c + 1) * width] for _, c in back], 1), cat(blocks, 0), NN)
+        value = inc[0, q] + dot(cat([weights[c] for _, c in back], 1), cat(blocks, 0), NN)
         if q in (0, last):
             value += side[q // last, 0]
             value += jnp.where(even, far, blank) if q == 0 else jnp.where(even, blank, far)
@@ -266,7 +273,7 @@
                 low[q] = value
 
 
-def outer(inc, side, held, rest, u, live, index, tapers):
+def outer(inc, side, held, tail, rest, u, live, index, tapers):
     rows, cols, width, cells = inc.shape
     return pl.pallas_call(
         outer_kernel,
@@ -275,12 +282,12 @@
             jax.ShapeDtypeStruct((2, width, cells), inc.dtype),
             jax.ShapeDtypeStruct(inc.shape[1:], inc.dtype),
         ),
-        in_specs=[VMEM] * 8,
+        in_specs=[VMEM] * 9,
         out_specs=(VMEM,) * 3,
         compiler_params=pltpu.CompilerParams(vmem_limit_bytes=GRANT),
         cost_estimate=pl.CostEstimate(flops=6 * cols * cells * cells * width, bytes_accessed=4 << 20, transcendentals=0),
         name="outer",
-    )(inc, side, held, rest, u, live, index, tapers)
+    )(inc, side, held, tail, rest, u, live, index, tapers)
 
 
 def finish_kernel(inc, top, low, back, from_inside, out, end, total, sem):
@@ -332,13 +339,13 @@
 
 
 def pack_row_kernel(u, w, out, sem):
-    rows, cols, members, _ = u.shape
+    rows, cols, members, cells = u.shape
     beside = (cols - 1) * even_column().astype(jnp.int32)
+    deep = cols * members
     copies = [
-        pltpu.make_async_copy(u.at[rows - 1, q], out.at[q * members : (q + 1) * members], sem.at[q])
-        for q in range(cols)
+        pltpu.make_async_copy(u.at[rows - 1].reshape(deep, cells), out.at[:deep], sem.at[0]),
+        pltpu.make_async_copy(w.at[rows - 1, beside], out.at[deep:], sem.at[1]),
     ]
-    copies.append(pltpu.make_async_copy(w.at[rows - 1, beside], out.at[cols * members :], sem.at[cols]))
     for copy in copies:
         copy.start()
     for copy in copies:
@@ -353,7 +360,7 @@
         out_shape=pltpu.VMEM(shape, u.dtype),
         in_specs=[HBM, HBM],
         out_specs=VMEM,
-        scratch_shapes=[pltpu.SemaphoreType.DMA((cols + 1,))],
+        scratch_shapes=[pltpu.SemaphoreType.DMA((2,))],
         cost_estimate=pl.CostEstimate(flops=0, bytes_accessed=4 * shape[0] * cells, transcendentals=0),
         name="pack_row",
     )(u, w)
@@ -361,17 +368,18 @@
 
 def pack_rest_kernel(w, outside, out):
     rows, cols, width, _ = w.shape
-    for q in range(cols):
-        out[q * width : (q + 1) * width] = w[rows - 1, q]
-    deep = out.shape[0] - cols * width
-    out[cols * width :] = outside[rows - 1, :deep]
+    skip = 1 - even_column().astype(jnp.int32)
+    for q in range(cols - 1):
+        out[q * width : (q + 1) * width] = w[rows - 1, q + skip]
+    start = (cols - 1) * width
+    out[start:] = outside[rows - 1, : out.shape[0] - start]
 
 
 def pack_rest(w, outside, members):
     _, cols, width, cells = w.shape
     return pl.pallas_call(
         pack_rest_kernel,
-        out_shape=jax.ShapeDtypeStruct((cols * width + members + width, cells), w.dtype),
+        out_shape=jax.ShapeDtypeStruct(((cols - 1) * width + members + width, cells), w.dtype),
         in_specs=[VMEM, VMEM],
         out_specs=VMEM,
         compiler_params=pltpu.CompilerParams(vmem_limit_bytes=GRANT),
@@ -420,15 +428,15 @@
     packed = pack_row(u, w)
     s = lax.ppermute(packed, "row", forward("row"))
     inner_side, outer_side = pack_columns(u, w, live, index, packed)
+    outside = lax.ppermute(outer_side, "col", swaps("col", 1))
     inside = lax.ppermute(inner_side, "col", swaps("col", 0))
-    outside = lax.ppermute(outer_side, "col", swaps("col", 1))
-    inc, inside, outside = lax.optimization_barrier((inner(u, w, live, index, tapers), inside, outside))
+    inc, outside, inside = lax.optimization_barrier((inner(u, w, live, index, tapers), outside, inside))
     rest = lax.ppermute(pack_rest(w, outside, u.shape[2]), "row", forward("row"))
-    back, held, to_inside = above(s, u, w, inside, outside, live, index, tapers)
+    back, held, to_inside, tail = above(s, u, w, inside, outside, live, index, tapers)
     back = lax.ppermute(back, "row", backward("row"))
     from_inside = lax.ppermute(to_inside, "col", swaps("col", 0))
     side = columns(u, w, inside, outside, live, index, tapers)
-    inc, top, low = outer(inc, side, held, rest, u, live, index, tapers)
+    inc, top, low = outer(inc, side, held, tail, rest, u, live, index, tapers)
     return finish(inc, top, low, back, from_inside)
 
 

time: 28.2 us -> 27.4 us (0.972)
  starting transfers between devices: 13 us -> 12.4 us
    ppermute x1, starting transfers between devices: 2.53 us -> 1.92 us  [body(): outside = lax.ppermute(outer_side, 'col', swaps('col', 1))]
    ppermute x1, waiting for transfers between devices: 1.32 us -> 0.77 us  [body(): s = lax.ppermute(packed, 'row', forward('row'))]
    ppermute x1, waiting for transfers between devices: 1.36 us -> 1.9 us  [body(): outside = lax.ppermute(outer_side, 'col', swaps('col', 1))]
where the time goes in v10:
time: 27.4 us; the launch traced here: 27.1 us
  starting transfers between devices  12.4 us (45%)
  Pallas kernels  10.5 us (38%)
  waiting for transfers between devices  4.1 us (15%)
    pallas_call x1, Pallas kernels, inner(): pl.pallas_call(inner_kernel, out_shape=jax.ShapeDtypeStruct((rows, cols,...  4.64 us
    ppermute x1, starting transfers between devices, body(): s = lax.ppermute(packed, 'row', forward('row'))  3.56 us
    ppermute x1, starting transfers between devices, body(): lax.ppermute(pack_rest(w, outside, u.shape[2]), 'row', forward('row'))  3.43 us
    ppermute x1, starting transfers between devices, body(): back = lax.ppermute(back, 'row', backward('row'))  3.32 us
    ppermute x1, starting transfers between devices, body(): outside = lax.ppermute(outer_side, 'col', swaps('col', 1))  1.92 us
    ppermute x1, waiting for transfers between devices, body(): outside = lax.ppermute(outer_side, 'col', swaps('col', 1))  1.9 us
    pallas_call x1, Pallas kernels, columns(): pl.pallas_call(columns_kernel, out_shape=jax.ShapeDtypeStruct((2, rows, w...  1.49 us
    pallas_call x1, Pallas kernels, outer(): pl.pallas_call(outer_kernel, out_shape=(jax.ShapeDtypeStruct(inc.shape, i...  1.43 us
  transfers between devices with their start and end apart: 6, of which 3 were waited for; matrix products, arithmetic and copies ran while one was open for 0% of the time, Pallas kernels for 31%

profile of v10, /device:TPU:22, one launch (start us, length us, event | category | flops | bytes accessed | tf_op | source)
XLA Modules:
  0.0 27.1 jit_solution(2202166776434345442)
XLA Ops:
  0.0 0.0 copy-start.1
  0.0 0.0 copy-start
  0.0 0.0 copy-start.4
  0.0 0.0 copy-start.3
  0.0 1.2 %pack_row.1.packed = bf16[2112,128]{1,0:T(8,128)(2,1)S(1)} custom-call(bf16[4,8,256,128]{3,2,1,0:T(8,128)(2,1)} %u.11, bf16[4,8,64,128]{3,2,1,0:T(8,128)(2,1)} %w.11), custom_call_target="tpu_custom_call" | custom-call | bytes 1081344 | tf_op jit(solution)/shard_map/pack_row/pallas_call | solution.py:358
  1.2 0.0 copy-start.2
  1.3 3.6 %collective-permute-start.2 = (bf16[2112,128]{1,0:T(8,128)(2,1)S(1)}, bf16[2112,128]{1,0:T(8,128)(2,1)S(1)}, u32[]{:S(2)}, u32[]{:S(2)}) collective-permute-start(bf16[2112,128]{1,0:T(8,128)(2,1)S(1)} %pack_row.1.packed), channel_id=1, source_target_pairs={{0,4},{4,8},{8,12},{12,16},{16,20},{20,24},{24,28},{1,5},{5,9},{9,... | collective-permute-start | bytes 1622024 | tf_op jit(solution)/shard_map/ppermute | solution.py:429
  4.8 0.0 copy-done.1
  4.8 0.0 copy-done
  4.8 0.0 copy-done.4
  4.8 0.0 copy-done.3
  4.9 0.1 pack_columns.1
  5.0 1.9 %collective-permute-start = (bf16[4,336,128]{2,1,0:T(8,128)(2,1)S(1)}, bf16[4,336,128]{2,1,0:T(8,128)(2,1)S(1)}, u32[]{:S(2)}, u32[]{:S(2)}) collective-permute-start(bf16[4,336,128]{2,1,0:T(8,128)(2,1)S(1)} %get-tuple-element.17), channel_id=1, source_target_pairs={{1,2},{2,1},{5,6},{6,5},{9,10},{10,9},{13,14},{14,13},{17,18},{18,... | collective-permute-start | bytes 1032200 | tf_op jit(solution)/shard_map/ppermute | solution.py:431
  6.9 0.1 collective-permute-start.1
  7.0 0.0 copy-done.2
  7.0 4.6 %inner.1.inc = f32[4,8,64,128]{3,2,1,0:T(8,128)S(1)} custom-call(bf16[4,8,256,128]{3,2,1,0:T(8,128)(2,1)S(1)} %copy-done, bf16[4,8,64,128]{3,2,1,0:T(8,128)(2,1)S(1)} %copy-done.1, s32[4,8,9]{2,1,0:T(8,128)S(1)} %copy-done.3, s32[4,8,9]{2,1,0:T(8,128)S(1)} %copy-done.4, bf16[16,128,128]{2,1,0:T(8,128)(2,1)S(1)} %copy-done.2), custom_call_target="tpu_custom_call" | custom-call | flops 2013265920 | bytes 4194304 | tf_op jit(solution)/shard_map/inner/pallas_call | solution.py:102
  11.7 1.9 %collective-permute-done.outside = bf16[4,336,128]{2,1,0:T(8,128)(2,1)S(1)} collective-permute-done((bf16[4,336,128]{2,1,0:T(8,128)(2,1)S(1)}, bf16[4,336,128]{2,1,0:T(8,128)(2,1)S(1)}, u32[]{:S(2)}, u32[]{:S(2)}) %collective-permute-start) | collective-permute-done | bytes 344096 | tf_op jit(solution)/shard_map/ppermute | solution.py:431
  13.6 0.0 collective-permute-done.1.inside
  13.6 3.4 %collective-permute-start.3 = (bf16[768,128]{1,0:T(8,128)(2,1)S(1)}, bf16[768,128]{1,0:T(8,128)(2,1)S(1)}, u32[]{:S(2)}, u32[]{:S(2)}) collective-permute-start(bf16[768,128]{1,0:T(8,128)(2,1)S(1)} %pack_rest.1), channel_id=1, source_target_pairs={{0,4},{4,8},{8,12},{12,16},{16,20},{20,24},{24,28},{1,5},{5,9},{9,... | collective-permute-start | bytes 589832 | tf_op jit(solution)/shard_map/ppermute | solution.py:434
  17.0 0.8 %collective-permute-done.2.s = bf16[2112,128]{1,0:T(8,128)(2,1)S(1)} collective-permute-done((bf16[2112,128]{1,0:T(8,128)(2,1)S(1)}, bf16[2112,128]{1,0:T(8,128)(2,1)S(1)}, u32[]{:S(2)}, u32[]{:S(2)}) %collective-permute-start.2) | collective-permute-done | bytes 540704 | tf_op jit(solution)/shard_map/ppermute | solution.py:429
  17.8 0.8 %above.1 = (bf16[8,64,128]{2,1,0:T(8,128)(2,1)S(1)}, bf16[8,128,384]{2,1,0:T(8,128)(2,1)S(1)}, f32[64,128]{1,0:T(8,128)S(1)}, bf16[64,128]{1,0:T(8,128)(2,1)S(1)}) custom-call(bf16[2112,128]{1,0:T(8,128)(2,1)S(1)} %collective-permute-done.2.s, bf16[4,8,256,128]{3,2,1,0:T(8,128)(2,1)S(1)} %copy-done, bf16[4,8,64,128]{3,2,1,0:T(8,128)(2,1)S(1)} %copy-done.1, ...), custom_call_target="tpu_custom_call" | custom-call | flops 251658240 | bytes 2097152 | tf_op jit(solution)/shard_map/above/pallas_call | solution.py:159
  18.6 3.3 %collective-permute-start.4 = (bf16[8,64,128]{2,1,0:T(8,128)(2,1)S(1)}, bf16[8,64,128]{2,1,0:T(8,128)(2,1)S(1)}, u32[]{:S(2)}, u32[]{:S(2)}) collective-permute-start(bf16[8,64,128]{2,1,0:T(8,128)(2,1)S(1)} %get-tuple-element.27), channel_id=1, source_target_pairs={{4,0},{8,4},{12,8},{16,12},{20,16},{24,20},{28,24},{5,1},{9,5},{13... | collective-permute-start | bytes 393224 | tf_op jit(solution)/shard_map/ppermute | solution.py:436
  22.0 0.1 collective-permute-start.5
  22.0 1.5 %columns.1.side = f32[2,4,64,128]{3,2,1,0:T(8,128)S(1)} custom-call(bf16[4,8,256,128]{3,2,1,0:T(8,128)(2,1)S(1)} %copy-done, bf16[4,8,64,128]{3,2,1,0:T(8,128)(2,1)S(1)} %copy-done.1, bf16[4,336,128]{2,1,0:T(8,128)(2,1)S(1)} %collective-permute-done.1.inside, bf16[4,336,128]{2,1,0:T(8,128)(2,1)S(1)} %collective-permute-done.outside, ...), custom_call_target="tpu_custom_call" | custom-call | flops 251658240 | bytes 2097152 | tf_op jit(solution)/shard_map/columns/pallas_call | solution.py:229
  23.5 0.0 collective-permute-done.3.rest
  23.5 1.4 %outer.1 = (f32[4,8,64,128]{3,2,1,0:T(8,128)}, f32[2,64,128]{2,1,0:T(8,128)S(1)}, f32[8,64,128]{2,1,0:T(8,128)S(1)}) custom-call(f32[4,8,64,128]{3,2,1,0:T(8,128)S(1)} %inner.1.inc, f32[2,4,64,128]{3,2,1,0:T(8,128)S(1)} %columns.1.side, bf16[8,128,384]{2,1,0:T(8,128)(2,1)S(1)} %get-tuple-element.22.held, bf16[64,128]{1,0:T(8,128)(2,1)S(1)} %get-tuple-element.23.tail, ...), custom_call_target="tpu_custom_call" | custom-call | flops 50331648 | bytes 4194304 | tf_op jit(solution)/shard_map/outer/pallas_call | solution.py:278
  25.0 0.0 collective-permute-done.5.from_inside
  25.0 1.4 %collective-permute-done.4.back = bf16[8,64,128]{2,1,0:T(8,128)(2,1)S(1)} collective-permute-done((bf16[8,64,128]{2,1,0:T(8,128)(2,1)S(1)}, bf16[8,64,128]{2,1,0:T(8,128)(2,1)S(1)}, u32[]{:S(2)}, u32[]{:S(2)}) %collective-permute-start.4) | collective-permute-done | bytes 131104 | tf_op jit(solution)/shard_map/ppermute | solution.py:436
  26.4 0.7 %finish.1 = f32[4,8,64,128]{3,2,1,0:T(8,128)} custom-call(f32[4,8,64,128]{3,2,1,0:T(8,128)} %get-tuple-element.24.inc, f32[2,64,128]{2,1,0:T(8,128)S(1)} %get-tuple-element.25.top, f32[8,64,128]{2,1,0:T(8,128)S(1)} %get-tuple-element.26.low, bf16[8,64,128]{2,1,0:T(8,128)(2,1)S(1)} %collective-permute-done.4.back, ...), custom_call_target="tpu_custom_call", output_to_operand_aliasing={{}: (0, {})} | custom-call | flops 65536 | bytes 655360 | tf_op jit(solution)/shard_map/finish/pallas_call | solution.py:311
  (1 shorter events, 0.0 us)
Async XLA Ops:
  0.0 4.8 %copy-start.1 = (bf16[4,8,64,128]{3,2,1,0:T(8,128)(2,1)S(1)}, bf16[4,8,64,128]{3,2,1,0:T(8,128)(2,1)}, u32[]{:S(2)}) copy-start(bf16[4,8,64,128]{3,2,1,0:T(8,128)(2,1)} %w.11) | copy-start | bytes 1572868
  0.0 4.8 %copy-start = (bf16[4,8,256,128]{3,2,1,0:T(8,128)(2,1)S(1)}, bf16[4,8,256,128]{3,2,1,0:T(8,128)(2,1)}, u32[]{:S(2)}) copy-start(bf16[4,8,256,128]{3,2,1,0:T(8,128)(2,1)} %u.11) | copy-start | bytes 6291460
  0.0 4.8 %copy-start.4 = (s32[4,8,9]{2,1,0:T(8,128)S(1)}, s32[4,8,9]{2,1,0:T(8,128)}, u32[]{:S(2)}) copy-start(s32[4,8,9]{2,1,0:T(8,128)} %index.9) | copy-start | bytes 3460
  0.0 4.8 %copy-start.3 = (s32[4,8,9]{2,1,0:T(8,128)S(1)}, s32[4,8,9]{2,1,0:T(8,128)}, u32[]{:S(2)}) copy-start(s32[4,8,9]{2,1,0:T(8,128)} %live.9) | copy-start | bytes 3460
  1.2 5.8 %copy-start.2 = (bf16[16,128,128]{2,1,0:T(8,128)(2,1)S(1)}, bf16[16,128,128]{2,1,0:T(8,128)(2,1)}, u32[]{:S(2)}) copy-start(bf16[16,128,128]{2,1,0:T(8,128)(2,1)} %tapers.7) | copy-start | bytes 1572868
  1.3 16.6 %collective-permute-start.2 = (bf16[2112,128]{1,0:T(8,128)(2,1)S(1)}, bf16[2112,128]{1,0:T(8,128)(2,1)S(1)}, u32[]{:S(2)}, u32[]{:S(2)}) collective-permute-start(bf16[2112,128]{1,0:T(8,128)(2,1)S(1)} %pack_row.1.packed), channel_id=1, source_target_pairs={{0,4},{4,8},{8,12},{12,16},{16,20},{20,24},{24,28},{1,5},{5,9},{9,... | collective-permute-start | bytes 1622024 | tf_op jit(solution)/shard_map/ppermute | solution.py:429
  5.0 8.6 %collective-permute-start = (bf16[4,336,128]{2,1,0:T(8,128)(2,1)S(1)}, bf16[4,336,128]{2,1,0:T(8,128)(2,1)S(1)}, u32[]{:S(2)}, u32[]{:S(2)}) collective-permute-start(bf16[4,336,128]{2,1,0:T(8,128)(2,1)S(1)} %get-tuple-element.17), channel_id=1, source_target_pairs={{1,2},{2,1},{5,6},{6,5},{9,10},{10,9},{13,14},{14,13},{17,18},{18,... | collective-permute-start | bytes 1032200 | tf_op jit(solution)/shard_map/ppermute | solution.py:431
  6.9 6.6 %collective-permute-start.1 = (bf16[4,336,128]{2,1,0:T(8,128)(2,1)S(1)}, bf16[4,336,128]{2,1,0:T(8,128)(2,1)S(1)}, u32[]{:S(2)}, u32[]{:S(2)}) collective-permute-start(bf16[4,336,128]{2,1,0:T(8,128)(2,1)S(1)} %get-tuple-element.18), channel_id=1, source_target_pairs={{0,1},{2,3},{1,0},{3,2},{4,5},{6,7},{5,4},{7,6},{8,9},{10,11},{9,8... | collective-permute-start | bytes 1032200 | tf_op jit(solution)/shard_map/ppermute | solution.py:432
  13.6 9.9 %collective-permute-start.3 = (bf16[768,128]{1,0:T(8,128)(2,1)S(1)}, bf16[768,128]{1,0:T(8,128)(2,1)S(1)}, u32[]{:S(2)}, u32[]{:S(2)}) collective-permute-start(bf16[768,128]{1,0:T(8,128)(2,1)S(1)} %pack_rest.1), channel_id=1, source_target_pairs={{0,4},{4,8},{8,12},{12,16},{16,20},{20,24},{24,28},{1,5},{5,9},{9,... | collective-permute-start | bytes 589832 | tf_op jit(solution)/shard_map/ppermute | solution.py:434
  18.6 7.8 %collective-permute-start.4 = (bf16[8,64,128]{2,1,0:T(8,128)(2,1)S(1)}, bf16[8,64,128]{2,1,0:T(8,128)(2,1)S(1)}, u32[]{:S(2)}, u32[]{:S(2)}) collective-permute-start(bf16[8,64,128]{2,1,0:T(8,128)(2,1)S(1)} %get-tuple-element.27), channel_id=1, source_target_pairs={{4,0},{8,4},{12,8},{16,12},{20,16},{24,20},{28,24},{5,1},{9,5},{13... | collective-permute-start | bytes 393224 | tf_op jit(solution)/shard_map/ppermute | solution.py:436
  22.0 3.0 %collective-permute-start.5 = (f32[64,128]{1,0:T(8,128)S(1)}, f32[64,128]{1,0:T(8,128)S(1)}, u32[]{:S(2)}, u32[]{:S(2)}) collective-permute-start(f32[64,128]{1,0:T(8,128)S(1)} %get-tuple-element.28), channel_id=1, source_target_pairs={{0,1},{2,3},{1,0},{3,2},{4,5},{6,7},{5,4},{7,6},{8,9},{10,11},{9,8... | collective-permute-start | bytes 98312 | tf_op jit(solution)/shard_map/ppermute | solution.py:437

commit v11 on v10

--- a/solution.py
+++ b/solution.py
@@ -239,7 +239,7 @@
     )(u, w, inside, outside, live, index, tapers)
 
 
-def outer_kernel(inc, side, held, tail, rest, u, live, index, tapers, out, top, low):
+def outer_kernel(inc, side, held, tail, rest, plain, u, live, index, tapers, out, top, low):
     rows, cols, members, cells = u.shape
     width = inc.shape[2]
     last = cols - 1
@@ -256,6 +256,9 @@
     weights = [jnp.where(even, parts[0], tail)]
     weights += [jnp.where(even, parts[c], parts[c - 1]) for c in range(1, last)]
     weights.append(jnp.where(even, tail, parts[last - 1]))
+    place = lax.axis_index("col")
+    alone = jnp.logical_or(place == 0, place == lax.axis_size("col") - 1)
+    weights = [jnp.where(alone, plain[c], weight) for c, weight in enumerate(weights)]
     for q in range(cols):
         back = [(k, q - (k - 7)) for k in (6, 7, 8) if 0 <= q - (k - 7) < cols]
         blocks = [held[c, :, (k - 6) * cells : (k - 5) * cells] for k, c in back]
@@ -273,7 +276,7 @@
                 low[q] = value
 
 
-def outer(inc, side, held, tail, rest, u, live, index, tapers):
+def outer(inc, side, held, tail, rest, plain, u, live, index, tapers):
     rows, cols, width, cells = inc.shape
     return pl.pallas_call(
         outer_kernel,
@@ -282,12 +285,12 @@
             jax.ShapeDtypeStruct((2, width, cells), inc.dtype),
             jax.ShapeDtypeStruct(inc.shape[1:], inc.dtype),
         ),
-        in_specs=[VMEM] * 9,
+        in_specs=[VMEM] * 10,
         out_specs=(VMEM,) * 3,
         compiler_params=pltpu.CompilerParams(vmem_limit_bytes=GRANT),
         cost_estimate=pl.CostEstimate(flops=6 * cols * cells * cells * width, bytes_accessed=4 << 20, transcendentals=0),
         name="outer",
-    )(inc, side, held, tail, rest, u, live, index, tapers)
+    )(inc, side, held, tail, rest, plain, u, live, index, tapers)
 
 
 def finish_kernel(inc, top, low, back, from_inside, out, end, total, sem):
@@ -366,22 +369,26 @@
     )(u, w)
 
 
-def pack_rest_kernel(w, outside, out):
+def pack_rest_kernel(w, outside, out, plain):
     rows, cols, width, _ = w.shape
     skip = 1 - even_column().astype(jnp.int32)
     for q in range(cols - 1):
         out[q * width : (q + 1) * width] = w[rows - 1, q + skip]
     start = (cols - 1) * width
     out[start:] = outside[rows - 1, : out.shape[0] - start]
+    plain[...] = w[rows - 1]
 
 
 def pack_rest(w, outside, members):
     _, cols, width, cells = w.shape
     return pl.pallas_call(
         pack_rest_kernel,
-        out_shape=jax.ShapeDtypeStruct(((cols - 1) * width + members + width, cells), w.dtype),
+        out_shape=(
+            jax.ShapeDtypeStruct(((cols - 1) * width + members + width, cells), w.dtype),
+            jax.ShapeDtypeStruct((cols, width, cells), w.dtype),
+        ),
         in_specs=[VMEM, VMEM],
-        out_specs=VMEM,
+        out_specs=(VMEM, VMEM),
         compiler_params=pltpu.CompilerParams(vmem_limit_bytes=GRANT),
         cost_estimate=pl.CostEstimate(flops=0, bytes_accessed=8 * cols * width * cells, transcendentals=0),
         name="pack_rest",
@@ -424,19 +431,27 @@
     )(u, w, live, index, packed)
 
 
+def down(row, col, chosen):
+    wide = lax.axis_size(col)
+    return [(r * wide + c, (r + 1) * wide + c) for r in range(lax.axis_size(row) - 1) for c in chosen]
+
+
 def body(u, w, live, index, tapers):
+    wide = lax.axis_size("col")
     packed = pack_row(u, w)
     s = lax.ppermute(packed, "row", forward("row"))
     inner_side, outer_side = pack_columns(u, w, live, index, packed)
     outside = lax.ppermute(outer_side, "col", swaps("col", 1))
     inside = lax.ppermute(inner_side, "col", swaps("col", 0))
     inc, outside, inside = lax.optimization_barrier((inner(u, w, live, index, tapers), outside, inside))
-    rest = lax.ppermute(pack_rest(w, outside, u.shape[2]), "row", forward("row"))
+    rest, plain = pack_rest(w, outside, u.shape[2])
+    rest = lax.ppermute(rest, ("row", "col"), down("row", "col", range(1, wide - 1)))
+    plain = lax.ppermute(plain, ("row", "col"), down("row", "col", sorted({0, wide - 1})))
     back, held, to_inside, tail = above(s, u, w, inside, outside, live, index, tapers)
     back = lax.ppermute(back, "row", backward("row"))
     from_inside = lax.ppermute(to_inside, "col", swaps("col", 0))
     side = columns(u, w, inside, outside, live, index, tapers)
-    inc, top, low = outer(inc, side, held, tail, rest, u, live, index, tapers)
+    inc, top, low = outer(inc, side, held, tail, rest, plain, u, live, index, tapers)
     return finish(inc, top, low, back, from_inside)
 
 

time: 27.4 us -> 28.1 us (1.026)
  the two profiles are of different devices: /device:TPU:22 before, /device:TPU:0 now
where the time goes in v11:
time: 28.1 us; the launch traced here: 27.9 us
  starting transfers between devices  14.3 us (51%)
  Pallas kernels  10.5 us (37%)
  waiting for transfers between devices  3 us (11%)
    ppermute x1, starting transfers between devices, body(): s = lax.ppermute(packed, 'row', forward('row'))  5.05 us
    pallas_call x1, Pallas kernels, inner(): pl.pallas_call(inner_kernel, out_shape=jax.ShapeDtypeStruct((rows, cols,...  4.64 us
    ppermute x1, starting transfers between devices, body(): lax.ppermute(plain, ('row', 'col'), down('row', 'col', sorted({0, wide -...  3.4 us
    ppermute x1, waiting for transfers between devices, body(): back = lax.ppermute(back, 'row', backward('row'))  2.98 us
    ppermute x1, starting transfers between devices, body(): inside = lax.ppermute(inner_side, 'col', swaps('col', 0))  2.9 us
    pallas_call x1, Pallas kernels, columns(): pl.pallas_call(columns_kernel, out_shape=jax.ShapeDtypeStruct((2, rows, w...  1.48 us
    pallas_call x1, Pallas kernels, outer(): pl.pallas_call(outer_kernel, out_shape=(jax.ShapeDtypeStruct(inc.shape, i...  1.43 us
    ppermute x1, starting transfers between devices, body(): back = lax.ppermute(back, 'row', backward('row'))  1.29 us
  transfers between devices with their start and end apart: 7, of which 1 were waited for; matrix products, arithmetic and copies ran while one was open for 0% of the time, Pallas kernels for 31%

profile of v11, /device:TPU:0, one launch (start us, length us, event | category | flops | bytes accessed | tf_op | source)
XLA Modules:
  0.0 27.9 jit_solution(8308633728099591820)
XLA Ops:
  0.0 0.0 copy-start.1
  0.0 0.0 copy-start
  0.0 0.0 copy-start.4
  0.0 0.0 copy-start.3
  0.0 1.2 %pack_row.1.packed = bf16[2112,128]{1,0:T(8,128)(2,1)S(1)} custom-call(bf16[4,8,256,128]{3,2,1,0:T(8,128)(2,1)} %u.11, bf16[4,8,64,128]{3,2,1,0:T(8,128)(2,1)} %w.11), custom_call_target="tpu_custom_call" | custom-call | bytes 1081344 | tf_op jit(solution)/shard_map/pack_row/pallas_call | solution.py:361
  1.2 0.0 copy-start.2
  1.2 5.0 %collective-permute-start.2 = (bf16[2112,128]{1,0:T(8,128)(2,1)S(1)}, bf16[2112,128]{1,0:T(8,128)(2,1)S(1)}, u32[]{:S(2)}, u32[]{:S(2)}) collective-permute-start(bf16[2112,128]{1,0:T(8,128)(2,1)S(1)} %pack_row.1.packed), channel_id=1, source_target_pairs={{0,4},{4,8},{8,12},{12,16},{16,20},{20,24},{24,28},{1,5},{5,9},{9,... | collective-permute-start | bytes 1622024 | tf_op jit(solution)/shard_map/ppermute | solution.py:442
  6.3 0.0 copy-done.1
  6.3 0.0 copy-done
  6.3 0.0 copy-done.4
  6.3 0.0 copy-done.3
  6.3 0.1 pack_columns.1
  6.5 0.7 %collective-permute-start = (bf16[4,336,128]{2,1,0:T(8,128)(2,1)S(1)}, bf16[4,336,128]{2,1,0:T(8,128)(2,1)S(1)}, u32[]{:S(2)}, u32[]{:S(2)}) collective-permute-start(bf16[4,336,128]{2,1,0:T(8,128)(2,1)S(1)} %get-tuple-element.19), channel_id=1, source_target_pairs={{1,2},{2,1},{5,6},{6,5},{9,10},{10,9},{13,14},{14,13},{17,18},{18,... | collective-permute-start | bytes 1032200 | tf_op jit(solution)/shard_map/ppermute | solution.py:444
  7.2 2.9 %collective-permute-start.1 = (bf16[4,336,128]{2,1,0:T(8,128)(2,1)S(1)}, bf16[4,336,128]{2,1,0:T(8,128)(2,1)S(1)}, u32[]{:S(2)}, u32[]{:S(2)}) collective-permute-start(bf16[4,336,128]{2,1,0:T(8,128)(2,1)S(1)} %get-tuple-element.20), channel_id=1, source_target_pairs={{0,1},{2,3},{1,0},{3,2},{4,5},{6,7},{5,4},{7,6},{8,9},{10,11},{9,8... | collective-permute-start | bytes 1032200 | tf_op jit(solution)/shard_map/ppermute | solution.py:445
  10.1 0.0 copy-done.2
  10.1 4.6 %inner.1.inc = f32[4,8,64,128]{3,2,1,0:T(8,128)S(1)} custom-call(bf16[4,8,256,128]{3,2,1,0:T(8,128)(2,1)S(1)} %copy-done, bf16[4,8,64,128]{3,2,1,0:T(8,128)(2,1)S(1)} %copy-done.1, s32[4,8,9]{2,1,0:T(8,128)S(1)} %copy-done.3, s32[4,8,9]{2,1,0:T(8,128)S(1)} %copy-done.4, bf16[16,128,128]{2,1,0:T(8,128)(2,1)S(1)} %copy-done.2), custom_call_target="tpu_custom_call" | custom-call | flops 2013265920 | bytes 4194304 | tf_op jit(solution)/shard_map/inner/pallas_call | solution.py:102
  14.7 0.0 collective-permute-done.outside
  14.7 0.0 collective-permute-done.1.inside
  14.8 0.7 %collective-permute-start.3 = (bf16[768,128]{1,0:T(8,128)(2,1)S(1)}, bf16[768,128]{1,0:T(8,128)(2,1)S(1)}, u32[]{:S(2)}, u32[]{:S(2)}) collective-permute-start(bf16[768,128]{1,0:T(8,128)(2,1)S(1)} %get-tuple-element.26), channel_id=1, source_target_pairs={{1,5},{2,6},{5,9},{6,10},{9,13},{10,14},{13,17},{14,18},{17,21},{1... | collective-permute-start | bytes 589832 | tf_op jit(solution)/shard_map/ppermute | solution.py:448
  15.5 3.4 %collective-permute-start.4 = (bf16[8,64,128]{2,1,0:T(8,128)(2,1)S(1)}, bf16[8,64,128]{2,1,0:T(8,128)(2,1)S(1)}, u32[]{:S(2)}, u32[]{:S(2)}) collective-permute-start(bf16[8,64,128]{2,1,0:T(8,128)(2,1)S(1)} %get-tuple-element.27), channel_id=1, source_target_pairs={{0,4},{3,7},{4,8},{7,11},{8,12},{11,15},{12,16},{15,19},{16,20},{1... | collective-permute-start | bytes 393224 | tf_op jit(solution)/shard_map/ppermute | solution.py:449
  18.9 0.0 collective-permute-done.2.s
  18.9 0.8 %above.1 = (bf16[8,64,128]{2,1,0:T(8,128)(2,1)S(1)}, bf16[8,128,384]{2,1,0:T(8,128)(2,1)S(1)}, f32[64,128]{1,0:T(8,128)S(1)}, bf16[64,128]{1,0:T(8,128)(2,1)S(1)}) custom-call(bf16[2112,128]{1,0:T(8,128)(2,1)S(1)} %collective-permute-done.2.s, bf16[4,8,256,128]{3,2,1,0:T(8,128)(2,1)S(1)} %copy-done, bf16[4,8,64,128]{3,2,1,0:T(8,128)(2,1)S(1)} %copy-done.1, ...), custom_call_target="tpu_custom_call" | custom-call | flops 251658240 | bytes 2097152 | tf_op jit(solution)/shard_map/above/pallas_call | solution.py:159
  19.7 1.3 %collective-permute-start.5 = (bf16[8,64,128]{2,1,0:T(8,128)(2,1)S(1)}, bf16[8,64,128]{2,1,0:T(8,128)(2,1)S(1)}, u32[]{:S(2)}, u32[]{:S(2)}) collective-permute-start(bf16[8,64,128]{2,1,0:T(8,128)(2,1)S(1)} %get-tuple-element.31), channel_id=1, source_target_pairs={{4,0},{8,4},{12,8},{16,12},{20,16},{24,20},{28,24},{5,1},{9,5},{13... | collective-permute-start | bytes 393224 | tf_op jit(solution)/shard_map/ppermute | solution.py:451
  21.0 0.3 collective-permute-start.6
  21.3 1.5 %columns.1.side = f32[2,4,64,128]{3,2,1,0:T(8,128)S(1)} custom-call(bf16[4,8,256,128]{3,2,1,0:T(8,128)(2,1)S(1)} %copy-done, bf16[4,8,64,128]{3,2,1,0:T(8,128)(2,1)S(1)} %copy-done.1, bf16[4,336,128]{2,1,0:T(8,128)(2,1)S(1)} %collective-permute-done.1.inside, bf16[4,336,128]{2,1,0:T(8,128)(2,1)S(1)} %collective-permute-done.outside, ...), custom_call_target="tpu_custom_call" | custom-call | flops 251658240 | bytes 2097152 | tf_op jit(solution)/shard_map/columns/pallas_call | solution.py:229
  22.7 0.0 collective-permute-done.4.plain
  22.8 0.0 collective-permute-done.3.rest
  22.8 1.4 %outer.1 = (f32[4,8,64,128]{3,2,1,0:T(8,128)}, f32[2,64,128]{2,1,0:T(8,128)S(1)}, f32[8,64,128]{2,1,0:T(8,128)S(1)}) custom-call(f32[4,8,64,128]{3,2,1,0:T(8,128)S(1)} %inner.1.inc, f32[2,4,64,128]{3,2,1,0:T(8,128)S(1)} %columns.1.side, bf16[8,128,384]{2,1,0:T(8,128)(2,1)S(1)} %get-tuple-element.24.held, bf16[64,128]{1,0:T(8,128)(2,1)S(1)} %get-tuple-element.25.tail, ...), custom_call_target="tpu_custom_call" | custom-call | flops 50331648 | bytes 4194304 | tf_op jit(solution)/shard_map/outer/pallas_call | solution.py:281
  24.2 0.0 collective-permute-done.6.from_inside
  24.2 3.0 %collective-permute-done.5.back = bf16[8,64,128]{2,1,0:T(8,128)(2,1)S(1)} collective-permute-done((bf16[8,64,128]{2,1,0:T(8,128)(2,1)S(1)}, bf16[8,64,128]{2,1,0:T(8,128)(2,1)S(1)}, u32[]{:S(2)}, u32[]{:S(2)}) %collective-permute-start.5) | collective-permute-done | bytes 131104 | tf_op jit(solution)/shard_map/ppermute | solution.py:451
  27.2 0.7 %finish.1 = f32[4,8,64,128]{3,2,1,0:T(8,128)} custom-call(f32[4,8,64,128]{3,2,1,0:T(8,128)} %get-tuple-element.28.inc, f32[2,64,128]{2,1,0:T(8,128)S(1)} %get-tuple-element.29.top, f32[8,64,128]{2,1,0:T(8,128)S(1)} %get-tuple-element.30.low, bf16[8,64,128]{2,1,0:T(8,128)(2,1)S(1)} %collective-permute-done.5.back, ...), custom_call_target="tpu_custom_call", output_to_operand_aliasing={{}: (0, {})} | custom-call | flops 65536 | bytes 655360 | tf_op jit(solution)/shard_map/finish/pallas_call | solution.py:314
  (1 shorter events, 0.0 us)
Async XLA Ops:
  0.0 6.3 %copy-start.1 = (bf16[4,8,64,128]{3,2,1,0:T(8,128)(2,1)S(1)}, bf16[4,8,64,128]{3,2,1,0:T(8,128)(2,1)}, u32[]{:S(2)}) copy-start(bf16[4,8,64,128]{3,2,1,0:T(8,128)(2,1)} %w.11) | copy-start | bytes 1572868
  0.0 6.3 %copy-start = (bf16[4,8,256,128]{3,2,1,0:T(8,128)(2,1)S(1)}, bf16[4,8,256,128]{3,2,1,0:T(8,128)(2,1)}, u32[]{:S(2)}) copy-start(bf16[4,8,256,128]{3,2,1,0:T(8,128)(2,1)} %u.11) | copy-start | bytes 6291460
  0.0 6.3 %copy-start.4 = (s32[4,8,9]{2,1,0:T(8,128)S(1)}, s32[4,8,9]{2,1,0:T(8,128)}, u32[]{:S(2)}) copy-start(s32[4,8,9]{2,1,0:T(8,128)} %index.9) | copy-start | bytes 3460
  0.0 6.3 %copy-start.3 = (s32[4,8,9]{2,1,0:T(8,128)S(1)}, s32[4,8,9]{2,1,0:T(8,128)}, u32[]{:S(2)}) copy-start(s32[4,8,9]{2,1,0:T(8,128)} %live.9) | copy-start | bytes 3460
  1.2 8.9 %copy-start.2 = (bf16[16,128,128]{2,1,0:T(8,128)(2,1)S(1)}, bf16[16,128,128]{2,1,0:T(8,128)(2,1)}, u32[]{:S(2)}) copy-start(bf16[16,128,128]{2,1,0:T(8,128)(2,1)} %tapers.7) | copy-start | bytes 1572868
  1.2 17.6 %collective-permute-start.2 = (bf16[2112,128]{1,0:T(8,128)(2,1)S(1)}, bf16[2112,128]{1,0:T(8,128)(2,1)S(1)}, u32[]{:S(2)}, u32[]{:S(2)}) collective-permute-start(bf16[2112,128]{1,0:T(8,128)(2,1)S(1)} %pack_row.1.packed), channel_id=1, source_target_pairs={{0,4},{4,8},{8,12},{12,16},{16,20},{20,24},{24,28},{1,5},{5,9},{9,... | collective-permute-start | bytes 1622024 | tf_op jit(solution)/shard_map/ppermute | solution.py:442
  6.5 8.2 %collective-permute-start = (bf16[4,336,128]{2,1,0:T(8,128)(2,1)S(1)}, bf16[4,336,128]{2,1,0:T(8,128)(2,1)S(1)}, u32[]{:S(2)}, u32[]{:S(2)}) collective-permute-start(bf16[4,336,128]{2,1,0:T(8,128)(2,1)S(1)} %get-tuple-element.19), channel_id=1, source_target_pairs={{1,2},{2,1},{5,6},{6,5},{9,10},{10,9},{13,14},{14,13},{17,18},{18,... | collective-permute-start | bytes 1032200 | tf_op jit(solution)/shard_map/ppermute | solution.py:444
  7.2 7.6 %collective-permute-start.1 = (bf16[4,336,128]{2,1,0:T(8,128)(2,1)S(1)}, bf16[4,336,128]{2,1,0:T(8,128)(2,1)S(1)}, u32[]{:S(2)}, u32[]{:S(2)}) collective-permute-start(bf16[4,336,128]{2,1,0:T(8,128)(2,1)S(1)} %get-tuple-element.20), channel_id=1, source_target_pairs={{0,1},{2,3},{1,0},{3,2},{4,5},{6,7},{5,4},{7,6},{8,9},{10,11},{9,8... | collective-permute-start | bytes 1032200 | tf_op jit(solution)/shard_map/ppermute | solution.py:445
  14.8 8.0 %collective-permute-start.3 = (bf16[768,128]{1,0:T(8,128)(2,1)S(1)}, bf16[768,128]{1,0:T(8,128)(2,1)S(1)}, u32[]{:S(2)}, u32[]{:S(2)}) collective-permute-start(bf16[768,128]{1,0:T(8,128)(2,1)S(1)} %get-tuple-element.26), channel_id=1, source_target_pairs={{1,5},{2,6},{5,9},{6,10},{9,13},{10,14},{13,17},{14,18},{17,21},{1... | collective-permute-start | bytes 589832 | tf_op jit(solution)/shard_map/ppermute | solution.py:448
  15.5 7.3 %collective-permute-start.4 = (bf16[8,64,128]{2,1,0:T(8,128)(2,1)S(1)}, bf16[8,64,128]{2,1,0:T(8,128)(2,1)S(1)}, u32[]{:S(2)}, u32[]{:S(2)}) collective-permute-start(bf16[8,64,128]{2,1,0:T(8,128)(2,1)S(1)} %get-tuple-element.27), channel_id=1, source_target_pairs={{0,4},{3,7},{4,8},{7,11},{8,12},{11,15},{12,16},{15,19},{16,20},{1... | collective-permute-start | bytes 393224 | tf_op jit(solution)/shard_map/ppermute | solution.py:449
  19.7 7.5 %collective-permute-start.5 = (bf16[8,64,128]{2,1,0:T(8,128)(2,1)S(1)}, bf16[8,64,128]{2,1,0:T(8,128)(2,1)S(1)}, u32[]{:S(2)}, u32[]{:S(2)}) collective-permute-start(bf16[8,64,128]{2,1,0:T(8,128)(2,1)S(1)} %get-tuple-element.31), channel_id=1, source_target_pairs={{4,0},{8,4},{12,8},{16,12},{20,16},{24,20},{28,24},{5,1},{9,5},{13... | collective-permute-start | bytes 393224 | tf_op jit(solution)/shard_map/ppermute | solution.py:451
  21.0 3.2 %collective-permute-start.6 = (f32[64,128]{1,0:T(8,128)S(1)}, f32[64,128]{1,0:T(8,128)S(1)}, u32[]{:S(2)}, u32[]{:S(2)}) collective-permute-start(f32[64,128]{1,0:T(8,128)S(1)} %get-tuple-element.32), channel_id=1, source_target_pairs={{0,1},{2,3},{1,0},{3,2},{4,5},{6,7},{5,4},{7,6},{8,9},{10,11},{9,8... | collective-permute-start | bytes 98312 | tf_op jit(solution)/shard_map/ppermute | solution.py:452

commit v12 on v10

--- a/solution.py
+++ b/solution.py
@@ -41,11 +41,12 @@
     )
 
 
-def inner_kernel(u, w, live, index, tapers, out, sym, held):
+def inner_kernel(u, w, live, index, tapers, out, turned, flipped, sym, held):
     rows, cols, _, cells = u.shape
     for n in range(tapers.shape[0]):
         t = tapers[n].astype(jnp.float32)
         sym[n] = 0.5 * (t + t.T)
+        flipped[n] = t.T.astype(jnp.bfloat16)
 
     def ahead(a, b, last):
         near = [(4, a, b)]
@@ -61,7 +62,9 @@
         on, which = live[a], index[a]
         for b in range(cols):
             near = ahead(a, b, last)
-            gram = dot(u[a, b], cat([u[p, q] for _, p, q in near], 1), TN)
+            side_on = u[a, b].T
+            turned[a, b] = side_on
+            gram = dot(side_on, cat([u[p, q] for _, p, q in near], 1), NN)
             for n, (k, _, _) in enumerate(near):
                 at = which[b, k]
                 rho = sym[at] if k == 4 else tapers[at]
@@ -101,9 +104,13 @@
     pairs = 5 * rows * cols
     return pl.pallas_call(
         inner_kernel,
-        out_shape=jax.ShapeDtypeStruct((rows, cols, columns, cells), jnp.float32),
+        out_shape=(
+            jax.ShapeDtypeStruct((rows, cols, columns, cells), jnp.float32),
+            jax.ShapeDtypeStruct((rows, cols, cells, members), jnp.bfloat16),
+            jax.ShapeDtypeStruct(tapers.shape, jnp.bfloat16),
+        ),
         in_specs=[VMEM] * 5,
-        out_specs=VMEM,
+        out_specs=(VMEM,) * 3,
         scratch_shapes=[
             pltpu.VMEM(tapers.shape, jnp.float32),
             pltpu.VMEM((cols, cells, 5 * cells), jnp.bfloat16),
@@ -118,43 +125,47 @@
     )(u, w, live, index, tapers)
 
 
-def above_kernel(s, u, w, inside, outside, live, index, tapers, back, held, to_inside, tail):
-    cols, members, cells = u.shape[1:]
+def above_kernel(s, turned, w, inside, outside, live, index, flipped, back, held, to_inside, tail):
+    _, cols, cells, members = turned.shape
     deep = members + w.shape[2]
     last = cols - 1
     left, right = sides(inside, outside)
     on, which = live[0], index[0]
+
+    def upper(c):
+        return s[c * members : (c + 1) * members]
+
     beyond = {}
     for q, near, k, line in ((-1, left, 2, last), (cols, right, 0, 0)):
         note = near(0, slice(deep, None)).astype(jnp.int32)
-        beyond[q] = near, note[line, k], note[cols + line, k]
-    sources = []
+        gram = dot(near(0, slice(0, members)), upper(min(max(q, 0), last)), TN)
+        block = tapered(gram, flipped[note[cols + line, k]], note[line, k])
+        beyond[q] = block, near(0, slice(members, deep))
+    for q in range(cols):
+        near = [c for c in (q - 1, q, q + 1) if 0 <= c < cols]
+        gram = dot(turned[0, q], cat([upper(c) for c in near], 1), NN)
+        for n, c in enumerate(near):
+            k = 1 + c - q
+            held[q, :, k * cells : (k + 1) * cells] = tapered(
+                gram[:, n * cells : (n + 1) * cells], flipped[which[q, k]], on[q, k]
+            )
     for c in range(cols):
-        grams, weights, lives, rhos = [], [], [], []
-        for k in (6, 7, 8):
-            q = c + k - 7
+        blocks, weights = [], []
+        for q in (c - 1, c, c + 1):
             if q in beyond:
-                near, lively, at = beyond[q]
-                grams.append(near(0, slice(0, members)))
-                weights.append(near(0, slice(members, deep)))
+                block, weight = beyond[q]
             else:
-                lively, at = on[q, 8 - k], which[q, 8 - k]
-                grams.append(u[0, q])
-                weights.append(w[0, q])
-            lives.append(lively)
-            rhos.append(tapers[at])
-        gram = dot(s[c * members : (c + 1) * members], cat(grams, 1), TN)
-        held[c] = cat([tapered(gram[:, m * cells : (m + 1) * cells], rhos[m], lives[m]) for m in range(3)], 1)
-        sources.append(cat(weights, 1))
-    for c in range(cols):
-        back[c] = dot(sources[c], held[c], NT).astype(jnp.bfloat16)
-    even = even_column()
+                k = 1 + c - q
+                block, weight = held[q, :, k * cells : (k + 1) * cells], w[0, q]
+            blocks.append(block)
+            weights.append(weight)
+        back[c] = dot(cat(weights, 1), cat(blocks, 0), NN).astype(jnp.bfloat16)
     tail[...] = s[cols * members :]
-    to_inside[...] = dot(s[cols * members :], jnp.where(even, held[last, :, 2 * cells :], held[0, :, :cells]), NN)
-
-
-def above(s, u, w, inside, outside, live, index, tapers):
-    cols, members, cells = u.shape[1:]
+    to_inside[...] = dot(s[cols * members :], jnp.where(even_column(), beyond[cols][0], beyond[-1][0]), NT)
+
+
+def above(s, turned, w, inside, outside, live, index, flipped):
+    _, cols, cells, members = turned.shape
     columns = w.shape[2]
     return pl.pallas_call(
         above_kernel,
@@ -173,7 +184,7 @@
             transcendentals=0,
         ),
         name="above",
-    )(s, u, w, inside, outside, live, index, tapers)
+    )(s, turned, w, inside, outside, live, index, flipped)
 
 
 def columns_kernel(u, w, inside, outside, live, index, tapers, side):
@@ -257,9 +268,9 @@
     weights += [jnp.where(even, parts[c], parts[c - 1]) for c in range(1, last)]
     weights.append(jnp.where(even, tail, parts[last - 1]))
     for q in range(cols):
-        back = [(k, q - (k - 7)) for k in (6, 7, 8) if 0 <= q - (k - 7) < cols]
-        blocks = [held[c, :, (k - 6) * cells : (k - 5) * cells] for k, c in back]
-        value = inc[0, q] + dot(cat([weights[c] for _, c in back], 1), cat(blocks, 0), NN)
+        near = [c for c in (q - 1, q, q + 1) if 0 <= c < cols]
+        block = held[q, :, (1 + near[0] - q) * cells : (2 + near[-1] - q) * cells]
+        value = inc[0, q] + dot(cat([weights[c] for c in near], 1), block, NT)
         if q in (0, last):
             value += side[q // last, 0]
             value += jnp.where(even, far, blank) if q == 0 else jnp.where(even, blank, far)
@@ -430,9 +441,10 @@
     inner_side, outer_side = pack_columns(u, w, live, index, packed)
     outside = lax.ppermute(outer_side, "col", swaps("col", 1))
     inside = lax.ppermute(inner_side, "col", swaps("col", 0))
-    inc, outside, inside = lax.optimization_barrier((inner(u, w, live, index, tapers), outside, inside))
+    inc, turned, flipped = inner(u, w, live, index, tapers)
+    inc, outside, inside = lax.optimization_barrier((inc, outside, inside))
     rest = lax.ppermute(pack_rest(w, outside, u.shape[2]), "row", forward("row"))
-    back, held, to_inside, tail = above(s, u, w, inside, outside, live, index, tapers)
+    back, held, to_inside, tail = above(s, turned, w, inside, outside, live, index, flipped)
     back = lax.ppermute(back, "row", backward("row"))
     from_inside = lax.ppermute(to_inside, "col", swaps("col", 0))
     side = columns(u, w, inside, outside, live, index, tapers)

time: 27.4 us -> 27.3 us (level)
  waiting for transfers between devices: 4.1 us -> 3.59 us
  transfers between devices with their start and end apart: 6 -> 6, of which waited for: 3 -> 3; matrix products, arithmetic and copies ran while one was open for 0% -> 0% of each run, Pallas kernels for 31% -> 33%
where the time goes in v12:
time: 27.3 us; the launch traced here: 26.8 us
  starting transfers between devices  12.4 us (45%)
  Pallas kernels  10.7 us (39%)
  waiting for transfers between devices  3.59 us (13%)
    pallas_call x1, Pallas kernels, inner(): pl.pallas_call(inner_kernel, out_shape=(jax.ShapeDtypeStruct((rows, cols,...  4.83 us
    ppermute x1, starting transfers between devices, body(): s = lax.ppermute(packed, 'row', forward('row'))  3.56 us
    ppermute x1, starting transfers between devices, body(): lax.ppermute(pack_rest(w, outside, u.shape[2]), 'row', forward('row'))  3.43 us
    ppermute x1, starting transfers between devices, body(): back = lax.ppermute(back, 'row', backward('row'))  3.31 us
    ppermute x1, starting transfers between devices, body(): outside = lax.ppermute(outer_side, 'col', swaps('col', 1))  1.92 us
    ppermute x1, waiting for transfers between devices, body(): outside = lax.ppermute(outer_side, 'col', swaps('col', 1))  1.72 us
    pallas_call x1, Pallas kernels, outer(): pl.pallas_call(outer_kernel, out_shape=(jax.ShapeDtypeStruct(inc.shape, i...  1.57 us
    pallas_call x1, Pallas kernels, columns(): pl.pallas_call(columns_kernel, out_shape=jax.ShapeDtypeStruct((2, rows, w...  1.49 us
  transfers between devices with their start and end apart: 6, of which 3 were waited for; matrix products, arithmetic and copies ran while one was open for 0% of the time, Pallas kernels for 33%

profile of v12, /device:TPU:22, one launch (start us, length us, event | category | flops | bytes accessed | tf_op | source)
XLA Modules:
  0.0 26.8 jit_solution(17004563880795832654)
XLA Ops:
  0.0 0.0 copy-start.1
  0.0 0.0 copy-start
  0.0 0.0 copy-start.4
  0.0 0.0 copy-start.3
  0.0 1.2 %pack_row.1.packed = bf16[2112,128]{1,0:T(8,128)(2,1)S(1)} custom-call(bf16[4,8,256,128]{3,2,1,0:T(8,128)(2,1)} %u.9, bf16[4,8,64,128]{3,2,1,0:T(8,128)(2,1)} %w.11), custom_call_target="tpu_custom_call" | custom-call | bytes 1081344 | tf_op jit(solution)/shard_map/pack_row/pallas_call | solution.py:369
  1.2 0.0 copy-start.2
  1.3 3.6 %collective-permute-start.2 = (bf16[2112,128]{1,0:T(8,128)(2,1)S(1)}, bf16[2112,128]{1,0:T(8,128)(2,1)S(1)}, u32[]{:S(2)}, u32[]{:S(2)}) collective-permute-start(bf16[2112,128]{1,0:T(8,128)(2,1)S(1)} %pack_row.1.packed), channel_id=1, source_target_pairs={{0,4},{4,8},{8,12},{12,16},{16,20},{20,24},{24,28},{1,5},{5,9},{9,... | collective-permute-start | bytes 1622024 | tf_op jit(solution)/shard_map/ppermute | solution.py:440
  4.8 0.0 copy-done.1
  4.8 0.0 copy-done
  4.8 0.0 copy-done.4
  4.8 0.0 copy-done.3
  4.9 0.1 pack_columns.1
  5.0 1.9 %collective-permute-start = (bf16[4,336,128]{2,1,0:T(8,128)(2,1)S(1)}, bf16[4,336,128]{2,1,0:T(8,128)(2,1)S(1)}, u32[]{:S(2)}, u32[]{:S(2)}) collective-permute-start(bf16[4,336,128]{2,1,0:T(8,128)(2,1)S(1)} %get-tuple-element.21), channel_id=1, source_target_pairs={{1,2},{2,1},{5,6},{6,5},{9,10},{10,9},{13,14},{14,13},{17,18},{18,... | collective-permute-start | bytes 1032200 | tf_op jit(solution)/shard_map/ppermute | solution.py:442
  6.9 0.1 collective-permute-start.1
  7.0 0.0 copy-done.2
  7.0 4.8 %inner.1 = (f32[4,8,64,128]{3,2,1,0:T(8,128)S(1)}, bf16[4,8,128,256]{3,2,1,0:T(8,128)(2,1)S(1)}, bf16[16,128,128]{2,1,0:T(8,128)(2,1)S(1)}) custom-call(bf16[4,8,256,128]{3,2,1,0:T(8,128)(2,1)S(1)} %copy-done, bf16[4,8,64,128]{3,2,1,0:T(8,128)(2,1)S(1)} %copy-done.1, s32[4,8,9]{2,1,0:T(8,128)S(1)} %copy-done.3, s32[4,8,9]{2,1,0:T(8,128)S(1)} %copy-done.4, ...), custom_call_target="tpu_custom_call" | custom-call | flops 2013265920 | bytes 4194304 | tf_op jit(solution)/shard_map/inner/pallas_call | solution.py:105
  11.9 1.7 %collective-permute-done.outside = bf16[4,336,128]{2,1,0:T(8,128)(2,1)S(1)} collective-permute-done((bf16[4,336,128]{2,1,0:T(8,128)(2,1)S(1)}, bf16[4,336,128]{2,1,0:T(8,128)(2,1)S(1)}, u32[]{:S(2)}, u32[]{:S(2)}) %collective-permute-start) | collective-permute-done | bytes 344096 | tf_op jit(solution)/shard_map/ppermute | solution.py:442
  13.6 0.0 collective-permute-done.1.inside
  13.6 3.4 %collective-permute-start.3 = (bf16[768,128]{1,0:T(8,128)(2,1)S(1)}, bf16[768,128]{1,0:T(8,128)(2,1)S(1)}, u32[]{:S(2)}, u32[]{:S(2)}) collective-permute-start(bf16[768,128]{1,0:T(8,128)(2,1)S(1)} %pack_rest.1), channel_id=1, source_target_pairs={{0,4},{4,8},{8,12},{12,16},{16,20},{20,24},{24,28},{1,5},{5,9},{9,... | collective-permute-start | bytes 589832 | tf_op jit(solution)/shard_map/ppermute | solution.py:446
  17.0 0.6 %collective-permute-done.2.s = bf16[2112,128]{1,0:T(8,128)(2,1)S(1)} collective-permute-done((bf16[2112,128]{1,0:T(8,128)(2,1)S(1)}, bf16[2112,128]{1,0:T(8,128)(2,1)S(1)}, u32[]{:S(2)}, u32[]{:S(2)}) %collective-permute-start.2) | collective-permute-done | bytes 540704 | tf_op jit(solution)/shard_map/ppermute | solution.py:440
  17.6 0.7 %above.1 = (bf16[8,64,128]{2,1,0:T(8,128)(2,1)S(1)}, bf16[8,128,384]{2,1,0:T(8,128)(2,1)S(1)}, f32[64,128]{1,0:T(8,128)S(1)}, bf16[64,128]{1,0:T(8,128)(2,1)S(1)}) custom-call(bf16[2112,128]{1,0:T(8,128)(2,1)S(1)} %collective-permute-done.2.s, bf16[4,8,128,256]{3,2,1,0:T(8,128)(2,1)S(1)} %get-tuple-element.26.turned, bf16[4,8,64,128]{3,2,1,0:T(8,128)(2,1)S(1)} %copy-done.1, ...), custom_call_target="tpu_custom_call" | custom-call | flops 251658240 | bytes 2097152 | tf_op jit(solution)/shard_map/above/pallas_call | solution.py:170
  18.3 3.3 %collective-permute-start.4 = (bf16[8,64,128]{2,1,0:T(8,128)(2,1)S(1)}, bf16[8,64,128]{2,1,0:T(8,128)(2,1)S(1)}, u32[]{:S(2)}, u32[]{:S(2)}) collective-permute-start(bf16[8,64,128]{2,1,0:T(8,128)(2,1)S(1)} %get-tuple-element.33), channel_id=1, source_target_pairs={{4,0},{8,4},{12,8},{16,12},{20,16},{24,20},{28,24},{5,1},{9,5},{13... | collective-permute-start | bytes 393224 | tf_op jit(solution)/shard_map/ppermute | solution.py:448
  21.6 0.1 collective-permute-start.5
  21.7 1.5 %columns.1.side = f32[2,4,64,128]{3,2,1,0:T(8,128)S(1)} custom-call(bf16[4,8,256,128]{3,2,1,0:T(8,128)(2,1)S(1)} %copy-done, bf16[4,8,64,128]{3,2,1,0:T(8,128)(2,1)S(1)} %copy-done.1, bf16[4,336,128]{2,1,0:T(8,128)(2,1)S(1)} %collective-permute-done.1.inside, bf16[4,336,128]{2,1,0:T(8,128)(2,1)S(1)} %collective-permute-done.outside, ...), custom_call_target="tpu_custom_call" | custom-call | flops 251658240 | bytes 2097152 | tf_op jit(solution)/shard_map/columns/pallas_call | solution.py:240
  23.2 0.0 collective-permute-done.3.rest
  23.2 1.6 %outer.1 = (f32[4,8,64,128]{3,2,1,0:T(8,128)}, f32[2,64,128]{2,1,0:T(8,128)S(1)}, f32[8,64,128]{2,1,0:T(8,128)S(1)}) custom-call(f32[4,8,64,128]{3,2,1,0:T(8,128)S(1)} %get-tuple-element.23.inc, f32[2,4,64,128]{3,2,1,0:T(8,128)S(1)} %columns.1.side, bf16[8,128,384]{2,1,0:T(8,128)(2,1)S(1)} %get-tuple-element.28.held, ...), custom_call_target="tpu_custom_call" | custom-call | flops 50331648 | bytes 4194304 | tf_op jit(solution)/shard_map/outer/pallas_call | solution.py:289
  24.8 0.0 collective-permute-done.5.from_inside
  24.8 1.3 %collective-permute-done.4.back = bf16[8,64,128]{2,1,0:T(8,128)(2,1)S(1)} collective-permute-done((bf16[8,64,128]{2,1,0:T(8,128)(2,1)S(1)}, bf16[8,64,128]{2,1,0:T(8,128)(2,1)S(1)}, u32[]{:S(2)}, u32[]{:S(2)}) %collective-permute-start.4) | collective-permute-done | bytes 131104 | tf_op jit(solution)/shard_map/ppermute | solution.py:448
  26.1 0.7 %finish.1 = f32[4,8,64,128]{3,2,1,0:T(8,128)} custom-call(f32[4,8,64,128]{3,2,1,0:T(8,128)} %get-tuple-element.30.inc, f32[2,64,128]{2,1,0:T(8,128)S(1)} %get-tuple-element.31.top, f32[8,64,128]{2,1,0:T(8,128)S(1)} %get-tuple-element.32.low, bf16[8,64,128]{2,1,0:T(8,128)(2,1)S(1)} %collective-permute-done.4.back, ...), custom_call_target="tpu_custom_call", output_to_operand_aliasing={{}: (0, {})} | custom-call | flops 65536 | bytes 655360 | tf_op jit(solution)/shard_map/finish/pallas_call | solution.py:322
  (1 shorter events, 0.0 us)
Async XLA Ops:
  0.0 4.8 %copy-start.1 = (bf16[4,8,64,128]{3,2,1,0:T(8,128)(2,1)S(1)}, bf16[4,8,64,128]{3,2,1,0:T(8,128)(2,1)}, u32[]{:S(2)}) copy-start(bf16[4,8,64,128]{3,2,1,0:T(8,128)(2,1)} %w.11) | copy-start | bytes 1572868
  0.0 4.8 %copy-start = (bf16[4,8,256,128]{3,2,1,0:T(8,128)(2,1)S(1)}, bf16[4,8,256,128]{3,2,1,0:T(8,128)(2,1)}, u32[]{:S(2)}) copy-start(bf16[4,8,256,128]{3,2,1,0:T(8,128)(2,1)} %u.9) | copy-start | bytes 6291460
  0.0 4.8 %copy-start.4 = (s32[4,8,9]{2,1,0:T(8,128)S(1)}, s32[4,8,9]{2,1,0:T(8,128)}, u32[]{:S(2)}) copy-start(s32[4,8,9]{2,1,0:T(8,128)} %index.9) | copy-start | bytes 3460
  0.0 4.8 %copy-start.3 = (s32[4,8,9]{2,1,0:T(8,128)S(1)}, s32[4,8,9]{2,1,0:T(8,128)}, u32[]{:S(2)}) copy-start(s32[4,8,9]{2,1,0:T(8,128)} %live.9) | copy-start | bytes 3460
  1.2 5.8 %copy-start.2 = (bf16[16,128,128]{2,1,0:T(8,128)(2,1)S(1)}, bf16[16,128,128]{2,1,0:T(8,128)(2,1)}, u32[]{:S(2)}) copy-start(bf16[16,128,128]{2,1,0:T(8,128)(2,1)} %tapers.5) | copy-start | bytes 1572868
  1.3 16.4 %collective-permute-start.2 = (bf16[2112,128]{1,0:T(8,128)(2,1)S(1)}, bf16[2112,128]{1,0:T(8,128)(2,1)S(1)}, u32[]{:S(2)}, u32[]{:S(2)}) collective-permute-start(bf16[2112,128]{1,0:T(8,128)(2,1)S(1)} %pack_row.1.packed), channel_id=1, source_target_pairs={{0,4},{4,8},{8,12},{12,16},{16,20},{20,24},{24,28},{1,5},{5,9},{9,... | collective-permute-start | bytes 1622024 | tf_op jit(solution)/shard_map/ppermute | solution.py:440
  5.0 8.6 %collective-permute-start = (bf16[4,336,128]{2,1,0:T(8,128)(2,1)S(1)}, bf16[4,336,128]{2,1,0:T(8,128)(2,1)S(1)}, u32[]{:S(2)}, u32[]{:S(2)}) collective-permute-start(bf16[4,336,128]{2,1,0:T(8,128)(2,1)S(1)} %get-tuple-element.21), channel_id=1, source_target_pairs={{1,2},{2,1},{5,6},{6,5},{9,10},{10,9},{13,14},{14,13},{17,18},{18,... | collective-permute-start | bytes 1032200 | tf_op jit(solution)/shard_map/ppermute | solution.py:442
  6.9 6.6 %collective-permute-start.1 = (bf16[4,336,128]{2,1,0:T(8,128)(2,1)S(1)}, bf16[4,336,128]{2,1,0:T(8,128)(2,1)S(1)}, u32[]{:S(2)}, u32[]{:S(2)}) collective-permute-start(bf16[4,336,128]{2,1,0:T(8,128)(2,1)S(1)} %get-tuple-element.22), channel_id=1, source_target_pairs={{0,1},{2,3},{1,0},{3,2},{4,5},{6,7},{5,4},{7,6},{8,9},{10,11},{9,8... | collective-permute-start | bytes 1032200 | tf_op jit(solution)/shard_map/ppermute | solution.py:443
  13.6 9.6 %collective-permute-start.3 = (bf16[768,128]{1,0:T(8,128)(2,1)S(1)}, bf16[768,128]{1,0:T(8,128)(2,1)S(1)}, u32[]{:S(2)}, u32[]{:S(2)}) collective-permute-start(bf16[768,128]{1,0:T(8,128)(2,1)S(1)} %pack_rest.1), channel_id=1, source_target_pairs={{0,4},{4,8},{8,12},{12,16},{16,20},{20,24},{24,28},{1,5},{5,9},{9,... | collective-permute-start | bytes 589832 | tf_op jit(solution)/shard_map/ppermute | solution.py:446
  18.3 7.8 %collective-permute-start.4 = (bf16[8,64,128]{2,1,0:T(8,128)(2,1)S(1)}, bf16[8,64,128]{2,1,0:T(8,128)(2,1)S(1)}, u32[]{:S(2)}, u32[]{:S(2)}) collective-permute-start(bf16[8,64,128]{2,1,0:T(8,128)(2,1)S(1)} %get-tuple-element.33), channel_id=1, source_target_pairs={{4,0},{8,4},{12,8},{16,12},{20,16},{24,20},{28,24},{5,1},{9,5},{13... | collective-permute-start | bytes 393224 | tf_op jit(solution)/shard_map/ppermute | solution.py:448
  21.6 3.2 %collective-permute-start.5 = (f32[64,128]{1,0:T(8,128)S(1)}, f32[64,128]{1,0:T(8,128)S(1)}, u32[]{:S(2)}, u32[]{:S(2)}) collective-permute-start(f32[64,128]{1,0:T(8,128)S(1)} %get-tuple-element.34), channel_id=1, source_target_pairs={{0,1},{2,3},{1,0},{3,2},{4,5},{6,7},{5,4},{7,6},{8,9},{10,11},{9,8... | collective-permute-start | bytes 98312 | tf_op jit(solution)/shard_map/ppermute | solution.py:449

commit v13 on v12

--- a/solution.py
+++ b/solution.py
@@ -58,7 +58,8 @@
                     near.append((k, a + 1, b + k - 7))
         return near
 
-    def row(a, last):
+    for a in range(rows):
+        last = a == rows - 1
         on, which = live[a], index[a]
         for b in range(cols):
             near = ahead(a, b, last)
@@ -68,34 +69,26 @@
             for n, (k, _, _) in enumerate(near):
                 at = which[b, k]
                 rho = sym[at] if k == 4 else tapers[at]
-                held[b, :, (k - 4) * cells : (k - 3) * cells] = tapered(
+                held[a % 2, b, :, (k - 4) * cells : (k - 3) * cells] = tapered(
                     gram[:, n * cells : (n + 1) * cells], rho, on[b, k]
                 )
         for b in range(cols):
             near = ahead(a, b, last)
             total = dot(
                 cat([w[p, q] for _, p, q in near], 1),
-                cat([held[b, :, (k - 4) * cells : (k - 3) * cells] for k, _, _ in near], 1),
+                cat([held[a % 2, b, :, (k - 4) * cells : (k - 3) * cells] for k, _, _ in near], 1),
                 NT,
             )
-            if b > 0:
-                total += dot(w[a, b - 1], held[b - 1, :, cells : 2 * cells], NN)
-            out[a, b] += total
-            if not last:
-                back = [(k, b - (k - 7)) for k in (6, 7, 8) if 0 <= b - (k - 7) < cols]
-                out[a + 1, b] = dot(
-                    cat([w[a, q] for _, q in back], 1),
-                    cat([held[q, :, (k - 4) * cells : (k - 3) * cells] for k, q in back], 0),
+            behind = [(5, a, b - 1)] if b > 0 else []
+            if a > 0:
+                behind += [(k, a - 1, b - (k - 7)) for k in (6, 7, 8) if 0 <= b - (k - 7) < cols]
+            if behind:
+                total += dot(
+                    cat([w[p, q] for _, p, q in behind], 1),
+                    cat([held[p % 2, q, :, (k - 4) * cells : (k - 3) * cells] for k, p, q in behind], 0),
                     NN,
                 )
-
-    out[0] = jnp.zeros_like(out[0])
-
-    @pl.loop(0, rows - 1)
-    def _(a):
-        row(a, False)
-
-    row(rows - 1, True)
+            out[a, b] = total
 
 
 def inner(u, w, live, index, tapers):
@@ -113,7 +106,7 @@
         out_specs=(VMEM,) * 3,
         scratch_shapes=[
             pltpu.VMEM(tapers.shape, jnp.float32),
-            pltpu.VMEM((cols, cells, 5 * cells), jnp.bfloat16),
+            pltpu.VMEM((2, cols, cells, 5 * cells), jnp.bfloat16),
         ],
         compiler_params=pltpu.CompilerParams(vmem_limit_bytes=GRANT),
         cost_estimate=pl.CostEstimate(

time: 27.3 us -> 27.8 us (1.018); the launches traced: 26.8 us -> 27.6 us
  waiting for transfers between devices: 3.59 us -> 5.35 us
  Pallas kernels: 10.7 us -> 9.74 us
    ppermute x1, waiting for transfers between devices: 1.72 us -> 2.67 us  [body(): outside = lax.ppermute(outer_side, 'col', swaps('col', 1))]
    pallas_call x1, Pallas kernels: 4.83 us -> 3.88 us  [inner(): pl.pallas_call(inner_kernel, out_shape=(jax.ShapeDtypeStruct((rows, cols,...]
    ppermute x1, waiting for transfers between devices: 0.58 us -> 1.39 us  [body(): s = lax.ppermute(packed, 'row', forward('row'))]
  transfers between devices with their start and end apart: 6 -> 6, of which waited for: 3 -> 3; matrix products, arithmetic and copies ran while one was open for 0% -> 0% of each run, Pallas kernels for 33% -> 28%
where the time goes in v13:
time: 27.8 us; the launch traced here: 27.6 us
  starting transfers between devices  12.4 us (45%)
  Pallas kernels  9.74 us (35%)
  waiting for transfers between devices  5.35 us (19%)
    pallas_call x1, Pallas kernels, inner(): pl.pallas_call(inner_kernel, out_shape=(jax.ShapeDtypeStruct((rows, cols,...  3.88 us
    ppermute x1, starting transfers between devices, body(): s = lax.ppermute(packed, 'row', forward('row'))  3.56 us
    ppermute x1, starting transfers between devices, body(): lax.ppermute(pack_rest(w, outside, u.shape[2]), 'row', forward('row'))  3.43 us
    ppermute x1, starting transfers between devices, body(): back = lax.ppermute(back, 'row', backward('row'))  3.31 us
    ppermute x1, waiting for transfers between devices, body(): outside = lax.ppermute(outer_side, 'col', swaps('col', 1))  2.67 us
    ppermute x1, starting transfers between devices, body(): outside = lax.ppermute(outer_side, 'col', swaps('col', 1))  1.92 us
    pallas_call x1, Pallas kernels, outer(): pl.pallas_call(outer_kernel, out_shape=(jax.ShapeDtypeStruct(inc.shape, i...  1.57 us
    pallas_call x1, Pallas kernels, columns(): pl.pallas_call(columns_kernel, out_shape=jax.ShapeDtypeStruct((2, rows, w...  1.48 us
  transfers between devices with their start and end apart: 6, of which 3 were waited for; matrix products, arithmetic and copies ran while one was open for 0% of the time, Pallas kernels for 28%

profile of v13, /device:TPU:22, one launch (start us, length us, event | category | flops | bytes accessed | tf_op | source)
XLA Modules:
  0.0 27.6 jit_solution(5581793801942754907)
XLA Ops:
  0.0 0.0 copy-start.1
  0.0 0.0 copy-start
  0.0 0.0 copy-start.4
  0.0 0.0 copy-start.3
  0.0 1.2 %pack_row.1.packed = bf16[2112,128]{1,0:T(8,128)(2,1)S(1)} custom-call(bf16[4,8,256,128]{3,2,1,0:T(8,128)(2,1)} %u.9, bf16[4,8,64,128]{3,2,1,0:T(8,128)(2,1)} %w.11), custom_call_target="tpu_custom_call" | custom-call | bytes 1081344 | tf_op jit(solution)/shard_map/pack_row/pallas_call | solution.py:362
  1.2 0.0 copy-start.2
  1.3 3.6 %collective-permute-start.2 = (bf16[2112,128]{1,0:T(8,128)(2,1)S(1)}, bf16[2112,128]{1,0:T(8,128)(2,1)S(1)}, u32[]{:S(2)}, u32[]{:S(2)}) collective-permute-start(bf16[2112,128]{1,0:T(8,128)(2,1)S(1)} %pack_row.1.packed), channel_id=1, source_target_pairs={{0,4},{4,8},{8,12},{12,16},{16,20},{20,24},{24,28},{1,5},{5,9},{9,... | collective-permute-start | bytes 1622024 | tf_op jit(solution)/shard_map/ppermute | solution.py:433
  4.8 0.0 copy-done.1
  4.8 0.0 copy-done
  4.8 0.0 copy-done.4
  4.8 0.0 copy-done.3
  4.9 0.1 pack_columns.1
  5.0 1.9 %collective-permute-start = (bf16[4,336,128]{2,1,0:T(8,128)(2,1)S(1)}, bf16[4,336,128]{2,1,0:T(8,128)(2,1)S(1)}, u32[]{:S(2)}, u32[]{:S(2)}) collective-permute-start(bf16[4,336,128]{2,1,0:T(8,128)(2,1)S(1)} %get-tuple-element.21), channel_id=1, source_target_pairs={{1,2},{2,1},{5,6},{6,5},{9,10},{10,9},{13,14},{14,13},{17,18},{18,... | collective-permute-start | bytes 1032200 | tf_op jit(solution)/shard_map/ppermute | solution.py:435
  6.9 0.1 collective-permute-start.1
  7.0 0.0 copy-done.2
  7.0 3.9 %inner.1 = (f32[4,8,64,128]{3,2,1,0:T(8,128)S(1)}, bf16[4,8,128,256]{3,2,1,0:T(8,128)(2,1)S(1)}, bf16[16,128,128]{2,1,0:T(8,128)(2,1)S(1)}) custom-call(bf16[4,8,256,128]{3,2,1,0:T(8,128)(2,1)S(1)} %copy-done, bf16[4,8,64,128]{3,2,1,0:T(8,128)(2,1)S(1)} %copy-done.1, s32[4,8,9]{2,1,0:T(8,128)S(1)} %copy-done.3, s32[4,8,9]{2,1,0:T(8,128)S(1)} %copy-done.4, ...), custom_call_target="tpu_custom_call" | custom-call | flops 2013265920 | bytes 4194304 | tf_op jit(solution)/shard_map/inner/pallas_call | solution.py:98
  10.9 2.7 %collective-permute-done.outside = bf16[4,336,128]{2,1,0:T(8,128)(2,1)S(1)} collective-permute-done((bf16[4,336,128]{2,1,0:T(8,128)(2,1)S(1)}, bf16[4,336,128]{2,1,0:T(8,128)(2,1)S(1)}, u32[]{:S(2)}, u32[]{:S(2)}) %collective-permute-start) | collective-permute-done | bytes 344096 | tf_op jit(solution)/shard_map/ppermute | solution.py:435
  13.6 0.0 collective-permute-done.1.inside
  13.6 3.4 %collective-permute-start.3 = (bf16[768,128]{1,0:T(8,128)(2,1)S(1)}, bf16[768,128]{1,0:T(8,128)(2,1)S(1)}, u32[]{:S(2)}, u32[]{:S(2)}) collective-permute-start(bf16[768,128]{1,0:T(8,128)(2,1)S(1)} %pack_rest.1), channel_id=1, source_target_pairs={{0,4},{4,8},{8,12},{12,16},{16,20},{20,24},{24,28},{1,5},{5,9},{9,... | collective-permute-start | bytes 589832 | tf_op jit(solution)/shard_map/ppermute | solution.py:439
  17.0 1.4 %collective-permute-done.2.s = bf16[2112,128]{1,0:T(8,128)(2,1)S(1)} collective-permute-done((bf16[2112,128]{1,0:T(8,128)(2,1)S(1)}, bf16[2112,128]{1,0:T(8,128)(2,1)S(1)}, u32[]{:S(2)}, u32[]{:S(2)}) %collective-permute-start.2) | collective-permute-done | bytes 540704 | tf_op jit(solution)/shard_map/ppermute | solution.py:433
  18.4 0.7 %above.1 = (bf16[8,64,128]{2,1,0:T(8,128)(2,1)S(1)}, bf16[8,128,384]{2,1,0:T(8,128)(2,1)S(1)}, f32[64,128]{1,0:T(8,128)S(1)}, bf16[64,128]{1,0:T(8,128)(2,1)S(1)}) custom-call(bf16[2112,128]{1,0:T(8,128)(2,1)S(1)} %collective-permute-done.2.s, bf16[4,8,128,256]{3,2,1,0:T(8,128)(2,1)S(1)} %get-tuple-element.26.turned, bf16[4,8,64,128]{3,2,1,0:T(8,128)(2,1)S(1)} %copy-done.1, ...), custom_call_target="tpu_custom_call" | custom-call | flops 251658240 | bytes 2097152 | tf_op jit(solution)/shard_map/above/pallas_call | solution.py:163
  19.1 3.3 %collective-permute-start.4 = (bf16[8,64,128]{2,1,0:T(8,128)(2,1)S(1)}, bf16[8,64,128]{2,1,0:T(8,128)(2,1)S(1)}, u32[]{:S(2)}, u32[]{:S(2)}) collective-permute-start(bf16[8,64,128]{2,1,0:T(8,128)(2,1)S(1)} %get-tuple-element.33), channel_id=1, source_target_pairs={{4,0},{8,4},{12,8},{16,12},{20,16},{24,20},{28,24},{5,1},{9,5},{13... | collective-permute-start | bytes 393224 | tf_op jit(solution)/shard_map/ppermute | solution.py:441
  22.4 0.1 collective-permute-start.5
  22.5 1.5 %columns.1.side = f32[2,4,64,128]{3,2,1,0:T(8,128)S(1)} custom-call(bf16[4,8,256,128]{3,2,1,0:T(8,128)(2,1)S(1)} %copy-done, bf16[4,8,64,128]{3,2,1,0:T(8,128)(2,1)S(1)} %copy-done.1, bf16[4,336,128]{2,1,0:T(8,128)(2,1)S(1)} %collective-permute-done.1.inside, bf16[4,336,128]{2,1,0:T(8,128)(2,1)S(1)} %collective-permute-done.outside, ...), custom_call_target="tpu_custom_call" | custom-call | flops 251658240 | bytes 2097152 | tf_op jit(solution)/shard_map/columns/pallas_call | solution.py:233
  24.0 0.0 collective-permute-done.3.rest
  24.0 1.6 %outer.1 = (f32[4,8,64,128]{3,2,1,0:T(8,128)}, f32[2,64,128]{2,1,0:T(8,128)S(1)}, f32[8,64,128]{2,1,0:T(8,128)S(1)}) custom-call(f32[4,8,64,128]{3,2,1,0:T(8,128)S(1)} %get-tuple-element.23.inc, f32[2,4,64,128]{3,2,1,0:T(8,128)S(1)} %columns.1.side, bf16[8,128,384]{2,1,0:T(8,128)(2,1)S(1)} %get-tuple-element.28.held, ...), custom_call_target="tpu_custom_call" | custom-call | flops 50331648 | bytes 4194304 | tf_op jit(solution)/shard_map/outer/pallas_call | solution.py:282
  25.6 0.0 collective-permute-done.5.from_inside
  25.6 1.3 %collective-permute-done.4.back = bf16[8,64,128]{2,1,0:T(8,128)(2,1)S(1)} collective-permute-done((bf16[8,64,128]{2,1,0:T(8,128)(2,1)S(1)}, bf16[8,64,128]{2,1,0:T(8,128)(2,1)S(1)}, u32[]{:S(2)}, u32[]{:S(2)}) %collective-permute-start.4) | collective-permute-done | bytes 131104 | tf_op jit(solution)/shard_map/ppermute | solution.py:441
  26.9 0.7 %finish.1 = f32[4,8,64,128]{3,2,1,0:T(8,128)} custom-call(f32[4,8,64,128]{3,2,1,0:T(8,128)} %get-tuple-element.30.inc, f32[2,64,128]{2,1,0:T(8,128)S(1)} %get-tuple-element.31.top, f32[8,64,128]{2,1,0:T(8,128)S(1)} %get-tuple-element.32.low, bf16[8,64,128]{2,1,0:T(8,128)(2,1)S(1)} %collective-permute-done.4.back, ...), custom_call_target="tpu_custom_call", output_to_operand_aliasing={{}: (0, {})} | custom-call | flops 65536 | bytes 655360 | tf_op jit(solution)/shard_map/finish/pallas_call | solution.py:315
  (1 shorter events, 0.0 us)
Async XLA Ops:
  0.0 4.8 %copy-start.1 = (bf16[4,8,64,128]{3,2,1,0:T(8,128)(2,1)S(1)}, bf16[4,8,64,128]{3,2,1,0:T(8,128)(2,1)}, u32[]{:S(2)}) copy-start(bf16[4,8,64,128]{3,2,1,0:T(8,128)(2,1)} %w.11) | copy-start | bytes 1572868
  0.0 4.8 %copy-start = (bf16[4,8,256,128]{3,2,1,0:T(8,128)(2,1)S(1)}, bf16[4,8,256,128]{3,2,1,0:T(8,128)(2,1)}, u32[]{:S(2)}) copy-start(bf16[4,8,256,128]{3,2,1,0:T(8,128)(2,1)} %u.9) | copy-start | bytes 6291460
  0.0 4.8 %copy-start.4 = (s32[4,8,9]{2,1,0:T(8,128)S(1)}, s32[4,8,9]{2,1,0:T(8,128)}, u32[]{:S(2)}) copy-start(s32[4,8,9]{2,1,0:T(8,128)} %index.9) | copy-start | bytes 3460
  0.0 4.8 %copy-start.3 = (s32[4,8,9]{2,1,0:T(8,128)S(1)}, s32[4,8,9]{2,1,0:T(8,128)}, u32[]{:S(2)}) copy-start(s32[4,8,9]{2,1,0:T(8,128)} %live.9) | copy-start | bytes 3460
  1.2 5.8 %copy-start.2 = (bf16[16,128,128]{2,1,0:T(8,128)(2,1)S(1)}, bf16[16,128,128]{2,1,0:T(8,128)(2,1)}, u32[]{:S(2)}) copy-start(bf16[16,128,128]{2,1,0:T(8,128)(2,1)} %tapers.5) | copy-start | bytes 1572868
  1.3 17.2 %collective-permute-start.2 = (bf16[2112,128]{1,0:T(8,128)(2,1)S(1)}, bf16[2112,128]{1,0:T(8,128)(2,1)S(1)}, u32[]{:S(2)}, u32[]{:S(2)}) collective-permute-start(bf16[2112,128]{1,0:T(8,128)(2,1)S(1)} %pack_row.1.packed), channel_id=1, source_target_pairs={{0,4},{4,8},{8,12},{12,16},{16,20},{20,24},{24,28},{1,5},{5,9},{9,... | collective-permute-start | bytes 1622024 | tf_op jit(solution)/shard_map/ppermute | solution.py:433
  5.0 8.6 %collective-permute-start = (bf16[4,336,128]{2,1,0:T(8,128)(2,1)S(1)}, bf16[4,336,128]{2,1,0:T(8,128)(2,1)S(1)}, u32[]{:S(2)}, u32[]{:S(2)}) collective-permute-start(bf16[4,336,128]{2,1,0:T(8,128)(2,1)S(1)} %get-tuple-element.21), channel_id=1, source_target_pairs={{1,2},{2,1},{5,6},{6,5},{9,10},{10,9},{13,14},{14,13},{17,18},{18,... | collective-permute-start | bytes 1032200 | tf_op jit(solution)/shard_map/ppermute | solution.py:435
  6.9 6.6 %collective-permute-start.1 = (bf16[4,336,128]{2,1,0:T(8,128)(2,1)S(1)}, bf16[4,336,128]{2,1,0:T(8,128)(2,1)S(1)}, u32[]{:S(2)}, u32[]{:S(2)}) collective-permute-start(bf16[4,336,128]{2,1,0:T(8,128)(2,1)S(1)} %get-tuple-element.22), channel_id=1, source_target_pairs={{0,1},{2,3},{1,0},{3,2},{4,5},{6,7},{5,4},{7,6},{8,9},{10,11},{9,8... | collective-permute-start | bytes 1032200 | tf_op jit(solution)/shard_map/ppermute | solution.py:436
  13.6 10.4 %collective-permute-start.3 = (bf16[768,128]{1,0:T(8,128)(2,1)S(1)}, bf16[768,128]{1,0:T(8,128)(2,1)S(1)}, u32[]{:S(2)}, u32[]{:S(2)}) collective-permute-start(bf16[768,128]{1,0:T(8,128)(2,1)S(1)} %pack_rest.1), channel_id=1, source_target_pairs={{0,4},{4,8},{8,12},{12,16},{16,20},{20,24},{24,28},{1,5},{5,9},{9,... | collective-permute-start | bytes 589832 | tf_op jit(solution)/shard_map/ppermute | solution.py:439
  19.1 7.8 %collective-permute-start.4 = (bf16[8,64,128]{2,1,0:T(8,128)(2,1)S(1)}, bf16[8,64,128]{2,1,0:T(8,128)(2,1)S(1)}, u32[]{:S(2)}, u32[]{:S(2)}) collective-permute-start(bf16[8,64,128]{2,1,0:T(8,128)(2,1)S(1)} %get-tuple-element.33), channel_id=1, source_target_pairs={{4,0},{8,4},{12,8},{16,12},{20,16},{24,20},{28,24},{5,1},{9,5},{13... | collective-permute-start | bytes 393224 | tf_op jit(solution)/shard_map/ppermute | solution.py:441
  22.4 3.2 %collective-permute-start.5 = (f32[64,128]{1,0:T(8,128)S(1)}, f32[64,128]{1,0:T(8,128)S(1)}, u32[]{:S(2)}, u32[]{:S(2)}) collective-permute-start(f32[64,128]{1,0:T(8,128)S(1)} %get-tuple-element.34), channel_id=1, source_target_pairs={{0,1},{2,3},{1,0},{3,2},{4,5},{6,7},{5,4},{7,6},{8,9},{10,11},{9,8... | collective-permute-start | bytes 98312 | tf_op jit(solution)/shard_map/ppermute | solution.py:442

commit v14 on v13

--- a/solution.py
+++ b/solution.py
@@ -1,3 +1,5 @@
+import functools
+
 import jax
 import jax.numpy as jnp
 from jax import lax
@@ -180,70 +182,48 @@
     )(s, turned, w, inside, outside, live, index, flipped)
 
 
-def columns_kernel(u, w, inside, outside, live, index, tapers, side):
-    rows, cols, members, cells = u.shape
+def column_kernel(outward, near, turned, w, live, index, tapers, flipped, side):
+    rows, cols, cells, members = turned.shape
     deep = members + w.shape[2]
     last = cols - 1
-    left, right = sides(inside, outside)
-    on = [live[a] for a in range(rows)]
-    which = [index[a] for a in range(rows)]
-    total = {}
-
-    def add(a, q, value):
-        total[a, q] = total[a, q] + value if (a, q) in total else value
-
+    on_left = even_column() if outward else jnp.logical_not(even_column())
+    b = jnp.where(on_left, 0, last)
     for a in range(rows):
-        near = [(5, a)] + ([(8, a + 1)] if a + 1 < rows else [])
-        gram = dot(left(a, slice(0, members)), cat([u[p, 0] for _, p in near], 1), TN)
-        blocks = cat(
-            [
-                tapered(gram[:, n * cells : (n + 1) * cells], tapers[which[p][0, 8 - k]], on[p][0, 8 - k])
-                for n, (k, p) in enumerate(near)
-            ],
-            1,
-        )
-        both = dot(left(a, slice(members, deep)), blocks, NN)
-        for n, (_, p) in enumerate(near):
-            add(p, 0, both[:, n * cells : (n + 1) * cells])
-        gram = dot(u[a, last], cat([right(p, slice(0, members)) for _, p in near], 1), TN)
-        blocks = cat(
-            [
-                tapered(gram[:, n * cells : (n + 1) * cells], tapers[which[a][last, k]], on[a][last, k])
-                for n, (k, _) in enumerate(near)
-            ],
-            1,
-        )
-        add(a, last, dot(cat([right(p, slice(members, deep)) for _, p in near], 1), blocks, NT))
-        if a + 1 < rows:
-            gram = dot(u[a, 0], left(a + 1, slice(0, members)), TN)
-            block = tapered(gram, tapers[which[a][0, 6]], on[a][0, 6])
-            add(a, 0, dot(left(a + 1, slice(members, deep)), block, NT))
-            gram = dot(right(a, slice(0, members)), u[a + 1, last], TN)
-            block = tapered(gram, tapers[which[a + 1][last, 2]], on[a + 1][last, 2])
-            add(a + 1, last, dot(right(a, slice(members, deep)), block, NN))
-
-    for a in range(rows):
-        side[0, a] = total[a, 0]
-        side[1, a] = total[a, last]
-
-
-def columns(u, w, inside, outside, live, index, tapers):
-    rows, _, members, cells = u.shape
+        on, which = live[a], index[a]
+        around = [q for q in (a - 1, a, a + 1) if 0 <= q < rows]
+        gram = dot(turned[a, b], cat([near[q, :members] for q in around], 1), NN)
+        blocks = []
+        for n, q in enumerate(around):
+            k = 3 * (q - a + 1)
+            at = jnp.where(on_left, which[0, k], which[last, k + 2])
+            if q < a:
+                rho = flipped[at]
+            elif q > a:
+                rho = tapers[at]
+            else:
+                rho = jnp.where(on_left, flipped[at], tapers[at])
+            lively = jnp.where(on_left, on[0, k], on[last, k + 2])
+            blocks.append(tapered(gram[:, n * cells : (n + 1) * cells], rho, lively))
+        side[a] = dot(cat([near[q, members:deep] for q in around], 1), cat(blocks, 1), NT)
+
+
+def column(near, turned, w, live, index, tapers, flipped, outward):
+    rows, _, cells, members = turned.shape
     width = w.shape[2]
     return pl.pallas_call(
-        columns_kernel,
-        out_shape=jax.ShapeDtypeStruct((2, rows, width, cells), jnp.float32),
+        functools.partial(column_kernel, outward),
+        out_shape=jax.ShapeDtypeStruct((rows, width, cells), jnp.float32),
         in_specs=[VMEM] * 7,
         out_specs=VMEM,
         compiler_params=pltpu.CompilerParams(vmem_limit_bytes=GRANT),
         cost_estimate=pl.CostEstimate(
-            flops=12 * rows * cells * cells * (members + width), bytes_accessed=2 << 20, transcendentals=0
-        ),
-        name="columns",
-    )(u, w, inside, outside, live, index, tapers)
-
-
-def outer_kernel(inc, side, held, tail, rest, u, live, index, tapers, out, top, low):
+            flops=6 * rows * cells * cells * (members + width), bytes_accessed=2 << 20, transcendentals=0
+        ),
+        name="column",
+    )(near, turned, w, live, index, tapers, flipped)
+
+
+def outer_kernel(inc, near_side, far_side, held, tail, rest, plain, u, live, index, tapers, out, top, low):
     rows, cols, members, cells = u.shape
     width = inc.shape[2]
     last = cols - 1
@@ -255,29 +235,37 @@
     block = tapered(gram, tapers[at], jnp.where(even, on[0, 0], on[last, 2]))
     far = dot(rest[start + members :], block, NN)
     blank = jnp.zeros_like(far)
+
+    def side(q, a):
+        near, other = near_side[a], far_side[a]
+        return jnp.where(even, other, near) if q == 0 else jnp.where(even, near, other)
+
     parts = [rest[c * width : (c + 1) * width] for c in range(cols - 1)]
     tail = tail[...]
     weights = [jnp.where(even, parts[0], tail)]
     weights += [jnp.where(even, parts[c], parts[c - 1]) for c in range(1, last)]
     weights.append(jnp.where(even, tail, parts[last - 1]))
+    place = lax.axis_index("col")
+    alone = jnp.logical_or(place == 0, place == lax.axis_size("col") - 1)
+    weights = [jnp.where(alone, plain[c], weight) for c, weight in enumerate(weights)]
     for q in range(cols):
         near = [c for c in (q - 1, q, q + 1) if 0 <= c < cols]
         block = held[q, :, (1 + near[0] - q) * cells : (2 + near[-1] - q) * cells]
         value = inc[0, q] + dot(cat([weights[c] for c in near], 1), block, NT)
         if q in (0, last):
-            value += side[q // last, 0]
+            value += side(q, 0)
             value += jnp.where(even, far, blank) if q == 0 else jnp.where(even, blank, far)
             top[q // last] = value
         out[0, q] = value
     for a in range(1, rows):
         for q in range(cols):
-            value = inc[a, q] + side[q // last, a] if q in (0, last) else inc[a, q]
+            value = inc[a, q] + side(q, a) if q in (0, last) else inc[a, q]
             out[a, q] = value
             if a == rows - 1:
                 low[q] = value
 
 
-def outer(inc, side, held, tail, rest, u, live, index, tapers):
+def outer(inc, near_side, far_side, held, tail, rest, plain, u, live, index, tapers):
     rows, cols, width, cells = inc.shape
     return pl.pallas_call(
         outer_kernel,
@@ -286,12 +274,12 @@
             jax.ShapeDtypeStruct((2, width, cells), inc.dtype),
             jax.ShapeDtypeStruct(inc.shape[1:], inc.dtype),
         ),
-        in_specs=[VMEM] * 9,
+        in_specs=[VMEM] * 11,
         out_specs=(VMEM,) * 3,
         compiler_params=pltpu.CompilerParams(vmem_limit_bytes=GRANT),
         cost_estimate=pl.CostEstimate(flops=6 * cols * cells * cells * width, bytes_accessed=4 << 20, transcendentals=0),
         name="outer",
-    )(inc, side, held, tail, rest, u, live, index, tapers)
+    )(inc, near_side, far_side, held, tail, rest, plain, u, live, index, tapers)
 
 
 def finish_kernel(inc, top, low, back, from_inside, out, end, total, sem):
@@ -370,22 +358,26 @@
     )(u, w)
 
 
-def pack_rest_kernel(w, outside, out):
+def pack_rest_kernel(w, outside, out, plain):
     rows, cols, width, _ = w.shape
     skip = 1 - even_column().astype(jnp.int32)
     for q in range(cols - 1):
         out[q * width : (q + 1) * width] = w[rows - 1, q + skip]
     start = (cols - 1) * width
     out[start:] = outside[rows - 1, : out.shape[0] - start]
+    plain[...] = w[rows - 1]
 
 
 def pack_rest(w, outside, members):
     _, cols, width, cells = w.shape
     return pl.pallas_call(
         pack_rest_kernel,
-        out_shape=jax.ShapeDtypeStruct(((cols - 1) * width + members + width, cells), w.dtype),
+        out_shape=(
+            jax.ShapeDtypeStruct(((cols - 1) * width + members + width, cells), w.dtype),
+            jax.ShapeDtypeStruct((cols, width, cells), w.dtype),
+        ),
         in_specs=[VMEM, VMEM],
-        out_specs=VMEM,
+        out_specs=(VMEM, VMEM),
         compiler_params=pltpu.CompilerParams(vmem_limit_bytes=GRANT),
         cost_estimate=pl.CostEstimate(flops=0, bytes_accessed=8 * cols * width * cells, transcendentals=0),
         name="pack_rest",
@@ -428,7 +420,13 @@
     )(u, w, live, index, packed)
 
 
+def down(row, col, chosen):
+    wide = lax.axis_size(col)
+    return [(r * wide + c, (r + 1) * wide + c) for r in range(lax.axis_size(row) - 1) for c in chosen]
+
+
 def body(u, w, live, index, tapers):
+    wide = lax.axis_size("col")
     packed = pack_row(u, w)
     s = lax.ppermute(packed, "row", forward("row"))
     inner_side, outer_side = pack_columns(u, w, live, index, packed)
@@ -436,12 +434,15 @@
     inside = lax.ppermute(inner_side, "col", swaps("col", 0))
     inc, turned, flipped = inner(u, w, live, index, tapers)
     inc, outside, inside = lax.optimization_barrier((inc, outside, inside))
-    rest = lax.ppermute(pack_rest(w, outside, u.shape[2]), "row", forward("row"))
+    rest, plain = pack_rest(w, outside, u.shape[2])
+    rest = lax.ppermute(rest, ("row", "col"), down("row", "col", range(1, wide - 1)))
+    plain = lax.ppermute(plain, ("row", "col"), down("row", "col", sorted({0, wide - 1})))
     back, held, to_inside, tail = above(s, turned, w, inside, outside, live, index, flipped)
     back = lax.ppermute(back, "row", backward("row"))
     from_inside = lax.ppermute(to_inside, "col", swaps("col", 0))
-    side = columns(u, w, inside, outside, live, index, tapers)
-    inc, top, low = outer(inc, side, held, tail, rest, u, live, index, tapers)
+    near_side = column(inside, turned, w, live, index, tapers, flipped, False)
+    far_side = column(outside, turned, w, live, index, tapers, flipped, True)
+    inc, top, low = outer(inc, near_side, far_side, held, tail, rest, plain, u, live, index, tapers)
     return finish(inc, top, low, back, from_inside)
 
 

time: 27.8 us -> 28 us (level)
  the two profiles are of different devices: /device:TPU:22 before, /device:TPU:0 now
where the time goes in v14:
time: 28 us; the launch traced here: 27.8 us
  starting transfers between devices  15 us (54%)
  Pallas kernels  9.78 us (35%)
  waiting for transfers between devices  2.83 us (10%)
    ppermute x1, starting transfers between devices, body(): s = lax.ppermute(packed, 'row', forward('row'))  5.05 us
    pallas_call x1, Pallas kernels, inner(): pl.pallas_call(inner_kernel, out_shape=(jax.ShapeDtypeStruct((rows, cols,...  3.88 us
    ppermute x1, starting transfers between devices, body(): lax.ppermute(plain, ('row', 'col'), down('row', 'col', sorted({0, wide -...  3.41 us
    ppermute x1, starting transfers between devices, body(): inside = lax.ppermute(inner_side, 'col', swaps('col', 0))  2.9 us
    ppermute x1, waiting for transfers between devices, body(): back = lax.ppermute(back, 'row', backward('row'))  2.8 us
    pallas_call x1, Pallas kernels, outer(): pl.pallas_call(outer_kernel, out_shape=(jax.ShapeDtypeStruct(inc.shape, i...  1.57 us
    pallas_call x2, Pallas kernels, column(): pl.pallas_call(functools.partial(column_kernel, outward), out_shape=jax.S...  1.52 us
    ppermute x1, starting transfers between devices, body(): back = lax.ppermute(back, 'row', backward('row'))  1.29 us
  transfers between devices with their start and end apart: 7, of which 1 were waited for; matrix products, arithmetic and copies ran while one was open for 0% of the time, Pallas kernels for 28%

profile of v14, /device:TPU:0, one launch (start us, length us, event | category | flops | bytes accessed | tf_op | source)
XLA Modules:
  0.0 27.8 jit_solution(928830386383602015)
XLA Ops:
  0.0 0.0 copy-start
  0.0 0.0 copy-start.1
  0.0 0.0 copy-start.3
  0.0 0.0 copy-start.4
  0.0 1.2 %pack_row.1.packed = bf16[2112,128]{1,0:T(8,128)(2,1)S(1)} custom-call(bf16[4,8,256,128]{3,2,1,0:T(8,128)(2,1)} %u.7, bf16[4,8,64,128]{3,2,1,0:T(8,128)(2,1)} %w.13), custom_call_target="tpu_custom_call" | custom-call | bytes 1081344 | tf_op jit(solution)/shard_map/pack_row/pallas_call | solution.py:350
  1.2 0.0 copy-start.2
  1.2 5.0 %collective-permute-start.2 = (bf16[2112,128]{1,0:T(8,128)(2,1)S(1)}, bf16[2112,128]{1,0:T(8,128)(2,1)S(1)}, u32[]{:S(2)}, u32[]{:S(2)}) collective-permute-start(bf16[2112,128]{1,0:T(8,128)(2,1)S(1)} %pack_row.1.packed), channel_id=1, source_target_pairs={{0,4},{4,8},{8,12},{12,16},{16,20},{20,24},{24,28},{1,5},{5,9},{9,... | collective-permute-start | bytes 1622024 | tf_op jit(solution)/shard_map/ppermute | solution.py:431
  6.3 0.0 copy-done
  6.3 0.0 copy-done.1
  6.3 0.0 copy-done.3
  6.3 0.0 copy-done.4
  6.3 0.1 pack_columns.1
  6.5 0.7 %collective-permute-start = (bf16[4,336,128]{2,1,0:T(8,128)(2,1)S(1)}, bf16[4,336,128]{2,1,0:T(8,128)(2,1)S(1)}, u32[]{:S(2)}, u32[]{:S(2)}) collective-permute-start(bf16[4,336,128]{2,1,0:T(8,128)(2,1)S(1)} %get-tuple-element.23), channel_id=1, source_target_pairs={{1,2},{2,1},{5,6},{6,5},{9,10},{10,9},{13,14},{14,13},{17,18},{18,... | collective-permute-start | bytes 1032200 | tf_op jit(solution)/shard_map/ppermute | solution.py:433
  7.2 2.9 %collective-permute-start.1 = (bf16[4,336,128]{2,1,0:T(8,128)(2,1)S(1)}, bf16[4,336,128]{2,1,0:T(8,128)(2,1)S(1)}, u32[]{:S(2)}, u32[]{:S(2)}) collective-permute-start(bf16[4,336,128]{2,1,0:T(8,128)(2,1)S(1)} %get-tuple-element.24), channel_id=1, source_target_pairs={{0,1},{2,3},{1,0},{3,2},{4,5},{6,7},{5,4},{7,6},{8,9},{10,11},{9,8... | collective-permute-start | bytes 1032200 | tf_op jit(solution)/shard_map/ppermute | solution.py:434
  10.1 0.0 copy-done.2
  10.1 3.9 %inner.1 = (f32[4,8,64,128]{3,2,1,0:T(8,128)S(1)}, bf16[4,8,128,256]{3,2,1,0:T(8,128)(2,1)S(1)}, bf16[16,128,128]{2,1,0:T(8,128)(2,1)S(1)}) custom-call(bf16[4,8,256,128]{3,2,1,0:T(8,128)(2,1)S(1)} %copy-done, bf16[4,8,64,128]{3,2,1,0:T(8,128)(2,1)S(1)} %copy-done.1, s32[4,8,9]{2,1,0:T(8,128)S(1)} %copy-done.3, s32[4,8,9]{2,1,0:T(8,128)S(1)} %copy-done.4, ...), custom_call_target="tpu_custom_call" | custom-call | flops 2013265920 | bytes 4194304 | tf_op jit(solution)/shard_map/inner/pallas_call | solution.py:100
  14.0 0.0 collective-permute-done.near.outside
  14.0 0.0 collective-permute-done.1.near.inside
  14.0 0.7 %collective-permute-start.3 = (bf16[768,128]{1,0:T(8,128)(2,1)S(1)}, bf16[768,128]{1,0:T(8,128)(2,1)S(1)}, u32[]{:S(2)}, u32[]{:S(2)}) collective-permute-start(bf16[768,128]{1,0:T(8,128)(2,1)S(1)} %get-tuple-element.32), channel_id=1, source_target_pairs={{1,5},{2,6},{5,9},{6,10},{9,13},{10,14},{13,17},{14,18},{17,21},{1... | collective-permute-start | bytes 589832 | tf_op jit(solution)/shard_map/ppermute | solution.py:438
  14.7 3.4 %collective-permute-start.4 = (bf16[8,64,128]{2,1,0:T(8,128)(2,1)S(1)}, bf16[8,64,128]{2,1,0:T(8,128)(2,1)S(1)}, u32[]{:S(2)}, u32[]{:S(2)}) collective-permute-start(bf16[8,64,128]{2,1,0:T(8,128)(2,1)S(1)} %get-tuple-element.33), channel_id=1, source_target_pairs={{0,4},{3,7},{4,8},{7,11},{8,12},{11,15},{12,16},{15,19},{16,20},{1... | collective-permute-start | bytes 393224 | tf_op jit(solution)/shard_map/ppermute | solution.py:439
  18.1 0.0 collective-permute-done.2.s
  18.1 0.7 %above.1 = (bf16[8,64,128]{2,1,0:T(8,128)(2,1)S(1)}, bf16[8,128,384]{2,1,0:T(8,128)(2,1)S(1)}, f32[64,128]{1,0:T(8,128)S(1)}, bf16[64,128]{1,0:T(8,128)(2,1)S(1)}) custom-call(bf16[2112,128]{1,0:T(8,128)(2,1)S(1)} %collective-permute-done.2.s, bf16[4,8,128,256]{3,2,1,0:T(8,128)(2,1)S(1)} %get-tuple-element.27.turned, bf16[4,8,64,128]{3,2,1,0:T(8,128)(2,1)S(1)} %copy-done.1, ...), custom_call_target="tpu_custom_call" | custom-call | flops 251658240 | bytes 2097152 | tf_op jit(solution)/shard_map/above/pallas_call | solution.py:165
  18.8 1.3 %collective-permute-start.5 = (bf16[8,64,128]{2,1,0:T(8,128)(2,1)S(1)}, bf16[8,64,128]{2,1,0:T(8,128)(2,1)S(1)}, u32[]{:S(2)}, u32[]{:S(2)}) collective-permute-start(bf16[8,64,128]{2,1,0:T(8,128)(2,1)S(1)} %get-tuple-element.37), channel_id=1, source_target_pairs={{4,0},{8,4},{12,8},{16,12},{20,16},{24,20},{28,24},{5,1},{9,5},{13... | collective-permute-start | bytes 393224 | tf_op jit(solution)/shard_map/ppermute | solution.py:441
  20.1 1.0 %collective-permute-start.6 = (f32[64,128]{1,0:T(8,128)S(1)}, f32[64,128]{1,0:T(8,128)S(1)}, u32[]{:S(2)}, u32[]{:S(2)}) collective-permute-start(f32[64,128]{1,0:T(8,128)S(1)} %get-tuple-element.38), channel_id=1, source_target_pairs={{0,1},{2,3},{1,0},{3,2},{4,5},{6,7},{5,4},{7,6},{8,9},{10,11},{9,8... | collective-permute-start | bytes 98312 | tf_op jit(solution)/shard_map/ppermute | solution.py:442
  21.1 0.7 %column.3.far_side = f32[4,64,128]{2,1,0:T(8,128)S(1)} custom-call(bf16[4,336,128]{2,1,0:T(8,128)(2,1)S(1)} %collective-permute-done.near.outside, bf16[4,8,128,256]{3,2,1,0:T(8,128)(2,1)S(1)} %get-tuple-element.27.turned, bf16[4,8,64,128]{3,2,1,0:T(8,128)(2,1)S(1)} %copy-done.1, s32[4,8,9]{2,1,0:T(8,128)S(1)} %copy-done.3, s32[4,8,9]{2,1,0:T(8,128)S(1)} %copy-done.4, ...), custom_call_target="tpu_custom_call" | custom-call | flops 125829120 | bytes 2097152 | tf_op jit(solution)/shard_map/column/pallas_call | solution.py:213
  21.9 0.8 %column.2.near_side = f32[4,64,128]{2,1,0:T(8,128)S(1)} custom-call(bf16[4,336,128]{2,1,0:T(8,128)(2,1)S(1)} %collective-permute-done.1.near.inside, bf16[4,8,128,256]{3,2,1,0:T(8,128)(2,1)S(1)} %get-tuple-element.27.turned, bf16[4,8,64,128]{3,2,1,0:T(8,128)(2,1)S(1)} %copy-done.1, s32[4,8,9]{2,1,0:T(8,128)S(1)} %copy-done.3, s32[4,8,9]{2,1,0:T(8,128)S(1)} %copy-done.4, ...), custom_call_target="tpu_custom_call" | custom-call | flops 125829120 | bytes 2097152 | tf_op jit(solution)/shard_map/column/pallas_call | solution.py:213
  22.6 0.0 collective-permute-done.4.plain
  22.7 0.0 collective-permute-done.3.rest
  22.7 1.6 %outer.1 = (f32[4,8,64,128]{3,2,1,0:T(8,128)}, f32[2,64,128]{2,1,0:T(8,128)S(1)}, f32[8,64,128]{2,1,0:T(8,128)S(1)}) custom-call(f32[4,8,64,128]{3,2,1,0:T(8,128)S(1)} %get-tuple-element.25.inc, f32[4,64,128]{2,1,0:T(8,128)S(1)} %column.2.near_side, f32[4,64,128]{2,1,0:T(8,128)S(1)} %column.3.far_side, bf16[8,128,384]{2,1,0:T(8,128)(2,1)S(1)} %get-tuple-element.30.held, ...), custom_call_target="tpu_custom_call" | custom-call | flops 50331648 | bytes 4194304 | tf_op jit(solution)/shard_map/outer/pallas_call | solution.py:270
  24.3 0.0 collective-permute-done.6.from_inside
  24.3 2.8 %collective-permute-done.5.back = bf16[8,64,128]{2,1,0:T(8,128)(2,1)S(1)} collective-permute-done((bf16[8,64,128]{2,1,0:T(8,128)(2,1)S(1)}, bf16[8,64,128]{2,1,0:T(8,128)(2,1)S(1)}, u32[]{:S(2)}, u32[]{:S(2)}) %collective-permute-start.5) | collective-permute-done | bytes 131104 | tf_op jit(solution)/shard_map/ppermute | solution.py:441
  27.1 0.7 %finish.1 = f32[4,8,64,128]{3,2,1,0:T(8,128)} custom-call(f32[4,8,64,128]{3,2,1,0:T(8,128)} %get-tuple-element.34.inc, f32[2,64,128]{2,1,0:T(8,128)S(1)} %get-tuple-element.35.top, f32[8,64,128]{2,1,0:T(8,128)S(1)} %get-tuple-element.36.low, bf16[8,64,128]{2,1,0:T(8,128)(2,1)S(1)} %collective-permute-done.5.back, ...), custom_call_target="tpu_custom_call", output_to_operand_aliasing={{}: (0, {})} | custom-call | flops 65536 | bytes 655360 | tf_op jit(solution)/shard_map/finish/pallas_call | solution.py:303
  (1 shorter events, 0.0 us)
Async XLA Ops:
  0.0 6.3 %copy-start = (bf16[4,8,256,128]{3,2,1,0:T(8,128)(2,1)S(1)}, bf16[4,8,256,128]{3,2,1,0:T(8,128)(2,1)}, u32[]{:S(2)}) copy-start(bf16[4,8,256,128]{3,2,1,0:T(8,128)(2,1)} %u.7) | copy-start | bytes 6291460
  0.0 6.3 %copy-start.1 = (bf16[4,8,64,128]{3,2,1,0:T(8,128)(2,1)S(1)}, bf16[4,8,64,128]{3,2,1,0:T(8,128)(2,1)}, u32[]{:S(2)}) copy-start(bf16[4,8,64,128]{3,2,1,0:T(8,128)(2,1)} %w.13) | copy-start | bytes 1572868
  0.0 6.3 %copy-start.3 = (s32[4,8,9]{2,1,0:T(8,128)S(1)}, s32[4,8,9]{2,1,0:T(8,128)}, u32[]{:S(2)}) copy-start(s32[4,8,9]{2,1,0:T(8,128)} %live.11) | copy-start | bytes 3460
  0.0 6.3 %copy-start.4 = (s32[4,8,9]{2,1,0:T(8,128)S(1)}, s32[4,8,9]{2,1,0:T(8,128)}, u32[]{:S(2)}) copy-start(s32[4,8,9]{2,1,0:T(8,128)} %index.11) | copy-start | bytes 3460
  1.2 8.9 %copy-start.2 = (bf16[16,128,128]{2,1,0:T(8,128)(2,1)S(1)}, bf16[16,128,128]{2,1,0:T(8,128)(2,1)}, u32[]{:S(2)}) copy-start(bf16[16,128,128]{2,1,0:T(8,128)(2,1)} %tapers.7) | copy-start | bytes 1572868
  1.2 16.9 %collective-permute-start.2 = (bf16[2112,128]{1,0:T(8,128)(2,1)S(1)}, bf16[2112,128]{1,0:T(8,128)(2,1)S(1)}, u32[]{:S(2)}, u32[]{:S(2)}) collective-permute-start(bf16[2112,128]{1,0:T(8,128)(2,1)S(1)} %pack_row.1.packed), channel_id=1, source_target_pairs={{0,4},{4,8},{8,12},{12,16},{16,20},{20,24},{24,28},{1,5},{5,9},{9,... | collective-permute-start | bytes 1622024 | tf_op jit(solution)/shard_map/ppermute | solution.py:431
  6.5 7.5 %collective-permute-start = (bf16[4,336,128]{2,1,0:T(8,128)(2,1)S(1)}, bf16[4,336,128]{2,1,0:T(8,128)(2,1)S(1)}, u32[]{:S(2)}, u32[]{:S(2)}) collective-permute-start(bf16[4,336,128]{2,1,0:T(8,128)(2,1)S(1)} %get-tuple-element.23), channel_id=1, source_target_pairs={{1,2},{2,1},{5,6},{6,5},{9,10},{10,9},{13,14},{14,13},{17,18},{18,... | collective-permute-start | bytes 1032200 | tf_op jit(solution)/shard_map/ppermute | solution.py:433
  7.2 6.8 %collective-permute-start.1 = (bf16[4,336,128]{2,1,0:T(8,128)(2,1)S(1)}, bf16[4,336,128]{2,1,0:T(8,128)(2,1)S(1)}, u32[]{:S(2)}, u32[]{:S(2)}) collective-permute-start(bf16[4,336,128]{2,1,0:T(8,128)(2,1)S(1)} %get-tuple-element.24), channel_id=1, source_target_pairs={{0,1},{2,3},{1,0},{3,2},{4,5},{6,7},{5,4},{7,6},{8,9},{10,11},{9,8... | collective-permute-start | bytes 1032200 | tf_op jit(solution)/shard_map/ppermute | solution.py:434
  14.0 8.7 %collective-permute-start.3 = (bf16[768,128]{1,0:T(8,128)(2,1)S(1)}, bf16[768,128]{1,0:T(8,128)(2,1)S(1)}, u32[]{:S(2)}, u32[]{:S(2)}) collective-permute-start(bf16[768,128]{1,0:T(8,128)(2,1)S(1)} %get-tuple-element.32), channel_id=1, source_target_pairs={{1,5},{2,6},{5,9},{6,10},{9,13},{10,14},{13,17},{14,18},{17,21},{1... | collective-permute-start | bytes 589832 | tf_op jit(solution)/shard_map/ppermute | solution.py:438
  14.7 8.0 %collective-permute-start.4 = (bf16[8,64,128]{2,1,0:T(8,128)(2,1)S(1)}, bf16[8,64,128]{2,1,0:T(8,128)(2,1)S(1)}, u32[]{:S(2)}, u32[]{:S(2)}) collective-permute-start(bf16[8,64,128]{2,1,0:T(8,128)(2,1)S(1)} %get-tuple-element.33), channel_id=1, source_target_pairs={{0,4},{3,7},{4,8},{7,11},{8,12},{11,15},{12,16},{15,19},{16,20},{1... | collective-permute-start | bytes 393224 | tf_op jit(solution)/shard_map/ppermute | solution.py:439
  18.8 8.2 %collective-permute-start.5 = (bf16[8,64,128]{2,1,0:T(8,128)(2,1)S(1)}, bf16[8,64,128]{2,1,0:T(8,128)(2,1)S(1)}, u32[]{:S(2)}, u32[]{:S(2)}) collective-permute-start(bf16[8,64,128]{2,1,0:T(8,128)(2,1)S(1)} %get-tuple-element.37), channel_id=1, source_target_pairs={{4,0},{8,4},{12,8},{16,12},{20,16},{24,20},{28,24},{5,1},{9,5},{13... | collective-permute-start | bytes 393224 | tf_op jit(solution)/shard_map/ppermute | solution.py:441
  20.1 4.1 %collective-permute-start.6 = (f32[64,128]{1,0:T(8,128)S(1)}, f32[64,128]{1,0:T(8,128)S(1)}, u32[]{:S(2)}, u32[]{:S(2)}) collective-permute-start(f32[64,128]{1,0:T(8,128)S(1)} %get-tuple-element.38), channel_id=1, source_target_pairs={{0,1},{2,3},{1,0},{3,2},{4,5},{6,7},{5,4},{7,6},{8,9},{10,11},{9,8... | collective-permute-start | bytes 98312 | tf_op jit(solution)/shard_map/ppermute | solution.py:442

commit v15 on v14

--- a/solution.py
+++ b/solution.py
@@ -223,7 +223,7 @@
     )(near, turned, w, live, index, tapers, flipped)
 
 
-def outer_kernel(inc, near_side, far_side, held, tail, rest, plain, u, live, index, tapers, out, top, low):
+def outer_kernel(inc, near_side, far_side, held, tail, rest, u, live, index, tapers, out, top, low):
     rows, cols, members, cells = u.shape
     width = inc.shape[2]
     last = cols - 1
@@ -245,9 +245,6 @@
     weights = [jnp.where(even, parts[0], tail)]
     weights += [jnp.where(even, parts[c], parts[c - 1]) for c in range(1, last)]
     weights.append(jnp.where(even, tail, parts[last - 1]))
-    place = lax.axis_index("col")
-    alone = jnp.logical_or(place == 0, place == lax.axis_size("col") - 1)
-    weights = [jnp.where(alone, plain[c], weight) for c, weight in enumerate(weights)]
     for q in range(cols):
         near = [c for c in (q - 1, q, q + 1) if 0 <= c < cols]
         block = held[q, :, (1 + near[0] - q) * cells : (2 + near[-1] - q) * cells]
@@ -265,7 +262,7 @@
                 low[q] = value
 
 
-def outer(inc, near_side, far_side, held, tail, rest, plain, u, live, index, tapers):
+def outer(inc, near_side, far_side, held, tail, rest, u, live, index, tapers):
     rows, cols, width, cells = inc.shape
     return pl.pallas_call(
         outer_kernel,
@@ -274,12 +271,12 @@
             jax.ShapeDtypeStruct((2, width, cells), inc.dtype),
             jax.ShapeDtypeStruct(inc.shape[1:], inc.dtype),
         ),
-        in_specs=[VMEM] * 11,
+        in_specs=[VMEM] * 10,
         out_specs=(VMEM,) * 3,
         compiler_params=pltpu.CompilerParams(vmem_limit_bytes=GRANT),
         cost_estimate=pl.CostEstimate(flops=6 * cols * cells * cells * width, bytes_accessed=4 << 20, transcendentals=0),
         name="outer",
-    )(inc, near_side, far_side, held, tail, rest, plain, u, live, index, tapers)
+    )(inc, near_side, far_side, held, tail, rest, u, live, index, tapers)
 
 
 def finish_kernel(inc, top, low, back, from_inside, out, end, total, sem):
@@ -358,26 +355,22 @@
     )(u, w)
 
 
-def pack_rest_kernel(w, outside, out, plain):
+def pack_rest_kernel(w, outside, out):
     rows, cols, width, _ = w.shape
     skip = 1 - even_column().astype(jnp.int32)
     for q in range(cols - 1):
         out[q * width : (q + 1) * width] = w[rows - 1, q + skip]
     start = (cols - 1) * width
     out[start:] = outside[rows - 1, : out.shape[0] - start]
-    plain[...] = w[rows - 1]
 
 
 def pack_rest(w, outside, members):
     _, cols, width, cells = w.shape
     return pl.pallas_call(
         pack_rest_kernel,
-        out_shape=(
-            jax.ShapeDtypeStruct(((cols - 1) * width + members + width, cells), w.dtype),
-            jax.ShapeDtypeStruct((cols, width, cells), w.dtype),
-        ),
+        out_shape=jax.ShapeDtypeStruct(((cols - 1) * width + members + width, cells), w.dtype),
         in_specs=[VMEM, VMEM],
-        out_specs=(VMEM, VMEM),
+        out_specs=VMEM,
         compiler_params=pltpu.CompilerParams(vmem_limit_bytes=GRANT),
         cost_estimate=pl.CostEstimate(flops=0, bytes_accessed=8 * cols * width * cells, transcendentals=0),
         name="pack_rest",
@@ -420,13 +413,7 @@
     )(u, w, live, index, packed)
 
 
-def down(row, col, chosen):
-    wide = lax.axis_size(col)
-    return [(r * wide + c, (r + 1) * wide + c) for r in range(lax.axis_size(row) - 1) for c in chosen]
-
-
 def body(u, w, live, index, tapers):
-    wide = lax.axis_size("col")
     packed = pack_row(u, w)
     s = lax.ppermute(packed, "row", forward("row"))
     inner_side, outer_side = pack_columns(u, w, live, index, packed)
@@ -434,15 +421,14 @@
     inside = lax.ppermute(inner_side, "col", swaps("col", 0))
     inc, turned, flipped = inner(u, w, live, index, tapers)
     inc, outside, inside = lax.optimization_barrier((inc, outside, inside))
-    rest, plain = pack_rest(w, outside, u.shape[2])
-    rest = lax.ppermute(rest, ("row", "col"), down("row", "col", range(1, wide - 1)))
-    plain = lax.ppermute(plain, ("row", "col"), down("row", "col", sorted({0, wide - 1})))
+    near_side = column(inside, turned, w, live, index, tapers, flipped, False)
+    near_side, outside = lax.optimization_barrier((near_side, outside))
+    rest = lax.ppermute(pack_rest(w, outside, u.shape[2]), "row", forward("row"))
     back, held, to_inside, tail = above(s, turned, w, inside, outside, live, index, flipped)
     back = lax.ppermute(back, "row", backward("row"))
     from_inside = lax.ppermute(to_inside, "col", swaps("col", 0))
-    near_side = column(inside, turned, w, live, index, tapers, flipped, False)
     far_side = column(outside, turned, w, live, index, tapers, flipped, True)
-    inc, top, low = outer(inc, near_side, far_side, held, tail, rest, plain, u, live, index, tapers)
+    inc, top, low = outer(inc, near_side, far_side, held, tail, rest, u, live, index, tapers)
     return finish(inc, top, low, back, from_inside)
 
 

time: 28 us -> 28.1 us (level)
  waiting for transfers between devices: 2.83 us -> 3.62 us
  starting transfers between devices: 15 us -> 14.3 us
    ppermute x2 -> x1, waiting for transfers between devices: 0.02 us -> 1.22 us  [body(): lax.ppermute(pack_rest(w, outside, u.shape[2]), 'row', forward('row'))]
    ppermute x2 -> x1, starting transfers between devices: 4.08 us -> 3.41 us  [body(): lax.ppermute(pack_rest(w, outside, u.shape[2]), 'row', forward('row'))]
    ppermute x1, waiting for transfers between devices: 2.8 us -> 2.39 us  [body(): back = lax.ppermute(back, 'row', backward('row'))]
  transfers between devices with their start and end apart: 7 -> 6, of which waited for: 1 -> 2; matrix products, arithmetic and copies ran while one was open for 0% -> 0% of each run, Pallas kernels for 28% -> 28%
where the time goes in v15:
time: 28.1 us; the launch traced here: 27.9 us
  starting transfers between devices  14.3 us (51%)
  Pallas kernels  9.77 us (35%)
  waiting for transfers between devices  3.62 us (13%)
    ppermute x1, starting transfers between devices, body(): s = lax.ppermute(packed, 'row', forward('row'))  5.05 us
    pallas_call x1, Pallas kernels, inner(): pl.pallas_call(inner_kernel, out_shape=(jax.ShapeDtypeStruct((rows, cols,...  3.88 us
    ppermute x1, starting transfers between devices, body(): lax.ppermute(pack_rest(w, outside, u.shape[2]), 'row', forward('row'))  3.41 us
    ppermute x1, starting transfers between devices, body(): inside = lax.ppermute(inner_side, 'col', swaps('col', 0))  2.9 us
    ppermute x1, waiting for transfers between devices, body(): back = lax.ppermute(back, 'row', backward('row'))  2.39 us
    pallas_call x1, Pallas kernels, outer(): pl.pallas_call(outer_kernel, out_shape=(jax.ShapeDtypeStruct(inc.shape, i...  1.57 us
    pallas_call x2, Pallas kernels, column(): pl.pallas_call(functools.partial(column_kernel, outward), out_shape=jax.S...  1.5 us
    ppermute x1, starting transfers between devices, body(): back = lax.ppermute(back, 'row', backward('row'))  1.29 us
  transfers between devices with their start and end apart: 6, of which 2 were waited for; matrix products, arithmetic and copies ran while one was open for 0% of the time, Pallas kernels for 28%

profile of v15, /device:TPU:0, one launch (start us, length us, event | category | flops | bytes accessed | tf_op | source)
XLA Modules:
  0.0 27.9 jit_solution(3634099831979445544)
XLA Ops:
  0.0 0.0 copy-start.1
  0.0 0.0 copy-start
  0.0 0.0 copy-start.4
  0.0 0.0 copy-start.3
  0.0 1.2 %pack_row.1.packed = bf16[2112,128]{1,0:T(8,128)(2,1)S(1)} custom-call(bf16[4,8,256,128]{3,2,1,0:T(8,128)(2,1)} %u.7, bf16[4,8,64,128]{3,2,1,0:T(8,128)(2,1)} %w.13), custom_call_target="tpu_custom_call" | custom-call | bytes 1081344 | tf_op jit(solution)/shard_map/pack_row/pallas_call | solution.py:347
  1.2 0.0 copy-start.2
  1.2 5.0 %collective-permute-start.2 = (bf16[2112,128]{1,0:T(8,128)(2,1)S(1)}, bf16[2112,128]{1,0:T(8,128)(2,1)S(1)}, u32[]{:S(2)}, u32[]{:S(2)}) collective-permute-start(bf16[2112,128]{1,0:T(8,128)(2,1)S(1)} %pack_row.1.packed), channel_id=1, source_target_pairs={{0,4},{4,8},{8,12},{12,16},{16,20},{20,24},{24,28},{1,5},{5,9},{9,... | collective-permute-start | bytes 1622024 | tf_op jit(solution)/shard_map/ppermute | solution.py:418
  6.3 0.0 copy-done.1
  6.3 0.0 copy-done
  6.3 0.0 copy-done.4
  6.3 0.0 copy-done.3
  6.3 0.1 pack_columns.1
  6.5 0.7 %collective-permute-start = (bf16[4,336,128]{2,1,0:T(8,128)(2,1)S(1)}, bf16[4,336,128]{2,1,0:T(8,128)(2,1)S(1)}, u32[]{:S(2)}, u32[]{:S(2)}) collective-permute-start(bf16[4,336,128]{2,1,0:T(8,128)(2,1)S(1)} %get-tuple-element.23), channel_id=1, source_target_pairs={{1,2},{2,1},{5,6},{6,5},{9,10},{10,9},{13,14},{14,13},{17,18},{18,... | collective-permute-start | bytes 1032200 | tf_op jit(solution)/shard_map/ppermute | solution.py:420
  7.2 2.9 %collective-permute-start.1 = (bf16[4,336,128]{2,1,0:T(8,128)(2,1)S(1)}, bf16[4,336,128]{2,1,0:T(8,128)(2,1)S(1)}, u32[]{:S(2)}, u32[]{:S(2)}) collective-permute-start(bf16[4,336,128]{2,1,0:T(8,128)(2,1)S(1)} %get-tuple-element.24), channel_id=1, source_target_pairs={{0,1},{2,3},{1,0},{3,2},{4,5},{6,7},{5,4},{7,6},{8,9},{10,11},{9,8... | collective-permute-start | bytes 1032200 | tf_op jit(solution)/shard_map/ppermute | solution.py:421
  10.1 0.0 copy-done.2
  10.1 3.9 %inner.1 = (f32[4,8,64,128]{3,2,1,0:T(8,128)S(1)}, bf16[4,8,128,256]{3,2,1,0:T(8,128)(2,1)S(1)}, bf16[16,128,128]{2,1,0:T(8,128)(2,1)S(1)}) custom-call(bf16[4,8,256,128]{3,2,1,0:T(8,128)(2,1)S(1)} %copy-done, bf16[4,8,64,128]{3,2,1,0:T(8,128)(2,1)S(1)} %copy-done.1, s32[4,8,9]{2,1,0:T(8,128)S(1)} %copy-done.3, s32[4,8,9]{2,1,0:T(8,128)S(1)} %copy-done.4, ...), custom_call_target="tpu_custom_call" | custom-call | flops 2013265920 | bytes 4194304 | tf_op jit(solution)/shard_map/inner/pallas_call | solution.py:100
  14.0 0.0 collective-permute-done.near.outside
  14.0 0.0 collective-permute-done.1.near.inside
  14.0 0.8 %column.2.near_side = f32[4,64,128]{2,1,0:T(8,128)S(1)} custom-call(bf16[4,336,128]{2,1,0:T(8,128)(2,1)S(1)} %collective-permute-done.1.near.inside, bf16[4,8,128,256]{3,2,1,0:T(8,128)(2,1)S(1)} %get-tuple-element.27.turned, bf16[4,8,64,128]{3,2,1,0:T(8,128)(2,1)S(1)} %copy-done.1, s32[4,8,9]{2,1,0:T(8,128)S(1)} %copy-done.3, s32[4,8,9]{2,1,0:T(8,128)S(1)} %copy-done.4, ...), custom_call_target="tpu_custom_call" | custom-call | flops 125829120 | bytes 2097152 | tf_op jit(solution)/shard_map/column/pallas_call | solution.py:213
  14.8 3.4 %collective-permute-start.3 = (bf16[768,128]{1,0:T(8,128)(2,1)S(1)}, bf16[768,128]{1,0:T(8,128)(2,1)S(1)}, u32[]{:S(2)}, u32[]{:S(2)}) collective-permute-start(bf16[768,128]{1,0:T(8,128)(2,1)S(1)} %pack_rest.1), channel_id=1, source_target_pairs={{0,4},{4,8},{8,12},{12,16},{16,20},{20,24},{24,28},{1,5},{5,9},{9,... | collective-permute-start | bytes 589832 | tf_op jit(solution)/shard_map/ppermute | solution.py:426
  18.2 0.0 collective-permute-done.2.s
  18.2 0.7 %above.1 = (bf16[8,64,128]{2,1,0:T(8,128)(2,1)S(1)}, bf16[8,128,384]{2,1,0:T(8,128)(2,1)S(1)}, f32[64,128]{1,0:T(8,128)S(1)}, bf16[64,128]{1,0:T(8,128)(2,1)S(1)}) custom-call(bf16[2112,128]{1,0:T(8,128)(2,1)S(1)} %collective-permute-done.2.s, bf16[4,8,128,256]{3,2,1,0:T(8,128)(2,1)S(1)} %get-tuple-element.27.turned, bf16[4,8,64,128]{3,2,1,0:T(8,128)(2,1)S(1)} %copy-done.1, ...), custom_call_target="tpu_custom_call" | custom-call | flops 251658240 | bytes 2097152 | tf_op jit(solution)/shard_map/above/pallas_call | solution.py:165
  18.9 1.3 %collective-permute-start.4 = (bf16[8,64,128]{2,1,0:T(8,128)(2,1)S(1)}, bf16[8,64,128]{2,1,0:T(8,128)(2,1)S(1)}, u32[]{:S(2)}, u32[]{:S(2)}) collective-permute-start(bf16[8,64,128]{2,1,0:T(8,128)(2,1)S(1)} %get-tuple-element.37), channel_id=1, source_target_pairs={{4,0},{8,4},{12,8},{16,12},{20,16},{24,20},{28,24},{5,1},{9,5},{13... | collective-permute-start | bytes 393224 | tf_op jit(solution)/shard_map/ppermute | solution.py:428
  20.2 1.0 %collective-permute-start.5 = (f32[64,128]{1,0:T(8,128)S(1)}, f32[64,128]{1,0:T(8,128)S(1)}, u32[]{:S(2)}, u32[]{:S(2)}) collective-permute-start(f32[64,128]{1,0:T(8,128)S(1)} %get-tuple-element.38), channel_id=1, source_target_pairs={{0,1},{2,3},{1,0},{3,2},{4,5},{6,7},{5,4},{7,6},{8,9},{10,11},{9,8... | collective-permute-start | bytes 98312 | tf_op jit(solution)/shard_map/ppermute | solution.py:429
  21.2 0.7 %column.3.far_side = f32[4,64,128]{2,1,0:T(8,128)S(1)} custom-call(bf16[4,336,128]{2,1,0:T(8,128)(2,1)S(1)} %collective-permute-done.near.outside, bf16[4,8,128,256]{3,2,1,0:T(8,128)(2,1)S(1)} %get-tuple-element.27.turned, bf16[4,8,64,128]{3,2,1,0:T(8,128)(2,1)S(1)} %copy-done.1, s32[4,8,9]{2,1,0:T(8,128)S(1)} %copy-done.3, s32[4,8,9]{2,1,0:T(8,128)S(1)} %copy-done.4, ...), custom_call_target="tpu_custom_call" | custom-call | flops 125829120 | bytes 2097152 | tf_op jit(solution)/shard_map/column/pallas_call | solution.py:213
  22.0 1.2 %collective-permute-done.3.rest = bf16[768,128]{1,0:T(8,128)(2,1)S(1)} collective-permute-done((bf16[768,128]{1,0:T(8,128)(2,1)S(1)}, bf16[768,128]{1,0:T(8,128)(2,1)S(1)}, u32[]{:S(2)}, u32[]{:S(2)}) %collective-permute-start.3) | collective-permute-done | bytes 196640 | tf_op jit(solution)/shard_map/ppermute | solution.py:426
  23.2 1.6 %outer.1 = (f32[4,8,64,128]{3,2,1,0:T(8,128)}, f32[2,64,128]{2,1,0:T(8,128)S(1)}, f32[8,64,128]{2,1,0:T(8,128)S(1)}) custom-call(f32[4,8,64,128]{3,2,1,0:T(8,128)S(1)} %get-tuple-element.25.inc, f32[4,64,128]{2,1,0:T(8,128)S(1)} %column.2.near_side, f32[4,64,128]{2,1,0:T(8,128)S(1)} %column.3.far_side, bf16[8,128,384]{2,1,0:T(8,128)(2,1)S(1)} %get-tuple-element.32.held, ...), custom_call_target="tpu_custom_call" | custom-call | flops 50331648 | bytes 4194304 | tf_op jit(solution)/shard_map/outer/pallas_call | solution.py:267
  24.8 0.0 collective-permute-done.5.from_inside
  24.8 2.4 %collective-permute-done.4.back = bf16[8,64,128]{2,1,0:T(8,128)(2,1)S(1)} collective-permute-done((bf16[8,64,128]{2,1,0:T(8,128)(2,1)S(1)}, bf16[8,64,128]{2,1,0:T(8,128)(2,1)S(1)}, u32[]{:S(2)}, u32[]{:S(2)}) %collective-permute-start.4) | collective-permute-done | bytes 131104 | tf_op jit(solution)/shard_map/ppermute | solution.py:428
  27.1 0.7 %finish.1 = f32[4,8,64,128]{3,2,1,0:T(8,128)} custom-call(f32[4,8,64,128]{3,2,1,0:T(8,128)} %get-tuple-element.34.inc, f32[2,64,128]{2,1,0:T(8,128)S(1)} %get-tuple-element.35.top, f32[8,64,128]{2,1,0:T(8,128)S(1)} %get-tuple-element.36.low, bf16[8,64,128]{2,1,0:T(8,128)(2,1)S(1)} %collective-permute-done.4.back, ...), custom_call_target="tpu_custom_call", output_to_operand_aliasing={{}: (0, {})} | custom-call | flops 65536 | bytes 655360 | tf_op jit(solution)/shard_map/finish/pallas_call | solution.py:300
  (1 shorter events, 0.0 us)
Async XLA Ops:
  0.0 6.3 %copy-start.1 = (bf16[4,8,64,128]{3,2,1,0:T(8,128)(2,1)S(1)}, bf16[4,8,64,128]{3,2,1,0:T(8,128)(2,1)}, u32[]{:S(2)}) copy-start(bf16[4,8,64,128]{3,2,1,0:T(8,128)(2,1)} %w.13) | copy-start | bytes 1572868
  0.0 6.3 %copy-start = (bf16[4,8,256,128]{3,2,1,0:T(8,128)(2,1)S(1)}, bf16[4,8,256,128]{3,2,1,0:T(8,128)(2,1)}, u32[]{:S(2)}) copy-start(bf16[4,8,256,128]{3,2,1,0:T(8,128)(2,1)} %u.7) | copy-start | bytes 6291460
  0.0 6.3 %copy-start.4 = (s32[4,8,9]{2,1,0:T(8,128)S(1)}, s32[4,8,9]{2,1,0:T(8,128)}, u32[]{:S(2)}) copy-start(s32[4,8,9]{2,1,0:T(8,128)} %index.11) | copy-start | bytes 3460
  0.0 6.3 %copy-start.3 = (s32[4,8,9]{2,1,0:T(8,128)S(1)}, s32[4,8,9]{2,1,0:T(8,128)}, u32[]{:S(2)}) copy-start(s32[4,8,9]{2,1,0:T(8,128)} %live.11) | copy-start | bytes 3460
  1.2 8.9 %copy-start.2 = (bf16[16,128,128]{2,1,0:T(8,128)(2,1)S(1)}, bf16[16,128,128]{2,1,0:T(8,128)(2,1)}, u32[]{:S(2)}) copy-start(bf16[16,128,128]{2,1,0:T(8,128)(2,1)} %tapers.7) | copy-start | bytes 1572868
  1.2 17.0 %collective-permute-start.2 = (bf16[2112,128]{1,0:T(8,128)(2,1)S(1)}, bf16[2112,128]{1,0:T(8,128)(2,1)S(1)}, u32[]{:S(2)}, u32[]{:S(2)}) collective-permute-start(bf16[2112,128]{1,0:T(8,128)(2,1)S(1)} %pack_row.1.packed), channel_id=1, source_target_pairs={{0,4},{4,8},{8,12},{12,16},{16,20},{20,24},{24,28},{1,5},{5,9},{9,... | collective-permute-start | bytes 1622024 | tf_op jit(solution)/shard_map/ppermute | solution.py:418
  6.5 7.5 %collective-permute-start = (bf16[4,336,128]{2,1,0:T(8,128)(2,1)S(1)}, bf16[4,336,128]{2,1,0:T(8,128)(2,1)S(1)}, u32[]{:S(2)}, u32[]{:S(2)}) collective-permute-start(bf16[4,336,128]{2,1,0:T(8,128)(2,1)S(1)} %get-tuple-element.23), channel_id=1, source_target_pairs={{1,2},{2,1},{5,6},{6,5},{9,10},{10,9},{13,14},{14,13},{17,18},{18,... | collective-permute-start | bytes 1032200 | tf_op jit(solution)/shard_map/ppermute | solution.py:420
  7.2 6.8 %collective-permute-start.1 = (bf16[4,336,128]{2,1,0:T(8,128)(2,1)S(1)}, bf16[4,336,128]{2,1,0:T(8,128)(2,1)S(1)}, u32[]{:S(2)}, u32[]{:S(2)}) collective-permute-start(bf16[4,336,128]{2,1,0:T(8,128)(2,1)S(1)} %get-tuple-element.24), channel_id=1, source_target_pairs={{0,1},{2,3},{1,0},{3,2},{4,5},{6,7},{5,4},{7,6},{8,9},{10,11},{9,8... | collective-permute-start | bytes 1032200 | tf_op jit(solution)/shard_map/ppermute | solution.py:421
  14.8 8.4 %collective-permute-start.3 = (bf16[768,128]{1,0:T(8,128)(2,1)S(1)}, bf16[768,128]{1,0:T(8,128)(2,1)S(1)}, u32[]{:S(2)}, u32[]{:S(2)}) collective-permute-start(bf16[768,128]{1,0:T(8,128)(2,1)S(1)} %pack_rest.1), channel_id=1, source_target_pairs={{0,4},{4,8},{8,12},{12,16},{16,20},{20,24},{24,28},{1,5},{5,9},{9,... | collective-permute-start | bytes 589832 | tf_op jit(solution)/shard_map/ppermute | solution.py:426
  18.9 8.2 %collective-permute-start.4 = (bf16[8,64,128]{2,1,0:T(8,128)(2,1)S(1)}, bf16[8,64,128]{2,1,0:T(8,128)(2,1)S(1)}, u32[]{:S(2)}, u32[]{:S(2)}) collective-permute-start(bf16[8,64,128]{2,1,0:T(8,128)(2,1)S(1)} %get-tuple-element.37), channel_id=1, source_target_pairs={{4,0},{8,4},{12,8},{16,12},{20,16},{24,20},{28,24},{5,1},{9,5},{13... | collective-permute-start | bytes 393224 | tf_op jit(solution)/shard_map/ppermute | solution.py:428
  20.2 4.6 %collective-permute-start.5 = (f32[64,128]{1,0:T(8,128)S(1)}, f32[64,128]{1,0:T(8,128)S(1)}, u32[]{:S(2)}, u32[]{:S(2)}) collective-permute-start(f32[64,128]{1,0:T(8,128)S(1)} %get-tuple-element.38), channel_id=1, source_target_pairs={{0,1},{2,3},{1,0},{3,2},{4,5},{6,7},{5,4},{7,6},{8,9},{10,11},{9,8... | collective-permute-start | bytes 98312 | tf_op jit(solution)/shard_map/ppermute | solution.py:429

commit v16 on v15

--- a/solution.py
+++ b/solution.py
@@ -182,7 +182,7 @@
     )(s, turned, w, inside, outside, live, index, flipped)
 
 
-def column_kernel(outward, near, turned, w, live, index, tapers, flipped, side):
+def column_part(outward, near, turned, w, live, index, tapers, flipped, side):
     rows, cols, cells, members = turned.shape
     deep = members + w.shape[2]
     last = cols - 1
@@ -207,11 +207,25 @@
         side[a] = dot(cat([near[q, members:deep] for q in around], 1), cat(blocks, 1), NT)
 
 
-def column(near, turned, w, live, index, tapers, flipped, outward):
+def column_kernel(outward, alone, near, turned, w, live, index, tapers, flipped, side):
+    place = lax.axis_index("col")
+    here = jnp.logical_or(place == 0, place == lax.axis_size("col") - 1)
+    here = here if alone else jnp.logical_not(here)
+
+    @pl.when(here)
+    def _():
+        column_part(outward, near, turned, w, live, index, tapers, flipped, side)
+
+    @pl.when(jnp.logical_not(here))
+    def _():
+        side[...] = jnp.zeros_like(side)
+
+
+def column(near, turned, w, live, index, tapers, flipped, outward, alone):
     rows, _, cells, members = turned.shape
     width = w.shape[2]
     return pl.pallas_call(
-        functools.partial(column_kernel, outward),
+        functools.partial(column_kernel, outward, alone),
         out_shape=jax.ShapeDtypeStruct((rows, width, cells), jnp.float32),
         in_specs=[VMEM] * 7,
         out_specs=VMEM,
@@ -223,7 +237,7 @@
     )(near, turned, w, live, index, tapers, flipped)
 
 
-def outer_kernel(inc, near_side, far_side, held, tail, rest, u, live, index, tapers, out, top, low):
+def outer_kernel(inc, near_side, more_side, far_side, held, tail, rest, u, live, index, tapers, out, top, low):
     rows, cols, members, cells = u.shape
     width = inc.shape[2]
     last = cols - 1
@@ -237,7 +251,7 @@
     blank = jnp.zeros_like(far)
 
     def side(q, a):
-        near, other = near_side[a], far_side[a]
+        near, other = near_side[a] + more_side[a], far_side[a]
         return jnp.where(even, other, near) if q == 0 else jnp.where(even, near, other)
 
     parts = [rest[c * width : (c + 1) * width] for c in range(cols - 1)]
@@ -262,7 +276,7 @@
                 low[q] = value
 
 
-def outer(inc, near_side, far_side, held, tail, rest, u, live, index, tapers):
+def outer(inc, near_side, more_side, far_side, held, tail, rest, u, live, index, tapers):
     rows, cols, width, cells = inc.shape
     return pl.pallas_call(
         outer_kernel,
@@ -271,12 +285,12 @@
             jax.ShapeDtypeStruct((2, width, cells), inc.dtype),
             jax.ShapeDtypeStruct(inc.shape[1:], inc.dtype),
         ),
-        in_specs=[VMEM] * 10,
+        in_specs=[VMEM] * 11,
         out_specs=(VMEM,) * 3,
         compiler_params=pltpu.CompilerParams(vmem_limit_bytes=GRANT),
         cost_estimate=pl.CostEstimate(flops=6 * cols * cells * cells * width, bytes_accessed=4 << 20, transcendentals=0),
         name="outer",
-    )(inc, near_side, far_side, held, tail, rest, u, live, index, tapers)
+    )(inc, near_side, more_side, far_side, held, tail, rest, u, live, index, tapers)
 
 
 def finish_kernel(inc, top, low, back, from_inside, out, end, total, sem):
@@ -421,14 +435,15 @@
     inside = lax.ppermute(inner_side, "col", swaps("col", 0))
     inc, turned, flipped = inner(u, w, live, index, tapers)
     inc, outside, inside = lax.optimization_barrier((inc, outside, inside))
-    near_side = column(inside, turned, w, live, index, tapers, flipped, False)
+    near_side = column(inside, turned, w, live, index, tapers, flipped, False, True)
     near_side, outside = lax.optimization_barrier((near_side, outside))
     rest = lax.ppermute(pack_rest(w, outside, u.shape[2]), "row", forward("row"))
     back, held, to_inside, tail = above(s, turned, w, inside, outside, live, index, flipped)
     back = lax.ppermute(back, "row", backward("row"))
     from_inside = lax.ppermute(to_inside, "col", swaps("col", 0))
-    far_side = column(outside, turned, w, live, index, tapers, flipped, True)
-    inc, top, low = outer(inc, near_side, far_side, held, tail, rest, u, live, index, tapers)
+    more_side = column(inside, turned, w, live, index, tapers, flipped, False, False)
+    far_side = column(outside, turned, w, live, index, tapers, flipped, True, False)
+    inc, top, low = outer(inc, near_side, more_side, far_side, held, tail, rest, u, live, index, tapers)
     return finish(inc, top, low, back, from_inside)
 
 

time: 28.1 us -> 27.3 us (0.972)
  the two profiles are of different devices: /device:TPU:0 before, /device:TPU:22 now
where the time goes in v16:
time: 27.3 us; the launch traced here: 27 us
  starting transfers between devices  12.4 us (45%)
  Pallas kernels  9.81 us (36%)
  waiting for transfers between devices  4.65 us (17%)
    pallas_call x1, Pallas kernels, inner(): pl.pallas_call(inner_kernel, out_shape=(jax.ShapeDtypeStruct((rows, cols,...  3.88 us
    ppermute x1, starting transfers between devices, body(): s = lax.ppermute(packed, 'row', forward('row'))  3.56 us
    ppermute x1, starting transfers between devices, body(): lax.ppermute(pack_rest(w, outside, u.shape[2]), 'row', forward('row'))  3.43 us
    ppermute x1, starting transfers between devices, body(): back = lax.ppermute(back, 'row', backward('row'))  3.31 us
    ppermute x1, waiting for transfers between devices, body(): outside = lax.ppermute(outer_side, 'col', swaps('col', 1))  2.67 us
    ppermute x1, starting transfers between devices, body(): outside = lax.ppermute(outer_side, 'col', swaps('col', 1))  1.92 us
    pallas_call x1, Pallas kernels, outer(): pl.pallas_call(outer_kernel, out_shape=(jax.ShapeDtypeStruct(inc.shape, i...  1.58 us
    pallas_call x3, Pallas kernels, column(): pl.pallas_call(functools.partial(column_kernel, outward, alone), out_shap...  1.54 us
  transfers between devices with their start and end apart: 6, of which 3 were waited for; matrix products, arithmetic and copies ran while one was open for 0% of the time, Pallas kernels for 29%

profile of v16, /device:TPU:22, one launch (start us, length us, event | category | flops | bytes accessed | tf_op | source)
XLA Modules:
  0.0 27.0 jit_solution(15064188296076934031)
XLA Ops:
  0.0 0.0 copy-start.1
  0.0 0.0 copy-start
  0.0 0.0 copy-start.3
  0.0 0.0 copy-start.4
  0.0 1.2 %pack_row.1.packed = bf16[2112,128]{1,0:T(8,128)(2,1)S(1)} custom-call(bf16[4,8,256,128]{3,2,1,0:T(8,128)(2,1)} %u.7, bf16[4,8,64,128]{3,2,1,0:T(8,128)(2,1)} %w.15), custom_call_target="tpu_custom_call" | custom-call | bytes 1081344 | tf_op jit(solution)/shard_map/pack_row/pallas_call | solution.py:361
  1.2 0.0 copy-start.2
  1.3 3.6 %collective-permute-start.2 = (bf16[2112,128]{1,0:T(8,128)(2,1)S(1)}, bf16[2112,128]{1,0:T(8,128)(2,1)S(1)}, u32[]{:S(2)}, u32[]{:S(2)}) collective-permute-start(bf16[2112,128]{1,0:T(8,128)(2,1)S(1)} %pack_row.1.packed), channel_id=1, source_target_pairs={{0,4},{4,8},{8,12},{12,16},{16,20},{20,24},{24,28},{1,5},{5,9},{9,... | collective-permute-start | bytes 1622024 | tf_op jit(solution)/shard_map/ppermute | solution.py:432
  4.8 0.0 copy-done.1
  4.8 0.0 copy-done
  4.8 0.0 copy-done.3
  4.8 0.0 copy-done.4
  4.9 0.1 pack_columns.1
  5.0 1.9 %collective-permute-start = (bf16[4,336,128]{2,1,0:T(8,128)(2,1)S(1)}, bf16[4,336,128]{2,1,0:T(8,128)(2,1)S(1)}, u32[]{:S(2)}, u32[]{:S(2)}) collective-permute-start(bf16[4,336,128]{2,1,0:T(8,128)(2,1)S(1)} %get-tuple-element.23), channel_id=1, source_target_pairs={{1,2},{2,1},{5,6},{6,5},{9,10},{10,9},{13,14},{14,13},{17,18},{18,... | collective-permute-start | bytes 1032200 | tf_op jit(solution)/shard_map/ppermute | solution.py:434
  6.9 0.1 collective-permute-start.1
  7.0 0.0 copy-done.2
  7.0 3.9 %inner.1 = (f32[4,8,64,128]{3,2,1,0:T(8,128)S(1)}, bf16[4,8,128,256]{3,2,1,0:T(8,128)(2,1)S(1)}, bf16[16,128,128]{2,1,0:T(8,128)(2,1)S(1)}) custom-call(bf16[4,8,256,128]{3,2,1,0:T(8,128)(2,1)S(1)} %copy-done.1, bf16[4,8,64,128]{3,2,1,0:T(8,128)(2,1)S(1)} %copy-done, s32[4,8,9]{2,1,0:T(8,128)S(1)} %copy-done.3, s32[4,8,9]{2,1,0:T(8,128)S(1)} %copy-done.4, ...), custom_call_target="tpu_custom_call" | custom-call | flops 2013265920 | bytes 4194304 | tf_op jit(solution)/shard_map/inner/pallas_call | solution.py:100
  10.9 2.7 %collective-permute-done.near.outside = bf16[4,336,128]{2,1,0:T(8,128)(2,1)S(1)} collective-permute-done((bf16[4,336,128]{2,1,0:T(8,128)(2,1)S(1)}, bf16[4,336,128]{2,1,0:T(8,128)(2,1)S(1)}, u32[]{:S(2)}, u32[]{:S(2)}) %collective-permute-start) | collective-permute-done | bytes 344096 | tf_op jit(solution)/shard_map/ppermute | solution.py:434
  13.6 0.0 collective-permute-done.1.near.inside
  13.6 3.4 %collective-permute-start.3 = (bf16[768,128]{1,0:T(8,128)(2,1)S(1)}, bf16[768,128]{1,0:T(8,128)(2,1)S(1)}, u32[]{:S(2)}, u32[]{:S(2)}) collective-permute-start(bf16[768,128]{1,0:T(8,128)(2,1)S(1)} %pack_rest.1), channel_id=1, source_target_pairs={{0,4},{4,8},{8,12},{12,16},{16,20},{20,24},{24,28},{1,5},{5,9},{9,... | collective-permute-start | bytes 589832 | tf_op jit(solution)/shard_map/ppermute | solution.py:440
  17.1 0.7 %collective-permute-done.2.s = bf16[2112,128]{1,0:T(8,128)(2,1)S(1)} collective-permute-done((bf16[2112,128]{1,0:T(8,128)(2,1)S(1)}, bf16[2112,128]{1,0:T(8,128)(2,1)S(1)}, u32[]{:S(2)}, u32[]{:S(2)}) %collective-permute-start.2) | collective-permute-done | bytes 540704 | tf_op jit(solution)/shard_map/ppermute | solution.py:432
  17.8 0.7 %above.1 = (bf16[8,64,128]{2,1,0:T(8,128)(2,1)S(1)}, bf16[8,128,384]{2,1,0:T(8,128)(2,1)S(1)}, f32[64,128]{1,0:T(8,128)S(1)}, bf16[64,128]{1,0:T(8,128)(2,1)S(1)}) custom-call(bf16[2112,128]{1,0:T(8,128)(2,1)S(1)} %collective-permute-done.2.s, bf16[4,8,128,256]{3,2,1,0:T(8,128)(2,1)S(1)} %get-tuple-element.27.turned, bf16[4,8,64,128]{3,2,1,0:T(8,128)(2,1)S(1)} %copy-done, ...), custom_call_target="tpu_custom_call" | custom-call | flops 251658240 | bytes 2097152 | tf_op jit(solution)/shard_map/above/pallas_call | solution.py:165
  18.5 3.3 %collective-permute-start.4 = (bf16[8,64,128]{2,1,0:T(8,128)(2,1)S(1)}, bf16[8,64,128]{2,1,0:T(8,128)(2,1)S(1)}, u32[]{:S(2)}, u32[]{:S(2)}) collective-permute-start(bf16[8,64,128]{2,1,0:T(8,128)(2,1)S(1)} %get-tuple-element.37), channel_id=1, source_target_pairs={{4,0},{8,4},{12,8},{16,12},{20,16},{24,20},{28,24},{5,1},{9,5},{13... | collective-permute-start | bytes 393224 | tf_op jit(solution)/shard_map/ppermute | solution.py:442
  21.8 0.1 collective-permute-start.5
  21.9 0.8 %column.5.far_side = f32[4,64,128]{2,1,0:T(8,128)S(1)} custom-call(bf16[4,336,128]{2,1,0:T(8,128)(2,1)S(1)} %collective-permute-done.near.outside, bf16[4,8,128,256]{3,2,1,0:T(8,128)(2,1)S(1)} %get-tuple-element.27.turned, bf16[4,8,64,128]{3,2,1,0:T(8,128)(2,1)S(1)} %copy-done, s32[4,8,9]{2,1,0:T(8,128)S(1)} %copy-done.3, s32[4,8,9]{2,1,0:T(8,128)S(1)} %copy-done.4, ...), custom_call_target="tpu_custom_call" | custom-call | flops 125829120 | bytes 2097152 | tf_op jit(solution)/shard_map/column/pallas_call | solution.py:227
  22.6 0.8 %column.4.more_side = f32[4,64,128]{2,1,0:T(8,128)S(1)} custom-call(bf16[4,336,128]{2,1,0:T(8,128)(2,1)S(1)} %collective-permute-done.1.near.inside, bf16[4,8,128,256]{3,2,1,0:T(8,128)(2,1)S(1)} %get-tuple-element.27.turned, bf16[4,8,64,128]{3,2,1,0:T(8,128)(2,1)S(1)} %copy-done, s32[4,8,9]{2,1,0:T(8,128)S(1)} %copy-done.3, s32[4,8,9]{2,1,0:T(8,128)S(1)} %copy-done.4, ...), custom_call_target="tpu_custom_call" | custom-call | flops 125829120 | bytes 2097152 | tf_op jit(solution)/shard_map/column/pallas_call | solution.py:227
  23.4 0.0 collective-permute-done.3.rest
  23.4 1.6 %outer.1 = (f32[4,8,64,128]{3,2,1,0:T(8,128)}, f32[2,64,128]{2,1,0:T(8,128)S(1)}, f32[8,64,128]{2,1,0:T(8,128)S(1)}) custom-call(f32[4,8,64,128]{3,2,1,0:T(8,128)S(1)} %get-tuple-element.25.inc, f32[4,64,128]{2,1,0:T(8,128)S(1)} %column.3.near_side, f32[4,64,128]{2,1,0:T(8,128)S(1)} %column.4.more_side, f32[4,64,128]{2,1,0:T(8,128)S(1)} %column.5.far_side, ...), custom_call_target="tpu_custom_call" | custom-call | flops 50331648 | bytes 4194304 | tf_op jit(solution)/shard_map/outer/pallas_call | solution.py:281
  25.0 0.0 collective-permute-done.5.from_inside
  25.0 1.2 %collective-permute-done.4.back = bf16[8,64,128]{2,1,0:T(8,128)(2,1)S(1)} collective-permute-done((bf16[8,64,128]{2,1,0:T(8,128)(2,1)S(1)}, bf16[8,64,128]{2,1,0:T(8,128)(2,1)S(1)}, u32[]{:S(2)}, u32[]{:S(2)}) %collective-permute-start.4) | collective-permute-done | bytes 131104 | tf_op jit(solution)/shard_map/ppermute | solution.py:442
  26.2 0.7 %finish.1 = f32[4,8,64,128]{3,2,1,0:T(8,128)} custom-call(f32[4,8,64,128]{3,2,1,0:T(8,128)} %get-tuple-element.34.inc, f32[2,64,128]{2,1,0:T(8,128)S(1)} %get-tuple-element.35.top, f32[8,64,128]{2,1,0:T(8,128)S(1)} %get-tuple-element.36.low, bf16[8,64,128]{2,1,0:T(8,128)(2,1)S(1)} %collective-permute-done.4.back, ...), custom_call_target="tpu_custom_call", output_to_operand_aliasing={{}: (0, {})} | custom-call | flops 65536 | bytes 655360 | tf_op jit(solution)/shard_map/finish/pallas_call | solution.py:314
  (2 shorter events, 0.0 us)
Async XLA Ops:
  0.0 4.8 %copy-start.1 = (bf16[4,8,256,128]{3,2,1,0:T(8,128)(2,1)S(1)}, bf16[4,8,256,128]{3,2,1,0:T(8,128)(2,1)}, u32[]{:S(2)}) copy-start(bf16[4,8,256,128]{3,2,1,0:T(8,128)(2,1)} %u.7) | copy-start | bytes 6291460
  0.0 4.8 %copy-start = (bf16[4,8,64,128]{3,2,1,0:T(8,128)(2,1)S(1)}, bf16[4,8,64,128]{3,2,1,0:T(8,128)(2,1)}, u32[]{:S(2)}) copy-start(bf16[4,8,64,128]{3,2,1,0:T(8,128)(2,1)} %w.15) | copy-start | bytes 1572868
  0.0 4.8 %copy-start.3 = (s32[4,8,9]{2,1,0:T(8,128)S(1)}, s32[4,8,9]{2,1,0:T(8,128)}, u32[]{:S(2)}) copy-start(s32[4,8,9]{2,1,0:T(8,128)} %live.13) | copy-start | bytes 3460
  0.0 4.8 %copy-start.4 = (s32[4,8,9]{2,1,0:T(8,128)S(1)}, s32[4,8,9]{2,1,0:T(8,128)}, u32[]{:S(2)}) copy-start(s32[4,8,9]{2,1,0:T(8,128)} %index.13) | copy-start | bytes 3460
  1.2 5.8 %copy-start.2 = (bf16[16,128,128]{2,1,0:T(8,128)(2,1)S(1)}, bf16[16,128,128]{2,1,0:T(8,128)(2,1)}, u32[]{:S(2)}) copy-start(bf16[16,128,128]{2,1,0:T(8,128)(2,1)} %tapers.9) | copy-start | bytes 1572868
  1.3 16.6 %collective-permute-start.2 = (bf16[2112,128]{1,0:T(8,128)(2,1)S(1)}, bf16[2112,128]{1,0:T(8,128)(2,1)S(1)}, u32[]{:S(2)}, u32[]{:S(2)}) collective-permute-start(bf16[2112,128]{1,0:T(8,128)(2,1)S(1)} %pack_row.1.packed), channel_id=1, source_target_pairs={{0,4},{4,8},{8,12},{12,16},{16,20},{20,24},{24,28},{1,5},{5,9},{9,... | collective-permute-start | bytes 1622024 | tf_op jit(solution)/shard_map/ppermute | solution.py:432
  5.0 8.6 %collective-permute-start = (bf16[4,336,128]{2,1,0:T(8,128)(2,1)S(1)}, bf16[4,336,128]{2,1,0:T(8,128)(2,1)S(1)}, u32[]{:S(2)}, u32[]{:S(2)}) collective-permute-start(bf16[4,336,128]{2,1,0:T(8,128)(2,1)S(1)} %get-tuple-element.23), channel_id=1, source_target_pairs={{1,2},{2,1},{5,6},{6,5},{9,10},{10,9},{13,14},{14,13},{17,18},{18,... | collective-permute-start | bytes 1032200 | tf_op jit(solution)/shard_map/ppermute | solution.py:434
  6.9 6.6 %collective-permute-start.1 = (bf16[4,336,128]{2,1,0:T(8,128)(2,1)S(1)}, bf16[4,336,128]{2,1,0:T(8,128)(2,1)S(1)}, u32[]{:S(2)}, u32[]{:S(2)}) collective-permute-start(bf16[4,336,128]{2,1,0:T(8,128)(2,1)S(1)} %get-tuple-element.24), channel_id=1, source_target_pairs={{0,1},{2,3},{1,0},{3,2},{4,5},{6,7},{5,4},{7,6},{8,9},{10,11},{9,8... | collective-permute-start | bytes 1032200 | tf_op jit(solution)/shard_map/ppermute | solution.py:435
  13.6 9.8 %collective-permute-start.3 = (bf16[768,128]{1,0:T(8,128)(2,1)S(1)}, bf16[768,128]{1,0:T(8,128)(2,1)S(1)}, u32[]{:S(2)}, u32[]{:S(2)}) collective-permute-start(bf16[768,128]{1,0:T(8,128)(2,1)S(1)} %pack_rest.1), channel_id=1, source_target_pairs={{0,4},{4,8},{8,12},{12,16},{16,20},{20,24},{24,28},{1,5},{5,9},{9,... | collective-permute-start | bytes 589832 | tf_op jit(solution)/shard_map/ppermute | solution.py:440
  18.5 7.8 %collective-permute-start.4 = (bf16[8,64,128]{2,1,0:T(8,128)(2,1)S(1)}, bf16[8,64,128]{2,1,0:T(8,128)(2,1)S(1)}, u32[]{:S(2)}, u32[]{:S(2)}) collective-permute-start(bf16[8,64,128]{2,1,0:T(8,128)(2,1)S(1)} %get-tuple-element.37), channel_id=1, source_target_pairs={{4,0},{8,4},{12,8},{16,12},{20,16},{24,20},{28,24},{5,1},{9,5},{13... | collective-permute-start | bytes 393224 | tf_op jit(solution)/shard_map/ppermute | solution.py:442
  21.8 3.2 %collective-permute-start.5 = (f32[64,128]{1,0:T(8,128)S(1)}, f32[64,128]{1,0:T(8,128)S(1)}, u32[]{:S(2)}, u32[]{:S(2)}) collective-permute-start(f32[64,128]{1,0:T(8,128)S(1)} %get-tuple-element.38), channel_id=1, source_target_pairs={{0,1},{2,3},{1,0},{3,2},{4,5},{6,7},{5,4},{7,6},{8,9},{10,11},{9,8... | collective-permute-start | bytes 98312 | tf_op jit(solution)/shard_map/ppermute | solution.py:443

commit v17 on v16

--- a/solution.py
+++ b/solution.py
@@ -209,7 +209,7 @@
 
 def column_kernel(outward, alone, near, turned, w, live, index, tapers, flipped, side):
     place = lax.axis_index("col")
-    here = jnp.logical_or(place == 0, place == lax.axis_size("col") - 1)
+    here = jnp.logical_and(place == lax.axis_size("col") - 1, jnp.logical_not(even_column()))
     here = here if alone else jnp.logical_not(here)
 
     @pl.when(here)

time: 27.3 us -> 27.3 us (level)
  no operation moved by 1% of the time
where the time goes in v17:
time: 27.3 us; the launch traced here: 27 us
  starting transfers between devices  12.4 us (45%)
  Pallas kernels  9.81 us (36%)
  waiting for transfers between devices  4.64 us (17%)
    pallas_call x1, Pallas kernels, inner(): pl.pallas_call(inner_kernel, out_shape=(jax.ShapeDtypeStruct((rows, cols,...  3.88 us
    ppermute x1, starting transfers between devices, body(): s = lax.ppermute(packed, 'row', forward('row'))  3.56 us
    ppermute x1, starting transfers between devices, body(): lax.ppermute(pack_rest(w, outside, u.shape[2]), 'row', forward('row'))  3.43 us
    ppermute x1, starting transfers between devices, body(): back = lax.ppermute(back, 'row', backward('row'))  3.31 us
    ppermute x1, waiting for transfers between devices, body(): outside = lax.ppermute(outer_side, 'col', swaps('col', 1))  2.67 us
    ppermute x1, starting transfers between devices, body(): outside = lax.ppermute(outer_side, 'col', swaps('col', 1))  1.92 us
    pallas_call x1, Pallas kernels, outer(): pl.pallas_call(outer_kernel, out_shape=(jax.ShapeDtypeStruct(inc.shape, i...  1.58 us
    pallas_call x3, Pallas kernels, column(): pl.pallas_call(functools.partial(column_kernel, outward, alone), out_shap...  1.54 us
  transfers between devices with their start and end apart: 6, of which 3 were waited for; matrix products, arithmetic and copies ran while one was open for 0% of the time, Pallas kernels for 29%

profile of v17, /device:TPU:22, one launch (start us, length us, event | category | flops | bytes accessed | tf_op | source)
XLA Modules:
  0.0 27.0 jit_solution(3183105625305232325)
XLA Ops:
  0.0 0.0 copy-start.1
  0.0 0.0 copy-start
  0.0 0.0 copy-start.3
  0.0 0.0 copy-start.4
  0.0 1.2 %pack_row.1.packed = bf16[2112,128]{1,0:T(8,128)(2,1)S(1)} custom-call(bf16[4,8,256,128]{3,2,1,0:T(8,128)(2,1)} %u.7, bf16[4,8,64,128]{3,2,1,0:T(8,128)(2,1)} %w.15), custom_call_target="tpu_custom_call" | custom-call | bytes 1081344 | tf_op jit(solution)/shard_map/pack_row/pallas_call | solution.py:361
  1.2 0.0 copy-start.2
  1.3 3.6 %collective-permute-start.2 = (bf16[2112,128]{1,0:T(8,128)(2,1)S(1)}, bf16[2112,128]{1,0:T(8,128)(2,1)S(1)}, u32[]{:S(2)}, u32[]{:S(2)}) collective-permute-start(bf16[2112,128]{1,0:T(8,128)(2,1)S(1)} %pack_row.1.packed), channel_id=1, source_target_pairs={{0,4},{4,8},{8,12},{12,16},{16,20},{20,24},{24,28},{1,5},{5,9},{9,... | collective-permute-start | bytes 1622024 | tf_op jit(solution)/shard_map/ppermute | solution.py:432
  4.8 0.0 copy-done.1
  4.8 0.0 copy-done
  4.8 0.0 copy-done.3
  4.8 0.0 copy-done.4
  4.9 0.1 pack_columns.1
  5.0 1.9 %collective-permute-start = (bf16[4,336,128]{2,1,0:T(8,128)(2,1)S(1)}, bf16[4,336,128]{2,1,0:T(8,128)(2,1)S(1)}, u32[]{:S(2)}, u32[]{:S(2)}) collective-permute-start(bf16[4,336,128]{2,1,0:T(8,128)(2,1)S(1)} %get-tuple-element.23), channel_id=1, source_target_pairs={{1,2},{2,1},{5,6},{6,5},{9,10},{10,9},{13,14},{14,13},{17,18},{18,... | collective-permute-start | bytes 1032200 | tf_op jit(solution)/shard_map/ppermute | solution.py:434
  6.9 0.1 collective-permute-start.1
  7.0 0.0 copy-done.2
  7.0 3.9 %inner.1 = (f32[4,8,64,128]{3,2,1,0:T(8,128)S(1)}, bf16[4,8,128,256]{3,2,1,0:T(8,128)(2,1)S(1)}, bf16[16,128,128]{2,1,0:T(8,128)(2,1)S(1)}) custom-call(bf16[4,8,256,128]{3,2,1,0:T(8,128)(2,1)S(1)} %copy-done.1, bf16[4,8,64,128]{3,2,1,0:T(8,128)(2,1)S(1)} %copy-done, s32[4,8,9]{2,1,0:T(8,128)S(1)} %copy-done.3, s32[4,8,9]{2,1,0:T(8,128)S(1)} %copy-done.4, ...), custom_call_target="tpu_custom_call" | custom-call | flops 2013265920 | bytes 4194304 | tf_op jit(solution)/shard_map/inner/pallas_call | solution.py:100
  10.9 2.7 %collective-permute-done.near.outside = bf16[4,336,128]{2,1,0:T(8,128)(2,1)S(1)} collective-permute-done((bf16[4,336,128]{2,1,0:T(8,128)(2,1)S(1)}, bf16[4,336,128]{2,1,0:T(8,128)(2,1)S(1)}, u32[]{:S(2)}, u32[]{:S(2)}) %collective-permute-start) | collective-permute-done | bytes 344096 | tf_op jit(solution)/shard_map/ppermute | solution.py:434
  13.6 0.0 collective-permute-done.1.near.inside
  13.6 3.4 %collective-permute-start.3 = (bf16[768,128]{1,0:T(8,128)(2,1)S(1)}, bf16[768,128]{1,0:T(8,128)(2,1)S(1)}, u32[]{:S(2)}, u32[]{:S(2)}) collective-permute-start(bf16[768,128]{1,0:T(8,128)(2,1)S(1)} %pack_rest.1), channel_id=1, source_target_pairs={{0,4},{4,8},{8,12},{12,16},{16,20},{20,24},{24,28},{1,5},{5,9},{9,... | collective-permute-start | bytes 589832 | tf_op jit(solution)/shard_map/ppermute | solution.py:440
  17.1 0.7 %collective-permute-done.2.s = bf16[2112,128]{1,0:T(8,128)(2,1)S(1)} collective-permute-done((bf16[2112,128]{1,0:T(8,128)(2,1)S(1)}, bf16[2112,128]{1,0:T(8,128)(2,1)S(1)}, u32[]{:S(2)}, u32[]{:S(2)}) %collective-permute-start.2) | collective-permute-done | bytes 540704 | tf_op jit(solution)/shard_map/ppermute | solution.py:432
  17.8 0.7 %above.1 = (bf16[8,64,128]{2,1,0:T(8,128)(2,1)S(1)}, bf16[8,128,384]{2,1,0:T(8,128)(2,1)S(1)}, f32[64,128]{1,0:T(8,128)S(1)}, bf16[64,128]{1,0:T(8,128)(2,1)S(1)}) custom-call(bf16[2112,128]{1,0:T(8,128)(2,1)S(1)} %collective-permute-done.2.s, bf16[4,8,128,256]{3,2,1,0:T(8,128)(2,1)S(1)} %get-tuple-element.27.turned, bf16[4,8,64,128]{3,2,1,0:T(8,128)(2,1)S(1)} %copy-done, ...), custom_call_target="tpu_custom_call" | custom-call | flops 251658240 | bytes 2097152 | tf_op jit(solution)/shard_map/above/pallas_call | solution.py:165
  18.5 3.3 %collective-permute-start.4 = (bf16[8,64,128]{2,1,0:T(8,128)(2,1)S(1)}, bf16[8,64,128]{2,1,0:T(8,128)(2,1)S(1)}, u32[]{:S(2)}, u32[]{:S(2)}) collective-permute-start(bf16[8,64,128]{2,1,0:T(8,128)(2,1)S(1)} %get-tuple-element.37), channel_id=1, source_target_pairs={{4,0},{8,4},{12,8},{16,12},{20,16},{24,20},{28,24},{5,1},{9,5},{13... | collective-permute-start | bytes 393224 | tf_op jit(solution)/shard_map/ppermute | solution.py:442
  21.8 0.1 collective-permute-start.5
  21.9 0.8 %column.5.far_side = f32[4,64,128]{2,1,0:T(8,128)S(1)} custom-call(bf16[4,336,128]{2,1,0:T(8,128)(2,1)S(1)} %collective-permute-done.near.outside, bf16[4,8,128,256]{3,2,1,0:T(8,128)(2,1)S(1)} %get-tuple-element.27.turned, bf16[4,8,64,128]{3,2,1,0:T(8,128)(2,1)S(1)} %copy-done, s32[4,8,9]{2,1,0:T(8,128)S(1)} %copy-done.3, s32[4,8,9]{2,1,0:T(8,128)S(1)} %copy-done.4, ...), custom_call_target="tpu_custom_call" | custom-call | flops 125829120 | bytes 2097152 | tf_op jit(solution)/shard_map/column/pallas_call | solution.py:227
  22.6 0.8 %column.4.more_side = f32[4,64,128]{2,1,0:T(8,128)S(1)} custom-call(bf16[4,336,128]{2,1,0:T(8,128)(2,1)S(1)} %collective-permute-done.1.near.inside, bf16[4,8,128,256]{3,2,1,0:T(8,128)(2,1)S(1)} %get-tuple-element.27.turned, bf16[4,8,64,128]{3,2,1,0:T(8,128)(2,1)S(1)} %copy-done, s32[4,8,9]{2,1,0:T(8,128)S(1)} %copy-done.3, s32[4,8,9]{2,1,0:T(8,128)S(1)} %copy-done.4, ...), custom_call_target="tpu_custom_call" | custom-call | flops 125829120 | bytes 2097152 | tf_op jit(solution)/shard_map/column/pallas_call | solution.py:227
  23.4 0.0 collective-permute-done.3.rest
  23.4 1.6 %outer.1 = (f32[4,8,64,128]{3,2,1,0:T(8,128)}, f32[2,64,128]{2,1,0:T(8,128)S(1)}, f32[8,64,128]{2,1,0:T(8,128)S(1)}) custom-call(f32[4,8,64,128]{3,2,1,0:T(8,128)S(1)} %get-tuple-element.25.inc, f32[4,64,128]{2,1,0:T(8,128)S(1)} %column.3.near_side, f32[4,64,128]{2,1,0:T(8,128)S(1)} %column.4.more_side, f32[4,64,128]{2,1,0:T(8,128)S(1)} %column.5.far_side, ...), custom_call_target="tpu_custom_call" | custom-call | flops 50331648 | bytes 4194304 | tf_op jit(solution)/shard_map/outer/pallas_call | solution.py:281
  25.0 0.0 collective-permute-done.5.from_inside
  25.0 1.2 %collective-permute-done.4.back = bf16[8,64,128]{2,1,0:T(8,128)(2,1)S(1)} collective-permute-done((bf16[8,64,128]{2,1,0:T(8,128)(2,1)S(1)}, bf16[8,64,128]{2,1,0:T(8,128)(2,1)S(1)}, u32[]{:S(2)}, u32[]{:S(2)}) %collective-permute-start.4) | collective-permute-done | bytes 131104 | tf_op jit(solution)/shard_map/ppermute | solution.py:442
  26.2 0.7 %finish.1 = f32[4,8,64,128]{3,2,1,0:T(8,128)} custom-call(f32[4,8,64,128]{3,2,1,0:T(8,128)} %get-tuple-element.34.inc, f32[2,64,128]{2,1,0:T(8,128)S(1)} %get-tuple-element.35.top, f32[8,64,128]{2,1,0:T(8,128)S(1)} %get-tuple-element.36.low, bf16[8,64,128]{2,1,0:T(8,128)(2,1)S(1)} %collective-permute-done.4.back, ...), custom_call_target="tpu_custom_call", output_to_operand_aliasing={{}: (0, {})} | custom-call | flops 65536 | bytes 655360 | tf_op jit(solution)/shard_map/finish/pallas_call | solution.py:314
  (2 shorter events, 0.0 us)
Async XLA Ops:
  0.0 4.8 %copy-start.1 = (bf16[4,8,256,128]{3,2,1,0:T(8,128)(2,1)S(1)}, bf16[4,8,256,128]{3,2,1,0:T(8,128)(2,1)}, u32[]{:S(2)}) copy-start(bf16[4,8,256,128]{3,2,1,0:T(8,128)(2,1)} %u.7) | copy-start | bytes 6291460
  0.0 4.8 %copy-start = (bf16[4,8,64,128]{3,2,1,0:T(8,128)(2,1)S(1)}, bf16[4,8,64,128]{3,2,1,0:T(8,128)(2,1)}, u32[]{:S(2)}) copy-start(bf16[4,8,64,128]{3,2,1,0:T(8,128)(2,1)} %w.15) | copy-start | bytes 1572868
  0.0 4.8 %copy-start.3 = (s32[4,8,9]{2,1,0:T(8,128)S(1)}, s32[4,8,9]{2,1,0:T(8,128)}, u32[]{:S(2)}) copy-start(s32[4,8,9]{2,1,0:T(8,128)} %live.13) | copy-start | bytes 3460
  0.0 4.8 %copy-start.4 = (s32[4,8,9]{2,1,0:T(8,128)S(1)}, s32[4,8,9]{2,1,0:T(8,128)}, u32[]{:S(2)}) copy-start(s32[4,8,9]{2,1,0:T(8,128)} %index.13) | copy-start | bytes 3460
  1.2 5.8 %copy-start.2 = (bf16[16,128,128]{2,1,0:T(8,128)(2,1)S(1)}, bf16[16,128,128]{2,1,0:T(8,128)(2,1)}, u32[]{:S(2)}) copy-start(bf16[16,128,128]{2,1,0:T(8,128)(2,1)} %tapers.9) | copy-start | bytes 1572868
  1.3 16.5 %collective-permute-start.2 = (bf16[2112,128]{1,0:T(8,128)(2,1)S(1)}, bf16[2112,128]{1,0:T(8,128)(2,1)S(1)}, u32[]{:S(2)}, u32[]{:S(2)}) collective-permute-start(bf16[2112,128]{1,0:T(8,128)(2,1)S(1)} %pack_row.1.packed), channel_id=1, source_target_pairs={{0,4},{4,8},{8,12},{12,16},{16,20},{20,24},{24,28},{1,5},{5,9},{9,... | collective-permute-start | bytes 1622024 | tf_op jit(solution)/shard_map/ppermute | solution.py:432
  5.0 8.6 %collective-permute-start = (bf16[4,336,128]{2,1,0:T(8,128)(2,1)S(1)}, bf16[4,336,128]{2,1,0:T(8,128)(2,1)S(1)}, u32[]{:S(2)}, u32[]{:S(2)}) collective-permute-start(bf16[4,336,128]{2,1,0:T(8,128)(2,1)S(1)} %get-tuple-element.23), channel_id=1, source_target_pairs={{1,2},{2,1},{5,6},{6,5},{9,10},{10,9},{13,14},{14,13},{17,18},{18,... | collective-permute-start | bytes 1032200 | tf_op jit(solution)/shard_map/ppermute | solution.py:434
  6.9 6.6 %collective-permute-start.1 = (bf16[4,336,128]{2,1,0:T(8,128)(2,1)S(1)}, bf16[4,336,128]{2,1,0:T(8,128)(2,1)S(1)}, u32[]{:S(2)}, u32[]{:S(2)}) collective-permute-start(bf16[4,336,128]{2,1,0:T(8,128)(2,1)S(1)} %get-tuple-element.24), channel_id=1, source_target_pairs={{0,1},{2,3},{1,0},{3,2},{4,5},{6,7},{5,4},{7,6},{8,9},{10,11},{9,8... | collective-permute-start | bytes 1032200 | tf_op jit(solution)/shard_map/ppermute | solution.py:435
  13.6 9.8 %collective-permute-start.3 = (bf16[768,128]{1,0:T(8,128)(2,1)S(1)}, bf16[768,128]{1,0:T(8,128)(2,1)S(1)}, u32[]{:S(2)}, u32[]{:S(2)}) collective-permute-start(bf16[768,128]{1,0:T(8,128)(2,1)S(1)} %pack_rest.1), channel_id=1, source_target_pairs={{0,4},{4,8},{8,12},{12,16},{16,20},{20,24},{24,28},{1,5},{5,9},{9,... | collective-permute-start | bytes 589832 | tf_op jit(solution)/shard_map/ppermute | solution.py:440
  18.5 7.8 %collective-permute-start.4 = (bf16[8,64,128]{2,1,0:T(8,128)(2,1)S(1)}, bf16[8,64,128]{2,1,0:T(8,128)(2,1)S(1)}, u32[]{:S(2)}, u32[]{:S(2)}) collective-permute-start(bf16[8,64,128]{2,1,0:T(8,128)(2,1)S(1)} %get-tuple-element.37), channel_id=1, source_target_pairs={{4,0},{8,4},{12,8},{16,12},{20,16},{24,20},{28,24},{5,1},{9,5},{13... | collective-permute-start | bytes 393224 | tf_op jit(solution)/shard_map/ppermute | solution.py:442
  21.8 3.2 %collective-permute-start.5 = (f32[64,128]{1,0:T(8,128)S(1)}, f32[64,128]{1,0:T(8,128)S(1)}, u32[]{:S(2)}, u32[]{:S(2)}) collective-permute-start(f32[64,128]{1,0:T(8,128)S(1)} %get-tuple-element.38), channel_id=1, source_target_pairs={{0,1},{2,3},{1,0},{3,2},{4,5},{6,7},{5,4},{7,6},{8,9},{10,11},{9,8... | collective-permute-start | bytes 98312 | tf_op jit(solution)/shard_map/ppermute | solution.py:443

commit v18 on v12

--- a/solution.py
+++ b/solution.py
@@ -353,8 +353,10 @@
     rows, cols, members, cells = u.shape
     beside = (cols - 1) * even_column().astype(jnp.int32)
     deep = cols * members
+    half = cols // 2 * members
     copies = [
-        pltpu.make_async_copy(u.at[rows - 1].reshape(deep, cells), out.at[:deep], sem.at[0]),
+        pltpu.make_async_copy(u.at[rows - 1, : cols // 2].reshape(half, cells), out.at[:half], sem.at[0]),
+        pltpu.make_async_copy(u.at[rows - 1, cols // 2 :].reshape(deep - half, cells), out.at[half:deep], sem.at[2]),
         pltpu.make_async_copy(w.at[rows - 1, beside], out.at[deep:], sem.at[1]),
     ]
     for copy in copies:
@@ -371,7 +373,7 @@
         out_shape=pltpu.VMEM(shape, u.dtype),
         in_specs=[HBM, HBM],
         out_specs=VMEM,
-        scratch_shapes=[pltpu.SemaphoreType.DMA((2,))],
+        scratch_shapes=[pltpu.SemaphoreType.DMA((3,))],
         cost_estimate=pl.CostEstimate(flops=0, bytes_accessed=4 * shape[0] * cells, transcendentals=0),
         name="pack_row",
     )(u, w)

time: 27.3 us -> 27.3 us (level)
  no operation moved by 1% of the time
where the time goes in v18:
time: 27.3 us; the launch traced here: 26.8 us
  starting transfers between devices  12.4 us (45%)
  Pallas kernels  10.7 us (39%)
  waiting for transfers between devices  3.6 us (13%)
    pallas_call x1, Pallas kernels, inner(): pl.pallas_call(inner_kernel, out_shape=(jax.ShapeDtypeStruct((rows, cols,...  4.82 us
    ppermute x1, starting transfers between devices, body(): s = lax.ppermute(packed, 'row', forward('row'))  3.56 us
    ppermute x1, starting transfers between devices, body(): lax.ppermute(pack_rest(w, outside, u.shape[2]), 'row', forward('row'))  3.43 us
    ppermute x1, starting transfers between devices, body(): back = lax.ppermute(back, 'row', backward('row'))  3.31 us
    ppermute x1, starting transfers between devices, body(): outside = lax.ppermute(outer_side, 'col', swaps('col', 1))  1.92 us
    ppermute x1, waiting for transfers between devices, body(): outside = lax.ppermute(outer_side, 'col', swaps('col', 1))  1.72 us
    pallas_call x1, Pallas kernels, outer(): pl.pallas_call(outer_kernel, out_shape=(jax.ShapeDtypeStruct(inc.shape, i...  1.57 us
    pallas_call x1, Pallas kernels, columns(): pl.pallas_call(columns_kernel, out_shape=jax.ShapeDtypeStruct((2, rows, w...  1.49 us
  transfers between devices with their start and end apart: 6, of which 3 were waited for; matrix products, arithmetic and copies ran while one was open for 0% of the time, Pallas kernels for 33%

profile of v18, /device:TPU:22, one launch (start us, length us, event | category | flops | bytes accessed | tf_op | source)
XLA Modules:
  0.0 26.8 jit_solution(737987793155552438)
XLA Ops:
  0.0 0.0 copy-start.1
  0.0 0.0 copy-start
  0.0 0.0 copy-start.4
  0.0 0.0 copy-start.3
  0.0 1.2 %pack_row.1.packed = bf16[2112,128]{1,0:T(8,128)(2,1)S(1)} custom-call(bf16[4,8,256,128]{3,2,1,0:T(8,128)(2,1)} %u.9, bf16[4,8,64,128]{3,2,1,0:T(8,128)(2,1)} %w.11), custom_call_target="tpu_custom_call" | custom-call | bytes 1081344 | tf_op jit(solution)/shard_map/pack_row/pallas_call | solution.py:371
  1.2 0.0 copy-start.2
  1.2 3.6 %collective-permute-start.2 = (bf16[2112,128]{1,0:T(8,128)(2,1)S(1)}, bf16[2112,128]{1,0:T(8,128)(2,1)S(1)}, u32[]{:S(2)}, u32[]{:S(2)}) collective-permute-start(bf16[2112,128]{1,0:T(8,128)(2,1)S(1)} %pack_row.1.packed), channel_id=1, source_target_pairs={{0,4},{4,8},{8,12},{12,16},{16,20},{20,24},{24,28},{1,5},{5,9},{9,... | collective-permute-start | bytes 1622024 | tf_op jit(solution)/shard_map/ppermute | solution.py:442
  4.8 0.0 copy-done.1
  4.8 0.0 copy-done
  4.8 0.0 copy-done.4
  4.8 0.0 copy-done.3
  4.9 0.1 pack_columns.1
  5.0 1.9 %collective-permute-start = (bf16[4,336,128]{2,1,0:T(8,128)(2,1)S(1)}, bf16[4,336,128]{2,1,0:T(8,128)(2,1)S(1)}, u32[]{:S(2)}, u32[]{:S(2)}) collective-permute-start(bf16[4,336,128]{2,1,0:T(8,128)(2,1)S(1)} %get-tuple-element.21), channel_id=1, source_target_pairs={{1,2},{2,1},{5,6},{6,5},{9,10},{10,9},{13,14},{14,13},{17,18},{18,... | collective-permute-start | bytes 1032200 | tf_op jit(solution)/shard_map/ppermute | solution.py:444
  6.9 0.1 collective-permute-start.1
  7.0 0.0 copy-done.2
  7.0 4.8 %inner.1 = (f32[4,8,64,128]{3,2,1,0:T(8,128)S(1)}, bf16[4,8,128,256]{3,2,1,0:T(8,128)(2,1)S(1)}, bf16[16,128,128]{2,1,0:T(8,128)(2,1)S(1)}) custom-call(bf16[4,8,256,128]{3,2,1,0:T(8,128)(2,1)S(1)} %copy-done, bf16[4,8,64,128]{3,2,1,0:T(8,128)(2,1)S(1)} %copy-done.1, s32[4,8,9]{2,1,0:T(8,128)S(1)} %copy-done.3, s32[4,8,9]{2,1,0:T(8,128)S(1)} %copy-done.4, ...), custom_call_target="tpu_custom_call" | custom-call | flops 2013265920 | bytes 4194304 | tf_op jit(solution)/shard_map/inner/pallas_call | solution.py:105
  11.9 1.7 %collective-permute-done.outside = bf16[4,336,128]{2,1,0:T(8,128)(2,1)S(1)} collective-permute-done((bf16[4,336,128]{2,1,0:T(8,128)(2,1)S(1)}, bf16[4,336,128]{2,1,0:T(8,128)(2,1)S(1)}, u32[]{:S(2)}, u32[]{:S(2)}) %collective-permute-start) | collective-permute-done | bytes 344096 | tf_op jit(solution)/shard_map/ppermute | solution.py:444
  13.6 0.0 collective-permute-done.1.inside
  13.6 3.4 %collective-permute-start.3 = (bf16[768,128]{1,0:T(8,128)(2,1)S(1)}, bf16[768,128]{1,0:T(8,128)(2,1)S(1)}, u32[]{:S(2)}, u32[]{:S(2)}) collective-permute-start(bf16[768,128]{1,0:T(8,128)(2,1)S(1)} %pack_rest.1), channel_id=1, source_target_pairs={{0,4},{4,8},{8,12},{12,16},{16,20},{20,24},{24,28},{1,5},{5,9},{9,... | collective-permute-start | bytes 589832 | tf_op jit(solution)/shard_map/ppermute | solution.py:448
  17.0 0.6 %collective-permute-done.2.s = bf16[2112,128]{1,0:T(8,128)(2,1)S(1)} collective-permute-done((bf16[2112,128]{1,0:T(8,128)(2,1)S(1)}, bf16[2112,128]{1,0:T(8,128)(2,1)S(1)}, u32[]{:S(2)}, u32[]{:S(2)}) %collective-permute-start.2) | collective-permute-done | bytes 540704 | tf_op jit(solution)/shard_map/ppermute | solution.py:442
  17.6 0.7 %above.1 = (bf16[8,64,128]{2,1,0:T(8,128)(2,1)S(1)}, bf16[8,128,384]{2,1,0:T(8,128)(2,1)S(1)}, f32[64,128]{1,0:T(8,128)S(1)}, bf16[64,128]{1,0:T(8,128)(2,1)S(1)}) custom-call(bf16[2112,128]{1,0:T(8,128)(2,1)S(1)} %collective-permute-done.2.s, bf16[4,8,128,256]{3,2,1,0:T(8,128)(2,1)S(1)} %get-tuple-element.26.turned, bf16[4,8,64,128]{3,2,1,0:T(8,128)(2,1)S(1)} %copy-done.1, ...), custom_call_target="tpu_custom_call" | custom-call | flops 251658240 | bytes 2097152 | tf_op jit(solution)/shard_map/above/pallas_call | solution.py:170
  18.3 3.3 %collective-permute-start.4 = (bf16[8,64,128]{2,1,0:T(8,128)(2,1)S(1)}, bf16[8,64,128]{2,1,0:T(8,128)(2,1)S(1)}, u32[]{:S(2)}, u32[]{:S(2)}) collective-permute-start(bf16[8,64,128]{2,1,0:T(8,128)(2,1)S(1)} %get-tuple-element.33), channel_id=1, source_target_pairs={{4,0},{8,4},{12,8},{16,12},{20,16},{24,20},{28,24},{5,1},{9,5},{13... | collective-permute-start | bytes 393224 | tf_op jit(solution)/shard_map/ppermute | solution.py:450
  21.6 0.1 collective-permute-start.5
  21.7 1.5 %columns.1.side = f32[2,4,64,128]{3,2,1,0:T(8,128)S(1)} custom-call(bf16[4,8,256,128]{3,2,1,0:T(8,128)(2,1)S(1)} %copy-done, bf16[4,8,64,128]{3,2,1,0:T(8,128)(2,1)S(1)} %copy-done.1, bf16[4,336,128]{2,1,0:T(8,128)(2,1)S(1)} %collective-permute-done.1.inside, bf16[4,336,128]{2,1,0:T(8,128)(2,1)S(1)} %collective-permute-done.outside, ...), custom_call_target="tpu_custom_call" | custom-call | flops 251658240 | bytes 2097152 | tf_op jit(solution)/shard_map/columns/pallas_call | solution.py:240
  23.2 0.0 collective-permute-done.3.rest
  23.2 1.6 %outer.1 = (f32[4,8,64,128]{3,2,1,0:T(8,128)}, f32[2,64,128]{2,1,0:T(8,128)S(1)}, f32[8,64,128]{2,1,0:T(8,128)S(1)}) custom-call(f32[4,8,64,128]{3,2,1,0:T(8,128)S(1)} %get-tuple-element.23.inc, f32[2,4,64,128]{3,2,1,0:T(8,128)S(1)} %columns.1.side, bf16[8,128,384]{2,1,0:T(8,128)(2,1)S(1)} %get-tuple-element.28.held, ...), custom_call_target="tpu_custom_call" | custom-call | flops 50331648 | bytes 4194304 | tf_op jit(solution)/shard_map/outer/pallas_call | solution.py:289
  24.8 0.0 collective-permute-done.5.from_inside
  24.8 1.3 %collective-permute-done.4.back = bf16[8,64,128]{2,1,0:T(8,128)(2,1)S(1)} collective-permute-done((bf16[8,64,128]{2,1,0:T(8,128)(2,1)S(1)}, bf16[8,64,128]{2,1,0:T(8,128)(2,1)S(1)}, u32[]{:S(2)}, u32[]{:S(2)}) %collective-permute-start.4) | collective-permute-done | bytes 131104 | tf_op jit(solution)/shard_map/ppermute | solution.py:450
  26.1 0.7 %finish.1 = f32[4,8,64,128]{3,2,1,0:T(8,128)} custom-call(f32[4,8,64,128]{3,2,1,0:T(8,128)} %get-tuple-element.30.inc, f32[2,64,128]{2,1,0:T(8,128)S(1)} %get-tuple-element.31.top, f32[8,64,128]{2,1,0:T(8,128)S(1)} %get-tuple-element.32.low, bf16[8,64,128]{2,1,0:T(8,128)(2,1)S(1)} %collective-permute-done.4.back, ...), custom_call_target="tpu_custom_call", output_to_operand_aliasing={{}: (0, {})} | custom-call | flops 65536 | bytes 655360 | tf_op jit(solution)/shard_map/finish/pallas_call | solution.py:322
  (1 shorter events, 0.0 us)
Async XLA Ops:
  0.0 4.8 %copy-start.1 = (bf16[4,8,64,128]{3,2,1,0:T(8,128)(2,1)S(1)}, bf16[4,8,64,128]{3,2,1,0:T(8,128)(2,1)}, u32[]{:S(2)}) copy-start(bf16[4,8,64,128]{3,2,1,0:T(8,128)(2,1)} %w.11) | copy-start | bytes 1572868
  0.0 4.8 %copy-start = (bf16[4,8,256,128]{3,2,1,0:T(8,128)(2,1)S(1)}, bf16[4,8,256,128]{3,2,1,0:T(8,128)(2,1)}, u32[]{:S(2)}) copy-start(bf16[4,8,256,128]{3,2,1,0:T(8,128)(2,1)} %u.9) | copy-start | bytes 6291460
  0.0 4.8 %copy-start.4 = (s32[4,8,9]{2,1,0:T(8,128)S(1)}, s32[4,8,9]{2,1,0:T(8,128)}, u32[]{:S(2)}) copy-start(s32[4,8,9]{2,1,0:T(8,128)} %index.9) | copy-start | bytes 3460
  0.0 4.8 %copy-start.3 = (s32[4,8,9]{2,1,0:T(8,128)S(1)}, s32[4,8,9]{2,1,0:T(8,128)}, u32[]{:S(2)}) copy-start(s32[4,8,9]{2,1,0:T(8,128)} %live.9) | copy-start | bytes 3460
  1.2 5.8 %copy-start.2 = (bf16[16,128,128]{2,1,0:T(8,128)(2,1)S(1)}, bf16[16,128,128]{2,1,0:T(8,128)(2,1)}, u32[]{:S(2)}) copy-start(bf16[16,128,128]{2,1,0:T(8,128)(2,1)} %tapers.5) | copy-start | bytes 1572868
  1.2 16.4 %collective-permute-start.2 = (bf16[2112,128]{1,0:T(8,128)(2,1)S(1)}, bf16[2112,128]{1,0:T(8,128)(2,1)S(1)}, u32[]{:S(2)}, u32[]{:S(2)}) collective-permute-start(bf16[2112,128]{1,0:T(8,128)(2,1)S(1)} %pack_row.1.packed), channel_id=1, source_target_pairs={{0,4},{4,8},{8,12},{12,16},{16,20},{20,24},{24,28},{1,5},{5,9},{9,... | collective-permute-start | bytes 1622024 | tf_op jit(solution)/shard_map/ppermute | solution.py:442
  5.0 8.6 %collective-permute-start = (bf16[4,336,128]{2,1,0:T(8,128)(2,1)S(1)}, bf16[4,336,128]{2,1,0:T(8,128)(2,1)S(1)}, u32[]{:S(2)}, u32[]{:S(2)}) collective-permute-start(bf16[4,336,128]{2,1,0:T(8,128)(2,1)S(1)} %get-tuple-element.21), channel_id=1, source_target_pairs={{1,2},{2,1},{5,6},{6,5},{9,10},{10,9},{13,14},{14,13},{17,18},{18,... | collective-permute-start | bytes 1032200 | tf_op jit(solution)/shard_map/ppermute | solution.py:444
  6.9 6.6 %collective-permute-start.1 = (bf16[4,336,128]{2,1,0:T(8,128)(2,1)S(1)}, bf16[4,336,128]{2,1,0:T(8,128)(2,1)S(1)}, u32[]{:S(2)}, u32[]{:S(2)}) collective-permute-start(bf16[4,336,128]{2,1,0:T(8,128)(2,1)S(1)} %get-tuple-element.22), channel_id=1, source_target_pairs={{0,1},{2,3},{1,0},{3,2},{4,5},{6,7},{5,4},{7,6},{8,9},{10,11},{9,8... | collective-permute-start | bytes 1032200 | tf_op jit(solution)/shard_map/ppermute | solution.py:445
  13.6 9.6 %collective-permute-start.3 = (bf16[768,128]{1,0:T(8,128)(2,1)S(1)}, bf16[768,128]{1,0:T(8,128)(2,1)S(1)}, u32[]{:S(2)}, u32[]{:S(2)}) collective-permute-start(bf16[768,128]{1,0:T(8,128)(2,1)S(1)} %pack_rest.1), channel_id=1, source_target_pairs={{0,4},{4,8},{8,12},{12,16},{16,20},{20,24},{24,28},{1,5},{5,9},{9,... | collective-permute-start | bytes 589832 | tf_op jit(solution)/shard_map/ppermute | solution.py:448
  18.3 7.8 %collective-permute-start.4 = (bf16[8,64,128]{2,1,0:T(8,128)(2,1)S(1)}, bf16[8,64,128]{2,1,0:T(8,128)(2,1)S(1)}, u32[]{:S(2)}, u32[]{:S(2)}) collective-permute-start(bf16[8,64,128]{2,1,0:T(8,128)(2,1)S(1)} %get-tuple-element.33), channel_id=1, source_target_pairs={{4,0},{8,4},{12,8},{16,12},{20,16},{24,20},{28,24},{5,1},{9,5},{13... | collective-permute-start | bytes 393224 | tf_op jit(solution)/shard_map/ppermute | solution.py:450
  21.6 3.2 %collective-permute-start.5 = (f32[64,128]{1,0:T(8,128)S(1)}, f32[64,128]{1,0:T(8,128)S(1)}, u32[]{:S(2)}, u32[]{:S(2)}) collective-permute-start(f32[64,128]{1,0:T(8,128)S(1)} %get-tuple-element.34), channel_id=1, source_target_pairs={{0,1},{2,3},{1,0},{3,2},{4,5},{6,7},{5,4},{7,6},{8,9},{10,11},{9,8... | collective-permute-start | bytes 98312 | tf_op jit(solution)/shard_map/ppermute | solution.py:451
